TPU v7x, 128 devices: a whole 4x4x4 slice. The times are simulated.
128 devices in a mesh: px: 8 (over y, x_lo), py: 16 (over z, x_hi, core).
Axes of the slice: x: 4 (x_hi: 2, x_lo: 2; x = x_hi * 2 + x_lo), y: 4, z: 4, core: 2. Of those that a mesh axis runs over, the one named last changes fastest.
Arguments:
- initial: float32 [256, 1024, 128], P('px', 'py'), may hold values from -6 to 6
- conduct: float32 [256, 1024, 128], P('px', 'py'), may hold values from 0.25 to 1.5
- cotangent: float32 [256, 1024, 128], P('px', 'py'), may hold values from -6 to 6
- inv_x: float32 [256, 256], replicated, may hold values from -2 to 2, as said below
- inv_y: float32 [1024, 1024], replicated, may hold values from -2 to 2, as said below
Outputs:
- adjoint: float32 [256, 1024, 128], P('px', 'py')
- gradient: float32 [256, 1024, 128], P('px', 'py')
Inputs may be any that keep to these rules, and one draw needn't show every extreme that they name: `inv_x`: a dense matrix of order one. `inv_y`: a dense matrix of order one.
All inputs are finite; a program needn't handle non-finite values.
Results may differ from a plain program's by a relative error of at most 0.00013.
Values sent between devices are 32-bit elements; how exact they have to be, the bound alone decides.
A program may use at most 64 MiB of HBM per device.

v0:
```python
import jax
import jax.numpy as jnp
from jax import lax
from jax.sharding import PartitionSpec as P

RATE = 0.2
LINES = ("py", "px")
HIGH = lax.Precision.HIGH


def ydiff_block(field):
    count = lax.axis_size("py")
    below = lax.ppermute(field[:, -1:], "py", [(i, i + 1) for i in range(count - 1)])
    above = lax.ppermute(field[:, :1], "py", [(i + 1, i) for i in range(count - 1)])
    padded = jnp.concatenate([below, field, above], axis=1)
    return padded[:, 2:] + padded[:, :-2] - 2.0 * field


def zoperate_block(field, conduct):
    upper = jnp.concatenate([field[:, :, 1:], jnp.zeros_like(field[:, :, :1])], axis=2)
    flux = conduct * (upper - field)
    lower = jnp.concatenate([jnp.zeros_like(flux[:, :, :1]), flux[:, :, :-1]], axis=2)
    return flux - lower


def zstep_block(field):
    upper = jnp.concatenate([field[:, :, 1:], jnp.zeros_like(field[:, :, :1])], axis=2)
    return upper - field


def zstep(field):
    upper = jnp.concatenate([field[1:], jnp.zeros_like(field[:1])], axis=0)
    return upper - field


def zoperate(field, conduct):
    flux = conduct * zstep(field)
    lower = jnp.concatenate([jnp.zeros_like(flux[:1]), flux[:-1]], axis=0)
    return flux - lower


def xdiff(field):
    padded = jnp.pad(field, ((0, 0), (0, 0), (1, 1)))
    return padded[:, :, 2:] + padded[:, :, :-2] - 2.0 * field


def mesh_index(line):
    rows = lax.axis_size("px")
    cols = lax.axis_size("py")
    return (line % rows) * cols + line // rows


def ydiff(field):
    count = lax.axis_size(LINES)
    up = [(mesh_index(i), mesh_index(i + 1)) for i in range(count - 1)]
    down = [(b, a) for a, b in up]
    below = lax.ppermute(field[:, -1:], ("px", "py"), up)
    above = lax.ppermute(field[:, :1], ("px", "py"), down)
    padded = jnp.concatenate([below, field, above], axis=1)
    return padded[:, 2:] + padded[:, :-2] - 2.0 * field


def along_x(field, matrix, transpose):
    dims = (((2,), (0,)), ((), ())) if transpose else (((2,), (1,)), ((), ()))
    return lax.dot_general(field, matrix, dims, precision=HIGH)


def along_y(matrix, field, transpose):
    dims = (((0,), (0,)), ((), ())) if transpose else (((1,), (0,)), ((), ()))
    return lax.dot_general(matrix, field, dims, precision=HIGH)


def block_to_x(*fields):
    joined = jnp.concatenate(fields, axis=2)
    lines = lax.all_to_all(joined, "px", split_axis=1, concat_axis=0, tiled=True)
    depth = fields[0].shape[2]
    return [jnp.transpose(lines[:, :, k * depth:(k + 1) * depth], (2, 1, 0)) for k in range(len(fields))]


def x_to_block(*fields):
    joined = jnp.concatenate([jnp.transpose(f, (2, 1, 0)) for f in fields], axis=2)
    block = lax.all_to_all(joined, "px", split_axis=0, concat_axis=1, tiled=True)
    depth = fields[0].shape[0]
    return [block[:, :, k * depth:(k + 1) * depth] for k in range(len(fields))]


def x_to_y(*fields):
    joined = jnp.concatenate(fields, axis=2)
    lines = lax.all_to_all(joined, LINES, split_axis=0, concat_axis=0, tiled=True)
    lines = lines.reshape(-1, lines.shape[2])
    width = fields[0].shape[2]
    return [lines[:, k * width:(k + 1) * width] for k in range(len(fields))]


def y_to_x(*fields):
    joined = jnp.concatenate(fields, axis=1)
    count = lax.axis_size(LINES)
    joined = joined.reshape(count, -1, joined.shape[1])
    lines = lax.all_to_all(joined, LINES, split_axis=0, concat_axis=0, tiled=True)
    width = fields[0].shape[1]
    return [lines[:, :, k * width:(k + 1) * width] for k in range(len(fields))]


def block_planes(field):
    count = lax.axis_size(LINES)
    planes = jnp.transpose(field, (2, 1, 0))
    return planes.reshape(count, -1, field.shape[0] * field.shape[1] * field.shape[2] // count // 8)


def planes_to_y(pieces, block):
    rows = lax.axis_size("px")
    cols = lax.axis_size("py")
    depth, width = block[0], block[1]
    tiles = pieces.reshape(cols, rows, width, depth)
    return jnp.transpose(tiles, (0, 2, 1, 3)).reshape(cols * width, rows * depth)


def local(initial, conduct, cotangent, inv_x, inv_y):
    first0 = initial + RATE * (ydiff_block(initial) + zoperate_block(initial, conduct))
    f0x, cx = block_to_x(first0, conduct)
    half0 = along_x(f0x, inv_x, False)
    second0 = half0 + RATE * (xdiff(half0) + zoperate(half0, cx))
    s0y, tp = x_to_y(second0, block_planes(cotangent))
    ty = planes_to_y(tp, (initial.shape[0], initial.shape[1]))
    state1_y = along_y(inv_y, s0y, False)
    lam_second1_y = along_y(inv_y, ty, True)
    state1, ls1 = y_to_x(state1_y, lam_second1_y)
    first1 = state1 + RATE * (ydiff(state1) + zoperate(state1, cx))
    half1 = along_x(first1, inv_x, False)
    grad = -RATE * zstep(ls1) * zstep(half1)
    lam_half1 = ls1 + RATE * (xdiff(ls1) + zoperate(ls1, cx))
    lam_first1 = along_x(lam_half1, inv_x, True)
    grad = grad - RATE * zstep(lam_first1) * zstep(state1)
    lam_state1 = lam_first1 + RATE * (ydiff(lam_first1) + zoperate(lam_first1, cx))
    (lsy,) = x_to_y(lam_state1)
    lam_second0_y = along_y(inv_y, lsy, True)
    (ls0,) = y_to_x(lam_second0_y)
    grad = grad - RATE * zstep(ls0) * zstep(half0)
    lam_half0 = ls0 + RATE * (xdiff(ls0) + zoperate(ls0, cx))
    lam_first0 = along_x(lam_half0, inv_x, True)
    lf0, gb = x_to_block(lam_first0, grad)
    gradient = gb - RATE * zstep_block(lf0) * zstep_block(initial)
    adjoint = lf0 + RATE * (ydiff_block(lf0) + zoperate_block(lf0, conduct))
    return (adjoint, gradient)


def solution(mesh):
    in_specs = (P("px", "py", None), P("px", "py", None), P("px", "py", None), P(), P())
    out_specs = (P("px", "py", None), P("px", "py", None))
    return jax.shard_map(local, mesh=mesh, in_specs=in_specs, out_specs=out_specs, check_vma=False)
```

profile of v0, /device:TPU:1, one launch (start us, length us, event | category | flops | bytes accessed | tf_op | source)
XLA Modules:
  0.0 279.8 jit_solution(407249772962394302)
XLA Ops:
  1.8 3.3 %collective-permute-start = (f32[32,1,128]{2,1,0:T(1,128)S(1)}, f32[32,1,128]{2,1,0:T(1,128)S(1)}, u32[]{:S(2)}, u32[]{:S(2)}) collective-permute-start(f32[32,1,128]{2,1,0:T(1,128)S(1)} %get-tuple-element.24), channel_id=1, source_target_pairs={{1,0},{2,1},{3,2},{4,3},{5,4},{6,5},{7,6},{8,7},{9,8},{10,9},{11,1... | collective-permute-start | bytes 49160 | tf_op jit(solution)/shard_map/ppermute | solution.py:14
  5.2 4.6 %collective-permute-start.1 = (f32[32,1,128]{2,1,0:T(1,128)S(1)}, f32[32,1,128]{2,1,0:T(1,128)S(1)}, u32[]{:S(2)}, u32[]{:S(2)}) collective-permute-start(f32[32,1,128]{2,1,0:T(1,128)S(1)} %get-tuple-element.25), channel_id=1, source_target_pairs={{0,1},{1,2},{2,3},{3,4},{4,5},{5,6},{6,7},{7,8},{8,9},{9,10},{10,1... | collective-permute-start | bytes 49160 | tf_op jit(solution)/shard_map/ppermute | solution.py:13
  13.1 2.6 copy.35
  15.7 5.1 %all-to-all-start = ((f32[32,64,256]{2,0,1:T(8,128)}), f32[32,64,256]{2,0,1:T(8,128)S(1)}, u32[]{:S(2)}, u32[]{:S(2)}) async-start(f32[32,64,256]{2,0,1:T(8,128)} %copy.35), calls=%async_computation | async-start | bytes 4194304 | tf_op jit(solution)/shard_map/all_to_all | solution.py:75
  20.7 1.8 copy.40
  23.9 22.8 %all-to-all-done = f32[32,64,256]{2,0,1:T(8,128)S(1)} async-done(((f32[32,64,256]{2,0,1:T(8,128)}), f32[32,64,256]{2,0,1:T(8,128)S(1)}, u32[]{:S(2)}, u32[]{:S(2)}) %all-to-all-start) | async-done | bytes 2097184 | tf_op jit(solution)/shard_map/all_to_all | solution.py:75
  53.3 40.5 %all_to_all.56 = f32[128,8,512]{2,1,0:T(8,128)S(1)} all-to-all(f32[128,8,512]{2,1,0:T(8,128)S(1)} %copy.42), channel_id=1, replica_groups=mesh['px'=8,'py'=16] {'py','px'}, dimensions={0} | all-to-all | bytes 4194304 | tf_op jit(solution)/shard_map/all_to_all | solution.py:89
  93.9 4.6 %convolution_bitcast_fusion.3 = f32[1024,256]{0,1:T(8,128)} fusion(f32[1024,1024]{1,0:T(8,128)S(1)} %copy-done.1, f32[1024,512]{1,0:T(8,128)S(1)} %bitcast.82), kind=kOutput, calls=%fused_computation.14 | convolution fusion | flops 1610612736 | bytes 6291456 | tf_op jit(solution)/shard_map/dot_general | solution.py:70
  98.5 2.4 reshape.27
  101.0 3.8 %copy.43 = f32[16,64,8,32]{1,0,3,2:T(8,128)} copy(f32[16,64,8,32]{3,1,2,0:T(8,128)} %bitcast.71) | data formatting | bytes 2097152 | tf_op jit(solution)/shard_map/transpose | solution.py:115
  104.8 2.0 reshape.28
  106.8 4.3 %convolution_bitcast_fusion.2 = f32[1024,256]{0,1:T(8,128)S(1)} fusion(f32[1024,256]{0,1:T(8,128)S(1)} %reshape.28, f32[1024,1024]{1,0:T(8,128)} %param.9), kind=kOutput, calls=%fused_computation.13 | convolution fusion | flops 1610612736 | bytes 6291456 | tf_op jit(solution)/shard_map/dot_general | solution.py:70
  112.6 2.9 %copy.44 = f32[1024,512]{1,0:T(8,128)} copy(f32[1024,512]{0,1:T(8,128)} %pad_maximum_fusion.2) | data formatting | bytes 4194304 | tf_op jit(solution)/shard_map/concatenate | solution.py:96
  115.5 35.3 %all_to_all.57 = f32[128,8,512]{2,1,0:T(8,128)S(1)} all-to-all(f32[128,8,512]{2,1,0:T(8,128)} %bitcast.83), channel_id=1, replica_groups=mesh['px'=8,'py'=16] {'py','px'}, dimensions={0} | all-to-all | bytes 4194304 | tf_op jit(solution)/shard_map/all_to_all | solution.py:99
  155.1 3.0 %collective-permute-start.2 = (f32[128,1,256]{2,0,1:T(8,128)S(1)}, f32[128,1,256]{2,0,1:T(8,128)S(1)}, u32[]{:S(2)}, u32[]{:S(2)}) collective-permute-start(f32[128,1,256]{2,0,1:T(8,128)S(1)} %get-tuple-element.20), channel_id=1, source_target_pairs={{16,0},{32,16},{48,32},{64,48},{80,64},{96,80},{112,96},{1,112},{1... | collective-permute-start | bytes 393224 | tf_op jit(solution)/shard_map/ppermute | solution.py:58
  158.1 2.5 collective-permute-start.3
  160.6 1.9 bitcast_multiply_fusion.2
  162.5 4.0 %collective-permute-done.3 = f32[128,1,256]{2,0,1:T(8,128)S(1)} collective-permute-done((f32[128,1,256]{2,0,1:T(8,128)S(1)}, f32[128,1,256]{2,0,1:T(8,128)S(1)}, u32[]{:S(2)}, u32[]{:S(2)}) %collective-permute-start.3) | collective-permute-done | bytes 131104 | tf_op jit(solution)/shard_map/ppermute | solution.py:57
  167.4 24.2 %all_to_all.58 = f32[128,8,256]{2,1,0:T(8,128)S(1)} all-to-all(f32[128,8,256]{2,1,0:T(8,128)S(1)} %copy.47), channel_id=1, replica_groups=mesh['px'=8,'py'=16] {'py','px'}, dimensions={0} | all-to-all | bytes 2097152 | tf_op jit(solution)/shard_map/all_to_all | solution.py:89
  191.6 3.0 %convolution_bitcast_fusion.1 = f32[1024,256]{0,1:T(8,128)} fusion(f32[1024,1024]{1,0:T(8,128)S(1)} %copy-done.2, f32[128,8,256]{2,1,0:T(8,128)S(1)} %all_to_all.58), kind=kOutput, calls=%fused_computation.12 | convolution fusion | flops 1610612736 | bytes 6291456 | tf_op jit(solution)/shard_map/dot_general | solution.py:70
  194.6 2.5 copy.48
  197.1 5.8 %all-to-all-start.4 = ((f32[128,8,256]{2,1,0:T(8,128)}), f32[128,8,256]{2,1,0:T(8,128)}, u32[]{:S(2)}, u32[]{:S(2)}) async-start(f32[128,8,256]{2,1,0:T(8,128)} %bitcast.85), calls=%async_computation.4 | async-start | bytes 2097152 | tf_op jit(solution)/shard_map/all_to_all | solution.py:99
  202.9 1.9 fusion.80
  204.9 3.3 %collective-permute-start.5 = (f32[128,1,256]{2,0,1:T(8,128)S(1)}, f32[128,1,256]{2,0,1:T(8,128)S(1)}, u32[]{:S(2)}, u32[]{:S(2)}) collective-permute-start(f32[128,1,256]{2,0,1:T(8,128)S(1)} %copy.67), channel_id=1, source_target_pairs={{0,16},{16,32},{32,48},{48,64},{64,80},{80,96},{96,112},{112,1},{1... | collective-permute-start | bytes 393224 | tf_op jit(solution)/shard_map/ppermute | solution.py:57
  208.2 4.5 %collective-permute-start.4 = (f32[128,1,256]{2,0,1:T(8,128)S(1)}, f32[128,1,256]{2,0,1:T(8,128)S(1)}, u32[]{:S(2)}, u32[]{:S(2)}) collective-permute-start(f32[128,1,256]{2,0,1:T(8,128)S(1)} %copy.66), channel_id=1, source_target_pairs={{16,0},{32,16},{48,32},{64,48},{80,64},{96,80},{112,96},{1,112},{1... | collective-permute-start | bytes 393224 | tf_op jit(solution)/shard_map/ppermute | solution.py:58
  212.7 8.6 %collective-permute-done.5 = f32[128,1,256]{2,0,1:T(8,128)S(1)} collective-permute-done((f32[128,1,256]{2,0,1:T(8,128)S(1)}, f32[128,1,256]{2,0,1:T(8,128)S(1)}, u32[]{:S(2)}, u32[]{:S(2)}) %collective-permute-start.5) | collective-permute-done | bytes 131104 | tf_op jit(solution)/shard_map/ppermute | solution.py:57
  221.3 3.4 %fusion.28 = f32[128,8,256]{2,0,1:T(8,128)S(1)} fusion(f32[128,8,256]{2,0,1:T(8,128)} %get-tuple-element.19, f32[128,1,256]{2,0,1:T(8,128)S(1)} %collective-permute-done.5, f32[128,1,256]{2,0,1:T(8,128)S(1)} %collective-permute-done.4, f32[128,8,256]{2,0,1:T(8,128)} %get-tuple-element.18, f32[127,8,256]{2,0,1:T(8,128)} %bitcast.78, f32[256,256]{1,0:T(8,128)S(1)} %copy-done), kind=kOutput, calls=%fused_computation.45 | convolution fusion | flops 405012480 | bytes 4710400 | tf_op jit(solution)/shard_map/dot_general | solution.py:65
  229.3 4.5 %bitcast_multiply_fusion.1 = (f32[128,8,256]{2,0,1:T(8,128)S(1)}, f32[256,8,128]{0,2,1:T(8,128)S(1)}) fusion(f32[256,8,128]{0,2,1:T(8,128)S(1)} %copy.62, f32[127,8,256]{2,0,1:T(8,128)S(1)} %slice.216, f32[128,8,256]{2,1,0:T(8,128)} %all-to-all-done.4, f32[128,8,256]{2,0,1:T(8,128)S(1)} %fusion.44, f32[127,8,256]{2,0,1:T(8,128)S(1)} %copy-done.7, ...), kind=kLoop, calls=%fused_computation.66 | loop fusion | flops 3932160 | bytes 15679488 | tf_op jit(solution)/shard_map/mul | solution.py:37
  235.1 2.0 copy.58
  237.1 30.0 %all_to_all.59 = f32[256,8,256]{2,1,0:T(8,128)S(1)} all-to-all(f32[256,8,256]{2,1,0:T(8,128)} %copy.58), channel_id=1, replica_groups=mesh['px'=8,'py'=16] {'px'}, dimensions={0} | all-to-all | bytes 4194304 | tf_op jit(solution)/shard_map/all_to_all | solution.py:82
  267.7 4.1 %collective-permute-start.6 = (f32[32,1,128]{2,1,0:T(1,128)S(1)}, f32[32,1,128]{2,1,0:T(1,128)S(1)}, u32[]{:S(2)}, u32[]{:S(2)}) collective-permute-start(f32[32,1,128]{2,1,0:T(1,128)S(1)} %get-tuple-element.5), channel_id=1, source_target_pairs={{1,0},{2,1},{3,2},{4,3},{5,4},{6,5},{7,6},{8,7},{9,8},{10,9},{11,1... | collective-permute-start | bytes 49160 | tf_op jit(solution)/shard_map/ppermute | solution.py:14
  271.8 4.5 %collective-permute-start.7 = (f32[32,1,128]{2,1,0:T(1,128)S(1)}, f32[32,1,128]{2,1,0:T(1,128)S(1)}, u32[]{:S(2)}, u32[]{:S(2)}) collective-permute-start(f32[32,1,128]{2,1,0:T(1,128)S(1)} %get-tuple-element.6), channel_id=1, source_target_pairs={{0,1},{1,2},{2,3},{3,4},{4,5},{5,6},{6,7},{7,8},{8,9},{9,10},{10,1... | collective-permute-start | bytes 49160 | tf_op jit(solution)/shard_map/ppermute | solution.py:13
  (93 shorter events, 28.7 us)
Async XLA Ops:
  0.6 48.2 %copy-start = (f32[256,256]{1,0:T(8,128)S(1)}, f32[256,256]{1,0:T(8,128)}, u32[]{:S(2)}) copy-start(f32[256,256]{1,0:T(8,128)} %param.8) | copy-start | bytes 786436
  0.6 10.7 %copy-start.4 = (f32[32,64,128]{2,1,0:T(8,128)S(1)}, f32[32,64,128]{2,1,0:T(8,128)}, u32[]{:S(2)}) copy-start(f32[32,64,128]{2,1,0:T(8,128)} %param.5) | copy-start | bytes 3145732
  0.7 10.7 %copy-start.12 = (f32[32,64,128]{2,1,0:T(8,128)S(1)}, f32[32,64,128]{2,1,0:T(8,128)}, u32[]{:S(2)}) copy-start(f32[32,64,128]{2,1,0:T(8,128)} %param.6) | copy-start | bytes 3145732
  1.8 9.9 %collective-permute-start = (f32[32,1,128]{2,1,0:T(1,128)S(1)}, f32[32,1,128]{2,1,0:T(1,128)S(1)}, u32[]{:S(2)}, u32[]{:S(2)}) collective-permute-start(f32[32,1,128]{2,1,0:T(1,128)S(1)} %get-tuple-element.24), channel_id=1, source_target_pairs={{1,0},{2,1},{3,2},{4,3},{5,4},{6,5},{7,6},{8,7},{9,8},{10,9},{11,1... | collective-permute-start | bytes 49160 | tf_op jit(solution)/shard_map/ppermute | solution.py:14
  5.2 6.6 %collective-permute-start.1 = (f32[32,1,128]{2,1,0:T(1,128)S(1)}, f32[32,1,128]{2,1,0:T(1,128)S(1)}, u32[]{:S(2)}, u32[]{:S(2)}) collective-permute-start(f32[32,1,128]{2,1,0:T(1,128)S(1)} %get-tuple-element.25), channel_id=1, source_target_pairs={{0,1},{1,2},{2,3},{3,4},{4,5},{5,6},{6,7},{7,8},{8,9},{9,10},{10,1... | collective-permute-start | bytes 49160 | tf_op jit(solution)/shard_map/ppermute | solution.py:13
  11.4 1.0 copy-start.10
  15.7 31.0 %all-to-all-start = ((f32[32,64,256]{2,0,1:T(8,128)}), f32[32,64,256]{2,0,1:T(8,128)S(1)}, u32[]{:S(2)}, u32[]{:S(2)}) async-start(f32[32,64,256]{2,0,1:T(8,128)} %copy.35), calls=%async_computation | async-start | bytes 4194304 | tf_op jit(solution)/shard_map/all_to_all | solution.py:75
  49.5 1.1 copy-start.6
  50.6 1.2 copy-start.21
  53.3 40.6 %copy-start.1 = (f32[1024,1024]{1,0:T(8,128)S(1)}, f32[1024,1024]{1,0:T(8,128)}, u32[]{:S(2)}) copy-start(f32[1024,1024]{1,0:T(8,128)} %param.9) | copy-start | bytes 12582916
  106.8 4.3 %copy-start.22 = (f32[1024,256]{0,1:T(8,128)S(1)}, f32[1024,256]{0,1:T(8,128)}, u32[]{:S(2)}) copy-start(f32[1024,256]{0,1:T(8,128)} %convolution_bitcast_fusion.3) | copy-start | bytes 3145732
  150.8 1.4 copy-start.3
  152.2 1.3 copy-start.8
  152.3 1.1 copy-start.14
  152.4 8.2 %copy-start.20 = (f32[128,8,256]{2,1,0:T(8,128)}, f32[128,8,256]{2,1,0:T(8,128)S(1)}, u32[]{:S(2)}) copy-start(f32[128,8,256]{2,1,0:T(8,128)S(1)} %get-tuple-element.10) | copy-start | bytes 3145732
  154.7 7.8 %copy-start.18 = (f32[127,8,256]{2,0,1:T(8,128)}, f32[127,8,256]{2,0,1:T(8,128)S(1)}, u32[]{:S(2)}) copy-start(f32[127,8,256]{2,0,1:T(8,128)S(1)} %slice.214) | copy-start | bytes 3121156
  155.0 7.5 %copy-start.19 = (f32[127,8,256]{2,0,1:T(8,128)}, f32[127,8,256]{2,0,1:T(8,128)S(1)}, u32[]{:S(2)}) copy-start(f32[127,8,256]{2,0,1:T(8,128)S(1)} %copy.68) | copy-start | bytes 3121156
  155.1 7.5 %collective-permute-start.2 = (f32[128,1,256]{2,0,1:T(8,128)S(1)}, f32[128,1,256]{2,0,1:T(8,128)S(1)}, u32[]{:S(2)}, u32[]{:S(2)}) collective-permute-start(f32[128,1,256]{2,0,1:T(8,128)S(1)} %get-tuple-element.20), channel_id=1, source_target_pairs={{16,0},{32,16},{48,32},{64,48},{80,64},{96,80},{112,96},{1,112},{1... | collective-permute-start | bytes 393224 | tf_op jit(solution)/shard_map/ppermute | solution.py:58
  158.1 8.4 %collective-permute-start.3 = (f32[128,1,256]{2,0,1:T(8,128)S(1)}, f32[128,1,256]{2,0,1:T(8,128)S(1)}, u32[]{:S(2)}, u32[]{:S(2)}) collective-permute-start(f32[128,1,256]{2,0,1:T(8,128)S(1)} %get-tuple-element.21), channel_id=1, source_target_pairs={{0,16},{16,32},{32,48},{48,64},{64,80},{80,96},{96,112},{112,1},{1... | collective-permute-start | bytes 393224 | tf_op jit(solution)/shard_map/ppermute | solution.py:57
  166.5 25.1 %copy-start.2 = (f32[1024,1024]{1,0:T(8,128)S(1)}, f32[1024,1024]{1,0:T(8,128)}, u32[]{:S(2)}) copy-start(f32[1024,1024]{1,0:T(8,128)} %param.9) | copy-start | bytes 12582916
  197.1 29.7 %all-to-all-start.4 = ((f32[128,8,256]{2,1,0:T(8,128)}), f32[128,8,256]{2,1,0:T(8,128)}, u32[]{:S(2)}, u32[]{:S(2)}) async-start(f32[128,8,256]{2,1,0:T(8,128)} %bitcast.85), calls=%async_computation.4 | async-start | bytes 2097152 | tf_op jit(solution)/shard_map/all_to_all | solution.py:99
  204.9 16.4 %collective-permute-start.5 = (f32[128,1,256]{2,0,1:T(8,128)S(1)}, f32[128,1,256]{2,0,1:T(8,128)S(1)}, u32[]{:S(2)}, u32[]{:S(2)}) collective-permute-start(f32[128,1,256]{2,0,1:T(8,128)S(1)} %copy.67), channel_id=1, source_target_pairs={{0,16},{16,32},{32,48},{48,64},{64,80},{80,96},{96,112},{112,1},{1... | collective-permute-start | bytes 393224 | tf_op jit(solution)/shard_map/ppermute | solution.py:57
  208.2 13.1 %collective-permute-start.4 = (f32[128,1,256]{2,0,1:T(8,128)S(1)}, f32[128,1,256]{2,0,1:T(8,128)S(1)}, u32[]{:S(2)}, u32[]{:S(2)}) collective-permute-start(f32[128,1,256]{2,0,1:T(8,128)S(1)} %copy.66), channel_id=1, source_target_pairs={{16,0},{32,16},{48,32},{64,48},{80,64},{96,80},{112,96},{1,112},{1... | collective-permute-start | bytes 393224 | tf_op jit(solution)/shard_map/ppermute | solution.py:58
  226.8 1.9 copy-start.7
  226.8 1.9 copy-start.9
  226.8 2.2 copy-start.15
  226.8 2.5 copy-start.17
  267.1 9.3 %copy-start.13 = (f32[32,64,128]{2,1,0:T(8,128)S(1)}, f32[32,64,128]{2,1,0:T(8,128)}, u32[]{:S(2)}) copy-start(f32[32,64,128]{2,1,0:T(8,128)} %param.6) | copy-start | bytes 3145732
  267.3 9.1 %copy-start.5 = (f32[32,64,128]{2,1,0:T(8,128)S(1)}, f32[32,64,128]{2,1,0:T(8,128)}, u32[]{:S(2)}) copy-start(f32[32,64,128]{2,1,0:T(8,128)} %param.5) | copy-start | bytes 3145732
  267.3 9.1 %copy-start.11 = (f32[32,64,127]{2,1,0:T(8,128)S(1)}, f32[32,64,127]{2,1,0:T(8,128)}, u32[]{:S(2)}) copy-start(f32[32,64,127]{2,1,0:T(8,128)} %copy-done.10) | copy-start | bytes 3121156
  267.7 10.5 %collective-permute-start.6 = (f32[32,1,128]{2,1,0:T(1,128)S(1)}, f32[32,1,128]{2,1,0:T(1,128)S(1)}, u32[]{:S(2)}, u32[]{:S(2)}) collective-permute-start(f32[32,1,128]{2,1,0:T(1,128)S(1)} %get-tuple-element.5), channel_id=1, source_target_pairs={{1,0},{2,1},{3,2},{4,3},{5,4},{6,5},{7,6},{8,7},{9,8},{10,9},{11,1... | collective-permute-start | bytes 49160 | tf_op jit(solution)/shard_map/ppermute | solution.py:14
  271.8 6.4 %collective-permute-start.7 = (f32[32,1,128]{2,1,0:T(1,128)S(1)}, f32[32,1,128]{2,1,0:T(1,128)S(1)}, u32[]{:S(2)}, u32[]{:S(2)}) collective-permute-start(f32[32,1,128]{2,1,0:T(1,128)S(1)} %get-tuple-element.6), channel_id=1, source_target_pairs={{0,1},{1,2},{2,3},{3,4},{4,5},{5,6},{6,7},{7,8},{8,9},{9,10},{10,1... | collective-permute-start | bytes 49160 | tf_op jit(solution)/shard_map/ppermute | solution.py:13
  (1 other events, 1.0 us)
where the time goes:
time: 281 us; the launch traced here: 280 us
  blocking collectives  130 us (46%)
  starting transfers between devices  40.7 us (14%)
  local copies, waits for them, and re-layouts  39.8 us (14%)
  waiting for transfers between devices  35.4 us (13%)
  matrix products  18 us (6%)
  other arithmetic  14.7 us (5%)
    all_to_all x2, blocking collectives, x_to_y(): lax.all_to_all(joined, LINES, split_axis=0, concat_axis=0, tiled=True)  64.6 us
    all_to_all x1, blocking collectives, y_to_x(): lax.all_to_all(joined, LINES, split_axis=0, concat_axis=0, tiled=True)  35.3 us
    all_to_all x1, blocking collectives, x_to_block(): lax.all_to_all(joined, 'px', split_axis=0, concat_axis=1, tiled=True)  30 us
    all_to_all x1, waiting for transfers between devices, block_to_x(): lax.all_to_all(joined, 'px', split_axis=1, concat_axis=0, tiled=True)  22.8 us
    ppermute x2, waiting for transfers between devices, ydiff(): below = lax.ppermute(field[:, -1:], ('px', 'py'), up)  12.6 us
    dot_general x3, matrix products, along_y(): return lax.dot_general(matrix, field, dims, precision=HIGH)  11.9 us
    ppermute x2, starting transfers between devices, ydiff_block(): lax.ppermute(field[:, -1:], 'py', [(i, i + 1) for i in range(count - 1)])  9.16 us
    unnamed x53, local copies, waits for them, and re-layouts  8.27 us
  transfers between devices with their start and end apart: 10, of which 3 were waited for; matrix products, arithmetic and copies ran while one was open for 5% of the time, Pallas kernels for 0%

commit v1 on v0

--- a/solution.py
+++ b/solution.py
@@ -1,6 +1,9 @@
+import functools
+
 import jax
 import jax.numpy as jnp
 from jax import lax
+from jax.experimental import pallas as pl
 from jax.sharding import PartitionSpec as P
 
 RATE = 0.2
@@ -65,11 +68,6 @@
     return lax.dot_general(field, matrix, dims, precision=HIGH)
 
 
-def along_y(matrix, field, transpose):
-    dims = (((0,), (0,)), ((), ())) if transpose else (((1,), (0,)), ((), ()))
-    return lax.dot_general(matrix, field, dims, precision=HIGH)
-
-
 def block_to_x(*fields):
     joined = jnp.concatenate(fields, axis=2)
     lines = lax.all_to_all(joined, "px", split_axis=1, concat_axis=0, tiled=True)
@@ -92,13 +90,12 @@
     return [lines[:, k * width:(k + 1) * width] for k in range(len(fields))]
 
 
-def y_to_x(*fields):
-    joined = jnp.concatenate(fields, axis=1)
+def y_to_x(joined, parts):
     count = lax.axis_size(LINES)
     joined = joined.reshape(count, -1, joined.shape[1])
     lines = lax.all_to_all(joined, LINES, split_axis=0, concat_axis=0, tiled=True)
-    width = fields[0].shape[1]
-    return [lines[:, :, k * width:(k + 1) * width] for k in range(len(fields))]
+    width = joined.shape[2] // parts
+    return [lines[:, :, k * width:(k + 1) * width] for k in range(parts)]
 
 
 def block_planes(field):
@@ -115,16 +112,59 @@
     return jnp.transpose(tiles, (0, 2, 1, 3)).reshape(cols * width, rows * depth)
 
 
+def split(value):
+    high = lax.reduce_precision(value, exponent_bits=8, mantissa_bits=7)
+    return high.astype(jnp.bfloat16), (value - high).astype(jnp.bfloat16)
+
+
+def _ymm_kernel(count, *refs):
+    out = refs[-1]
+    for k in range(count):
+        high, low, f_high, f_low = refs[4 * k:4 * k + 4]
+        a_high = high[...]
+        top = f_high[...]
+        acc = jnp.dot(a_high, top, preferred_element_type=jnp.float32)
+        acc = acc + jnp.dot(a_high, f_low[...], preferred_element_type=jnp.float32)
+        acc = acc + jnp.dot(low[...], top, preferred_element_type=jnp.float32)
+        width = top.shape[1]
+        out[:, k * width:(k + 1) * width] = acc
+
+
+def y_products(*pairs):
+    count = len(pairs)
+    size, width = pairs[0][1].shape
+    step = 256
+    operands, specs = [], []
+    for (high, low), field in pairs:
+        operands += [high, low, *split(field)]
+        specs += [
+            pl.BlockSpec((step, size), lambda i: (i, 0)),
+            pl.BlockSpec((step, size), lambda i: (i, 0)),
+            pl.BlockSpec((size, width), lambda i: (0, 0)),
+            pl.BlockSpec((size, width), lambda i: (0, 0)),
+        ]
+    flops = 6 * size * size * width * count
+    return pl.pallas_call(
+        functools.partial(_ymm_kernel, count),
+        grid=(size // step,),
+        out_shape=jax.ShapeDtypeStruct((size, width * count), jnp.float32),
+        in_specs=specs,
+        out_specs=pl.BlockSpec((step, width * count), lambda i: (i, 0)),
+        cost_estimate=pl.CostEstimate(flops=flops, transcendentals=0, bytes_accessed=count * (4 * size * size + 8 * size * width)),
+    )(*operands)
+
+
 def local(initial, conduct, cotangent, inv_x, inv_y):
+    forward_y = split(inv_y)
+    backward_y = split(jnp.transpose(inv_y))
     first0 = initial + RATE * (ydiff_block(initial) + zoperate_block(initial, conduct))
     f0x, cx = block_to_x(first0, conduct)
     half0 = along_x(f0x, inv_x, False)
     second0 = half0 + RATE * (xdiff(half0) + zoperate(half0, cx))
     s0y, tp = x_to_y(second0, block_planes(cotangent))
     ty = planes_to_y(tp, (initial.shape[0], initial.shape[1]))
-    state1_y = along_y(inv_y, s0y, False)
-    lam_second1_y = along_y(inv_y, ty, True)
-    state1, ls1 = y_to_x(state1_y, lam_second1_y)
+    joined = y_products((forward_y, s0y), (backward_y, ty))
+    state1, ls1 = y_to_x(joined, 2)
     first1 = state1 + RATE * (ydiff(state1) + zoperate(state1, cx))
     half1 = along_x(first1, inv_x, False)
     grad = -RATE * zstep(ls1) * zstep(half1)
@@ -133,8 +173,8 @@
     grad = grad - RATE * zstep(lam_first1) * zstep(state1)
     lam_state1 = lam_first1 + RATE * (ydiff(lam_first1) + zoperate(lam_first1, cx))
     (lsy,) = x_to_y(lam_state1)
-    lam_second0_y = along_y(inv_y, lsy, True)
-    (ls0,) = y_to_x(lam_second0_y)
+    lam_second0_y = y_products((backward_y, lsy))
+    (ls0,) = y_to_x(lam_second0_y, 1)
     grad = grad - RATE * zstep(ls0) * zstep(half0)
     lam_half0 = ls0 + RATE * (xdiff(ls0) + zoperate(ls0, cx))
     lam_first0 = along_x(lam_half0, inv_x, True)

time: 281 us -> 285 us (1.014)
  blocking collectives: 130 us -> 89.5 us
  waiting for transfers between devices: 35.4 us -> 51.4 us
  Pallas kernels: 0 us -> 13.4 us
  other arithmetic: 14.7 us -> 27.7 us
  matrix products: 18 us -> 6.18 us
  starting transfers between devices: 40.7 us -> 52 us
    all_to_all x2 -> x1, blocking collectives: 64.6 us -> 24.2 us  [x_to_y(): lax.all_to_all(joined, LINES, split_axis=0, concat_axis=0, tiled=True)]
    all_to_all x0 -> x1, waiting for transfers between devices: none -> 15.8 us  [x_to_y(): lax.all_to_all(joined, LINES, split_axis=0, concat_axis=0, tiled=True)]
    pallas_call x0 -> x2, Pallas kernels: none -> 13.4 us  [y_products(): pl.pallas_call(functools.partial(_ymm_kernel, count), grid=(size // step,...]
    convert_element_type x0 -> x3, other arithmetic: none -> 11.9 us  [split(): return (high.astype(jnp.bfloat16), (value - high).astype(jnp.bfloat16))]
    dot_general x3 -> x0, matrix products: 11.9 us -> none  [along_y(): return lax.dot_general(matrix, field, dims, precision=HIGH)]
    all_to_all x0 -> x1, starting transfers between devices: none -> 11.2 us  [x_to_y(): lax.all_to_all(joined, LINES, split_axis=0, concat_axis=0, tiled=True)]
    unnamed x53 -> x48, local copies, waits for them, and re-layouts: 8.27 us -> 13.7 us
    concatenate x1 -> x0, local copies, waits for them, and re-layouts: 2.9 us -> none  [y_to_x(): joined = jnp.concatenate(fields, axis=1)]
  transfers between devices with their start and end apart: 10 -> 11, of which waited for: 3 -> 4; matrix products, arithmetic and copies ran while one was open for 5% -> 10% of each run, Pallas kernels for 0% -> 0%
where the time goes in v1:
time: 285 us; the launch traced here: 283 us
  blocking collectives  89.5 us (31%)
  starting transfers between devices  52 us (18%)
  waiting for transfers between devices  51.4 us (18%)
  local copies, waits for them, and re-layouts  42.2 us (15%)
  other arithmetic  27.7 us (10%)
  Pallas kernels  13.4 us (5%)
  matrix products  6.18 us (2%)
    all_to_all x1, blocking collectives, y_to_x(): lax.all_to_all(joined, LINES, split_axis=0, concat_axis=0, tiled=True)  35.3 us
    all_to_all x1, blocking collectives, x_to_block(): lax.all_to_all(joined, 'px', split_axis=0, concat_axis=1, tiled=True)  30 us
    all_to_all x1, blocking collectives, x_to_y(): lax.all_to_all(joined, LINES, split_axis=0, concat_axis=0, tiled=True)  24.2 us
    all_to_all x1, waiting for transfers between devices, block_to_x(): lax.all_to_all(joined, 'px', split_axis=1, concat_axis=0, tiled=True)  22.8 us
    all_to_all x1, waiting for transfers between devices, x_to_y(): lax.all_to_all(joined, LINES, split_axis=0, concat_axis=0, tiled=True)  15.8 us
    unnamed x48, local copies, waits for them, and re-layouts  13.7 us
    pallas_call x2, Pallas kernels, y_products(): pl.pallas_call(functools.partial(_ymm_kernel, count), grid=(size // step,...  13.4 us
    ppermute x2, waiting for transfers between devices, ydiff(): below = lax.ppermute(field[:, -1:], ('px', 'py'), up)  12.8 us
  transfers between devices with their start and end apart: 11, of which 4 were waited for; matrix products, arithmetic and copies ran while one was open for 10% of the time, Pallas kernels for 0%

profile of v1, /device:TPU:1, one launch (start us, length us, event | category | flops | bytes accessed | tf_op | source)
XLA Modules:
  0.0 283.5 jit_solution(17796809308649634893)
XLA Ops:
  1.8 3.3 %collective-permute-start = (f32[32,1,128]{2,1,0:T(1,128)S(1)}, f32[32,1,128]{2,1,0:T(1,128)S(1)}, u32[]{:S(2)}, u32[]{:S(2)}) collective-permute-start(f32[32,1,128]{2,1,0:T(1,128)S(1)} %get-tuple-element.35), channel_id=1, source_target_pairs={{1,0},{2,1},{3,2},{4,3},{5,4},{6,5},{7,6},{8,7},{9,8},{10,9},{11,1... | collective-permute-start | bytes 49160 | tf_op jit(solution)/shard_map/ppermute | solution.py:17
  5.2 4.6 %collective-permute-start.1 = (f32[32,1,128]{2,1,0:T(1,128)S(1)}, f32[32,1,128]{2,1,0:T(1,128)S(1)}, u32[]{:S(2)}, u32[]{:S(2)}) collective-permute-start(f32[32,1,128]{2,1,0:T(1,128)S(1)} %get-tuple-element.36), channel_id=1, source_target_pairs={{0,1},{1,2},{2,3},{3,4},{4,5},{5,6},{6,7},{7,8},{8,9},{9,10},{10,1... | collective-permute-start | bytes 49160 | tf_op jit(solution)/shard_map/ppermute | solution.py:16
  13.1 2.6 copy.44
  15.7 5.1 %all-to-all-start = ((f32[32,64,256]{2,0,1:T(8,128)}), f32[32,64,256]{2,0,1:T(8,128)S(1)}, u32[]{:S(2)}, u32[]{:S(2)}) async-start(f32[32,64,256]{2,0,1:T(8,128)} %copy.44), calls=%async_computation | async-start | bytes 4194304 | tf_op jit(solution)/shard_map/all_to_all | solution.py:73
  23.9 22.8 %all-to-all-done = f32[32,64,256]{2,0,1:T(8,128)S(1)} async-done(((f32[32,64,256]{2,0,1:T(8,128)}), f32[32,64,256]{2,0,1:T(8,128)S(1)}, u32[]{:S(2)}, u32[]{:S(2)}) %all-to-all-start) | async-done | bytes 2097184 | tf_op jit(solution)/shard_map/all_to_all | solution.py:73
  52.1 2.5 copy.51
  54.6 11.2 %all-to-all-start.1 = ((f32[128,8,512]{2,1,0:T(8,128)}), f32[128,8,512]{2,1,0:T(8,128)}, u32[]{:S(2)}, u32[]{:S(2)}) async-start(f32[128,8,512]{2,1,0:T(8,128)} %copy.51), calls=%async_computation.1 | async-start | bytes 4194304 | tf_op jit(solution)/shard_map/all_to_all | solution.py:87
  65.8 5.4 %copy.43 = f32[1024,1024]{0,1:T(8,128)} copy(f32[1024,1024]{1,0:T(8,128)} %param.9) | data formatting | bytes 8388608 | tf_op args[4]
  71.1 8.4 %fusion = (bf16[1024,1024]{1,0:T(8,128)(2,1)}, bf16[1024,1024]{1,0:T(8,128)(2,1)}, bf16[1024,1024]{1,0:T(8,128)(2,1)}, bf16[1024,1024]{1,0:T(8,128)(2,1)}) fusion(f32[1024,1024]{0,1:T(8,128)} %copy.43, f32[1024,1024]{1,0:T(8,128)} %param.9), kind=kLoop, calls=%fused_computation.4 | loop fusion | flops 8388608 | bytes 16777216 | tf_op jit(solution)/shard_map/convert_element_type | solution.py:117
  79.6 15.8 %all-to-all-done.1 = f32[128,8,512]{2,1,0:T(8,128)} async-done(((f32[128,8,512]{2,1,0:T(8,128)}), f32[128,8,512]{2,1,0:T(8,128)}, u32[]{:S(2)}, u32[]{:S(2)}) %all-to-all-start.1) | async-done | bytes 2097184 | tf_op jit(solution)/shard_map/all_to_all | solution.py:87
  95.4 2.7 fusion.84
  98.1 2.5 reshape.27
  100.5 3.8 %copy.52 = f32[16,64,8,32]{1,0,3,2:T(8,128)} copy(f32[16,64,8,32]{3,1,2,0:T(8,128)} %bitcast.64) | data formatting | bytes 2097152 | tf_op jit(solution)/shard_map/transpose | solution.py:112
  104.4 2.0 reshape.28
  107.7 2.4 fusion.3
  110.1 8.0 %shard_map.68 = f32[1024,512]{1,0:T(8,128)} custom-call(bf16[1024,1024]{1,0:T(8,128)(2,1)} %get-tuple-element.37.refs_0_, bf16[1024,1024]{1,0:T(8,128)(2,1)} %get-tuple-element.38.refs_1_, bf16[1024,256]{1,0:T(8,128)(2,1)} %get-tuple-element.21.refs_2_, bf16[1024,256]{1,0:T(8,128)(2,1)} %get-tuple-element.20.refs_3_, ...), custom_call_target="tpu_custom_call" | custom-call | flops 3221225472 | bytes 12582912 | tf_op jit(solution)/shard_map/pallas_call | solution.py:147
  118.1 35.3 %all_to_all.56 = f32[128,8,512]{2,1,0:T(8,128)S(1)} all-to-all(f32[128,8,512]{2,1,0:T(8,128)} %bitcast.75), channel_id=1, replica_groups=mesh['px'=8,'py'=16] {'py','px'}, dimensions={0} | all-to-all | bytes 4194304 | tf_op jit(solution)/shard_map/all_to_all | solution.py:96
  157.5 3.0 %collective-permute-start.2 = (f32[128,1,256]{2,0,1:T(8,128)S(1)}, f32[128,1,256]{2,0,1:T(8,128)S(1)}, u32[]{:S(2)}, u32[]{:S(2)}) collective-permute-start(f32[128,1,256]{2,0,1:T(8,128)S(1)} %get-tuple-element.29), channel_id=1, source_target_pairs={{16,0},{32,16},{48,32},{64,48},{80,64},{96,80},{112,96},{1,112},{1... | collective-permute-start | bytes 393224 | tf_op jit(solution)/shard_map/ppermute | solution.py:61
  160.5 2.3 collective-permute-start.3
  164.8 4.2 %collective-permute-done.3 = f32[128,1,256]{2,0,1:T(8,128)S(1)} collective-permute-done((f32[128,1,256]{2,0,1:T(8,128)S(1)}, f32[128,1,256]{2,0,1:T(8,128)S(1)}, u32[]{:S(2)}, u32[]{:S(2)}) %collective-permute-start.3) | collective-permute-done | bytes 131104 | tf_op jit(solution)/shard_map/ppermute | solution.py:60
  169.9 24.2 %all_to_all.57 = f32[128,8,256]{2,1,0:T(8,128)S(1)} all-to-all(f32[128,8,256]{2,1,0:T(8,128)S(1)} %copy.57), channel_id=1, replica_groups=mesh['px'=8,'py'=16] {'py','px'}, dimensions={0} | all-to-all | bytes 2097152 | tf_op jit(solution)/shard_map/all_to_all | solution.py:87
  195.1 5.4 %shard_map.69 = f32[1024,256]{1,0:T(8,128)} custom-call(bf16[1024,1024]{1,0:T(8,128)(2,1)} %get-tuple-element.3.refs_4_.refs_0_, bf16[1024,1024]{1,0:T(8,128)(2,1)} %get-tuple-element.2.refs_5_.refs_1_, bf16[1024,256]{1,0:T(8,128)(2,1)} %get-tuple-element.25.refs_2_, bf16[1024,256]{1,0:T(8,128)(2,1)} %get-tuple-element.24.refs_3_), custom_call_target="tpu_custom_call" | custom-call | flops 1610612736 | bytes 6291456 | tf_op jit(solution)/shard_map/pallas_call | solution.py:147
  200.5 6.0 %all-to-all-start.4 = ((f32[128,8,256]{2,1,0:T(8,128)}), f32[128,8,256]{2,1,0:T(8,128)}, u32[]{:S(2)}, u32[]{:S(2)}) async-start(f32[128,8,256]{2,1,0:T(8,128)} %bitcast.79), calls=%async_computation.4 | async-start | bytes 2097152 | tf_op jit(solution)/shard_map/all_to_all | solution.py:96
  208.6 3.3 %collective-permute-start.5 = (f32[128,1,256]{2,0,1:T(8,128)S(1)}, f32[128,1,256]{2,0,1:T(8,128)S(1)}, u32[]{:S(2)}, u32[]{:S(2)}) collective-permute-start(f32[128,1,256]{2,0,1:T(8,128)S(1)} %copy.76), channel_id=1, source_target_pairs={{0,16},{16,32},{32,48},{48,64},{64,80},{80,96},{96,112},{112,1},{1... | collective-permute-start | bytes 393224 | tf_op jit(solution)/shard_map/ppermute | solution.py:60
  211.9 4.5 %collective-permute-start.4 = (f32[128,1,256]{2,0,1:T(8,128)S(1)}, f32[128,1,256]{2,0,1:T(8,128)S(1)}, u32[]{:S(2)}, u32[]{:S(2)}) collective-permute-start(f32[128,1,256]{2,0,1:T(8,128)S(1)} %copy.75), channel_id=1, source_target_pairs={{16,0},{32,16},{48,32},{64,48},{80,64},{96,80},{112,96},{1,112},{1... | collective-permute-start | bytes 393224 | tf_op jit(solution)/shard_map/ppermute | solution.py:61
  216.4 8.6 %collective-permute-done.5 = f32[128,1,256]{2,0,1:T(8,128)S(1)} collective-permute-done((f32[128,1,256]{2,0,1:T(8,128)S(1)}, f32[128,1,256]{2,0,1:T(8,128)S(1)}, u32[]{:S(2)}, u32[]{:S(2)}) %collective-permute-start.5) | collective-permute-done | bytes 131104 | tf_op jit(solution)/shard_map/ppermute | solution.py:60
  225.0 3.5 %fusion.33 = f32[128,8,256]{2,0,1:T(8,128)S(1)} fusion(f32[128,8,256]{2,0,1:T(8,128)} %get-tuple-element.28, f32[128,1,256]{2,0,1:T(8,128)S(1)} %collective-permute-done.5, f32[128,1,256]{2,0,1:T(8,128)S(1)} %collective-permute-done.4, f32[128,8,256]{2,0,1:T(8,128)} %get-tuple-element.27, f32[127,8,256]{2,0,1:T(8,128)} %bitcast.71, f32[256,256]{1,0:T(8,128)S(1)} %copy-done), kind=kOutput, calls=%fused_computation.56 | convolution fusion | flops 405012480 | bytes 4710400 | tf_op jit(solution)/shard_map/dot_general | solution.py:68
  233.0 4.5 %bitcast_multiply_fusion.1 = (f32[128,8,256]{2,0,1:T(8,128)S(1)}, f32[256,8,128]{0,2,1:T(8,128)S(1)}) fusion(f32[256,8,128]{0,2,1:T(8,128)S(1)} %copy.71, f32[127,8,256]{2,0,1:T(8,128)S(1)} %slice.216, f32[128,8,256]{2,1,0:T(8,128)} %all-to-all-done.4, f32[128,8,256]{2,0,1:T(8,128)S(1)} %fusion.47, f32[127,8,256]{2,0,1:T(8,128)S(1)} %copy-done.5, ...), kind=kLoop, calls=%fused_computation.75 | loop fusion | flops 3932160 | bytes 15679488 | tf_op jit(solution)/shard_map/mul | solution.py:40
  238.8 2.0 copy.67
  240.8 30.0 %all_to_all.58 = f32[256,8,256]{2,1,0:T(8,128)S(1)} all-to-all(f32[256,8,256]{2,1,0:T(8,128)} %copy.67), channel_id=1, replica_groups=mesh['px'=8,'py'=16] {'px'}, dimensions={0} | all-to-all | bytes 4194304 | tf_op jit(solution)/shard_map/all_to_all | solution.py:80
  271.4 4.1 %collective-permute-start.6 = (f32[32,1,128]{2,1,0:T(1,128)S(1)}, f32[32,1,128]{2,1,0:T(1,128)S(1)}, u32[]{:S(2)}, u32[]{:S(2)}) collective-permute-start(f32[32,1,128]{2,1,0:T(1,128)S(1)} %get-tuple-element.9), channel_id=1, source_target_pairs={{1,0},{2,1},{3,2},{4,3},{5,4},{6,5},{7,6},{8,7},{9,8},{10,9},{11,1... | collective-permute-start | bytes 49160 | tf_op jit(solution)/shard_map/ppermute | solution.py:17
  275.5 4.5 %collective-permute-start.7 = (f32[32,1,128]{2,1,0:T(1,128)S(1)}, f32[32,1,128]{2,1,0:T(1,128)S(1)}, u32[]{:S(2)}, u32[]{:S(2)}) collective-permute-start(f32[32,1,128]{2,1,0:T(1,128)S(1)} %get-tuple-element.10), channel_id=1, source_target_pairs={{0,1},{1,2},{2,3},{3,4},{4,5},{5,6},{6,7},{7,8},{8,9},{9,10},{10,1... | collective-permute-start | bytes 49160 | tf_op jit(solution)/shard_map/ppermute | solution.py:16
  (89 shorter events, 33.9 us)
Async XLA Ops:
  0.6 48.2 %copy-start = (f32[256,256]{1,0:T(8,128)S(1)}, f32[256,256]{1,0:T(8,128)}, u32[]{:S(2)}) copy-start(f32[256,256]{1,0:T(8,128)} %param.8) | copy-start | bytes 786436
  0.6 10.7 %copy-start.2 = (f32[32,64,128]{2,1,0:T(8,128)S(1)}, f32[32,64,128]{2,1,0:T(8,128)}, u32[]{:S(2)}) copy-start(f32[32,64,128]{2,1,0:T(8,128)} %param.5) | copy-start | bytes 3145732
  0.7 10.7 %copy-start.10 = (f32[32,64,128]{2,1,0:T(8,128)S(1)}, f32[32,64,128]{2,1,0:T(8,128)}, u32[]{:S(2)}) copy-start(f32[32,64,128]{2,1,0:T(8,128)} %param.6) | copy-start | bytes 3145732
  1.8 9.9 %collective-permute-start = (f32[32,1,128]{2,1,0:T(1,128)S(1)}, f32[32,1,128]{2,1,0:T(1,128)S(1)}, u32[]{:S(2)}, u32[]{:S(2)}) collective-permute-start(f32[32,1,128]{2,1,0:T(1,128)S(1)} %get-tuple-element.35), channel_id=1, source_target_pairs={{1,0},{2,1},{3,2},{4,3},{5,4},{6,5},{7,6},{8,7},{9,8},{10,9},{11,1... | collective-permute-start | bytes 49160 | tf_op jit(solution)/shard_map/ppermute | solution.py:17
  5.2 6.5 %collective-permute-start.1 = (f32[32,1,128]{2,1,0:T(1,128)S(1)}, f32[32,1,128]{2,1,0:T(1,128)S(1)}, u32[]{:S(2)}, u32[]{:S(2)}) collective-permute-start(f32[32,1,128]{2,1,0:T(1,128)S(1)} %get-tuple-element.36), channel_id=1, source_target_pairs={{0,1},{1,2},{2,3},{3,4},{4,5},{5,6},{6,7},{7,8},{8,9},{9,10},{10,1... | collective-permute-start | bytes 49160 | tf_op jit(solution)/shard_map/ppermute | solution.py:16
  11.4 1.0 copy-start.8
  15.7 31.0 %all-to-all-start = ((f32[32,64,256]{2,0,1:T(8,128)}), f32[32,64,256]{2,0,1:T(8,128)S(1)}, u32[]{:S(2)}, u32[]{:S(2)}) async-start(f32[32,64,256]{2,0,1:T(8,128)} %copy.44), calls=%async_computation | async-start | bytes 4194304 | tf_op jit(solution)/shard_map/all_to_all | solution.py:73
  49.5 1.0 copy-start.4
  50.5 1.2 copy-start.19
  54.6 40.8 %all-to-all-start.1 = ((f32[128,8,512]{2,1,0:T(8,128)}), f32[128,8,512]{2,1,0:T(8,128)}, u32[]{:S(2)}, u32[]{:S(2)}) async-start(f32[128,8,512]{2,1,0:T(8,128)} %copy.51), calls=%async_computation.1 | async-start | bytes 4194304 | tf_op jit(solution)/shard_map/all_to_all | solution.py:87
  153.3 1.3 copy-start.1
  154.7 1.3 copy-start.6
  154.8 1.1 copy-start.12
  154.8 8.0 %copy-start.18 = (f32[128,8,256]{2,1,0:T(8,128)}, f32[128,8,256]{2,1,0:T(8,128)S(1)}, u32[]{:S(2)}) copy-start(f32[128,8,256]{2,1,0:T(8,128)S(1)} %get-tuple-element.14) | copy-start | bytes 3145732
  157.1 7.6 %copy-start.16 = (f32[127,8,256]{2,0,1:T(8,128)}, f32[127,8,256]{2,0,1:T(8,128)S(1)}, u32[]{:S(2)}) copy-start(f32[127,8,256]{2,0,1:T(8,128)S(1)} %slice.214) | copy-start | bytes 3121156
  157.5 7.2 %copy-start.17 = (f32[127,8,256]{2,0,1:T(8,128)}, f32[127,8,256]{2,0,1:T(8,128)S(1)}, u32[]{:S(2)}) copy-start(f32[127,8,256]{2,0,1:T(8,128)S(1)} %copy.77) | copy-start | bytes 3121156
  157.5 7.2 %collective-permute-start.2 = (f32[128,1,256]{2,0,1:T(8,128)S(1)}, f32[128,1,256]{2,0,1:T(8,128)S(1)}, u32[]{:S(2)}, u32[]{:S(2)}) collective-permute-start(f32[128,1,256]{2,0,1:T(8,128)S(1)} %get-tuple-element.29), channel_id=1, source_target_pairs={{16,0},{32,16},{48,32},{64,48},{80,64},{96,80},{112,96},{1,112},{1... | collective-permute-start | bytes 393224 | tf_op jit(solution)/shard_map/ppermute | solution.py:61
  160.5 8.4 %collective-permute-start.3 = (f32[128,1,256]{2,0,1:T(8,128)S(1)}, f32[128,1,256]{2,0,1:T(8,128)S(1)}, u32[]{:S(2)}, u32[]{:S(2)}) collective-permute-start(f32[128,1,256]{2,0,1:T(8,128)S(1)} %get-tuple-element.30), channel_id=1, source_target_pairs={{0,16},{16,32},{32,48},{48,64},{64,80},{80,96},{96,112},{112,1},{1... | collective-permute-start | bytes 393224 | tf_op jit(solution)/shard_map/ppermute | solution.py:60
  200.5 30.0 %all-to-all-start.4 = ((f32[128,8,256]{2,1,0:T(8,128)}), f32[128,8,256]{2,1,0:T(8,128)}, u32[]{:S(2)}, u32[]{:S(2)}) async-start(f32[128,8,256]{2,1,0:T(8,128)} %bitcast.79), calls=%async_computation.4 | async-start | bytes 2097152 | tf_op jit(solution)/shard_map/all_to_all | solution.py:96
  208.6 16.4 %collective-permute-start.5 = (f32[128,1,256]{2,0,1:T(8,128)S(1)}, f32[128,1,256]{2,0,1:T(8,128)S(1)}, u32[]{:S(2)}, u32[]{:S(2)}) collective-permute-start(f32[128,1,256]{2,0,1:T(8,128)S(1)} %copy.76), channel_id=1, source_target_pairs={{0,16},{16,32},{32,48},{48,64},{64,80},{80,96},{96,112},{112,1},{1... | collective-permute-start | bytes 393224 | tf_op jit(solution)/shard_map/ppermute | solution.py:60
  211.9 13.1 %collective-permute-start.4 = (f32[128,1,256]{2,0,1:T(8,128)S(1)}, f32[128,1,256]{2,0,1:T(8,128)S(1)}, u32[]{:S(2)}, u32[]{:S(2)}) collective-permute-start(f32[128,1,256]{2,0,1:T(8,128)S(1)} %copy.75), channel_id=1, source_target_pairs={{16,0},{32,16},{48,32},{64,48},{80,64},{96,80},{112,96},{1,112},{1... | collective-permute-start | bytes 393224 | tf_op jit(solution)/shard_map/ppermute | solution.py:61
  228.5 1.0 copy-start.14
  230.5 1.9 copy-start.5
  230.5 1.9 copy-start.7
  230.5 2.2 copy-start.13
  230.6 2.5 copy-start.15
  270.8 9.3 %copy-start.11 = (f32[32,64,128]{2,1,0:T(8,128)S(1)}, f32[32,64,128]{2,1,0:T(8,128)}, u32[]{:S(2)}) copy-start(f32[32,64,128]{2,1,0:T(8,128)} %param.6) | copy-start | bytes 3145732
  271.0 9.1 %copy-start.3 = (f32[32,64,128]{2,1,0:T(8,128)S(1)}, f32[32,64,128]{2,1,0:T(8,128)}, u32[]{:S(2)}) copy-start(f32[32,64,128]{2,1,0:T(8,128)} %param.5) | copy-start | bytes 3145732
  271.0 9.1 %copy-start.9 = (f32[32,64,127]{2,1,0:T(8,128)S(1)}, f32[32,64,127]{2,1,0:T(8,128)}, u32[]{:S(2)}) copy-start(f32[32,64,127]{2,1,0:T(8,128)} %copy-done.8) | copy-start | bytes 3121156
  271.4 10.5 %collective-permute-start.6 = (f32[32,1,128]{2,1,0:T(1,128)S(1)}, f32[32,1,128]{2,1,0:T(1,128)S(1)}, u32[]{:S(2)}, u32[]{:S(2)}) collective-permute-start(f32[32,1,128]{2,1,0:T(1,128)S(1)} %get-tuple-element.9), channel_id=1, source_target_pairs={{1,0},{2,1},{3,2},{4,3},{5,4},{6,5},{7,6},{8,7},{9,8},{10,9},{11,1... | collective-permute-start | bytes 49160 | tf_op jit(solution)/shard_map/ppermute | solution.py:17
  275.5 6.4 %collective-permute-start.7 = (f32[32,1,128]{2,1,0:T(1,128)S(1)}, f32[32,1,128]{2,1,0:T(1,128)S(1)}, u32[]{:S(2)}, u32[]{:S(2)}) collective-permute-start(f32[32,1,128]{2,1,0:T(1,128)S(1)} %get-tuple-element.10), channel_id=1, source_target_pairs={{0,1},{1,2},{2,3},{3,4},{4,5},{5,6},{6,7},{7,8},{8,9},{9,10},{10,1... | collective-permute-start | bytes 49160 | tf_op jit(solution)/shard_map/ppermute | solution.py:16

commit v2 on v0

--- a/solution.py
+++ b/solution.py
@@ -50,14 +50,19 @@
     return (line % rows) * cols + line // rows
 
 
-def ydiff(field):
+def ydiff(*fields):
     count = lax.axis_size(LINES)
     up = [(mesh_index(i), mesh_index(i + 1)) for i in range(count - 1)]
     down = [(b, a) for a, b in up]
-    below = lax.ppermute(field[:, -1:], ("px", "py"), up)
-    above = lax.ppermute(field[:, :1], ("px", "py"), down)
-    padded = jnp.concatenate([below, field, above], axis=1)
-    return padded[:, 2:] + padded[:, :-2] - 2.0 * field
+    depth = fields[0].shape[0]
+    below = lax.ppermute(jnp.concatenate([f[:, -1:] for f in fields]), ("px", "py"), up)
+    above = lax.ppermute(jnp.concatenate([f[:, :1] for f in fields]), ("px", "py"), down)
+    diffs = []
+    for k, field in enumerate(fields):
+        edge = slice(k * depth, (k + 1) * depth)
+        padded = jnp.concatenate([below[edge], field, above[edge]], axis=1)
+        diffs.append(padded[:, 2:] + padded[:, :-2] - 2.0 * field)
+    return diffs
 
 
 def along_x(field, matrix, transpose):
@@ -125,13 +130,14 @@
     state1_y = along_y(inv_y, s0y, False)
     lam_second1_y = along_y(inv_y, ty, True)
     state1, ls1 = y_to_x(state1_y, lam_second1_y)
-    first1 = state1 + RATE * (ydiff(state1) + zoperate(state1, cx))
+    lam_half1 = ls1 + RATE * (xdiff(ls1) + zoperate(ls1, cx))
+    lam_first1 = along_x(lam_half1, inv_x, True)
+    dy_state1, dy_lam_first1 = ydiff(state1, lam_first1)
+    lam_state1 = lam_first1 + RATE * (dy_lam_first1 + zoperate(lam_first1, cx))
+    first1 = state1 + RATE * (dy_state1 + zoperate(state1, cx))
     half1 = along_x(first1, inv_x, False)
     grad = -RATE * zstep(ls1) * zstep(half1)
-    lam_half1 = ls1 + RATE * (xdiff(ls1) + zoperate(ls1, cx))
-    lam_first1 = along_x(lam_half1, inv_x, True)
     grad = grad - RATE * zstep(lam_first1) * zstep(state1)
-    lam_state1 = lam_first1 + RATE * (ydiff(lam_first1) + zoperate(lam_first1, cx))
     (lsy,) = x_to_y(lam_state1)
     lam_second0_y = along_y(inv_y, lsy, True)
     (ls0,) = y_to_x(lam_second0_y)

time: 281 us -> 280 us (level)
  starting transfers between devices: 40.7 us -> 34.3 us
  waiting for transfers between devices: 35.4 us -> 38.8 us
  blocking collectives: 130 us -> 133 us
    all_to_all x1, waiting for transfers between devices: 0.01 us -> 13.1 us  [y_to_x(): lax.all_to_all(joined, LINES, split_axis=0, concat_axis=0, tiled=True)]
    ppermute x4 -> x2, waiting for transfers between devices: 12.6 us -> 2.83 us  [the longest x1 2.2 us: ydiff(): lax.ppermute(jnp.concatenate([f[:, -1:] for f in fields]), ('px', 'py'), up)]
    ppermute x4 -> x2, starting transfers between devices: 13.3 us -> 7.89 us  [the longest x1 5.68 us: ydiff(): lax.ppermute(jnp.concatenate([f[:, :1] for f in fields]), ('px', 'py'), d...]
    all_to_all x2, blocking collectives: 64.6 us -> 68.8 us  [x_to_y(): lax.all_to_all(joined, LINES, split_axis=0, concat_axis=0, tiled=True)]
    unnamed x53 -> x51, local copies, waits for them, and re-layouts: 8.27 us -> 7.79 us
  transfers between devices with their start and end apart: 10 -> 8, of which waited for: 3 -> 4; matrix products, arithmetic and copies ran while one was open for 5% -> 5% of each run, Pallas kernels for 0% -> 0%
where the time goes in v2:
time: 280 us; the launch traced here: 278 us
  blocking collectives  133 us (48%)
  waiting for transfers between devices  38.8 us (14%)
  local copies, waits for them, and re-layouts  38.2 us (14%)
  starting transfers between devices  34.3 us (12%)
  matrix products  18.1 us (6%)
  other arithmetic  14.6 us (5%)
    all_to_all x2, blocking collectives, x_to_y(): lax.all_to_all(joined, LINES, split_axis=0, concat_axis=0, tiled=True)  68.8 us
    all_to_all x1, blocking collectives, y_to_x(): lax.all_to_all(joined, LINES, split_axis=0, concat_axis=0, tiled=True)  35.3 us
    all_to_all x1, blocking collectives, x_to_block(): lax.all_to_all(joined, 'px', split_axis=0, concat_axis=1, tiled=True)  29.1 us
    all_to_all x1, waiting for transfers between devices, block_to_x(): lax.all_to_all(joined, 'px', split_axis=1, concat_axis=0, tiled=True)  22.8 us
    all_to_all x1, waiting for transfers between devices, y_to_x(): lax.all_to_all(joined, LINES, split_axis=0, concat_axis=0, tiled=True)  13.1 us
    dot_general x3, matrix products, along_y(): return lax.dot_general(matrix, field, dims, precision=HIGH)  11.9 us
    ppermute x2, starting transfers between devices, ydiff_block(): lax.ppermute(field[:, -1:], 'py', [(i, i + 1) for i in range(count - 1)])  7.96 us
    unnamed x51, local copies, waits for them, and re-layouts  7.79 us
  transfers between devices with their start and end apart: 8, of which 4 were waited for; matrix products, arithmetic and copies ran while one was open for 5% of the time, Pallas kernels for 0%

profile of v2, /device:TPU:1, one launch (start us, length us, event | category | flops | bytes accessed | tf_op | source)
XLA Modules:
  0.0 278.4 jit_solution(4168258122369963983)
XLA Ops:
  1.8 3.3 %collective-permute-start = (f32[32,1,128]{2,1,0:T(1,128)S(1)}, f32[32,1,128]{2,1,0:T(1,128)S(1)}, u32[]{:S(2)}, u32[]{:S(2)}) collective-permute-start(f32[32,1,128]{2,1,0:T(1,128)S(1)} %get-tuple-element.24), channel_id=1, source_target_pairs={{1,0},{2,1},{3,2},{4,3},{5,4},{6,5},{7,6},{8,7},{9,8},{10,9},{11,1... | collective-permute-start | bytes 49160 | tf_op jit(solution)/shard_map/ppermute | solution.py:14
  5.2 4.6 %collective-permute-start.1 = (f32[32,1,128]{2,1,0:T(1,128)S(1)}, f32[32,1,128]{2,1,0:T(1,128)S(1)}, u32[]{:S(2)}, u32[]{:S(2)}) collective-permute-start(f32[32,1,128]{2,1,0:T(1,128)S(1)} %get-tuple-element.25), channel_id=1, source_target_pairs={{0,1},{1,2},{2,3},{3,4},{4,5},{5,6},{6,7},{7,8},{8,9},{9,10},{10,1... | collective-permute-start | bytes 49160 | tf_op jit(solution)/shard_map/ppermute | solution.py:13
  9.8 1.6 slice.173
  13.4 2.6 copy.35
  15.9 5.1 %all-to-all-start = ((f32[32,64,256]{2,0,1:T(8,128)}), f32[32,64,256]{2,0,1:T(8,128)S(1)}, u32[]{:S(2)}, u32[]{:S(2)}) async-start(f32[32,64,256]{2,0,1:T(8,128)} %copy.35), calls=%async_computation | async-start | bytes 4194304 | tf_op jit(solution)/shard_map/all_to_all | solution.py:80
  21.0 1.8 copy.40
  24.1 22.8 %all-to-all-done = f32[32,64,256]{2,0,1:T(8,128)S(1)} async-done(((f32[32,64,256]{2,0,1:T(8,128)}), f32[32,64,256]{2,0,1:T(8,128)S(1)}, u32[]{:S(2)}, u32[]{:S(2)}) %all-to-all-start) | async-done | bytes 2097184 | tf_op jit(solution)/shard_map/all_to_all | solution.py:80
  53.6 40.3 %all_to_all.56 = f32[128,8,512]{2,1,0:T(8,128)S(1)} all-to-all(f32[128,8,512]{2,1,0:T(8,128)S(1)} %copy.42), channel_id=1, replica_groups=mesh['px'=8,'py'=16] {'py','px'}, dimensions={0} | all-to-all | bytes 4194304 | tf_op jit(solution)/shard_map/all_to_all | solution.py:94
  94.0 4.6 %convolution_bitcast_fusion.3 = f32[1024,256]{0,1:T(8,128)} fusion(f32[1024,1024]{1,0:T(8,128)S(1)} %copy-done.1, f32[1024,512]{1,0:T(8,128)S(1)} %bitcast.82), kind=kOutput, calls=%fused_computation.14 | convolution fusion | flops 1610612736 | bytes 6291456 | tf_op jit(solution)/shard_map/dot_general | solution.py:75
  98.6 2.5 reshape.27
  101.0 3.8 %copy.43 = f32[16,64,8,32]{1,0,3,2:T(8,128)} copy(f32[16,64,8,32]{3,1,2,0:T(8,128)} %bitcast.71) | data formatting | bytes 2097152 | tf_op jit(solution)/shard_map/transpose | solution.py:120
  104.9 2.0 reshape.28
  106.9 4.3 %convolution_bitcast_fusion.2 = f32[1024,256]{0,1:T(8,128)S(1)} fusion(f32[1024,256]{0,1:T(8,128)S(1)} %reshape.28, f32[1024,1024]{1,0:T(8,128)} %param.9), kind=kOutput, calls=%fused_computation.13 | convolution fusion | flops 1610612736 | bytes 6291456 | tf_op jit(solution)/shard_map/dot_general | solution.py:75
  112.7 2.9 %copy.44 = f32[1024,512]{1,0:T(8,128)} copy(f32[1024,512]{0,1:T(8,128)} %pad_maximum_fusion.2) | data formatting | bytes 4194304 | tf_op jit(solution)/shard_map/concatenate | solution.py:101
  115.6 35.3 %all_to_all.57 = f32[128,8,512]{2,1,0:T(8,128)S(1)} all-to-all(f32[128,8,512]{2,1,0:T(8,128)} %bitcast.83), channel_id=1, replica_groups=mesh['px'=8,'py'=16] {'py','px'}, dimensions={0} | all-to-all | bytes 4194304 | tf_op jit(solution)/shard_map/all_to_all | solution.py:104
  154.5 2.2 collective-permute-start.3
  156.8 5.7 %collective-permute-start.2 = (f32[256,1,256]{2,0,1:T(8,128)S(1)}, f32[256,1,256]{2,0,1:T(8,128)S(1)}, u32[]{:S(2)}, u32[]{:S(2)}) collective-permute-start(f32[256,1,256]{2,0,1:T(8,128)S(1)} %pad_maximum_fusion.13), channel_id=1, source_target_pairs={{16,0},{32,16},{48,32},{64,48},{80,64},{96,80},{112,96},{1,112},{1... | collective-permute-start | bytes 786440 | tf_op jit(solution)/shard_map/ppermute | solution.py:59
  162.5 1.9 bitcast_multiply_fusion.2
  164.4 2.2 collective-permute-done.3
  168.9 28.5 %all_to_all.58 = f32[128,8,256]{2,1,0:T(8,128)S(1)} all-to-all(f32[128,8,256]{2,1,0:T(8,128)S(1)} %copy.49), channel_id=1, replica_groups=mesh['px'=8,'py'=16] {'py','px'}, dimensions={0} | all-to-all | bytes 2097152 | tf_op jit(solution)/shard_map/all_to_all | solution.py:94
  197.4 3.0 %convolution_bitcast_fusion.1 = f32[1024,256]{0,1:T(8,128)} fusion(f32[1024,1024]{1,0:T(8,128)S(1)} %copy-done.2, f32[128,8,256]{2,1,0:T(8,128)S(1)} %all_to_all.58), kind=kOutput, calls=%fused_computation.12 | convolution fusion | flops 1610612736 | bytes 6291456 | tf_op jit(solution)/shard_map/dot_general | solution.py:75
  200.4 2.5 copy.50
  202.9 5.8 %all-to-all-start.4 = ((f32[128,8,256]{2,1,0:T(8,128)}), f32[128,8,256]{2,1,0:T(8,128)}, u32[]{:S(2)}, u32[]{:S(2)}) async-start(f32[128,8,256]{2,1,0:T(8,128)} %bitcast.85), calls=%async_computation.4 | async-start | bytes 2097152 | tf_op jit(solution)/shard_map/all_to_all | solution.py:104
  208.7 3.5 %fusion.28 = f32[128,8,256]{2,0,1:T(8,128)S(1)} fusion(f32[128,8,256]{2,0,1:T(8,128)} %get-tuple-element.19, f32[128,1,256]{2,0,1:T(8,128)S(1)} %get-tuple-element.29, f32[128,1,256]{2,0,1:T(8,128)} %get-tuple-element.27, f32[128,8,256]{2,0,1:T(8,128)} %get-tuple-element.18, f32[127,8,256]{2,0,1:T(8,128)} %bitcast.78, f32[256,256]{1,0:T(8,128)S(1)} %copy-done), kind=kOutput, calls=%fused_computation.45 | convolution fusion | flops 405012480 | bytes 4710400 | tf_op jit(solution)/shard_map/dot_general | solution.py:70
  214.3 13.1 %all-to-all-done.4 = f32[128,8,256]{2,1,0:T(8,128)} async-done(((f32[128,8,256]{2,1,0:T(8,128)}), f32[128,8,256]{2,1,0:T(8,128)}, u32[]{:S(2)}, u32[]{:S(2)}) %all-to-all-start.4) | async-done | bytes 1048608 | tf_op jit(solution)/shard_map/all_to_all | solution.py:104
  227.4 1.7 copy.55
  229.9 4.5 %bitcast_multiply_fusion.1 = (f32[128,8,256]{2,0,1:T(8,128)S(1)}, f32[256,8,128]{0,2,1:T(8,128)S(1)}) fusion(f32[256,8,128]{0,2,1:T(8,128)S(1)} %copy.62, f32[127,8,256]{2,0,1:T(8,128)S(1)} %slice.236, f32[128,8,256]{2,1,0:T(8,128)} %all-to-all-done.4, f32[128,8,256]{2,0,1:T(8,128)S(1)} %fusion.44, f32[127,8,256]{2,0,1:T(8,128)S(1)} %copy-done.6, ...), kind=kLoop, calls=%fused_computation.66 | loop fusion | flops 3932160 | bytes 15679488 | tf_op jit(solution)/shard_map/mul | solution.py:37
  235.6 2.0 copy.58
  237.6 29.1 %all_to_all.59 = f32[256,8,256]{2,1,0:T(8,128)S(1)} all-to-all(f32[256,8,256]{2,1,0:T(8,128)} %copy.58), channel_id=1, replica_groups=mesh['px'=8,'py'=16] {'px'}, dimensions={0} | all-to-all | bytes 4194304 | tf_op jit(solution)/shard_map/all_to_all | solution.py:87
  267.3 4.3 %collective-permute-start.4 = (f32[32,1,128]{2,1,0:T(1,128)S(1)}, f32[32,1,128]{2,1,0:T(1,128)S(1)}, u32[]{:S(2)}, u32[]{:S(2)}) collective-permute-start(f32[32,1,128]{2,1,0:T(1,128)S(1)} %get-tuple-element.5), channel_id=1, source_target_pairs={{1,0},{2,1},{3,2},{4,3},{5,4},{6,5},{7,6},{8,7},{9,8},{10,9},{11,1... | collective-permute-start | bytes 49160 | tf_op jit(solution)/shard_map/ppermute | solution.py:14
  271.7 3.3 %collective-permute-start.5 = (f32[32,1,128]{2,1,0:T(1,128)S(1)}, f32[32,1,128]{2,1,0:T(1,128)S(1)}, u32[]{:S(2)}, u32[]{:S(2)}) collective-permute-start(f32[32,1,128]{2,1,0:T(1,128)S(1)} %get-tuple-element.6), channel_id=1, source_target_pairs={{0,1},{1,2},{2,3},{3,4},{4,5},{5,6},{6,7},{7,8},{8,9},{9,10},{10,1... | collective-permute-start | bytes 49160 | tf_op jit(solution)/shard_map/ppermute | solution.py:13
  275.0 1.8 slice_subtract_fusion
  (91 shorter events, 24.4 us)
Async XLA Ops:
  0.6 48.4 %copy-start = (f32[256,256]{1,0:T(8,128)S(1)}, f32[256,256]{1,0:T(8,128)}, u32[]{:S(2)}) copy-start(f32[256,256]{1,0:T(8,128)} %param.8) | copy-start | bytes 786436
  0.6 11.7 %copy-start.3 = (f32[32,64,128]{2,1,0:T(8,128)S(1)}, f32[32,64,128]{2,1,0:T(8,128)}, u32[]{:S(2)}) copy-start(f32[32,64,128]{2,1,0:T(8,128)} %param.5) | copy-start | bytes 3145732
  0.7 11.7 %copy-start.11 = (f32[32,64,128]{2,1,0:T(8,128)S(1)}, f32[32,64,128]{2,1,0:T(8,128)}, u32[]{:S(2)}) copy-start(f32[32,64,128]{2,1,0:T(8,128)} %param.6) | copy-start | bytes 3145732
  1.8 10.8 %collective-permute-start = (f32[32,1,128]{2,1,0:T(1,128)S(1)}, f32[32,1,128]{2,1,0:T(1,128)S(1)}, u32[]{:S(2)}, u32[]{:S(2)}) collective-permute-start(f32[32,1,128]{2,1,0:T(1,128)S(1)} %get-tuple-element.24), channel_id=1, source_target_pairs={{1,0},{2,1},{3,2},{4,3},{5,4},{6,5},{7,6},{8,7},{9,8},{10,9},{11,1... | collective-permute-start | bytes 49160 | tf_op jit(solution)/shard_map/ppermute | solution.py:14
  5.2 7.5 %collective-permute-start.1 = (f32[32,1,128]{2,1,0:T(1,128)S(1)}, f32[32,1,128]{2,1,0:T(1,128)S(1)}, u32[]{:S(2)}, u32[]{:S(2)}) collective-permute-start(f32[32,1,128]{2,1,0:T(1,128)S(1)} %get-tuple-element.25), channel_id=1, source_target_pairs={{0,1},{1,2},{2,3},{3,4},{4,5},{5,6},{6,7},{7,8},{8,9},{9,10},{10,1... | collective-permute-start | bytes 49160 | tf_op jit(solution)/shard_map/ppermute | solution.py:13
  11.4 1.0 copy-start.9
  15.9 31.0 %all-to-all-start = ((f32[32,64,256]{2,0,1:T(8,128)}), f32[32,64,256]{2,0,1:T(8,128)S(1)}, u32[]{:S(2)}, u32[]{:S(2)}) async-start(f32[32,64,256]{2,0,1:T(8,128)} %copy.35), calls=%async_computation | async-start | bytes 4194304 | tf_op jit(solution)/shard_map/all_to_all | solution.py:80
  49.8 1.1 copy-start.5
  50.9 1.2 copy-start.20
  53.6 40.4 %copy-start.1 = (f32[1024,1024]{1,0:T(8,128)S(1)}, f32[1024,1024]{1,0:T(8,128)}, u32[]{:S(2)}) copy-start(f32[1024,1024]{1,0:T(8,128)} %param.9) | copy-start | bytes 12582916
  106.9 4.3 %copy-start.21 = (f32[1024,256]{0,1:T(8,128)S(1)}, f32[1024,256]{0,1:T(8,128)}, u32[]{:S(2)}) copy-start(f32[1024,256]{0,1:T(8,128)} %convolution_bitcast_fusion.3) | copy-start | bytes 3145732
  151.4 1.3 copy-start.7
  151.6 1.1 copy-start.13
  151.6 10.9 %copy-start.19 = (f32[128,8,256]{2,1,0:T(8,128)}, f32[128,8,256]{2,1,0:T(8,128)S(1)}, u32[]{:S(2)}) copy-start(f32[128,8,256]{2,1,0:T(8,128)S(1)} %get-tuple-element.14) | copy-start | bytes 3145732
  153.9 8.5 %copy-start.17 = (f32[127,8,256]{2,0,1:T(8,128)}, f32[127,8,256]{2,0,1:T(8,128)S(1)}, u32[]{:S(2)}) copy-start(f32[127,8,256]{2,0,1:T(8,128)S(1)} %slice.234) | copy-start | bytes 3121156
  154.5 9.9 %copy-start.18 = (f32[127,8,256]{2,0,1:T(8,128)}, f32[127,8,256]{2,0,1:T(8,128)S(1)}, u32[]{:S(2)}) copy-start(f32[127,8,256]{2,0,1:T(8,128)S(1)} %copy.68) | copy-start | bytes 3121156
  154.5 12.1 %collective-permute-start.3 = (f32[256,1,256]{2,0,1:T(8,128)S(1)}, f32[256,1,256]{2,0,1:T(8,128)S(1)}, u32[]{:S(2)}, u32[]{:S(2)}) collective-permute-start(f32[256,1,256]{2,0,1:T(8,128)S(1)} %pad_maximum_fusion.14), channel_id=1, source_target_pairs={{0,16},{16,32},{32,48},{48,64},{64,80},{80,96},{96,112},{112,1},{1... | collective-permute-start | bytes 786440 | tf_op jit(solution)/shard_map/ppermute | solution.py:58
  156.8 10.5 %collective-permute-start.2 = (f32[256,1,256]{2,0,1:T(8,128)S(1)}, f32[256,1,256]{2,0,1:T(8,128)S(1)}, u32[]{:S(2)}, u32[]{:S(2)}) collective-permute-start(f32[256,1,256]{2,0,1:T(8,128)S(1)} %pad_maximum_fusion.13), channel_id=1, source_target_pairs={{16,0},{32,16},{48,32},{64,48},{80,64},{96,80},{112,96},{1,112},{1... | collective-permute-start | bytes 786440 | tf_op jit(solution)/shard_map/ppermute | solution.py:59
  167.9 29.5 %copy-start.2 = (f32[1024,1024]{1,0:T(8,128)S(1)}, f32[1024,1024]{1,0:T(8,128)}, u32[]{:S(2)}) copy-start(f32[1024,1024]{1,0:T(8,128)} %param.9) | copy-start | bytes 12582916
  202.9 24.5 %all-to-all-start.4 = ((f32[128,8,256]{2,1,0:T(8,128)}), f32[128,8,256]{2,1,0:T(8,128)}, u32[]{:S(2)}, u32[]{:S(2)}) async-start(f32[128,8,256]{2,1,0:T(8,128)} %bitcast.85), calls=%async_computation.4 | async-start | bytes 2097152 | tf_op jit(solution)/shard_map/all_to_all | solution.py:104
  212.2 1.0 copy-start.15
  227.4 1.8 copy-start.6
  227.4 1.9 copy-start.8
  227.4 2.2 copy-start.14
  227.4 2.5 copy-start.16
  266.7 8.3 %copy-start.12 = (f32[32,64,128]{2,1,0:T(8,128)S(1)}, f32[32,64,128]{2,1,0:T(8,128)}, u32[]{:S(2)}) copy-start(f32[32,64,128]{2,1,0:T(8,128)} %param.6) | copy-start | bytes 3145732
  266.9 8.1 %copy-start.4 = (f32[32,64,128]{2,1,0:T(8,128)S(1)}, f32[32,64,128]{2,1,0:T(8,128)}, u32[]{:S(2)}) copy-start(f32[32,64,128]{2,1,0:T(8,128)} %param.5) | copy-start | bytes 3145732
  267.0 8.0 %copy-start.10 = (f32[32,64,127]{2,1,0:T(8,128)S(1)}, f32[32,64,127]{2,1,0:T(8,128)}, u32[]{:S(2)}) copy-start(f32[32,64,127]{2,1,0:T(8,128)} %copy-done.9) | copy-start | bytes 3121156
  267.3 9.5 %collective-permute-start.4 = (f32[32,1,128]{2,1,0:T(1,128)S(1)}, f32[32,1,128]{2,1,0:T(1,128)S(1)}, u32[]{:S(2)}, u32[]{:S(2)}) collective-permute-start(f32[32,1,128]{2,1,0:T(1,128)S(1)} %get-tuple-element.5), channel_id=1, source_target_pairs={{1,0},{2,1},{3,2},{4,3},{5,4},{6,5},{7,6},{8,7},{9,8},{10,9},{11,1... | collective-permute-start | bytes 49160 | tf_op jit(solution)/shard_map/ppermute | solution.py:14
  271.7 5.2 %collective-permute-start.5 = (f32[32,1,128]{2,1,0:T(1,128)S(1)}, f32[32,1,128]{2,1,0:T(1,128)S(1)}, u32[]{:S(2)}, u32[]{:S(2)}) collective-permute-start(f32[32,1,128]{2,1,0:T(1,128)S(1)} %get-tuple-element.6), channel_id=1, source_target_pairs={{0,1},{1,2},{2,3},{3,4},{4,5},{5,6},{6,7},{7,8},{8,9},{9,10},{10,1... | collective-permute-start | bytes 49160 | tf_op jit(solution)/shard_map/ppermute | solution.py:13

commit v3 on v2

--- a/solution.py
+++ b/solution.py
@@ -121,14 +121,15 @@
 
 
 def local(initial, conduct, cotangent, inv_x, inv_y):
+    (tp,) = x_to_y(block_planes(cotangent))
+    ty = planes_to_y(tp, (initial.shape[0], initial.shape[1]))
+    lam_second1_y = along_y(inv_y, ty, True)
     first0 = initial + RATE * (ydiff_block(initial) + zoperate_block(initial, conduct))
     f0x, cx = block_to_x(first0, conduct)
     half0 = along_x(f0x, inv_x, False)
     second0 = half0 + RATE * (xdiff(half0) + zoperate(half0, cx))
-    s0y, tp = x_to_y(second0, block_planes(cotangent))
-    ty = planes_to_y(tp, (initial.shape[0], initial.shape[1]))
+    (s0y,) = x_to_y(second0)
     state1_y = along_y(inv_y, s0y, False)
-    lam_second1_y = along_y(inv_y, ty, True)
     state1, ls1 = y_to_x(state1_y, lam_second1_y)
     lam_half1 = ls1 + RATE * (xdiff(ls1) + zoperate(ls1, cx))
     lam_first1 = along_x(lam_half1, inv_x, True)

time: 280 us -> 276 us (0.986)
  blocking collectives: 133 us -> 92.8 us
  starting transfers between devices: 34.3 us -> 50.9 us
  waiting for transfers between devices: 38.8 us -> 52.3 us
  matrix products: 18.1 us -> 21.5 us
    all_to_all x2 -> x1, blocking collectives: 68.8 us -> 28.5 us  [x_to_y(): lax.all_to_all(joined, LINES, split_axis=0, concat_axis=0, tiled=True)]
    all_to_all x0 -> x2, starting transfers between devices: none -> 16.6 us  [x_to_y(): lax.all_to_all(joined, LINES, split_axis=0, concat_axis=0, tiled=True)]
    all_to_all x0 -> x2, waiting for transfers between devices: none -> 13.6 us  [x_to_y(): lax.all_to_all(joined, LINES, split_axis=0, concat_axis=0, tiled=True)]
    unnamed x51 -> x47, local copies, waits for them, and re-layouts: 7.79 us -> 9.15 us
  transfers between devices with their start and end apart: 8 -> 10, of which waited for: 4 -> 6; matrix products, arithmetic and copies ran while one was open for 5% -> 13% of each run, Pallas kernels for 0% -> 0%
where the time goes in v3:
time: 276 us; the launch traced here: 274 us
  blocking collectives  92.8 us (34%)
  waiting for transfers between devices  52.3 us (19%)
  starting transfers between devices  50.9 us (18%)
  local copies, waits for them, and re-layouts  40.8 us (15%)
  matrix products  21.5 us (8%)
  other arithmetic  14.5 us (5%)
    all_to_all x1, blocking collectives, y_to_x(): lax.all_to_all(joined, LINES, split_axis=0, concat_axis=0, tiled=True)  35.1 us
    all_to_all x1, blocking collectives, x_to_block(): lax.all_to_all(joined, 'px', split_axis=0, concat_axis=1, tiled=True)  29.1 us
    all_to_all x1, blocking collectives, x_to_y(): lax.all_to_all(joined, LINES, split_axis=0, concat_axis=0, tiled=True)  28.5 us
    all_to_all x1, waiting for transfers between devices, block_to_x(): lax.all_to_all(joined, 'px', split_axis=1, concat_axis=0, tiled=True)  22.7 us
    all_to_all x2, starting transfers between devices, x_to_y(): lax.all_to_all(joined, LINES, split_axis=0, concat_axis=0, tiled=True)  16.6 us
    dot_general x3, matrix products, along_y(): return lax.dot_general(matrix, field, dims, precision=HIGH)  14.1 us
    all_to_all x2, waiting for transfers between devices, x_to_y(): lax.all_to_all(joined, LINES, split_axis=0, concat_axis=0, tiled=True)  13.6 us
    all_to_all x1, waiting for transfers between devices, y_to_x(): lax.all_to_all(joined, LINES, split_axis=0, concat_axis=0, tiled=True)  13.2 us
  transfers between devices with their start and end apart: 10, of which 6 were waited for; matrix products, arithmetic and copies ran while one was open for 13% of the time, Pallas kernels for 0%

profile of v3, /device:TPU:1, one launch (start us, length us, event | category | flops | bytes accessed | tf_op | source)
XLA Modules:
  0.0 273.8 jit_solution(7898724076164331334)
XLA Ops:
  1.8 3.3 %collective-permute-start = (f32[32,1,128]{2,1,0:T(1,128)S(1)}, f32[32,1,128]{2,1,0:T(1,128)S(1)}, u32[]{:S(2)}, u32[]{:S(2)}) collective-permute-start(f32[32,1,128]{2,1,0:T(1,128)S(1)} %get-tuple-element.24), channel_id=1, source_target_pairs={{1,0},{2,1},{3,2},{4,3},{5,4},{6,5},{7,6},{8,7},{9,8},{10,9},{11,1... | collective-permute-start | bytes 49160 | tf_op jit(solution)/shard_map/ppermute | solution.py:14
  5.2 4.6 %collective-permute-start.1 = (f32[32,1,128]{2,1,0:T(1,128)S(1)}, f32[32,1,128]{2,1,0:T(1,128)S(1)}, u32[]{:S(2)}, u32[]{:S(2)}) collective-permute-start(f32[32,1,128]{2,1,0:T(1,128)S(1)} %get-tuple-element.25), channel_id=1, source_target_pairs={{0,1},{1,2},{2,3},{3,4},{4,5},{5,6},{6,7},{7,8},{8,9},{9,10},{10,1... | collective-permute-start | bytes 49160 | tf_op jit(solution)/shard_map/ppermute | solution.py:13
  13.1 2.6 copy.35
  15.7 5.1 %all-to-all-start = ((f32[32,64,256]{2,0,1:T(8,128)}), f32[32,64,256]{2,0,1:T(8,128)S(1)}, u32[]{:S(2)}, u32[]{:S(2)}) async-start(f32[32,64,256]{2,0,1:T(8,128)} %copy.35), calls=%async_computation | async-start | bytes 4194304 | tf_op jit(solution)/shard_map/all_to_all | solution.py:80
  23.9 22.7 %all-to-all-done = f32[32,64,256]{2,0,1:T(8,128)S(1)} async-done(((f32[32,64,256]{2,0,1:T(8,128)}), f32[32,64,256]{2,0,1:T(8,128)S(1)}, u32[]{:S(2)}, u32[]{:S(2)}) %all-to-all-start) | async-done | bytes 2097184 | tf_op jit(solution)/shard_map/all_to_all | solution.py:80
  46.6 10.7 %all-to-all-start.2 = ((f32[128,8,256]{2,1,0:T(8,128)}), f32[128,8,256]{2,1,0:T(8,128)S(1)}, u32[]{:S(2)}, u32[]{:S(2)}) async-start(f32[128,8,256]{2,1,0:T(8,128)} %copy.42), calls=%async_computation.2 | async-start | bytes 2097152 | tf_op jit(solution)/shard_map/all_to_all | solution.py:94
  62.6 1.8 fusion.44
  68.0 8.3 %all-to-all-done.2 = f32[128,8,256]{2,1,0:T(8,128)S(1)} async-done(((f32[128,8,256]{2,1,0:T(8,128)}), f32[128,8,256]{2,1,0:T(8,128)S(1)}, u32[]{:S(2)}, u32[]{:S(2)}) %all-to-all-start.2) | async-done | bytes 1048608 | tf_op jit(solution)/shard_map/all_to_all | solution.py:94
  76.2 5.8 %all-to-all-start.1 = ((f32[128,8,256]{2,1,0:T(8,128)}), f32[128,8,256]{2,1,0:T(8,128)}, u32[]{:S(2)}, u32[]{:S(2)}) async-start(f32[128,8,256]{2,1,0:T(8,128)} %copy.40), calls=%async_computation.1 | async-start | bytes 2097152 | tf_op jit(solution)/shard_map/all_to_all | solution.py:94
  82.1 2.5 reshape_reshape.3
  84.5 3.8 %copy.43 = f32[16,64,8,32]{1,0,3,2:T(8,128)} copy(f32[16,64,8,32]{3,1,2,0:T(8,128)} %bitcast.71) | data formatting | bytes 2097152 | tf_op jit(solution)/shard_map/transpose | solution.py:120
  88.4 2.0 reshape.24
  90.4 5.1 %fusion.86 = f32[1024,256]{0,1:T(8,128)} fusion(f32[1024,1024]{1,0:T(8,128)} %param.9, f32[1024,256]{0,1:T(8,128)S(1)} %reshape.24), kind=kOutput, calls=%fused_computation.120 | convolution fusion | flops 1610612736 | bytes 6291456 | tf_op jit(solution)/shard_map/dot_general | solution.py:75
  95.5 5.3 %all-to-all-done.1 = f32[128,8,256]{2,1,0:T(8,128)} async-done(((f32[128,8,256]{2,1,0:T(8,128)}), f32[128,8,256]{2,1,0:T(8,128)}, u32[]{:S(2)}, u32[]{:S(2)}) %all-to-all-start.1) | async-done | bytes 1048608 | tf_op jit(solution)/shard_map/all_to_all | solution.py:94
  100.8 6.0 %convolution_bitcast_fusion.2 = f32[1024,256]{0,1:T(8,128)S(1)} fusion(f32[1024,1024]{1,0:T(8,128)} %param.9, f32[128,8,256]{2,1,0:T(8,128)} %all-to-all-done.1), kind=kOutput, calls=%fused_computation.12 | convolution fusion | flops 1610612736 | bytes 6291456 | tf_op jit(solution)/shard_map/dot_general | solution.py:75
  108.3 2.9 %copy.44 = f32[1024,512]{1,0:T(8,128)} copy(f32[1024,512]{0,1:T(8,128)} %pad_maximum_fusion.1) | data formatting | bytes 4194304 | tf_op jit(solution)/shard_map/concatenate | solution.py:101
  111.1 35.1 %all_to_all.61 = f32[128,8,512]{2,1,0:T(8,128)S(1)} all-to-all(f32[128,8,512]{2,1,0:T(8,128)} %bitcast.81), channel_id=1, replica_groups=mesh['px'=8,'py'=16] {'py','px'}, dimensions={0} | all-to-all | bytes 4194304 | tf_op jit(solution)/shard_map/all_to_all | solution.py:104
  149.9 2.2 collective-permute-start.3
  152.1 5.7 %collective-permute-start.2 = (f32[256,1,256]{2,0,1:T(8,128)S(1)}, f32[256,1,256]{2,0,1:T(8,128)S(1)}, u32[]{:S(2)}, u32[]{:S(2)}) collective-permute-start(f32[256,1,256]{2,0,1:T(8,128)S(1)} %pad_maximum_fusion.12), channel_id=1, source_target_pairs={{16,0},{32,16},{48,32},{64,48},{80,64},{96,80},{112,96},{1,112},{1... | collective-permute-start | bytes 786440 | tf_op jit(solution)/shard_map/ppermute | solution.py:59
  157.8 1.9 bitcast_multiply_fusion.2
  159.8 2.2 collective-permute-done.3
  164.2 28.5 %all_to_all.62 = f32[128,8,256]{2,1,0:T(8,128)S(1)} all-to-all(f32[128,8,256]{2,1,0:T(8,128)S(1)} %copy.49), channel_id=1, replica_groups=mesh['px'=8,'py'=16] {'py','px'}, dimensions={0} | all-to-all | bytes 2097152 | tf_op jit(solution)/shard_map/all_to_all | solution.py:94
  192.7 3.0 %convolution_bitcast_fusion.1 = f32[1024,256]{0,1:T(8,128)} fusion(f32[1024,1024]{1,0:T(8,128)S(1)} %copy-done.1, f32[128,8,256]{2,1,0:T(8,128)S(1)} %all_to_all.62), kind=kOutput, calls=%fused_computation.11 | convolution fusion | flops 1610612736 | bytes 6291456 | tf_op jit(solution)/shard_map/dot_general | solution.py:75
  195.7 2.5 copy.50
  198.3 5.8 %all-to-all-start.5 = ((f32[128,8,256]{2,1,0:T(8,128)}), f32[128,8,256]{2,1,0:T(8,128)}, u32[]{:S(2)}, u32[]{:S(2)}) async-start(f32[128,8,256]{2,1,0:T(8,128)} %bitcast.83), calls=%async_computation.5 | async-start | bytes 2097152 | tf_op jit(solution)/shard_map/all_to_all | solution.py:104
  204.1 3.5 %fusion.28 = f32[128,8,256]{2,0,1:T(8,128)S(1)} fusion(f32[128,8,256]{2,0,1:T(8,128)} %get-tuple-element.19, f32[128,1,256]{2,0,1:T(8,128)S(1)} %get-tuple-element.29, f32[128,1,256]{2,0,1:T(8,128)} %get-tuple-element.27, f32[128,8,256]{2,0,1:T(8,128)} %get-tuple-element.18, f32[127,8,256]{2,0,1:T(8,128)} %bitcast.78, f32[256,256]{1,0:T(8,128)S(1)} %copy-done), kind=kOutput, calls=%fused_computation.43 | convolution fusion | flops 405012480 | bytes 4710400 | tf_op jit(solution)/shard_map/dot_general | solution.py:70
  209.6 13.2 %all-to-all-done.5 = f32[128,8,256]{2,1,0:T(8,128)} async-done(((f32[128,8,256]{2,1,0:T(8,128)}), f32[128,8,256]{2,1,0:T(8,128)}, u32[]{:S(2)}, u32[]{:S(2)}) %all-to-all-start.5) | async-done | bytes 1048608 | tf_op jit(solution)/shard_map/all_to_all | solution.py:104
  225.3 4.5 %bitcast_multiply_fusion.1 = (f32[128,8,256]{2,0,1:T(8,128)S(1)}, f32[256,8,128]{0,2,1:T(8,128)S(1)}) fusion(f32[256,8,128]{0,2,1:T(8,128)S(1)} %copy.62, f32[127,8,256]{2,0,1:T(8,128)S(1)} %slice.226, f32[128,8,256]{2,1,0:T(8,128)} %all-to-all-done.5, f32[128,8,256]{2,0,1:T(8,128)S(1)} %fusion.44, f32[127,8,256]{2,0,1:T(8,128)S(1)} %copy-done.5, ...), kind=kLoop, calls=%fused_computation.64 | loop fusion | flops 3932160 | bytes 15679488 | tf_op jit(solution)/shard_map/mul | solution.py:37
  231.0 2.0 copy.58
  233.0 29.1 %all_to_all.63 = f32[256,8,256]{2,1,0:T(8,128)S(1)} all-to-all(f32[256,8,256]{2,1,0:T(8,128)} %copy.58), channel_id=1, replica_groups=mesh['px'=8,'py'=16] {'px'}, dimensions={0} | all-to-all | bytes 4194304 | tf_op jit(solution)/shard_map/all_to_all | solution.py:87
  262.8 4.3 %collective-permute-start.4 = (f32[32,1,128]{2,1,0:T(1,128)S(1)}, f32[32,1,128]{2,1,0:T(1,128)S(1)}, u32[]{:S(2)}, u32[]{:S(2)}) collective-permute-start(f32[32,1,128]{2,1,0:T(1,128)S(1)} %get-tuple-element.5), channel_id=1, source_target_pairs={{1,0},{2,1},{3,2},{4,3},{5,4},{6,5},{7,6},{8,7},{9,8},{10,9},{11,1... | collective-permute-start | bytes 49160 | tf_op jit(solution)/shard_map/ppermute | solution.py:14
  267.1 3.3 %collective-permute-start.5 = (f32[32,1,128]{2,1,0:T(1,128)S(1)}, f32[32,1,128]{2,1,0:T(1,128)S(1)}, u32[]{:S(2)}, u32[]{:S(2)}) collective-permute-start(f32[32,1,128]{2,1,0:T(1,128)S(1)} %get-tuple-element.6), channel_id=1, source_target_pairs={{0,1},{1,2},{2,3},{3,4},{4,5},{5,6},{6,7},{7,8},{8,9},{9,10},{10,1... | collective-permute-start | bytes 49160 | tf_op jit(solution)/shard_map/ppermute | solution.py:13
  (88 shorter events, 33.3 us)
Async XLA Ops:
  0.6 62.0 %copy-start = (f32[256,256]{1,0:T(8,128)S(1)}, f32[256,256]{1,0:T(8,128)}, u32[]{:S(2)}) copy-start(f32[256,256]{1,0:T(8,128)} %param.8) | copy-start | bytes 786436
  0.6 10.7 %copy-start.2 = (f32[32,64,128]{2,1,0:T(8,128)S(1)}, f32[32,64,128]{2,1,0:T(8,128)}, u32[]{:S(2)}) copy-start(f32[32,64,128]{2,1,0:T(8,128)} %param.5) | copy-start | bytes 3145732
  0.7 10.7 %copy-start.10 = (f32[32,64,128]{2,1,0:T(8,128)S(1)}, f32[32,64,128]{2,1,0:T(8,128)}, u32[]{:S(2)}) copy-start(f32[32,64,128]{2,1,0:T(8,128)} %param.6) | copy-start | bytes 3145732
  1.8 9.9 %collective-permute-start = (f32[32,1,128]{2,1,0:T(1,128)S(1)}, f32[32,1,128]{2,1,0:T(1,128)S(1)}, u32[]{:S(2)}, u32[]{:S(2)}) collective-permute-start(f32[32,1,128]{2,1,0:T(1,128)S(1)} %get-tuple-element.24), channel_id=1, source_target_pairs={{1,0},{2,1},{3,2},{4,3},{5,4},{6,5},{7,6},{8,7},{9,8},{10,9},{11,1... | collective-permute-start | bytes 49160 | tf_op jit(solution)/shard_map/ppermute | solution.py:14
  5.2 6.6 %collective-permute-start.1 = (f32[32,1,128]{2,1,0:T(1,128)S(1)}, f32[32,1,128]{2,1,0:T(1,128)S(1)}, u32[]{:S(2)}, u32[]{:S(2)}) collective-permute-start(f32[32,1,128]{2,1,0:T(1,128)S(1)} %get-tuple-element.25), channel_id=1, source_target_pairs={{0,1},{1,2},{2,3},{3,4},{4,5},{5,6},{6,7},{7,8},{8,9},{9,10},{10,1... | collective-permute-start | bytes 49160 | tf_op jit(solution)/shard_map/ppermute | solution.py:13
  11.4 1.0 copy-start.8
  15.7 31.0 %all-to-all-start = ((f32[32,64,256]{2,0,1:T(8,128)}), f32[32,64,256]{2,0,1:T(8,128)S(1)}, u32[]{:S(2)}, u32[]{:S(2)}) async-start(f32[32,64,256]{2,0,1:T(8,128)} %copy.35), calls=%async_computation | async-start | bytes 4194304 | tf_op jit(solution)/shard_map/all_to_all | solution.py:80
  46.6 29.6 %all-to-all-start.2 = ((f32[128,8,256]{2,1,0:T(8,128)}), f32[128,8,256]{2,1,0:T(8,128)S(1)}, u32[]{:S(2)}, u32[]{:S(2)}) async-start(f32[128,8,256]{2,1,0:T(8,128)} %copy.42), calls=%async_computation.2 | async-start | bytes 2097152 | tf_op jit(solution)/shard_map/all_to_all | solution.py:94
  64.6 1.0 copy-start.4
  76.2 24.5 %all-to-all-start.1 = ((f32[128,8,256]{2,1,0:T(8,128)}), f32[128,8,256]{2,1,0:T(8,128)}, u32[]{:S(2)}, u32[]{:S(2)}) async-start(f32[128,8,256]{2,1,0:T(8,128)} %copy.40), calls=%async_computation.1 | async-start | bytes 2097152 | tf_op jit(solution)/shard_map/all_to_all | solution.py:94
  95.5 11.3 %copy-start.19 = (f32[1024,256]{0,1:T(8,128)S(1)}, f32[1024,256]{0,1:T(8,128)}, u32[]{:S(2)}) copy-start(f32[1024,256]{0,1:T(8,128)} %fusion.86) | copy-start | bytes 3145732
  146.7 1.3 copy-start.6
  146.9 1.1 copy-start.12
  146.9 10.9 %copy-start.18 = (f32[128,8,256]{2,1,0:T(8,128)}, f32[128,8,256]{2,1,0:T(8,128)S(1)}, u32[]{:S(2)}) copy-start(f32[128,8,256]{2,1,0:T(8,128)S(1)} %get-tuple-element.14) | copy-start | bytes 3145732
  149.3 8.5 %copy-start.16 = (f32[127,8,256]{2,0,1:T(8,128)}, f32[127,8,256]{2,0,1:T(8,128)S(1)}, u32[]{:S(2)}) copy-start(f32[127,8,256]{2,0,1:T(8,128)S(1)} %slice.224) | copy-start | bytes 3121156
  149.8 9.9 %copy-start.17 = (f32[127,8,256]{2,0,1:T(8,128)}, f32[127,8,256]{2,0,1:T(8,128)S(1)}, u32[]{:S(2)}) copy-start(f32[127,8,256]{2,0,1:T(8,128)S(1)} %copy.68) | copy-start | bytes 3121156
  149.9 12.1 %collective-permute-start.3 = (f32[256,1,256]{2,0,1:T(8,128)S(1)}, f32[256,1,256]{2,0,1:T(8,128)S(1)}, u32[]{:S(2)}, u32[]{:S(2)}) collective-permute-start(f32[256,1,256]{2,0,1:T(8,128)S(1)} %pad_maximum_fusion.13), channel_id=1, source_target_pairs={{0,16},{16,32},{32,48},{48,64},{64,80},{80,96},{96,112},{112,1},{1... | collective-permute-start | bytes 786440 | tf_op jit(solution)/shard_map/ppermute | solution.py:58
  152.1 10.5 %collective-permute-start.2 = (f32[256,1,256]{2,0,1:T(8,128)S(1)}, f32[256,1,256]{2,0,1:T(8,128)S(1)}, u32[]{:S(2)}, u32[]{:S(2)}) collective-permute-start(f32[256,1,256]{2,0,1:T(8,128)S(1)} %pad_maximum_fusion.12), channel_id=1, source_target_pairs={{16,0},{32,16},{48,32},{64,48},{80,64},{96,80},{112,96},{1,112},{1... | collective-permute-start | bytes 786440 | tf_op jit(solution)/shard_map/ppermute | solution.py:59
  163.3 29.5 %copy-start.1 = (f32[1024,1024]{1,0:T(8,128)S(1)}, f32[1024,1024]{1,0:T(8,128)}, u32[]{:S(2)}) copy-start(f32[1024,1024]{1,0:T(8,128)} %param.9) | copy-start | bytes 12582916
  198.3 24.5 %all-to-all-start.5 = ((f32[128,8,256]{2,1,0:T(8,128)}), f32[128,8,256]{2,1,0:T(8,128)}, u32[]{:S(2)}, u32[]{:S(2)}) async-start(f32[128,8,256]{2,1,0:T(8,128)} %bitcast.83), calls=%async_computation.5 | async-start | bytes 2097152 | tf_op jit(solution)/shard_map/all_to_all | solution.py:104
  207.6 1.0 copy-start.14
  222.8 1.8 copy-start.5
  222.8 1.9 copy-start.7
  222.8 2.2 copy-start.13
  222.8 2.5 copy-start.15
  262.1 8.3 %copy-start.11 = (f32[32,64,128]{2,1,0:T(8,128)S(1)}, f32[32,64,128]{2,1,0:T(8,128)}, u32[]{:S(2)}) copy-start(f32[32,64,128]{2,1,0:T(8,128)} %param.6) | copy-start | bytes 3145732
  262.4 8.1 %copy-start.3 = (f32[32,64,128]{2,1,0:T(8,128)S(1)}, f32[32,64,128]{2,1,0:T(8,128)}, u32[]{:S(2)}) copy-start(f32[32,64,128]{2,1,0:T(8,128)} %param.5) | copy-start | bytes 3145732
  262.4 8.0 %copy-start.9 = (f32[32,64,127]{2,1,0:T(8,128)S(1)}, f32[32,64,127]{2,1,0:T(8,128)}, u32[]{:S(2)}) copy-start(f32[32,64,127]{2,1,0:T(8,128)} %copy-done.8) | copy-start | bytes 3121156
  262.8 9.5 %collective-permute-start.4 = (f32[32,1,128]{2,1,0:T(1,128)S(1)}, f32[32,1,128]{2,1,0:T(1,128)S(1)}, u32[]{:S(2)}, u32[]{:S(2)}) collective-permute-start(f32[32,1,128]{2,1,0:T(1,128)S(1)} %get-tuple-element.5), channel_id=1, source_target_pairs={{1,0},{2,1},{3,2},{4,3},{5,4},{6,5},{7,6},{8,7},{9,8},{10,9},{11,1... | collective-permute-start | bytes 49160 | tf_op jit(solution)/shard_map/ppermute | solution.py:14
  267.1 5.2 %collective-permute-start.5 = (f32[32,1,128]{2,1,0:T(1,128)S(1)}, f32[32,1,128]{2,1,0:T(1,128)S(1)}, u32[]{:S(2)}, u32[]{:S(2)}) collective-permute-start(f32[32,1,128]{2,1,0:T(1,128)S(1)} %get-tuple-element.6), channel_id=1, source_target_pairs={{0,1},{1,2},{2,3},{3,4},{4,5},{5,6},{6,7},{7,8},{8,9},{9,10},{10,1... | collective-permute-start | bytes 49160 | tf_op jit(solution)/shard_map/ppermute | solution.py:13

commit v4 on v3

--- a/solution.py
+++ b/solution.py
@@ -128,12 +128,15 @@
     f0x, cx = block_to_x(first0, conduct)
     half0 = along_x(f0x, inv_x, False)
     second0 = half0 + RATE * (xdiff(half0) + zoperate(half0, cx))
-    (s0y,) = x_to_y(second0)
+    count = lax.axis_size(LINES)
+    s0y, ls1 = x_to_y(second0, lam_second1_y.reshape(count, -1, lam_second1_y.shape[1]))
+    ls1 = ls1.reshape(second0.shape)
     state1_y = along_y(inv_y, s0y, False)
-    state1, ls1 = y_to_x(state1_y, lam_second1_y)
+    (state1,) = y_to_x(state1_y)
     lam_half1 = ls1 + RATE * (xdiff(ls1) + zoperate(ls1, cx))
     lam_first1 = along_x(lam_half1, inv_x, True)
-    dy_state1, dy_lam_first1 = ydiff(state1, lam_first1)
+    (dy_lam_first1,) = ydiff(lam_first1)
+    (dy_state1,) = ydiff(state1)
     lam_state1 = lam_first1 + RATE * (dy_lam_first1 + zoperate(lam_first1, cx))
     first1 = state1 + RATE * (dy_state1 + zoperate(state1, cx))
     half1 = along_x(first1, inv_x, False)

time: 276 us -> 267 us (0.967)
  waiting for transfers between devices: 52.3 us -> 31.1 us
  starting transfers between devices: 50.9 us -> 57.9 us
  local copies, waits for them, and re-layouts: 40.8 us -> 46.8 us
    all_to_all x1 -> x2, blocking collectives: 28.5 us -> 64.2 us  [x_to_y(): lax.all_to_all(joined, LINES, split_axis=0, concat_axis=0, tiled=True)]
    all_to_all x1 -> x0, blocking collectives: 35.1 us -> none  [y_to_x(): lax.all_to_all(joined, LINES, split_axis=0, concat_axis=0, tiled=True)]
    all_to_all x1, waiting for transfers between devices: 22.7 us -> 8.57 us  [block_to_x(): lax.all_to_all(joined, 'px', split_axis=1, concat_axis=0, tiled=True)]
    all_to_all x2 -> x1, waiting for transfers between devices: 13.6 us -> 0.46 us  [x_to_y(): lax.all_to_all(joined, LINES, split_axis=0, concat_axis=0, tiled=True)]
    all_to_all x1 -> x2, waiting for transfers between devices: 13.2 us -> 4.47 us  [y_to_x(): lax.all_to_all(joined, LINES, split_axis=0, concat_axis=0, tiled=True)]
    ppermute x2, waiting for transfers between devices: 0.01 us -> 6.61 us  [ydiff_block(): lax.ppermute(field[:, :1], 'py', [(i + 1, i) for i in range(count - 1)])]
    all_to_all x1 -> x2, starting transfers between devices: 5.81 us -> 12.1 us  [y_to_x(): lax.all_to_all(joined, LINES, split_axis=0, concat_axis=0, tiled=True)]
    ppermute x1 -> x2, starting transfers between devices: 5.68 us -> 11.7 us  [ydiff(): lax.ppermute(jnp.concatenate([f[:, :1] for f in fields]), ('px', 'py'), d...]
  transfers between devices with their start and end apart: 10 -> 12, of which waited for: 6 -> 6; matrix products, arithmetic and copies ran while one was open for 13% -> 15% of each run, Pallas kernels for 0% -> 0%
where the time goes in v4:
time: 267 us; the launch traced here: 266 us
  blocking collectives  94.5 us (35%)
  starting transfers between devices  57.9 us (22%)
  local copies, waits for them, and re-layouts  46.8 us (18%)
  waiting for transfers between devices  31.1 us (12%)
  matrix products  19.1 us (7%)
  other arithmetic  15.4 us (6%)
    all_to_all x2, blocking collectives, x_to_y(): lax.all_to_all(joined, LINES, split_axis=0, concat_axis=0, tiled=True)  64.2 us
    all_to_all x1, blocking collectives, x_to_block(): lax.all_to_all(joined, 'px', split_axis=0, concat_axis=1, tiled=True)  30.3 us
    unnamed x48, local copies, waits for them, and re-layouts  13 us
    all_to_all x2, starting transfers between devices, y_to_x(): lax.all_to_all(joined, LINES, split_axis=0, concat_axis=0, tiled=True)  12.1 us
    dot_general x3, matrix products, along_y(): return lax.dot_general(matrix, field, dims, precision=HIGH)  11.8 us
    ppermute x2, starting transfers between devices, ydiff(): lax.ppermute(jnp.concatenate([f[:, :1] for f in fields]), ('px', 'py'), d...  11.7 us
    all_to_all x1, starting transfers between devices, x_to_y(): lax.all_to_all(joined, LINES, split_axis=0, concat_axis=0, tiled=True)  11.5 us
    all_to_all x1, waiting for transfers between devices, block_to_x(): lax.all_to_all(joined, 'px', split_axis=1, concat_axis=0, tiled=True)  8.57 us
  transfers between devices with their start and end apart: 12, of which 6 were waited for; matrix products, arithmetic and copies ran while one was open for 15% of the time, Pallas kernels for 0%

profile of v4, /device:TPU:1, one launch (start us, length us, event | category | flops | bytes accessed | tf_op | source)
XLA Modules:
  0.0 266.0 jit_solution(10072199869039609564)
XLA Ops:
  3.9 11.5 %all-to-all-start.1 = ((f32[128,8,256]{2,1,0:T(8,128)}), f32[128,8,256]{2,1,0:T(8,128)S(1)}, u32[]{:S(2)}, u32[]{:S(2)}) async-start(f32[128,8,256]{2,1,0:T(8,128)} %copy.59), calls=%async_computation.1 | async-start | bytes 2097152 | tf_op jit(solution)/shard_map/all_to_all | solution.py:94
  15.5 3.0 %collective-permute-start = (f32[32,1,128]{2,1,0:T(1,128)S(1)}, f32[32,1,128]{2,1,0:T(1,128)S(1)}, u32[]{:S(2)}, u32[]{:S(2)}) collective-permute-start(f32[32,1,128]{2,1,0:T(1,128)S(1)} %get-tuple-element.19), channel_id=1, source_target_pairs={{1,0},{2,1},{3,2},{4,3},{5,4},{6,5},{7,6},{8,7},{9,8},{10,9},{11,1... | collective-permute-start | bytes 49160 | tf_op jit(solution)/shard_map/ppermute | solution.py:14
  18.4 4.1 %collective-permute-start.1 = (f32[32,1,128]{2,1,0:T(1,128)S(1)}, f32[32,1,128]{2,1,0:T(1,128)S(1)}, u32[]{:S(2)}, u32[]{:S(2)}) collective-permute-start(f32[32,1,128]{2,1,0:T(1,128)S(1)} %get-tuple-element.20), channel_id=1, source_target_pairs={{0,1},{1,2},{2,3},{3,4},{4,5},{5,6},{6,7},{7,8},{8,9},{9,10},{10,1... | collective-permute-start | bytes 49160 | tf_op jit(solution)/shard_map/ppermute | solution.py:13
  23.9 6.6 %collective-permute-done = f32[32,1,128]{2,1,0:T(1,128)S(1)} collective-permute-done((f32[32,1,128]{2,1,0:T(1,128)S(1)}, f32[32,1,128]{2,1,0:T(1,128)S(1)}, u32[]{:S(2)}, u32[]{:S(2)}) %collective-permute-start) | collective-permute-done | bytes 16416 | tf_op jit(solution)/shard_map/ppermute | solution.py:14
  31.2 2.6 copy.52
  34.3 4.6 %all-to-all-start = ((f32[32,64,256]{2,0,1:T(8,128)}), f32[32,64,256]{2,0,1:T(8,128)}, u32[]{:S(2)}, u32[]{:S(2)}) async-start(f32[32,64,256]{2,0,1:T(8,128)} %copy.52), calls=%async_computation | async-start | bytes 4194304 | tf_op jit(solution)/shard_map/all_to_all | solution.py:80
  38.9 5.4 %copy.57 = f32[1024,1024]{0,1:T(8,128)} copy(f32[1024,1024]{1,0:T(8,128)} %param.9) | data formatting | bytes 8388608 | tf_op args[4]
  44.3 2.5 reshape_reshape.3
  46.8 3.0 %copy.60 = f32[16,64,8,32]{1,0,3,2:T(8,128)S(1)} copy(f32[16,64,8,32]{3,1,2,0:T(8,128)} %bitcast.79) | data formatting | bytes 2097152 | tf_op jit(solution)/shard_map/transpose | solution.py:120
  50.3 4.0 %fusion = f32[128,8,256]{2,1,0:T(8,128)S(1)} fusion(f32[1024,1024]{0,1:T(8,128)} %copy.57, f32[1024,256]{0,1:T(8,128)S(1)} %reshape.29), kind=kOutput, calls=%fused_computation | convolution fusion | flops 1610612736 | bytes 6291456 | tf_op jit(solution)/shard_map/dot_general | solution.py:75
  55.6 8.6 %all-to-all-done = f32[32,64,256]{2,0,1:T(8,128)} async-done(((f32[32,64,256]{2,0,1:T(8,128)}), f32[32,64,256]{2,0,1:T(8,128)}, u32[]{:S(2)}, u32[]{:S(2)}) %all-to-all-start) | async-done | bytes 2097184 | tf_op jit(solution)/shard_map/all_to_all | solution.py:80
  64.2 2.8 %copy.54 = f32[8,32,8,256]{3,2,1,0:T(8,128)S(1)} copy(f32[8,32,8,256]{3,1,2,0:T(8,128)} %bitcast.2) | data formatting | bytes 4194304 | tf_op jit(solution)/shard_map/all_to_all | solution.py:80
  72.4 38.8 %all_to_all.61 = f32[128,8,512]{2,1,0:T(8,128)S(1)} all-to-all(f32[128,8,512]{2,1,0:T(8,128)S(1)} %copy.63), channel_id=1, replica_groups=mesh['px'=8,'py'=16] {'py','px'}, dimensions={0} | all-to-all | bytes 4194304 | tf_op jit(solution)/shard_map/all_to_all | solution.py:94
  111.3 4.6 %convolution_bitcast_fusion = f32[1024,256]{0,1:T(8,128)} fusion(f32[1024,1024]{1,0:T(8,128)S(1)} %copy-done.1, f32[1024,512]{1,0:T(8,128)S(1)} %bitcast.84), kind=kOutput, calls=%fused_computation.12 | convolution fusion | flops 1610612736 | bytes 6291456 | tf_op jit(solution)/shard_map/dot_general | solution.py:75
  116.3 3.0 %copy.76 = f32[1024,256]{1,0:T(8,128)} copy(f32[1024,256]{0,1:T(8,128)} %convolution_bitcast_fusion) | data formatting | bytes 2097152 | tf_op jit(solution)/shard_map/dot_general | solution.py:75
  119.2 6.0 %all-to-all-start.5 = ((f32[128,8,256]{2,1,0:T(8,128)}), f32[128,8,256]{2,1,0:T(8,128)}, u32[]{:S(2)}, u32[]{:S(2)}) async-start(f32[128,8,256]{2,1,0:T(8,128)} %bitcast.93), calls=%async_computation.5 | async-start | bytes 2097152 | tf_op jit(solution)/shard_map/all_to_all | solution.py:104
  127.5 2.3 fusion.12
  131.6 5.8 %collective-permute-start.2 = (f32[128,1,256]{2,0,1:T(8,128)}, f32[128,1,256]{2,0,1:T(8,128)S(1)}, u32[]{:S(2)}, u32[]{:S(2)}) collective-permute-start(f32[128,1,256]{2,0,1:T(8,128)} %get-tuple-element.13), channel_id=1, source_target_pairs={{16,0},{32,16},{48,32},{64,48},{80,64},{96,80},{112,96},{1,112},{1... | collective-permute-start | bytes 393224 | tf_op jit(solution)/shard_map/ppermute | solution.py:59
  139.4 4.5 %all-to-all-done.5 = f32[128,8,256]{2,1,0:T(8,128)} async-done(((f32[128,8,256]{2,1,0:T(8,128)}), f32[128,8,256]{2,1,0:T(8,128)}, u32[]{:S(2)}, u32[]{:S(2)}) %all-to-all-start.5) | async-done | bytes 1048608 | tf_op jit(solution)/shard_map/all_to_all | solution.py:104
  146.6 3.2 %bitcast_multiply_fusion.2 = (f32[128,8,256]{2,0,1:T(8,128)S(1)}, f32[128,8,256]{2,0,1:T(8,128)}) fusion(f32[256,8,128]{0,2,1:T(8,128)S(1)} %copy.93, f32[128,8,256]{2,0,1:T(8,128)S(1)} %fusion.12, f32[127,8,256]{2,0,1:T(8,128)S(1)} %copy-done.17, f32[128,8,256]{2,1,0:T(8,128)} %all-to-all-done.5, f32[127,8,256]{2,0,1:T(8,128)S(1)} %slice.212), kind=kLoop, calls=%fused_computation.69 | loop fusion | flops 1048576 | bytes 7323648 | tf_op jit(solution)/shard_map/mul | solution.py:37
  151.8 25.4 %all_to_all.62 = f32[128,8,256]{2,1,0:T(8,128)S(1)} all-to-all(f32[128,8,256]{2,1,0:T(8,128)S(1)} %copy.69), channel_id=1, replica_groups=mesh['px'=8,'py'=16] {'py','px'}, dimensions={0} | all-to-all | bytes 2097152 | tf_op jit(solution)/shard_map/all_to_all | solution.py:94
  177.2 3.2 %convolution_bitcast_fusion.2 = f32[1024,256]{0,1:T(8,128)} fusion(f32[1024,1024]{1,0:T(8,128)S(1)} %copy-done.2, f32[128,8,256]{2,1,0:T(8,128)S(1)} %all_to_all.62), kind=kOutput, calls=%fused_computation.14 | convolution fusion | flops 1610612736 | bytes 6291456 | tf_op jit(solution)/shard_map/dot_general | solution.py:75
  180.4 2.6 copy.70
  183.0 6.1 %all-to-all-start.4 = ((f32[128,8,256]{2,1,0:T(8,128)}), f32[128,8,256]{2,1,0:T(8,128)}, u32[]{:S(2)}, u32[]{:S(2)}) async-start(f32[128,8,256]{2,1,0:T(8,128)} %bitcast.92), calls=%async_computation.4 | async-start | bytes 2097152 | tf_op jit(solution)/shard_map/all_to_all | solution.py:104
  190.1 5.9 %collective-permute-start.4 = (f32[128,1,256]{2,0,1:T(8,128)S(1)}, f32[128,1,256]{2,0,1:T(8,128)S(1)}, u32[]{:S(2)}, u32[]{:S(2)}) collective-permute-start(f32[128,1,256]{2,0,1:T(8,128)S(1)} %get-tuple-element.17), channel_id=1, source_target_pairs={{16,0},{32,16},{48,32},{64,48},{80,64},{96,80},{112,96},{1,112},{1... | collective-permute-start | bytes 393224 | tf_op jit(solution)/shard_map/ppermute | solution.py:59
  197.9 6.4 %collective-permute-done.4 = f32[128,1,256]{2,0,1:T(8,128)S(1)} collective-permute-done((f32[128,1,256]{2,0,1:T(8,128)S(1)}, f32[128,1,256]{2,0,1:T(8,128)S(1)}, u32[]{:S(2)}, u32[]{:S(2)}) %collective-permute-start.4) | collective-permute-done | bytes 131104 | tf_op jit(solution)/shard_map/ppermute | solution.py:59
  204.3 4.6 %collective-permute-done.5 = f32[128,1,256]{2,0,1:T(8,128)S(1)} collective-permute-done((f32[128,1,256]{2,0,1:T(8,128)S(1)}, f32[128,1,256]{2,0,1:T(8,128)S(1)}, u32[]{:S(2)}, u32[]{:S(2)}) %collective-permute-start.5) | collective-permute-done | bytes 131104 | tf_op jit(solution)/shard_map/ppermute | solution.py:58
  208.9 3.3 %fusion.30 = f32[128,8,256]{2,0,1:T(8,128)S(1)} fusion(f32[128,8,256]{2,0,1:T(8,128)} %copy-done.10, f32[128,1,256]{2,0,1:T(8,128)S(1)} %collective-permute-done.5, f32[128,1,256]{2,0,1:T(8,128)S(1)} %collective-permute-done.4, f32[128,8,256]{2,0,1:T(8,128)} %get-tuple-element.12, f32[127,8,256]{2,0,1:T(8,128)} %bitcast.87, f32[256,256]{1,0:T(8,128)S(1)} %copy-done), kind=kOutput, calls=%fused_computation.45 | convolution fusion | flops 405012480 | bytes 4710400 | tf_op jit(solution)/shard_map/dot_general | solution.py:70
  216.8 4.5 %bitcast_multiply_fusion.1 = (f32[128,8,256]{2,0,1:T(8,128)S(1)}, f32[256,8,128]{0,2,1:T(8,128)S(1)}) fusion(f32[256,8,128]{0,2,1:T(8,128)S(1)} %copy.93, f32[127,8,256]{2,0,1:T(8,128)S(1)} %slice.207, f32[128,8,256]{2,1,0:T(8,128)} %all-to-all-done.4, f32[128,8,256]{2,0,1:T(8,128)S(1)} %fusion.47, f32[127,8,256]{2,0,1:T(8,128)S(1)} %copy-done.6, ...), kind=kLoop, calls=%fused_computation.68 | loop fusion | flops 3932160 | bytes 15679488 | tf_op jit(solution)/shard_map/mul | solution.py:37
  224.4 30.3 %all_to_all.63 = f32[256,8,256]{2,1,0:T(8,128)S(1)} all-to-all(f32[256,8,256]{2,1,0:T(8,128)} %copy.85), channel_id=1, replica_groups=mesh['px'=8,'py'=16] {'px'}, dimensions={0} | all-to-all | bytes 4194304 | tf_op jit(solution)/shard_map/all_to_all | solution.py:87
  255.4 3.1 %collective-permute-start.6 = (f32[32,1,128]{2,1,0:T(1,128)S(1)}, f32[32,1,128]{2,1,0:T(1,128)S(1)}, u32[]{:S(2)}, u32[]{:S(2)}) collective-permute-start(f32[32,1,128]{2,1,0:T(1,128)S(1)} %get-tuple-element.5), channel_id=1, source_target_pairs={{1,0},{2,1},{3,2},{4,3},{5,4},{6,5},{7,6},{8,7},{9,8},{10,9},{11,1... | collective-permute-start | bytes 49160 | tf_op jit(solution)/shard_map/ppermute | solution.py:14
  258.5 4.1 %collective-permute-start.7 = (f32[32,1,128]{2,1,0:T(1,128)S(1)}, f32[32,1,128]{2,1,0:T(1,128)S(1)}, u32[]{:S(2)}, u32[]{:S(2)}) collective-permute-start(f32[32,1,128]{2,1,0:T(1,128)S(1)} %get-tuple-element.6), channel_id=1, source_target_pairs={{0,1},{1,2},{2,3},{3,4},{4,5},{5,6},{6,7},{7,8},{8,9},{9,10},{10,1... | collective-permute-start | bytes 49160 | tf_op jit(solution)/shard_map/ppermute | solution.py:13
  (93 shorter events, 38.6 us)
Async XLA Ops:
  0.6 67.3 %copy-start = (f32[256,256]{1,0:T(8,128)S(1)}, f32[256,256]{1,0:T(8,128)}, u32[]{:S(2)}) copy-start(f32[256,256]{1,0:T(8,128)} %param.8) | copy-start | bytes 786436
  2.5 12.9 %copy-start.3 = (f32[32,64,128]{2,1,0:T(8,128)S(1)}, f32[32,64,128]{2,1,0:T(8,128)}, u32[]{:S(2)}) copy-start(f32[32,64,128]{2,1,0:T(8,128)} %param.5) | copy-start | bytes 3145732
  3.9 19.0 %copy-start.13 = (f32[32,64,128]{2,1,0:T(8,128)S(1)}, f32[32,64,128]{2,1,0:T(8,128)}, u32[]{:S(2)}) copy-start(f32[32,64,128]{2,1,0:T(8,128)} %param.6) | copy-start | bytes 3145732
  3.9 30.4 %all-to-all-start.1 = ((f32[128,8,256]{2,1,0:T(8,128)}), f32[128,8,256]{2,1,0:T(8,128)S(1)}, u32[]{:S(2)}, u32[]{:S(2)}) async-start(f32[128,8,256]{2,1,0:T(8,128)} %copy.59), calls=%async_computation.1 | async-start | bytes 2097152 | tf_op jit(solution)/shard_map/all_to_all | solution.py:94
  15.5 15.0 %collective-permute-start = (f32[32,1,128]{2,1,0:T(1,128)S(1)}, f32[32,1,128]{2,1,0:T(1,128)S(1)}, u32[]{:S(2)}, u32[]{:S(2)}) collective-permute-start(f32[32,1,128]{2,1,0:T(1,128)S(1)} %get-tuple-element.19), channel_id=1, source_target_pairs={{1,0},{2,1},{3,2},{4,3},{5,4},{6,5},{7,6},{8,7},{9,8},{10,9},{11,1... | collective-permute-start | bytes 49160 | tf_op jit(solution)/shard_map/ppermute | solution.py:14
  18.4 12.0 %collective-permute-start.1 = (f32[32,1,128]{2,1,0:T(1,128)S(1)}, f32[32,1,128]{2,1,0:T(1,128)S(1)}, u32[]{:S(2)}, u32[]{:S(2)}) collective-permute-start(f32[32,1,128]{2,1,0:T(1,128)S(1)} %get-tuple-element.20), channel_id=1, source_target_pairs={{0,1},{1,2},{2,3},{3,4},{4,5},{5,6},{6,7},{7,8},{8,9},{9,10},{10,1... | collective-permute-start | bytes 49160 | tf_op jit(solution)/shard_map/ppermute | solution.py:13
  34.3 29.9 %all-to-all-start = ((f32[32,64,256]{2,0,1:T(8,128)}), f32[32,64,256]{2,0,1:T(8,128)}, u32[]{:S(2)}, u32[]{:S(2)}) async-start(f32[32,64,256]{2,0,1:T(8,128)} %copy.52), calls=%async_computation | async-start | bytes 4194304 | tf_op jit(solution)/shard_map/all_to_all | solution.py:80
  69.7 1.2 copy-start.21
  72.4 38.9 %copy-start.1 = (f32[1024,1024]{1,0:T(8,128)S(1)}, f32[1024,1024]{1,0:T(8,128)}, u32[]{:S(2)}) copy-start(f32[1024,1024]{1,0:T(8,128)} %param.9) | copy-start | bytes 12582916
  111.2 4.7 %copy-start.9 = (f32[128,8,512]{2,1,0:T(8,128)}, f32[128,8,512]{2,1,0:T(8,128)S(1)}, u32[]{:S(2)}) copy-start(f32[128,8,512]{2,1,0:T(8,128)S(1)} %all_to_all.61) | copy-start | bytes 6291460
  116.2 10.3 %copy-start.7 = (f32[127,8,256]{2,0,1:T(8,128)}, f32[127,8,256]{2,0,1:T(8,128)S(1)}, u32[]{:S(2)}) copy-start(f32[127,8,256]{2,0,1:T(8,128)S(1)} %copy.66) | copy-start | bytes 3121156
  119.2 24.7 %all-to-all-start.5 = ((f32[128,8,256]{2,1,0:T(8,128)}), f32[128,8,256]{2,1,0:T(8,128)}, u32[]{:S(2)}, u32[]{:S(2)}) async-start(f32[128,8,256]{2,1,0:T(8,128)} %bitcast.93), calls=%async_computation.5 | async-start | bytes 2097152 | tf_op jit(solution)/shard_map/all_to_all | solution.py:104
  126.5 1.0 copy-start.15
  131.6 18.2 %collective-permute-start.2 = (f32[128,1,256]{2,0,1:T(8,128)}, f32[128,1,256]{2,0,1:T(8,128)S(1)}, u32[]{:S(2)}, u32[]{:S(2)}) collective-permute-start(f32[128,1,256]{2,0,1:T(8,128)} %get-tuple-element.13), channel_id=1, source_target_pairs={{16,0},{32,16},{48,32},{64,48},{80,64},{96,80},{112,96},{1,112},{1... | collective-permute-start | bytes 393224 | tf_op jit(solution)/shard_map/ppermute | solution.py:59
  137.5 12.3 %collective-permute-start.3 = (f32[128,1,256]{2,0,1:T(8,128)}, f32[128,1,256]{2,0,1:T(8,128)}, u32[]{:S(2)}, u32[]{:S(2)}) collective-permute-start(f32[128,1,256]{2,0,1:T(8,128)} %get-tuple-element.14), channel_id=1, source_target_pairs={{0,16},{16,32},{32,48},{48,64},{64,80},{80,96},{96,112},{112,1},{1... | collective-permute-start | bytes 393224 | tf_op jit(solution)/shard_map/ppermute | solution.py:58
  143.9 2.7 %copy-start.17 = (f32[127,8,256]{2,0,1:T(8,128)S(1)}, f32[127,8,256]{2,0,1:T(8,128)}, u32[]{:S(2)}) copy-start(f32[127,8,256]{2,0,1:T(8,128)} %slice.205) | copy-start | bytes 3121156
  145.5 1.0 copy-start.10
  146.6 3.2 %copy-start.19 = (f32[127,8,256]{2,0,1:T(8,128)}, f32[127,8,256]{2,0,1:T(8,128)S(1)}, u32[]{:S(2)}) copy-start(f32[127,8,256]{2,0,1:T(8,128)S(1)} %slice.212) | copy-start | bytes 3121156
  149.8 27.4 %copy-start.2 = (f32[1024,1024]{1,0:T(8,128)S(1)}, f32[1024,1024]{1,0:T(8,128)}, u32[]{:S(2)}) copy-start(f32[1024,1024]{1,0:T(8,128)} %param.9) | copy-start | bytes 12582916
  183.0 31.2 %all-to-all-start.4 = ((f32[128,8,256]{2,1,0:T(8,128)}), f32[128,8,256]{2,1,0:T(8,128)}, u32[]{:S(2)}, u32[]{:S(2)}) async-start(f32[128,8,256]{2,1,0:T(8,128)} %bitcast.92), calls=%async_computation.4 | async-start | bytes 2097152 | tf_op jit(solution)/shard_map/all_to_all | solution.py:104
  190.1 14.2 %collective-permute-start.4 = (f32[128,1,256]{2,0,1:T(8,128)S(1)}, f32[128,1,256]{2,0,1:T(8,128)S(1)}, u32[]{:S(2)}, u32[]{:S(2)}) collective-permute-start(f32[128,1,256]{2,0,1:T(8,128)S(1)} %get-tuple-element.17), channel_id=1, source_target_pairs={{16,0},{32,16},{48,32},{64,48},{80,64},{96,80},{112,96},{1,112},{1... | collective-permute-start | bytes 393224 | tf_op jit(solution)/shard_map/ppermute | solution.py:59
  196.0 12.9 %collective-permute-start.5 = (f32[128,1,256]{2,0,1:T(8,128)S(1)}, f32[128,1,256]{2,0,1:T(8,128)S(1)}, u32[]{:S(2)}, u32[]{:S(2)}) collective-permute-start(f32[128,1,256]{2,0,1:T(8,128)S(1)} %get-tuple-element.18), channel_id=1, source_target_pairs={{0,16},{16,32},{32,48},{48,64},{64,80},{80,96},{96,112},{112,1},{1... | collective-permute-start | bytes 393224 | tf_op jit(solution)/shard_map/ppermute | solution.py:58
  212.2 1.0 copy-start.20
  214.3 1.9 copy-start.6
  214.3 1.9 copy-start.8
  214.3 2.2 copy-start.16
  214.3 2.5 copy-start.18
  254.7 7.8 %copy-start.14 = (f32[32,64,128]{2,1,0:T(8,128)S(1)}, f32[32,64,128]{2,1,0:T(8,128)}, u32[]{:S(2)}) copy-start(f32[32,64,128]{2,1,0:T(8,128)} %param.6) | copy-start | bytes 3145732
  255.0 7.6 %copy-start.4 = (f32[32,64,128]{2,1,0:T(8,128)S(1)}, f32[32,64,128]{2,1,0:T(8,128)}, u32[]{:S(2)}) copy-start(f32[32,64,128]{2,1,0:T(8,128)} %param.5) | copy-start | bytes 3145732
  255.0 7.6 %copy-start.12 = (f32[32,64,127]{2,1,0:T(8,128)S(1)}, f32[32,64,127]{2,1,0:T(8,128)}, u32[]{:S(2)}) copy-start(f32[32,64,127]{2,1,0:T(8,128)} %copy-done.11) | copy-start | bytes 3121156
  255.4 9.1 %collective-permute-start.6 = (f32[32,1,128]{2,1,0:T(1,128)S(1)}, f32[32,1,128]{2,1,0:T(1,128)S(1)}, u32[]{:S(2)}, u32[]{:S(2)}) collective-permute-start(f32[32,1,128]{2,1,0:T(1,128)S(1)} %get-tuple-element.5), channel_id=1, source_target_pairs={{1,0},{2,1},{3,2},{4,3},{5,4},{6,5},{7,6},{8,7},{9,8},{10,9},{11,1... | collective-permute-start | bytes 49160 | tf_op jit(solution)/shard_map/ppermute | solution.py:14
  258.5 5.9 %collective-permute-start.7 = (f32[32,1,128]{2,1,0:T(1,128)S(1)}, f32[32,1,128]{2,1,0:T(1,128)S(1)}, u32[]{:S(2)}, u32[]{:S(2)}) collective-permute-start(f32[32,1,128]{2,1,0:T(1,128)S(1)} %get-tuple-element.6), channel_id=1, source_target_pairs={{0,1},{1,2},{2,3},{3,4},{4,5},{5,6},{6,7},{7,8},{8,9},{9,10},{10,1... | collective-permute-start | bytes 49160 | tf_op jit(solution)/shard_map/ppermute | solution.py:13
  (2 other events, 1.9 us)

commit v5 on v4

--- a/solution.py
+++ b/solution.py
@@ -132,17 +132,17 @@
     s0y, ls1 = x_to_y(second0, lam_second1_y.reshape(count, -1, lam_second1_y.shape[1]))
     ls1 = ls1.reshape(second0.shape)
     state1_y = along_y(inv_y, s0y, False)
-    (state1,) = y_to_x(state1_y)
     lam_half1 = ls1 + RATE * (xdiff(ls1) + zoperate(ls1, cx))
     lam_first1 = along_x(lam_half1, inv_x, True)
     (dy_lam_first1,) = ydiff(lam_first1)
+    lam_state1 = lam_first1 + RATE * (dy_lam_first1 + zoperate(lam_first1, cx))
+    lsy, state1 = x_to_y(lam_state1, state1_y.reshape(lam_state1.shape))
+    state1 = state1.reshape(lam_state1.shape)
     (dy_state1,) = ydiff(state1)
-    lam_state1 = lam_first1 + RATE * (dy_lam_first1 + zoperate(lam_first1, cx))
     first1 = state1 + RATE * (dy_state1 + zoperate(state1, cx))
     half1 = along_x(first1, inv_x, False)
     grad = -RATE * zstep(ls1) * zstep(half1)
     grad = grad - RATE * zstep(lam_first1) * zstep(state1)
-    (lsy,) = x_to_y(lam_state1)
     lam_second0_y = along_y(inv_y, lsy, True)
     (ls0,) = y_to_x(lam_second0_y)
     grad = grad - RATE * zstep(ls0) * zstep(half0)

time: 267 us -> 259 us (0.970)
  blocking collectives: 94.5 us -> 105 us
  starting transfers between devices: 57.9 us -> 49.8 us
  waiting for transfers between devices: 31.1 us -> 25.6 us
  matrix products: 19.1 us -> 15.3 us
    all_to_all x2, blocking collectives: 64.2 us -> 74.8 us  [x_to_y(): lax.all_to_all(joined, LINES, split_axis=0, concat_axis=0, tiled=True)]
    all_to_all x2 -> x1, starting transfers between devices: 12.1 us -> 6.25 us  [y_to_x(): lax.all_to_all(joined, LINES, split_axis=0, concat_axis=0, tiled=True)]
    all_to_all x2 -> x1, waiting for transfers between devices: 4.47 us -> 0.01 us  [y_to_x(): lax.all_to_all(joined, LINES, split_axis=0, concat_axis=0, tiled=True)]
    dot_general x4, matrix products: 7.24 us -> 3.54 us  [along_x(): return lax.dot_general(field, matrix, dims, precision=HIGH)]
    reshape x0 -> x2, local copies, waits for them, and re-layouts: none -> 2.9 us  [the longest x1 1.65 us: local(): lsy, state1 = x_to_y(lam_state1, state1_y.reshape(lam_state1.shape))]
    ppermute x2, starting transfers between devices: 11.7 us -> 8.86 us  [ydiff(): lax.ppermute(jnp.concatenate([f[:, :1] for f in fields]), ('px', 'py'), d...]
    mul x4 -> x5, other arithmetic: 8.38 us -> 7.08 us  [zoperate(): flux = conduct * zstep(field)]
    unnamed x48 -> x50, local copies, waits for them, and re-layouts: 13 us -> 13.4 us
  transfers between devices with their start and end apart: 12 -> 11, of which waited for: 6 -> 6; matrix products, arithmetic and copies ran while one was open for 15% -> 13% of each run, Pallas kernels for 0% -> 0%
where the time goes in v5:
time: 259 us; the launch traced here: 258 us
  blocking collectives  105 us (41%)
  starting transfers between devices  49.8 us (19%)
  local copies, waits for them, and re-layouts  47 us (18%)
  waiting for transfers between devices  25.6 us (10%)
  matrix products  15.3 us (6%)
  other arithmetic  14.2 us (5%)
    all_to_all x2, blocking collectives, x_to_y(): lax.all_to_all(joined, LINES, split_axis=0, concat_axis=0, tiled=True)  74.8 us
    all_to_all x1, blocking collectives, x_to_block(): lax.all_to_all(joined, 'px', split_axis=0, concat_axis=1, tiled=True)  29.7 us
    unnamed x50, local copies, waits for them, and re-layouts  13.4 us
    dot_general x3, matrix products, along_y(): return lax.dot_general(matrix, field, dims, precision=HIGH)  11.8 us
    all_to_all x1, starting transfers between devices, x_to_y(): lax.all_to_all(joined, LINES, split_axis=0, concat_axis=0, tiled=True)  11.5 us
    ppermute x2, starting transfers between devices, ydiff(): lax.ppermute(jnp.concatenate([f[:, :1] for f in fields]), ('px', 'py'), d...  8.86 us
    all_to_all x1, waiting for transfers between devices, block_to_x(): lax.all_to_all(joined, 'px', split_axis=1, concat_axis=0, tiled=True)  8.58 us
    ppermute x2, starting transfers between devices, ydiff_block(): lax.ppermute(field[:, -1:], 'py', [(i, i + 1) for i in range(count - 1)])  7.77 us
  transfers between devices with their start and end apart: 11, of which 6 were waited for; matrix products, arithmetic and copies ran while one was open for 13% of the time, Pallas kernels for 0%

profile of v5, /device:TPU:1, one launch (start us, length us, event | category | flops | bytes accessed | tf_op | source)
XLA Modules:
  0.0 257.7 jit_solution(6288822681674554100)
XLA Ops:
  0.6 1.9 copy.74
  3.9 11.5 %all-to-all-start.1 = ((f32[128,8,256]{2,1,0:T(8,128)}), f32[128,8,256]{2,1,0:T(8,128)S(1)}, u32[]{:S(2)}, u32[]{:S(2)}) async-start(f32[128,8,256]{2,1,0:T(8,128)} %copy.75), calls=%async_computation.1 | async-start | bytes 2097152 | tf_op jit(solution)/shard_map/all_to_all | solution.py:94
  15.5 3.0 %collective-permute-start = (f32[32,1,128]{2,1,0:T(1,128)S(1)}, f32[32,1,128]{2,1,0:T(1,128)S(1)}, u32[]{:S(2)}, u32[]{:S(2)}) collective-permute-start(f32[32,1,128]{2,1,0:T(1,128)S(1)} %get-tuple-element.19), channel_id=1, source_target_pairs={{1,0},{2,1},{3,2},{4,3},{5,4},{6,5},{7,6},{8,7},{9,8},{10,9},{11,1... | collective-permute-start | bytes 49160 | tf_op jit(solution)/shard_map/ppermute | solution.py:14
  18.4 4.1 %collective-permute-start.1 = (f32[32,1,128]{2,1,0:T(1,128)S(1)}, f32[32,1,128]{2,1,0:T(1,128)S(1)}, u32[]{:S(2)}, u32[]{:S(2)}) collective-permute-start(f32[32,1,128]{2,1,0:T(1,128)S(1)} %get-tuple-element.20), channel_id=1, source_target_pairs={{0,1},{1,2},{2,3},{3,4},{4,5},{5,6},{6,7},{7,8},{8,9},{9,10},{10,1... | collective-permute-start | bytes 49160 | tf_op jit(solution)/shard_map/ppermute | solution.py:13
  23.9 6.6 %collective-permute-done = f32[32,1,128]{2,1,0:T(1,128)S(1)} collective-permute-done((f32[32,1,128]{2,1,0:T(1,128)S(1)}, f32[32,1,128]{2,1,0:T(1,128)S(1)}, u32[]{:S(2)}, u32[]{:S(2)}) %collective-permute-start) | collective-permute-done | bytes 16416 | tf_op jit(solution)/shard_map/ppermute | solution.py:14
  31.2 2.6 %copy.68 = f32[32,64,256]{2,0,1:T(8,128)} copy(f32[32,64,256]{2,1,0:T(8,128)S(1)} %pad_maximum_fusion) | data formatting | bytes 4194304 | tf_op jit(solution)/shard_map/concatenate | solution.py:79
  34.3 4.5 %all-to-all-start = ((f32[32,64,256]{2,0,1:T(8,128)}), f32[32,64,256]{2,0,1:T(8,128)}, u32[]{:S(2)}, u32[]{:S(2)}) async-start(f32[32,64,256]{2,0,1:T(8,128)} %copy.68), calls=%async_computation | async-start | bytes 4194304 | tf_op jit(solution)/shard_map/all_to_all | solution.py:80
  38.9 5.4 %copy.73 = f32[1024,1024]{0,1:T(8,128)} copy(f32[1024,1024]{1,0:T(8,128)} %param.9) | data formatting | bytes 8388608 | tf_op args[4]
  44.2 2.5 reshape_reshape.3
  46.7 3.0 %copy.76 = f32[16,64,8,32]{1,0,3,2:T(8,128)S(1)} copy(f32[16,64,8,32]{3,1,2,0:T(8,128)} %bitcast.81) | data formatting | bytes 2097152 | tf_op jit(solution)/shard_map/transpose | solution.py:120
  50.3 4.0 %fusion = f32[128,8,256]{2,1,0:T(8,128)S(1)} fusion(f32[1024,1024]{0,1:T(8,128)} %copy.73, f32[1024,256]{0,1:T(8,128)S(1)} %reshape.33), kind=kOutput, calls=%fused_computation | convolution fusion | flops 1610612736 | bytes 6291456 | tf_op jit(solution)/shard_map/dot_general | solution.py:75
  55.6 8.6 %all-to-all-done = f32[32,64,256]{2,0,1:T(8,128)} async-done(((f32[32,64,256]{2,0,1:T(8,128)}), f32[32,64,256]{2,0,1:T(8,128)}, u32[]{:S(2)}, u32[]{:S(2)}) %all-to-all-start) | async-done | bytes 2097184 | tf_op jit(solution)/shard_map/all_to_all | solution.py:80
  64.2 2.8 %copy.70 = f32[8,32,8,256]{3,2,1,0:T(8,128)S(1)} copy(f32[8,32,8,256]{3,1,2,0:T(8,128)} %bitcast.2) | data formatting | bytes 4194304 | tf_op jit(solution)/shard_map/all_to_all | solution.py:80
  72.4 38.8 %all_to_all.56 = f32[128,8,512]{2,1,0:T(8,128)S(1)} all-to-all(f32[128,8,512]{2,1,0:T(8,128)S(1)} %copy.79), channel_id=1, replica_groups=mesh['px'=8,'py'=16] {'py','px'}, dimensions={0} | all-to-all | bytes 4194304 | tf_op jit(solution)/shard_map/all_to_all | solution.py:94
  115.2 4.6 %convolution_bitcast_fusion.2 = f32[1024,256]{0,1:T(8,128)} fusion(f32[1024,1024]{1,0:T(8,128)S(1)} %copy-done.1, f32[1024,512]{1,0:T(8,128)S(1)} %bitcast.87), kind=kOutput, calls=%fused_computation.15 | convolution fusion | flops 1610612736 | bytes 6291456 | tf_op jit(solution)/shard_map/dot_general | solution.py:75
  119.7 3.0 %collective-permute-start.2 = (f32[128,1,256]{2,0,1:T(8,128)}, f32[128,1,256]{2,0,1:T(8,128)S(1)}, u32[]{:S(2)}, u32[]{:S(2)}) collective-permute-start(f32[128,1,256]{2,0,1:T(8,128)} %get-tuple-element.15), channel_id=1, source_target_pairs={{16,0},{32,16},{48,32},{64,48},{80,64},{96,80},{112,96},{1,112},{1... | collective-permute-start | bytes 393224 | tf_op jit(solution)/shard_map/ppermute | solution.py:59
  122.7 2.3 collective-permute-start.3
  126.3 2.5 copy.85
  134.2 36.1 %all_to_all.57 = f32[128,8,512]{2,1,0:T(8,128)S(1)} all-to-all(f32[128,8,512]{2,1,0:T(8,128)S(1)} %copy.87), channel_id=1, replica_groups=mesh['px'=8,'py'=16] {'py','px'}, dimensions={0} | all-to-all | bytes 4194304 | tf_op jit(solution)/shard_map/all_to_all | solution.py:94
  172.0 3.1 %convolution_bitcast_fusion.1 = f32[1024,256]{0,1:T(8,128)} fusion(f32[1024,1024]{1,0:T(8,128)S(1)} %copy-done.2, f32[1024,512]{1,0:T(8,128)S(1)} %bitcast.89), kind=kOutput, calls=%fused_computation.14 | convolution fusion | flops 1610612736 | bytes 6291456 | tf_op jit(solution)/shard_map/dot_general | solution.py:75
  175.1 2.5 copy.88
  177.6 6.2 %all-to-all-start.4 = ((f32[128,8,256]{2,1,0:T(8,128)}), f32[128,8,256]{2,1,0:T(8,128)}, u32[]{:S(2)}, u32[]{:S(2)}) async-start(f32[128,8,256]{2,1,0:T(8,128)} %bitcast.97), calls=%async_computation.4 | async-start | bytes 2097152 | tf_op jit(solution)/shard_map/all_to_all | solution.py:104
  186.6 5.9 %collective-permute-start.4 = (f32[128,1,256]{2,0,1:T(8,128)S(1)}, f32[128,1,256]{2,0,1:T(8,128)S(1)}, u32[]{:S(2)}, u32[]{:S(2)}) collective-permute-start(f32[128,1,256]{2,0,1:T(8,128)S(1)} %get-tuple-element.13), channel_id=1, source_target_pairs={{16,0},{32,16},{48,32},{64,48},{80,64},{96,80},{112,96},{1,112},{1... | collective-permute-start | bytes 393224 | tf_op jit(solution)/shard_map/ppermute | solution.py:59
  192.5 1.9 collective-permute-start.5
  194.4 4.6 %collective-permute-done.4 = f32[128,1,256]{2,0,1:T(8,128)S(1)} collective-permute-done((f32[128,1,256]{2,0,1:T(8,128)S(1)}, f32[128,1,256]{2,0,1:T(8,128)S(1)}, u32[]{:S(2)}, u32[]{:S(2)}) %collective-permute-start.4) | collective-permute-done | bytes 131104 | tf_op jit(solution)/shard_map/ppermute | solution.py:59
  199.1 4.4 %collective-permute-done.5 = f32[128,1,256]{2,0,1:T(8,128)S(1)} collective-permute-done((f32[128,1,256]{2,0,1:T(8,128)S(1)}, f32[128,1,256]{2,0,1:T(8,128)S(1)}, u32[]{:S(2)}, u32[]{:S(2)}) %collective-permute-start.5) | collective-permute-done | bytes 131104 | tf_op jit(solution)/shard_map/ppermute | solution.py:58
  208.9 4.5 %bitcast_multiply_fusion.1 = (f32[128,8,256]{2,0,1:T(8,128)S(1)}, f32[256,8,128]{0,2,1:T(8,128)S(1)}) fusion(f32[256,8,128]{0,2,1:T(8,128)S(1)} %copy.110, f32[127,8,256]{2,0,1:T(8,128)S(1)} %slice.222, f32[128,8,256]{2,1,0:T(8,128)} %all-to-all-done.4, f32[128,8,256]{2,0,1:T(8,128)S(1)} %fusion.47, f32[127,8,256]{2,0,1:T(8,128)S(1)} %copy-done.6, ...), kind=kLoop, calls=%fused_computation.70 | loop fusion | flops 3932160 | bytes 15679488 | tf_op jit(solution)/shard_map/mul | solution.py:37
  214.6 2.0 copy.102
  216.5 29.7 %all_to_all.58 = f32[256,8,256]{2,1,0:T(8,128)S(1)} all-to-all(f32[256,8,256]{2,1,0:T(8,128)} %copy.102), channel_id=1, replica_groups=mesh['px'=8,'py'=16] {'px'}, dimensions={0} | all-to-all | bytes 4194304 | tf_op jit(solution)/shard_map/all_to_all | solution.py:87
  246.9 3.7 %collective-permute-start.6 = (f32[32,1,128]{2,1,0:T(1,128)S(1)}, f32[32,1,128]{2,1,0:T(1,128)S(1)}, u32[]{:S(2)}, u32[]{:S(2)}) collective-permute-start(f32[32,1,128]{2,1,0:T(1,128)S(1)} %get-tuple-element.5), channel_id=1, source_target_pairs={{1,0},{2,1},{3,2},{4,3},{5,4},{6,5},{7,6},{8,7},{9,8},{10,9},{11,1... | collective-permute-start | bytes 49160 | tf_op jit(solution)/shard_map/ppermute | solution.py:14
  250.6 3.7 %collective-permute-start.7 = (f32[32,1,128]{2,1,0:T(1,128)S(1)}, f32[32,1,128]{2,1,0:T(1,128)S(1)}, u32[]{:S(2)}, u32[]{:S(2)}) collective-permute-start(f32[32,1,128]{2,1,0:T(1,128)S(1)} %get-tuple-element.6), channel_id=1, source_target_pairs={{0,1},{1,2},{2,3},{3,4},{4,5},{5,6},{6,7},{7,8},{8,9},{9,10},{10,1... | collective-permute-start | bytes 49160 | tf_op jit(solution)/shard_map/ppermute | solution.py:13
  254.3 1.8 slice_subtract_fusion
  (97 shorter events, 34.7 us)
Async XLA Ops:
  0.6 67.3 %copy-start = (f32[256,256]{1,0:T(8,128)S(1)}, f32[256,256]{1,0:T(8,128)}, u32[]{:S(2)}) copy-start(f32[256,256]{1,0:T(8,128)} %param.8) | copy-start | bytes 786436
  2.5 12.9 %copy-start.3 = (f32[32,64,128]{2,1,0:T(8,128)S(1)}, f32[32,64,128]{2,1,0:T(8,128)}, u32[]{:S(2)}) copy-start(f32[32,64,128]{2,1,0:T(8,128)} %param.5) | copy-start | bytes 3145732
  3.9 19.0 %copy-start.13 = (f32[32,64,128]{2,1,0:T(8,128)S(1)}, f32[32,64,128]{2,1,0:T(8,128)}, u32[]{:S(2)}) copy-start(f32[32,64,128]{2,1,0:T(8,128)} %param.6) | copy-start | bytes 3145732
  3.9 30.4 %all-to-all-start.1 = ((f32[128,8,256]{2,1,0:T(8,128)}), f32[128,8,256]{2,1,0:T(8,128)S(1)}, u32[]{:S(2)}, u32[]{:S(2)}) async-start(f32[128,8,256]{2,1,0:T(8,128)} %copy.75), calls=%async_computation.1 | async-start | bytes 2097152 | tf_op jit(solution)/shard_map/all_to_all | solution.py:94
  15.5 15.0 %collective-permute-start = (f32[32,1,128]{2,1,0:T(1,128)S(1)}, f32[32,1,128]{2,1,0:T(1,128)S(1)}, u32[]{:S(2)}, u32[]{:S(2)}) collective-permute-start(f32[32,1,128]{2,1,0:T(1,128)S(1)} %get-tuple-element.19), channel_id=1, source_target_pairs={{1,0},{2,1},{3,2},{4,3},{5,4},{6,5},{7,6},{8,7},{9,8},{10,9},{11,1... | collective-permute-start | bytes 49160 | tf_op jit(solution)/shard_map/ppermute | solution.py:14
  18.4 12.0 %collective-permute-start.1 = (f32[32,1,128]{2,1,0:T(1,128)S(1)}, f32[32,1,128]{2,1,0:T(1,128)S(1)}, u32[]{:S(2)}, u32[]{:S(2)}) collective-permute-start(f32[32,1,128]{2,1,0:T(1,128)S(1)} %get-tuple-element.20), channel_id=1, source_target_pairs={{0,1},{1,2},{2,3},{3,4},{4,5},{5,6},{6,7},{7,8},{8,9},{9,10},{10,1... | collective-permute-start | bytes 49160 | tf_op jit(solution)/shard_map/ppermute | solution.py:13
  22.9 1.0 copy-start.11
  34.3 29.9 %all-to-all-start = ((f32[32,64,256]{2,0,1:T(8,128)}), f32[32,64,256]{2,0,1:T(8,128)}, u32[]{:S(2)}, u32[]{:S(2)}) async-start(f32[32,64,256]{2,0,1:T(8,128)} %copy.68), calls=%async_computation | async-start | bytes 4194304 | tf_op jit(solution)/shard_map/all_to_all | solution.py:80
  68.7 1.0 copy-start.5
  69.7 1.2 copy-start.22
  111.8 1.0 copy-start.7
  112.8 2.4 copy-start.1
  113.9 11.1 %copy-start.20 = (f32[127,8,256]{2,0,1:T(8,128)}, f32[127,8,256]{2,0,1:T(8,128)S(1)}, u32[]{:S(2)}) copy-start(f32[127,8,256]{2,0,1:T(8,128)S(1)} %slice.218) | copy-start | bytes 3121156
  119.7 10.8 %collective-permute-start.2 = (f32[128,1,256]{2,0,1:T(8,128)}, f32[128,1,256]{2,0,1:T(8,128)S(1)}, u32[]{:S(2)}, u32[]{:S(2)}) collective-permute-start(f32[128,1,256]{2,0,1:T(8,128)} %get-tuple-element.15), channel_id=1, source_target_pairs={{16,0},{32,16},{48,32},{64,48},{80,64},{96,80},{112,96},{1,112},{1... | collective-permute-start | bytes 393224 | tf_op jit(solution)/shard_map/ppermute | solution.py:59
  122.7 8.7 %collective-permute-start.3 = (f32[128,1,256]{2,0,1:T(8,128)}, f32[128,1,256]{2,0,1:T(8,128)}, u32[]{:S(2)}, u32[]{:S(2)}) collective-permute-start(f32[128,1,256]{2,0,1:T(8,128)} %get-tuple-element.16), channel_id=1, source_target_pairs={{0,16},{16,32},{32,48},{48,64},{64,80},{80,96},{96,112},{112,1},{1... | collective-permute-start | bytes 393224 | tf_op jit(solution)/shard_map/ppermute | solution.py:58
  128.8 2.6 %copy-start.10 = (f32[128,8,256]{2,0,1:T(8,128)S(1)}, f32[128,8,256]{2,0,1:T(8,128)}, u32[]{:S(2)}) copy-start(f32[128,8,256]{2,0,1:T(8,128)} %bitcast_multiply_fusion.2) | copy-start | bytes 3145732
  134.2 37.8 %copy-start.2 = (f32[1024,1024]{1,0:T(8,128)S(1)}, f32[1024,1024]{1,0:T(8,128)}, u32[]{:S(2)}) copy-start(f32[1024,1024]{1,0:T(8,128)} %param.9) | copy-start | bytes 12582916
  170.2 1.7 copy-start.9
  177.6 28.7 %all-to-all-start.4 = ((f32[128,8,256]{2,1,0:T(8,128)}), f32[128,8,256]{2,1,0:T(8,128)}, u32[]{:S(2)}, u32[]{:S(2)}) async-start(f32[128,8,256]{2,1,0:T(8,128)} %bitcast.97), calls=%async_computation.4 | async-start | bytes 2097152 | tf_op jit(solution)/shard_map/all_to_all | solution.py:104
  183.9 1.7 copy-start.17
  186.6 12.4 %collective-permute-start.4 = (f32[128,1,256]{2,0,1:T(8,128)S(1)}, f32[128,1,256]{2,0,1:T(8,128)S(1)}, u32[]{:S(2)}, u32[]{:S(2)}) collective-permute-start(f32[128,1,256]{2,0,1:T(8,128)S(1)} %get-tuple-element.13), channel_id=1, source_target_pairs={{16,0},{32,16},{48,32},{64,48},{80,64},{96,80},{112,96},{1,112},{1... | collective-permute-start | bytes 393224 | tf_op jit(solution)/shard_map/ppermute | solution.py:59
  192.5 10.9 %collective-permute-start.5 = (f32[128,1,256]{2,0,1:T(8,128)S(1)}, f32[128,1,256]{2,0,1:T(8,128)S(1)}, u32[]{:S(2)}, u32[]{:S(2)}) collective-permute-start(f32[128,1,256]{2,0,1:T(8,128)S(1)} %get-tuple-element.14), channel_id=1, source_target_pairs={{0,16},{16,32},{32,48},{48,64},{64,80},{80,96},{96,112},{112,1},{1... | collective-permute-start | bytes 393224 | tf_op jit(solution)/shard_map/ppermute | solution.py:58
  204.3 1.0 copy-start.21
  206.4 1.8 copy-start.6
  206.4 1.9 copy-start.8
  206.4 2.2 copy-start.16
  206.4 2.5 copy-start.18
  246.3 8.0 %copy-start.14 = (f32[32,64,128]{2,1,0:T(8,128)S(1)}, f32[32,64,128]{2,1,0:T(8,128)}, u32[]{:S(2)}) copy-start(f32[32,64,128]{2,1,0:T(8,128)} %param.6) | copy-start | bytes 3145732
  246.5 7.8 %copy-start.4 = (f32[32,64,128]{2,1,0:T(8,128)S(1)}, f32[32,64,128]{2,1,0:T(8,128)}, u32[]{:S(2)}) copy-start(f32[32,64,128]{2,1,0:T(8,128)} %param.5) | copy-start | bytes 3145732
  246.5 7.8 %copy-start.12 = (f32[32,64,127]{2,1,0:T(8,128)S(1)}, f32[32,64,127]{2,1,0:T(8,128)}, u32[]{:S(2)}) copy-start(f32[32,64,127]{2,1,0:T(8,128)} %copy-done.11) | copy-start | bytes 3121156
  246.9 9.3 %collective-permute-start.6 = (f32[32,1,128]{2,1,0:T(1,128)S(1)}, f32[32,1,128]{2,1,0:T(1,128)S(1)}, u32[]{:S(2)}, u32[]{:S(2)}) collective-permute-start(f32[32,1,128]{2,1,0:T(1,128)S(1)} %get-tuple-element.5), channel_id=1, source_target_pairs={{1,0},{2,1},{3,2},{4,3},{5,4},{6,5},{7,6},{8,7},{9,8},{10,9},{11,1... | collective-permute-start | bytes 49160 | tf_op jit(solution)/shard_map/ppermute | solution.py:14
  250.6 5.6 %collective-permute-start.7 = (f32[32,1,128]{2,1,0:T(1,128)S(1)}, f32[32,1,128]{2,1,0:T(1,128)S(1)}, u32[]{:S(2)}, u32[]{:S(2)}) collective-permute-start(f32[32,1,128]{2,1,0:T(1,128)S(1)} %get-tuple-element.6), channel_id=1, source_target_pairs={{0,1},{1,2},{2,3},{3,4},{4,5},{5,6},{6,7},{7,8},{8,9},{9,10},{10,1... | collective-permute-start | bytes 49160 | tf_op jit(solution)/shard_map/ppermute | solution.py:13
  (2 other events, 1.9 us)

commit v6 on v5

--- a/solution.py
+++ b/solution.py
@@ -1,6 +1,7 @@
 import jax
 import jax.numpy as jnp
 from jax import lax
+from jax.experimental.layout import Layout, with_layout_constraint
 from jax.sharding import PartitionSpec as P
 
 RATE = 0.2
@@ -120,6 +121,10 @@
     return jnp.transpose(tiles, (0, 2, 1, 3)).reshape(cols * width, rows * depth)
 
 
+def rows(field):
+    return with_layout_constraint(field, Layout(tuple(range(field.ndim))))
+
+
 def local(initial, conduct, cotangent, inv_x, inv_y):
     (tp,) = x_to_y(block_planes(cotangent))
     ty = planes_to_y(tp, (initial.shape[0], initial.shape[1]))
@@ -130,14 +135,14 @@
     second0 = half0 + RATE * (xdiff(half0) + zoperate(half0, cx))
     count = lax.axis_size(LINES)
     s0y, ls1 = x_to_y(second0, lam_second1_y.reshape(count, -1, lam_second1_y.shape[1]))
-    ls1 = ls1.reshape(second0.shape)
+    ls1 = rows(ls1.reshape(second0.shape))
     state1_y = along_y(inv_y, s0y, False)
     lam_half1 = ls1 + RATE * (xdiff(ls1) + zoperate(ls1, cx))
     lam_first1 = along_x(lam_half1, inv_x, True)
     (dy_lam_first1,) = ydiff(lam_first1)
     lam_state1 = lam_first1 + RATE * (dy_lam_first1 + zoperate(lam_first1, cx))
-    lsy, state1 = x_to_y(lam_state1, state1_y.reshape(lam_state1.shape))
-    state1 = state1.reshape(lam_state1.shape)
+    lsy, state1 = x_to_y(rows(lam_state1), state1_y.reshape(lam_state1.shape))
+    state1 = rows(state1.reshape(lam_state1.shape))
     (dy_state1,) = ydiff(state1)
     first1 = state1 + RATE * (dy_state1 + zoperate(state1, cx))
     half1 = along_x(first1, inv_x, False)
@@ -145,6 +150,7 @@
     grad = grad - RATE * zstep(lam_first1) * zstep(state1)
     lam_second0_y = along_y(inv_y, lsy, True)
     (ls0,) = y_to_x(lam_second0_y)
+    ls0 = rows(ls0)
     grad = grad - RATE * zstep(ls0) * zstep(half0)
     lam_half0 = ls0 + RATE * (xdiff(ls0) + zoperate(ls0, cx))
     lam_first0 = along_x(lam_half0, inv_x, True)

time: 259 us -> 259 us (level)
  local copies, waits for them, and re-layouts: 47 us -> 42.6 us
  matrix products: 15.3 us -> 18.6 us
    dot_general x3 -> x2, local copies, waits for them, and re-layouts: 6.35 us -> 5.06 us  [along_y(): return lax.dot_general(matrix, field, dims, precision=HIGH)]
    unnamed x50 -> x47, local copies, waits for them, and re-layouts: 13.4 us -> 14.3 us
  transfers between devices with their start and end apart: 11 -> 11, of which waited for: 6 -> 6; matrix products, arithmetic and copies ran while one was open for 13% -> 12% of each run, Pallas kernels for 0% -> 0%
where the time goes in v6:
time: 259 us; the launch traced here: 258 us
  blocking collectives  105 us (41%)
  starting transfers between devices  49.6 us (19%)
  local copies, waits for them, and re-layouts  42.6 us (16%)
  waiting for transfers between devices  27.6 us (11%)
  matrix products  18.6 us (7%)
  other arithmetic  13.4 us (5%)
    all_to_all x2, blocking collectives, x_to_y(): lax.all_to_all(joined, LINES, split_axis=0, concat_axis=0, tiled=True)  74.3 us
    all_to_all x1, blocking collectives, x_to_block(): lax.all_to_all(joined, 'px', split_axis=0, concat_axis=1, tiled=True)  30.7 us
    unnamed x47, local copies, waits for them, and re-layouts  14.3 us
    dot_general x3, matrix products, along_y(): return lax.dot_general(matrix, field, dims, precision=HIGH)  12.7 us
    all_to_all x1, starting transfers between devices, x_to_y(): lax.all_to_all(joined, LINES, split_axis=0, concat_axis=0, tiled=True)  11.5 us
    all_to_all x1, waiting for transfers between devices, block_to_x(): lax.all_to_all(joined, 'px', split_axis=1, concat_axis=0, tiled=True)  8.89 us
    ppermute x2, starting transfers between devices, ydiff(): lax.ppermute(jnp.concatenate([f[:, :1] for f in fields]), ('px', 'py'), d...  8.86 us
    ppermute x2, starting transfers between devices, ydiff_block(): lax.ppermute(field[:, -1:], 'py', [(i, i + 1) for i in range(count - 1)])  8.53 us
  transfers between devices with their start and end apart: 11, of which 6 were waited for; matrix products, arithmetic and copies ran while one was open for 12% of the time, Pallas kernels for 0%

profile of v6, /device:TPU:1, one launch (start us, length us, event | category | flops | bytes accessed | tf_op | source)
XLA Modules:
  0.0 257.9 jit_solution(17971068298559925988)
XLA Ops:
  3.9 11.5 %all-to-all-start.1 = ((f32[128,8,256]{2,1,0:T(8,128)}), f32[128,8,256]{2,1,0:T(8,128)S(1)}, u32[]{:S(2)}, u32[]{:S(2)}) async-start(f32[128,8,256]{2,1,0:T(8,128)} %copy.141), calls=%async_computation.1 | async-start | bytes 2097152 | tf_op jit(solution)/shard_map/all_to_all | solution.py:95
  15.5 3.0 %collective-permute-start = (f32[32,1,128]{2,1,0:T(1,128)S(1)}, f32[32,1,128]{2,1,0:T(1,128)S(1)}, u32[]{:S(2)}, u32[]{:S(2)}) collective-permute-start(f32[32,1,128]{2,1,0:T(1,128)S(1)} %get-tuple-element.15), channel_id=1, source_target_pairs={{1,0},{2,1},{3,2},{4,3},{5,4},{6,5},{7,6},{8,7},{9,8},{10,9},{11,1... | collective-permute-start | bytes 49160 | tf_op jit(solution)/shard_map/ppermute | solution.py:15
  18.4 4.1 %collective-permute-start.1 = (f32[32,1,128]{2,1,0:T(1,128)S(1)}, f32[32,1,128]{2,1,0:T(1,128)S(1)}, u32[]{:S(2)}, u32[]{:S(2)}) collective-permute-start(f32[32,1,128]{2,1,0:T(1,128)S(1)} %get-tuple-element.16), channel_id=1, source_target_pairs={{0,1},{1,2},{2,3},{3,4},{4,5},{5,6},{6,7},{7,8},{8,9},{9,10},{10,1... | collective-permute-start | bytes 49160 | tf_op jit(solution)/shard_map/ppermute | solution.py:14
  23.9 6.6 %collective-permute-done = f32[32,1,128]{2,1,0:T(1,128)S(1)} collective-permute-done((f32[32,1,128]{2,1,0:T(1,128)S(1)}, f32[32,1,128]{2,1,0:T(1,128)S(1)}, u32[]{:S(2)}, u32[]{:S(2)}) %collective-permute-start) | collective-permute-done | bytes 16416 | tf_op jit(solution)/shard_map/ppermute | solution.py:15
  31.2 2.6 %copy.129 = f32[32,64,256]{2,0,1:T(8,128)} copy(f32[32,64,256]{2,1,0:T(8,128)S(1)} %pad_maximum_fusion) | data formatting | bytes 4194304 | tf_op jit(solution)/shard_map/concatenate | solution.py:80
  34.3 4.5 %all-to-all-start = ((f32[32,64,256]{2,0,1:T(8,128)}), f32[32,64,256]{2,0,1:T(8,128)}, u32[]{:S(2)}, u32[]{:S(2)}) async-start(f32[32,64,256]{2,0,1:T(8,128)} %copy.129), calls=%async_computation | async-start | bytes 4194304 | tf_op jit(solution)/shard_map/all_to_all | solution.py:81
  38.9 5.4 %copy.139 = f32[1024,1024]{0,1:T(8,128)} copy(f32[1024,1024]{1,0:T(8,128)} %param.9) | data formatting | bytes 8388608 | tf_op args[4]
  44.3 2.5 reshape_reshape.3
  46.8 3.0 %copy.142 = f32[16,64,8,32]{1,0,3,2:T(8,128)S(1)} copy(f32[16,64,8,32]{3,1,2,0:T(8,128)} %bitcast.89) | data formatting | bytes 2097152 | tf_op jit(solution)/shard_map/transpose | solution.py:121
  50.3 5.0 %fusion = f32[128,8,256]{2,1,0:T(8,128)} fusion(f32[1024,1024]{0,1:T(8,128)} %copy.139, f32[1024,256]{0,1:T(8,128)S(1)} %reshape.31), kind=kOutput, calls=%fused_computation | convolution fusion | flops 1610612736 | bytes 6291456 | tf_op jit(solution)/shard_map/dot_general | solution.py:76
  55.3 8.9 %all-to-all-done = f32[32,64,256]{2,0,1:T(8,128)} async-done(((f32[32,64,256]{2,0,1:T(8,128)}), f32[32,64,256]{2,0,1:T(8,128)}, u32[]{:S(2)}, u32[]{:S(2)}) %all-to-all-start) | async-done | bytes 2097184 | tf_op jit(solution)/shard_map/all_to_all | solution.py:81
  64.2 2.8 %copy.131 = f32[8,32,8,256]{3,2,1,0:T(8,128)S(1)} copy(f32[8,32,8,256]{3,1,2,0:T(8,128)} %bitcast.2) | data formatting | bytes 4194304 | tf_op jit(solution)/shard_map/all_to_all | solution.py:81
  71.5 38.8 %all_to_all.56 = f32[128,8,512]{2,1,0:T(8,128)S(1)} all-to-all(f32[128,8,512]{2,1,0:T(8,128)S(1)} %pad_maximum_fusion.1), channel_id=1, replica_groups=mesh['px'=8,'py'=16] {'py','px'}, dimensions={0} | all-to-all | bytes 4194304 | tf_op jit(solution)/shard_map/all_to_all | solution.py:95
  114.0 4.6 %convolution_bitcast_fusion.2 = f32[1024,256]{0,1:T(8,128)} fusion(f32[1024,1024]{1,0:T(8,128)S(1)} %copy-done.1, f32[1024,512]{1,0:T(8,128)S(1)} %bitcast.83), kind=kOutput, calls=%fused_computation.15 | convolution fusion | flops 1610612736 | bytes 6291456 | tf_op jit(solution)/shard_map/dot_general | solution.py:76
  118.5 3.0 %collective-permute-start.2 = (f32[128,1,256]{2,1,0:T(1,128)}, f32[128,1,256]{2,1,0:T(1,128)S(1)}, u32[]{:S(2)}, u32[]{:S(2)}) collective-permute-start(f32[128,1,256]{2,1,0:T(1,128)} %get-tuple-element.13), channel_id=1, source_target_pairs={{16,0},{32,16},{48,32},{64,48},{80,64},{96,80},{112,96},{1,112},{1... | collective-permute-start | bytes 393224 | tf_op jit(solution)/shard_map/ppermute | solution.py:60
  121.5 2.3 collective-permute-start.3
  126.2 2.5 copy.155
  130.3 2.2 fusion.40
  132.7 35.5 %all_to_all.57 = f32[128,8,512]{2,1,0:T(8,128)S(1)} all-to-all(f32[128,8,512]{2,1,0:T(8,128)S(1)} %pad_maximum_fusion.2), channel_id=1, replica_groups=mesh['px'=8,'py'=16] {'py','px'}, dimensions={0} | all-to-all | bytes 4194304 | tf_op jit(solution)/shard_map/all_to_all | solution.py:95
  169.6 3.1 %convolution_bitcast_fusion.1 = f32[1024,256]{0,1:T(8,128)} fusion(f32[1024,1024]{1,0:T(8,128)S(1)} %copy-done.2, f32[1024,512]{1,0:T(8,128)S(1)} %bitcast.85), kind=kOutput, calls=%fused_computation.14 | convolution fusion | flops 1610612736 | bytes 6291456 | tf_op jit(solution)/shard_map/dot_general | solution.py:76
  172.7 2.5 copy.156
  175.2 6.0 %all-to-all-start.4 = ((f32[128,8,256]{2,1,0:T(8,128)}), f32[128,8,256]{2,1,0:T(8,128)}, u32[]{:S(2)}, u32[]{:S(2)}) async-start(f32[128,8,256]{2,1,0:T(8,128)} %bitcast.97), calls=%async_computation.4 | async-start | bytes 2097152 | tf_op jit(solution)/shard_map/all_to_all | solution.py:105
  183.0 5.9 %collective-permute-start.4 = (f32[128,1,256]{2,1,0:T(1,128)S(1)}, f32[128,1,256]{2,1,0:T(1,128)S(1)}, u32[]{:S(2)}, u32[]{:S(2)}) collective-permute-start(f32[128,1,256]{2,1,0:T(1,128)S(1)} %get-tuple-element.11), channel_id=1, source_target_pairs={{16,0},{32,16},{48,32},{64,48},{80,64},{96,80},{112,96},{1,112},{1... | collective-permute-start | bytes 393224 | tf_op jit(solution)/shard_map/ppermute | solution.py:60
  188.8 2.2 collective-permute-start.5
  191.4 5.0 %collective-permute-done.4 = f32[128,1,256]{2,1,0:T(1,128)S(1)} collective-permute-done((f32[128,1,256]{2,1,0:T(1,128)S(1)}, f32[128,1,256]{2,1,0:T(1,128)S(1)}, u32[]{:S(2)}, u32[]{:S(2)}) %collective-permute-start.4) | collective-permute-done | bytes 131104 | tf_op jit(solution)/shard_map/ppermute | solution.py:60
  196.4 5.0 %collective-permute-done.5 = f32[128,1,256]{2,1,0:T(1,128)S(1)} collective-permute-done((f32[128,1,256]{2,1,0:T(1,128)S(1)}, f32[128,1,256]{2,1,0:T(1,128)S(1)}, u32[]{:S(2)}, u32[]{:S(2)}) %collective-permute-start.5) | collective-permute-done | bytes 131104 | tf_op jit(solution)/shard_map/ppermute | solution.py:59
  206.4 4.1 %bitcast_multiply_fusion.1 = (f32[128,8,256]{2,1,0:T(8,128)S(1)}, f32[256,8,128]{0,1,2:T(8,128)S(1)}) fusion(f32[256,8,128]{0,1,2:T(8,128)S(1)} %copy.174, f32[128,8,256]{2,1,0:T(8,128)} %all-to-all-done.4, f32[127,8,256]{2,1,0:T(8,128)S(1)} %slice.212, f32[128,8,256]{2,1,0:T(8,128)S(1)} %fusion.67, f32[127,8,256]{2,1,0:T(8,128)S(1)} %copy-done.9, ...), kind=kLoop, calls=%fused_computation.71 | loop fusion | flops 3932160 | bytes 15679488 | tf_op jit(solution)/shard_map/mul | solution.py:38
  210.6 3.2 %convolution_bitcast_fusion = f32[256,8,128]{0,1,2:T(8,128)S(1)} fusion(f32[128,8,256]{2,1,0:T(8,128)} %all-to-all-done.4, f32[127,8,256]{2,1,0:T(8,128)S(1)} %slice.213, f32[256,8,128]{0,1,2:T(8,128)S(1)} %copy.174, f32[127,8,256]{2,1,0:T(8,128)S(1)} %slice.212, f32[256,256]{1,0:T(8,128)S(1)} %copy-done), kind=kOutput, calls=%fused_computation.13 | convolution fusion | flops 405012480 | bytes 5488640 | tf_op jit(solution)/shard_map/dot_general | solution.py:71
  213.9 2.1 copy.160
  216.0 30.7 %all_to_all.58 = f32[256,8,256]{2,1,0:T(8,128)S(1)} all-to-all(f32[256,8,256]{2,1,0:T(8,128)} %copy.160), channel_id=1, replica_groups=mesh['px'=8,'py'=16] {'px'}, dimensions={0} | all-to-all | bytes 4194304 | tf_op jit(solution)/shard_map/all_to_all | solution.py:88
  247.3 2.8 %collective-permute-start.6 = (f32[32,1,128]{2,1,0:T(1,128)S(1)}, f32[32,1,128]{2,1,0:T(1,128)S(1)}, u32[]{:S(2)}, u32[]{:S(2)}) collective-permute-start(f32[32,1,128]{2,1,0:T(1,128)S(1)} %get-tuple-element.5), channel_id=1, source_target_pairs={{1,0},{2,1},{3,2},{4,3},{5,4},{6,5},{7,6},{8,7},{9,8},{10,9},{11,1... | collective-permute-start | bytes 49160 | tf_op jit(solution)/shard_map/ppermute | solution.py:15
  250.1 4.4 %collective-permute-start.7 = (f32[32,1,128]{2,1,0:T(1,128)S(1)}, f32[32,1,128]{2,1,0:T(1,128)S(1)}, u32[]{:S(2)}, u32[]{:S(2)}) collective-permute-start(f32[32,1,128]{2,1,0:T(1,128)S(1)} %get-tuple-element.6), channel_id=1, source_target_pairs={{0,1},{1,2},{2,3},{3,4},{4,5},{5,6},{6,7},{7,8},{8,9},{9,10},{10,1... | collective-permute-start | bytes 49160 | tf_op jit(solution)/shard_map/ppermute | solution.py:14
  (93 shorter events, 31.1 us)
Async XLA Ops:
  0.6 67.7 %copy-start = (f32[256,256]{1,0:T(8,128)S(1)}, f32[256,256]{1,0:T(8,128)}, u32[]{:S(2)}) copy-start(f32[256,256]{1,0:T(8,128)} %param.8) | copy-start | bytes 786436
  2.5 12.9 %copy-start.6 = (f32[32,64,128]{2,1,0:T(8,128)S(1)}, f32[32,64,128]{2,1,0:T(8,128)}, u32[]{:S(2)}) copy-start(f32[32,64,128]{2,1,0:T(8,128)} %param.5) | copy-start | bytes 3145732
  3.9 19.0 %copy-start.14 = (f32[32,64,128]{2,1,0:T(8,128)S(1)}, f32[32,64,128]{2,1,0:T(8,128)}, u32[]{:S(2)}) copy-start(f32[32,64,128]{2,1,0:T(8,128)} %param.6) | copy-start | bytes 3145732
  3.9 30.4 %all-to-all-start.1 = ((f32[128,8,256]{2,1,0:T(8,128)}), f32[128,8,256]{2,1,0:T(8,128)S(1)}, u32[]{:S(2)}, u32[]{:S(2)}) async-start(f32[128,8,256]{2,1,0:T(8,128)} %copy.141), calls=%async_computation.1 | async-start | bytes 2097152 | tf_op jit(solution)/shard_map/all_to_all | solution.py:95
  15.5 15.0 %collective-permute-start = (f32[32,1,128]{2,1,0:T(1,128)S(1)}, f32[32,1,128]{2,1,0:T(1,128)S(1)}, u32[]{:S(2)}, u32[]{:S(2)}) collective-permute-start(f32[32,1,128]{2,1,0:T(1,128)S(1)} %get-tuple-element.15), channel_id=1, source_target_pairs={{1,0},{2,1},{3,2},{4,3},{5,4},{6,5},{7,6},{8,7},{9,8},{10,9},{11,1... | collective-permute-start | bytes 49160 | tf_op jit(solution)/shard_map/ppermute | solution.py:15
  18.4 12.0 %collective-permute-start.1 = (f32[32,1,128]{2,1,0:T(1,128)S(1)}, f32[32,1,128]{2,1,0:T(1,128)S(1)}, u32[]{:S(2)}, u32[]{:S(2)}) collective-permute-start(f32[32,1,128]{2,1,0:T(1,128)S(1)} %get-tuple-element.16), channel_id=1, source_target_pairs={{0,1},{1,2},{2,3},{3,4},{4,5},{5,6},{6,7},{7,8},{8,9},{9,10},{10,1... | collective-permute-start | bytes 49160 | tf_op jit(solution)/shard_map/ppermute | solution.py:14
  22.9 1.0 copy-start.12
  34.3 29.9 %all-to-all-start = ((f32[32,64,256]{2,0,1:T(8,128)}), f32[32,64,256]{2,0,1:T(8,128)}, u32[]{:S(2)}, u32[]{:S(2)}) async-start(f32[32,64,256]{2,0,1:T(8,128)} %copy.129), calls=%async_computation | async-start | bytes 4194304 | tf_op jit(solution)/shard_map/all_to_all | solution.py:81
  69.0 1.0 copy-start.8
  70.0 1.2 copy-start.21
  110.3 3.4 %copy-start.3 = (f32[128,8,512]{2,1,0:T(8,128)}, f32[128,8,512]{2,1,0:T(8,128)S(1)}, u32[]{:S(2)}) copy-start(f32[128,8,512]{2,1,0:T(8,128)S(1)} %all_to_all.56) | copy-start | bytes 6291460
  110.5 1.2 copy-start.10
  111.7 2.3 copy-start.1
  114.0 9.9 %copy-start.18 = (f32[127,8,256]{2,1,0:T(8,128)}, f32[127,8,256]{2,1,0:T(8,128)S(1)}, u32[]{:S(2)}) copy-start(f32[127,8,256]{2,1,0:T(8,128)S(1)} %slice.208) | copy-start | bytes 3121156
  118.5 10.2 %collective-permute-start.2 = (f32[128,1,256]{2,1,0:T(1,128)}, f32[128,1,256]{2,1,0:T(1,128)S(1)}, u32[]{:S(2)}, u32[]{:S(2)}) collective-permute-start(f32[128,1,256]{2,1,0:T(1,128)} %get-tuple-element.13), channel_id=1, source_target_pairs={{16,0},{32,16},{48,32},{64,48},{80,64},{96,80},{112,96},{1,112},{1... | collective-permute-start | bytes 393224 | tf_op jit(solution)/shard_map/ppermute | solution.py:60
  121.5 8.7 %collective-permute-start.3 = (f32[128,1,256]{2,1,0:T(1,128)}, f32[128,1,256]{2,1,0:T(1,128)}, u32[]{:S(2)}, u32[]{:S(2)}) collective-permute-start(f32[128,1,256]{2,1,0:T(1,128)} %get-tuple-element.14), channel_id=1, source_target_pairs={{0,16},{16,32},{32,48},{48,64},{64,80},{80,96},{96,112},{112,1},{1... | collective-permute-start | bytes 393224 | tf_op jit(solution)/shard_map/ppermute | solution.py:59
  124.1 1.0 copy-start.17
  128.7 3.8 %copy-start.20 = (f32[1024,256]{1,0:T(8,128)S(1)}, f32[1024,256]{1,0:T(8,128)}, u32[]{:S(2)}) copy-start(f32[1024,256]{1,0:T(8,128)} %copy.155) | copy-start | bytes 3145732
  132.7 36.9 %copy-start.2 = (f32[1024,1024]{1,0:T(8,128)S(1)}, f32[1024,1024]{1,0:T(8,128)}, u32[]{:S(2)}) copy-start(f32[1024,1024]{1,0:T(8,128)} %param.9) | copy-start | bytes 12582916
  168.3 1.3 copy-start.4
  175.2 29.3 %all-to-all-start.4 = ((f32[128,8,256]{2,1,0:T(8,128)}), f32[128,8,256]{2,1,0:T(8,128)}, u32[]{:S(2)}, u32[]{:S(2)}) async-start(f32[128,8,256]{2,1,0:T(8,128)} %bitcast.97), calls=%async_computation.4 | async-start | bytes 2097152 | tf_op jit(solution)/shard_map/all_to_all | solution.py:105
  181.2 9.8 %copy-start.5 = (f32[128,8,512]{2,1,0:T(8,128)S(1)}, f32[128,8,512]{2,1,0:T(8,128)}, u32[]{:S(2)}) copy-start(f32[128,8,512]{2,1,0:T(8,128)} %copy-done.4) | copy-start | bytes 6291460
  182.8 8.5 %copy-start.19 = (f32[127,8,256]{2,1,0:T(8,128)}, f32[127,8,256]{2,1,0:T(8,128)S(1)}, u32[]{:S(2)}) copy-start(f32[127,8,256]{2,1,0:T(8,128)S(1)} %slice.217) | copy-start | bytes 3121156
  183.0 13.5 %collective-permute-start.4 = (f32[128,1,256]{2,1,0:T(1,128)S(1)}, f32[128,1,256]{2,1,0:T(1,128)S(1)}, u32[]{:S(2)}, u32[]{:S(2)}) collective-permute-start(f32[128,1,256]{2,1,0:T(1,128)S(1)} %get-tuple-element.11), channel_id=1, source_target_pairs={{16,0},{32,16},{48,32},{64,48},{80,64},{96,80},{112,96},{1,112},{1... | collective-permute-start | bytes 393224 | tf_op jit(solution)/shard_map/ppermute | solution.py:60
  188.8 12.6 %collective-permute-start.5 = (f32[128,1,256]{2,1,0:T(1,128)S(1)}, f32[128,1,256]{2,1,0:T(1,128)S(1)}, u32[]{:S(2)}, u32[]{:S(2)}) collective-permute-start(f32[128,1,256]{2,1,0:T(1,128)S(1)} %get-tuple-element.12), channel_id=1, source_target_pairs={{0,16},{16,32},{32,48},{48,64},{64,80},{80,96},{96,112},{112,1},{1... | collective-permute-start | bytes 393224 | tf_op jit(solution)/shard_map/ppermute | solution.py:59
  204.6 1.5 copy-start.9
  204.6 1.8 copy-start.11
  246.7 7.8 %copy-start.15 = (f32[32,64,128]{2,1,0:T(8,128)S(1)}, f32[32,64,128]{2,1,0:T(8,128)}, u32[]{:S(2)}) copy-start(f32[32,64,128]{2,1,0:T(8,128)} %param.6) | copy-start | bytes 3145732
  246.9 7.6 %copy-start.7 = (f32[32,64,128]{2,1,0:T(8,128)S(1)}, f32[32,64,128]{2,1,0:T(8,128)}, u32[]{:S(2)}) copy-start(f32[32,64,128]{2,1,0:T(8,128)} %param.5) | copy-start | bytes 3145732
  246.9 7.6 %copy-start.13 = (f32[32,64,127]{2,1,0:T(8,128)S(1)}, f32[32,64,127]{2,1,0:T(8,128)}, u32[]{:S(2)}) copy-start(f32[32,64,127]{2,1,0:T(8,128)} %copy-done.12) | copy-start | bytes 3121156
  247.3 9.1 %collective-permute-start.6 = (f32[32,1,128]{2,1,0:T(1,128)S(1)}, f32[32,1,128]{2,1,0:T(1,128)S(1)}, u32[]{:S(2)}, u32[]{:S(2)}) collective-permute-start(f32[32,1,128]{2,1,0:T(1,128)S(1)} %get-tuple-element.5), channel_id=1, source_target_pairs={{1,0},{2,1},{3,2},{4,3},{5,4},{6,5},{7,6},{8,7},{9,8},{10,9},{11,1... | collective-permute-start | bytes 49160 | tf_op jit(solution)/shard_map/ppermute | solution.py:15
  250.1 6.3 %collective-permute-start.7 = (f32[32,1,128]{2,1,0:T(1,128)S(1)}, f32[32,1,128]{2,1,0:T(1,128)S(1)}, u32[]{:S(2)}, u32[]{:S(2)}) collective-permute-start(f32[32,1,128]{2,1,0:T(1,128)S(1)} %get-tuple-element.6), channel_id=1, source_target_pairs={{0,1},{1,2},{2,3},{3,4},{4,5},{5,6},{6,7},{7,8},{8,9},{9,10},{10,1... | collective-permute-start | bytes 49160 | tf_op jit(solution)/shard_map/ppermute | solution.py:14
  (1 other events, 1.0 us)

commit v7 on v6

--- a/solution.py
+++ b/solution.py
@@ -136,7 +136,7 @@
     count = lax.axis_size(LINES)
     s0y, ls1 = x_to_y(second0, lam_second1_y.reshape(count, -1, lam_second1_y.shape[1]))
     ls1 = rows(ls1.reshape(second0.shape))
-    state1_y = along_y(inv_y, s0y, False)
+    state1_y = rows(along_y(inv_y, s0y, False))
     lam_half1 = ls1 + RATE * (xdiff(ls1) + zoperate(ls1, cx))
     lam_first1 = along_x(lam_half1, inv_x, True)
     (dy_lam_first1,) = ydiff(lam_first1)
@@ -148,7 +148,7 @@
     half1 = along_x(first1, inv_x, False)
     grad = -RATE * zstep(ls1) * zstep(half1)
     grad = grad - RATE * zstep(lam_first1) * zstep(state1)
-    lam_second0_y = along_y(inv_y, lsy, True)
+    lam_second0_y = rows(along_y(inv_y, lsy, True))
     (ls0,) = y_to_x(lam_second0_y)
     ls0 = rows(ls0)
     grad = grad - RATE * zstep(ls0) * zstep(half0)

time: 259 us -> 253 us (0.977)
  local copies, waits for them, and re-layouts: 42.6 us -> 35.4 us
  waiting for transfers between devices: 27.6 us -> 31.8 us
    dot_general x2 -> x0, local copies, waits for them, and re-layouts: 5.06 us -> none  [along_y(): return lax.dot_general(matrix, field, dims, precision=HIGH)]
    ppermute x2, waiting for transfers between devices: 6.56 us -> 10.7 us  [ydiff(): lax.ppermute(jnp.concatenate([f[:, -1:] for f in fields]), ('px', 'py'), up)]
    unnamed x47 -> x41, local copies, waits for them, and re-layouts: 14.3 us -> 13.9 us
  transfers between devices with their start and end apart: 11 -> 11, of which waited for: 6 -> 7; matrix products, arithmetic and copies ran while one was open for 12% -> 11% of each run, Pallas kernels for 0% -> 0%
where the time goes in v7:
time: 253 us; the launch traced here: 252 us
  blocking collectives  105 us (42%)
  starting transfers between devices  49.6 us (20%)
  local copies, waits for them, and re-layouts  35.4 us (14%)
  waiting for transfers between devices  31.8 us (13%)
  matrix products  17.3 us (7%)
  other arithmetic  11.7 us (5%)
    all_to_all x2, blocking collectives, x_to_y(): lax.all_to_all(joined, LINES, split_axis=0, concat_axis=0, tiled=True)  74 us
    all_to_all x1, blocking collectives, x_to_block(): lax.all_to_all(joined, 'px', split_axis=0, concat_axis=1, tiled=True)  30.7 us
    unnamed x41, local copies, waits for them, and re-layouts  13.9 us
    all_to_all x1, starting transfers between devices, x_to_y(): lax.all_to_all(joined, LINES, split_axis=0, concat_axis=0, tiled=True)  11.5 us
    dot_general x3, matrix products, along_y(): return lax.dot_general(matrix, field, dims, precision=HIGH)  11.4 us
    ppermute x2, waiting for transfers between devices, ydiff(): lax.ppermute(jnp.concatenate([f[:, -1:] for f in fields]), ('px', 'py'), up)  10.7 us
    all_to_all x1, waiting for transfers between devices, block_to_x(): lax.all_to_all(joined, 'px', split_axis=1, concat_axis=0, tiled=True)  8.89 us
    ppermute x2, starting transfers between devices, ydiff(): lax.ppermute(jnp.concatenate([f[:, :1] for f in fields]), ('px', 'py'), d...  8.86 us
  transfers between devices with their start and end apart: 11, of which 7 were waited for; matrix products, arithmetic and copies ran while one was open for 11% of the time, Pallas kernels for 0%

profile of v7, /device:TPU:1, one launch (start us, length us, event | category | flops | bytes accessed | tf_op | source)
XLA Modules:
  0.0 251.7 jit_solution(17955555762730385222)
XLA Ops:
  0.6 1.9 copy.132
  3.9 11.5 %all-to-all-start.1 = ((f32[128,8,256]{2,1,0:T(8,128)}), f32[128,8,256]{2,1,0:T(8,128)S(1)}, u32[]{:S(2)}, u32[]{:S(2)}) async-start(f32[128,8,256]{2,1,0:T(8,128)} %copy.133), calls=%async_computation.1 | async-start | bytes 2097152 | tf_op jit(solution)/shard_map/all_to_all | solution.py:95
  15.5 3.0 %collective-permute-start = (f32[32,1,128]{2,1,0:T(1,128)S(1)}, f32[32,1,128]{2,1,0:T(1,128)S(1)}, u32[]{:S(2)}, u32[]{:S(2)}) collective-permute-start(f32[32,1,128]{2,1,0:T(1,128)S(1)} %get-tuple-element.15), channel_id=1, source_target_pairs={{1,0},{2,1},{3,2},{4,3},{5,4},{6,5},{7,6},{8,7},{9,8},{10,9},{11,1... | collective-permute-start | bytes 49160 | tf_op jit(solution)/shard_map/ppermute | solution.py:15
  18.4 4.1 %collective-permute-start.1 = (f32[32,1,128]{2,1,0:T(1,128)S(1)}, f32[32,1,128]{2,1,0:T(1,128)S(1)}, u32[]{:S(2)}, u32[]{:S(2)}) collective-permute-start(f32[32,1,128]{2,1,0:T(1,128)S(1)} %get-tuple-element.16), channel_id=1, source_target_pairs={{0,1},{1,2},{2,3},{3,4},{4,5},{5,6},{6,7},{7,8},{8,9},{9,10},{10,1... | collective-permute-start | bytes 49160 | tf_op jit(solution)/shard_map/ppermute | solution.py:14
  23.9 6.6 %collective-permute-done = f32[32,1,128]{2,1,0:T(1,128)S(1)} collective-permute-done((f32[32,1,128]{2,1,0:T(1,128)S(1)}, f32[32,1,128]{2,1,0:T(1,128)S(1)}, u32[]{:S(2)}, u32[]{:S(2)}) %collective-permute-start) | collective-permute-done | bytes 16416 | tf_op jit(solution)/shard_map/ppermute | solution.py:15
  31.2 2.6 %copy.121 = f32[32,64,256]{2,0,1:T(8,128)} copy(f32[32,64,256]{2,1,0:T(8,128)S(1)} %pad_maximum_fusion) | data formatting | bytes 4194304 | tf_op jit(solution)/shard_map/concatenate | solution.py:80
  34.3 4.5 %all-to-all-start = ((f32[32,64,256]{2,0,1:T(8,128)}), f32[32,64,256]{2,0,1:T(8,128)}, u32[]{:S(2)}, u32[]{:S(2)}) async-start(f32[32,64,256]{2,0,1:T(8,128)} %copy.121), calls=%async_computation | async-start | bytes 4194304 | tf_op jit(solution)/shard_map/all_to_all | solution.py:81
  38.9 5.4 %copy.131 = f32[1024,1024]{0,1:T(8,128)} copy(f32[1024,1024]{1,0:T(8,128)} %param.9) | data formatting | bytes 8388608 | tf_op args[4]
  44.2 2.5 reshape_reshape.3
  46.8 3.0 %copy.134 = f32[16,64,8,32]{1,0,3,2:T(8,128)S(1)} copy(f32[16,64,8,32]{3,1,2,0:T(8,128)} %bitcast.91) | data formatting | bytes 2097152 | tf_op jit(solution)/shard_map/transpose | solution.py:121
  50.3 5.0 %fusion = f32[128,8,256]{2,1,0:T(8,128)} fusion(f32[1024,1024]{0,1:T(8,128)} %copy.131, f32[1024,256]{0,1:T(8,128)S(1)} %reshape.31), kind=kOutput, calls=%fused_computation | convolution fusion | flops 1610612736 | bytes 6291456 | tf_op jit(solution)/shard_map/dot_general | solution.py:76
  55.3 8.9 %all-to-all-done = f32[32,64,256]{2,0,1:T(8,128)} async-done(((f32[32,64,256]{2,0,1:T(8,128)}), f32[32,64,256]{2,0,1:T(8,128)}, u32[]{:S(2)}, u32[]{:S(2)}) %all-to-all-start) | async-done | bytes 2097184 | tf_op jit(solution)/shard_map/all_to_all | solution.py:81
  64.2 2.8 %copy.123 = f32[8,32,8,256]{3,2,1,0:T(8,128)S(1)} copy(f32[8,32,8,256]{3,1,2,0:T(8,128)} %bitcast.2) | data formatting | bytes 4194304 | tf_op jit(solution)/shard_map/all_to_all | solution.py:81
  71.5 38.7 %all_to_all.56 = f32[128,8,512]{2,1,0:T(8,128)S(1)} all-to-all(f32[128,8,512]{2,1,0:T(8,128)S(1)} %pad_maximum_fusion.1), channel_id=1, replica_groups=mesh['px'=8,'py'=16] {'py','px'}, dimensions={0} | all-to-all | bytes 4194304 | tf_op jit(solution)/shard_map/all_to_all | solution.py:95
  113.8 1.9 convolution_bitcast_fusion.2
  115.7 3.0 %collective-permute-start.2 = (f32[128,1,256]{2,1,0:T(1,128)S(1)}, f32[128,1,256]{2,1,0:T(1,128)S(1)}, u32[]{:S(2)}, u32[]{:S(2)}) collective-permute-start(f32[128,1,256]{2,1,0:T(1,128)S(1)} %get-tuple-element.13), channel_id=1, source_target_pairs={{16,0},{32,16},{48,32},{64,48},{80,64},{96,80},{112,96},{1,112},{1... | collective-permute-start | bytes 393224 | tf_op jit(solution)/shard_map/ppermute | solution.py:60
  118.7 2.3 collective-permute-start.3
  121.4 5.7 %collective-permute-done.3 = f32[128,1,256]{2,1,0:T(1,128)S(1)} collective-permute-done((f32[128,1,256]{2,1,0:T(1,128)S(1)}, f32[128,1,256]{2,1,0:T(1,128)S(1)}, u32[]{:S(2)}, u32[]{:S(2)}) %collective-permute-start.3) | collective-permute-done | bytes 131104 | tf_op jit(solution)/shard_map/ppermute | solution.py:59
  128.0 35.2 %all_to_all.57 = f32[128,8,512]{2,1,0:T(8,128)S(1)} all-to-all(f32[128,8,512]{2,1,0:T(8,128)S(1)} %pad_maximum_fusion.2), channel_id=1, replica_groups=mesh['px'=8,'py'=16] {'py','px'}, dimensions={0} | all-to-all | bytes 4194304 | tf_op jit(solution)/shard_map/all_to_all | solution.py:95
  164.5 4.5 %convolution_bitcast_fusion.1 = f32[128,8,256]{2,1,0:T(8,128)} fusion(f32[1024,1024]{1,0:T(8,128)S(1)} %copy-done.1, f32[1024,512]{1,0:T(8,128)S(1)} %bitcast.87), kind=kOutput, calls=%fused_computation.14 | convolution fusion | flops 1610612736 | bytes 6291456 | tf_op jit(solution)/shard_map/dot_general | solution.py:76
  169.0 6.0 %all-to-all-start.4 = ((f32[128,8,256]{2,1,0:T(8,128)}), f32[128,8,256]{2,1,0:T(8,128)}, u32[]{:S(2)}, u32[]{:S(2)}) async-start(f32[128,8,256]{2,1,0:T(8,128)} %convolution_bitcast_fusion.1), calls=%async_computation.4 | async-start | bytes 2097152 | tf_op jit(solution)/shard_map/all_to_all | solution.py:105
  176.7 5.9 %collective-permute-start.4 = (f32[128,1,256]{2,1,0:T(1,128)S(1)}, f32[128,1,256]{2,1,0:T(1,128)S(1)}, u32[]{:S(2)}, u32[]{:S(2)}) collective-permute-start(f32[128,1,256]{2,1,0:T(1,128)S(1)} %get-tuple-element.11), channel_id=1, source_target_pairs={{16,0},{32,16},{48,32},{64,48},{80,64},{96,80},{112,96},{1,112},{1... | collective-permute-start | bytes 393224 | tf_op jit(solution)/shard_map/ppermute | solution.py:60
  182.6 2.2 collective-permute-start.5
  185.2 5.0 %collective-permute-done.4 = f32[128,1,256]{2,1,0:T(1,128)S(1)} collective-permute-done((f32[128,1,256]{2,1,0:T(1,128)S(1)}, f32[128,1,256]{2,1,0:T(1,128)S(1)}, u32[]{:S(2)}, u32[]{:S(2)}) %collective-permute-start.4) | collective-permute-done | bytes 131104 | tf_op jit(solution)/shard_map/ppermute | solution.py:60
  190.2 5.0 %collective-permute-done.5 = f32[128,1,256]{2,1,0:T(1,128)S(1)} collective-permute-done((f32[128,1,256]{2,1,0:T(1,128)S(1)}, f32[128,1,256]{2,1,0:T(1,128)S(1)}, u32[]{:S(2)}, u32[]{:S(2)}) %collective-permute-start.5) | collective-permute-done | bytes 131104 | tf_op jit(solution)/shard_map/ppermute | solution.py:59
  200.2 4.1 %bitcast_multiply_fusion.1 = (f32[128,8,256]{2,1,0:T(8,128)S(1)}, f32[256,8,128]{0,1,2:T(8,128)S(1)}) fusion(f32[256,8,128]{0,1,2:T(8,128)S(1)} %copy.164, f32[128,8,256]{2,1,0:T(8,128)} %all-to-all-done.4, f32[127,8,256]{2,1,0:T(8,128)S(1)} %slice.212, f32[128,8,256]{2,1,0:T(8,128)S(1)} %fusion.67, f32[127,8,256]{2,1,0:T(8,128)S(1)} %copy-done.8, ...), kind=kLoop, calls=%fused_computation.71 | loop fusion | flops 3932160 | bytes 15679488 | tf_op jit(solution)/shard_map/mul | solution.py:38
  204.4 3.2 %convolution_bitcast_fusion = f32[256,8,128]{0,1,2:T(8,128)S(1)} fusion(f32[128,8,256]{2,1,0:T(8,128)} %all-to-all-done.4, f32[127,8,256]{2,1,0:T(8,128)S(1)} %slice.213, f32[256,8,128]{0,1,2:T(8,128)S(1)} %copy.164, f32[127,8,256]{2,1,0:T(8,128)S(1)} %slice.212, f32[256,256]{1,0:T(8,128)S(1)} %copy-done), kind=kOutput, calls=%fused_computation.13 | convolution fusion | flops 405012480 | bytes 5488640 | tf_op jit(solution)/shard_map/dot_general | solution.py:71
  207.7 2.0 copy.150
  209.8 30.7 %all_to_all.58 = f32[256,8,256]{2,1,0:T(8,128)S(1)} all-to-all(f32[256,8,256]{2,1,0:T(8,128)} %copy.150), channel_id=1, replica_groups=mesh['px'=8,'py'=16] {'px'}, dimensions={0} | all-to-all | bytes 4194304 | tf_op jit(solution)/shard_map/all_to_all | solution.py:88
  241.1 2.8 %collective-permute-start.6 = (f32[32,1,128]{2,1,0:T(1,128)S(1)}, f32[32,1,128]{2,1,0:T(1,128)S(1)}, u32[]{:S(2)}, u32[]{:S(2)}) collective-permute-start(f32[32,1,128]{2,1,0:T(1,128)S(1)} %get-tuple-element.5), channel_id=1, source_target_pairs={{1,0},{2,1},{3,2},{4,3},{5,4},{6,5},{7,6},{8,7},{9,8},{10,9},{11,1... | collective-permute-start | bytes 49160 | tf_op jit(solution)/shard_map/ppermute | solution.py:15
  243.9 4.4 %collective-permute-start.7 = (f32[32,1,128]{2,1,0:T(1,128)S(1)}, f32[32,1,128]{2,1,0:T(1,128)S(1)}, u32[]{:S(2)}, u32[]{:S(2)}) collective-permute-start(f32[32,1,128]{2,1,0:T(1,128)S(1)} %get-tuple-element.6), channel_id=1, source_target_pairs={{0,1},{1,2},{2,3},{3,4},{4,5},{5,6},{6,7},{7,8},{8,9},{9,10},{10,1... | collective-permute-start | bytes 49160 | tf_op jit(solution)/shard_map/ppermute | solution.py:14
  248.3 1.8 slice_subtract_fusion
  (85 shorter events, 24.4 us)
Async XLA Ops:
  0.6 67.7 %copy-start = (f32[256,256]{1,0:T(8,128)S(1)}, f32[256,256]{1,0:T(8,128)}, u32[]{:S(2)}) copy-start(f32[256,256]{1,0:T(8,128)} %param.8) | copy-start | bytes 786436
  2.5 12.9 %copy-start.5 = (f32[32,64,128]{2,1,0:T(8,128)S(1)}, f32[32,64,128]{2,1,0:T(8,128)}, u32[]{:S(2)}) copy-start(f32[32,64,128]{2,1,0:T(8,128)} %param.5) | copy-start | bytes 3145732
  3.9 19.0 %copy-start.13 = (f32[32,64,128]{2,1,0:T(8,128)S(1)}, f32[32,64,128]{2,1,0:T(8,128)}, u32[]{:S(2)}) copy-start(f32[32,64,128]{2,1,0:T(8,128)} %param.6) | copy-start | bytes 3145732
  3.9 30.4 %all-to-all-start.1 = ((f32[128,8,256]{2,1,0:T(8,128)}), f32[128,8,256]{2,1,0:T(8,128)S(1)}, u32[]{:S(2)}, u32[]{:S(2)}) async-start(f32[128,8,256]{2,1,0:T(8,128)} %copy.133), calls=%async_computation.1 | async-start | bytes 2097152 | tf_op jit(solution)/shard_map/all_to_all | solution.py:95
  15.5 15.0 %collective-permute-start = (f32[32,1,128]{2,1,0:T(1,128)S(1)}, f32[32,1,128]{2,1,0:T(1,128)S(1)}, u32[]{:S(2)}, u32[]{:S(2)}) collective-permute-start(f32[32,1,128]{2,1,0:T(1,128)S(1)} %get-tuple-element.15), channel_id=1, source_target_pairs={{1,0},{2,1},{3,2},{4,3},{5,4},{6,5},{7,6},{8,7},{9,8},{10,9},{11,1... | collective-permute-start | bytes 49160 | tf_op jit(solution)/shard_map/ppermute | solution.py:15
  18.4 12.0 %collective-permute-start.1 = (f32[32,1,128]{2,1,0:T(1,128)S(1)}, f32[32,1,128]{2,1,0:T(1,128)S(1)}, u32[]{:S(2)}, u32[]{:S(2)}) collective-permute-start(f32[32,1,128]{2,1,0:T(1,128)S(1)} %get-tuple-element.16), channel_id=1, source_target_pairs={{0,1},{1,2},{2,3},{3,4},{4,5},{5,6},{6,7},{7,8},{8,9},{9,10},{10,1... | collective-permute-start | bytes 49160 | tf_op jit(solution)/shard_map/ppermute | solution.py:14
  22.9 1.0 copy-start.11
  34.3 29.9 %all-to-all-start = ((f32[32,64,256]{2,0,1:T(8,128)}), f32[32,64,256]{2,0,1:T(8,128)}, u32[]{:S(2)}, u32[]{:S(2)}) async-start(f32[32,64,256]{2,0,1:T(8,128)} %copy.121), calls=%async_computation | async-start | bytes 4194304 | tf_op jit(solution)/shard_map/all_to_all | solution.py:81
  69.0 1.0 copy-start.7
  70.0 1.2 copy-start.18
  110.3 2.6 %copy-start.2 = (f32[128,8,512]{2,1,0:T(8,128)}, f32[128,8,512]{2,1,0:T(8,128)S(1)}, u32[]{:S(2)}) copy-start(f32[128,8,512]{2,1,0:T(8,128)S(1)} %all_to_all.56) | copy-start | bytes 6291460
  110.5 1.2 copy-start.9
  111.6 2.2 copy-start.1
  113.8 7.2 %copy-start.16 = (f32[127,8,256]{2,1,0:T(8,128)}, f32[127,8,256]{2,1,0:T(8,128)S(1)}, u32[]{:S(2)}) copy-start(f32[127,8,256]{2,1,0:T(8,128)S(1)} %slice.208) | copy-start | bytes 3121156
  115.7 5.7 %collective-permute-start.2 = (f32[128,1,256]{2,1,0:T(1,128)S(1)}, f32[128,1,256]{2,1,0:T(1,128)S(1)}, u32[]{:S(2)}, u32[]{:S(2)}) collective-permute-start(f32[128,1,256]{2,1,0:T(1,128)S(1)} %get-tuple-element.13), channel_id=1, source_target_pairs={{16,0},{32,16},{48,32},{64,48},{80,64},{96,80},{112,96},{1,112},{1... | collective-permute-start | bytes 393224 | tf_op jit(solution)/shard_map/ppermute | solution.py:60
  118.7 8.4 %collective-permute-start.3 = (f32[128,1,256]{2,1,0:T(1,128)S(1)}, f32[128,1,256]{2,1,0:T(1,128)S(1)}, u32[]{:S(2)}, u32[]{:S(2)}) collective-permute-start(f32[128,1,256]{2,1,0:T(1,128)S(1)} %get-tuple-element.14), channel_id=1, source_target_pairs={{0,16},{16,32},{32,48},{48,64},{64,80},{80,96},{96,112},{112,1},{1... | collective-permute-start | bytes 393224 | tf_op jit(solution)/shard_map/ppermute | solution.py:59
  163.2 1.3 copy-start.3
  169.0 29.4 %all-to-all-start.4 = ((f32[128,8,256]{2,1,0:T(8,128)}), f32[128,8,256]{2,1,0:T(8,128)}, u32[]{:S(2)}, u32[]{:S(2)}) async-start(f32[128,8,256]{2,1,0:T(8,128)} %convolution_bitcast_fusion.1), calls=%async_computation.4 | async-start | bytes 2097152 | tf_op jit(solution)/shard_map/all_to_all | solution.py:105
  175.0 9.8 %copy-start.4 = (f32[128,8,512]{2,1,0:T(8,128)S(1)}, f32[128,8,512]{2,1,0:T(8,128)}, u32[]{:S(2)}) copy-start(f32[128,8,512]{2,1,0:T(8,128)} %copy-done.3) | copy-start | bytes 6291460
  176.6 8.5 %copy-start.17 = (f32[127,8,256]{2,1,0:T(8,128)}, f32[127,8,256]{2,1,0:T(8,128)S(1)}, u32[]{:S(2)}) copy-start(f32[127,8,256]{2,1,0:T(8,128)S(1)} %slice.217) | copy-start | bytes 3121156
  176.7 13.5 %collective-permute-start.4 = (f32[128,1,256]{2,1,0:T(1,128)S(1)}, f32[128,1,256]{2,1,0:T(1,128)S(1)}, u32[]{:S(2)}, u32[]{:S(2)}) collective-permute-start(f32[128,1,256]{2,1,0:T(1,128)S(1)} %get-tuple-element.11), channel_id=1, source_target_pairs={{16,0},{32,16},{48,32},{64,48},{80,64},{96,80},{112,96},{1,112},{1... | collective-permute-start | bytes 393224 | tf_op jit(solution)/shard_map/ppermute | solution.py:60
  182.6 12.6 %collective-permute-start.5 = (f32[128,1,256]{2,1,0:T(1,128)S(1)}, f32[128,1,256]{2,1,0:T(1,128)S(1)}, u32[]{:S(2)}, u32[]{:S(2)}) collective-permute-start(f32[128,1,256]{2,1,0:T(1,128)S(1)} %get-tuple-element.12), channel_id=1, source_target_pairs={{0,16},{16,32},{32,48},{48,64},{64,80},{80,96},{96,112},{112,1},{1... | collective-permute-start | bytes 393224 | tf_op jit(solution)/shard_map/ppermute | solution.py:59
  196.4 1.0 copy-start.15
  198.4 1.5 copy-start.8
  198.4 1.8 copy-start.10
  240.5 7.8 %copy-start.14 = (f32[32,64,128]{2,1,0:T(8,128)S(1)}, f32[32,64,128]{2,1,0:T(8,128)}, u32[]{:S(2)}) copy-start(f32[32,64,128]{2,1,0:T(8,128)} %param.6) | copy-start | bytes 3145732
  240.7 7.6 %copy-start.6 = (f32[32,64,128]{2,1,0:T(8,128)S(1)}, f32[32,64,128]{2,1,0:T(8,128)}, u32[]{:S(2)}) copy-start(f32[32,64,128]{2,1,0:T(8,128)} %param.5) | copy-start | bytes 3145732
  240.7 7.6 %copy-start.12 = (f32[32,64,127]{2,1,0:T(8,128)S(1)}, f32[32,64,127]{2,1,0:T(8,128)}, u32[]{:S(2)}) copy-start(f32[32,64,127]{2,1,0:T(8,128)} %copy-done.11) | copy-start | bytes 3121156
  241.1 9.1 %collective-permute-start.6 = (f32[32,1,128]{2,1,0:T(1,128)S(1)}, f32[32,1,128]{2,1,0:T(1,128)S(1)}, u32[]{:S(2)}, u32[]{:S(2)}) collective-permute-start(f32[32,1,128]{2,1,0:T(1,128)S(1)} %get-tuple-element.5), channel_id=1, source_target_pairs={{1,0},{2,1},{3,2},{4,3},{5,4},{6,5},{7,6},{8,7},{9,8},{10,9},{11,1... | collective-permute-start | bytes 49160 | tf_op jit(solution)/shard_map/ppermute | solution.py:15
  243.9 6.3 %collective-permute-start.7 = (f32[32,1,128]{2,1,0:T(1,128)S(1)}, f32[32,1,128]{2,1,0:T(1,128)S(1)}, u32[]{:S(2)}, u32[]{:S(2)}) collective-permute-start(f32[32,1,128]{2,1,0:T(1,128)S(1)} %get-tuple-element.6), channel_id=1, source_target_pairs={{0,1},{1,2},{2,3},{3,4},{4,5},{5,6},{6,7},{7,8},{8,9},{9,10},{10,1... | collective-permute-start | bytes 49160 | tf_op jit(solution)/shard_map/ppermute | solution.py:14

commit v8 on v7

--- a/solution.py
+++ b/solution.py
@@ -150,7 +150,6 @@
     grad = grad - RATE * zstep(lam_first1) * zstep(state1)
     lam_second0_y = rows(along_y(inv_y, lsy, True))
     (ls0,) = y_to_x(lam_second0_y)
-    ls0 = rows(ls0)
     grad = grad - RATE * zstep(ls0) * zstep(half0)
     lam_half0 = ls0 + RATE * (xdiff(ls0) + zoperate(ls0, cx))
     lam_first0 = along_x(lam_half0, inv_x, True)

time: 253 us -> 253 us (level)
  no operation moved by 1% of the time
where the time goes in v8:
time: 253 us; the launch traced here: 252 us
  blocking collectives  105 us (42%)
  starting transfers between devices  49.6 us (20%)
  local copies, waits for them, and re-layouts  35.4 us (14%)
  waiting for transfers between devices  31.8 us (13%)
  matrix products  17.3 us (7%)
  other arithmetic  11.7 us (5%)
    all_to_all x2, blocking collectives, x_to_y(): lax.all_to_all(joined, LINES, split_axis=0, concat_axis=0, tiled=True)  74 us
    all_to_all x1, blocking collectives, x_to_block(): lax.all_to_all(joined, 'px', split_axis=0, concat_axis=1, tiled=True)  30.7 us
    unnamed x41, local copies, waits for them, and re-layouts  13.9 us
    all_to_all x1, starting transfers between devices, x_to_y(): lax.all_to_all(joined, LINES, split_axis=0, concat_axis=0, tiled=True)  11.5 us
    dot_general x3, matrix products, along_y(): return lax.dot_general(matrix, field, dims, precision=HIGH)  11.4 us
    ppermute x2, waiting for transfers between devices, ydiff(): lax.ppermute(jnp.concatenate([f[:, -1:] for f in fields]), ('px', 'py'), up)  10.7 us
    all_to_all x1, waiting for transfers between devices, block_to_x(): lax.all_to_all(joined, 'px', split_axis=1, concat_axis=0, tiled=True)  8.89 us
    ppermute x2, starting transfers between devices, ydiff(): lax.ppermute(jnp.concatenate([f[:, :1] for f in fields]), ('px', 'py'), d...  8.86 us
  transfers between devices with their start and end apart: 11, of which 7 were waited for; matrix products, arithmetic and copies ran while one was open for 11% of the time, Pallas kernels for 0%

profile of v8, /device:TPU:1, one launch (start us, length us, event | category | flops | bytes accessed | tf_op | source)
XLA Modules:
  0.0 251.7 jit_solution(17955555762730385222)
XLA Ops:
  0.6 1.9 copy.132
  3.9 11.5 %all-to-all-start.1 = ((f32[128,8,256]{2,1,0:T(8,128)}), f32[128,8,256]{2,1,0:T(8,128)S(1)}, u32[]{:S(2)}, u32[]{:S(2)}) async-start(f32[128,8,256]{2,1,0:T(8,128)} %copy.133), calls=%async_computation.1 | async-start | bytes 2097152 | tf_op jit(solution)/shard_map/all_to_all | solution.py:95
  15.5 3.0 %collective-permute-start = (f32[32,1,128]{2,1,0:T(1,128)S(1)}, f32[32,1,128]{2,1,0:T(1,128)S(1)}, u32[]{:S(2)}, u32[]{:S(2)}) collective-permute-start(f32[32,1,128]{2,1,0:T(1,128)S(1)} %get-tuple-element.15), channel_id=1, source_target_pairs={{1,0},{2,1},{3,2},{4,3},{5,4},{6,5},{7,6},{8,7},{9,8},{10,9},{11,1... | collective-permute-start | bytes 49160 | tf_op jit(solution)/shard_map/ppermute | solution.py:15
  18.4 4.1 %collective-permute-start.1 = (f32[32,1,128]{2,1,0:T(1,128)S(1)}, f32[32,1,128]{2,1,0:T(1,128)S(1)}, u32[]{:S(2)}, u32[]{:S(2)}) collective-permute-start(f32[32,1,128]{2,1,0:T(1,128)S(1)} %get-tuple-element.16), channel_id=1, source_target_pairs={{0,1},{1,2},{2,3},{3,4},{4,5},{5,6},{6,7},{7,8},{8,9},{9,10},{10,1... | collective-permute-start | bytes 49160 | tf_op jit(solution)/shard_map/ppermute | solution.py:14
  23.9 6.6 %collective-permute-done = f32[32,1,128]{2,1,0:T(1,128)S(1)} collective-permute-done((f32[32,1,128]{2,1,0:T(1,128)S(1)}, f32[32,1,128]{2,1,0:T(1,128)S(1)}, u32[]{:S(2)}, u32[]{:S(2)}) %collective-permute-start) | collective-permute-done | bytes 16416 | tf_op jit(solution)/shard_map/ppermute | solution.py:15
  31.2 2.6 %copy.121 = f32[32,64,256]{2,0,1:T(8,128)} copy(f32[32,64,256]{2,1,0:T(8,128)S(1)} %pad_maximum_fusion) | data formatting | bytes 4194304 | tf_op jit(solution)/shard_map/concatenate | solution.py:80
  34.3 4.5 %all-to-all-start = ((f32[32,64,256]{2,0,1:T(8,128)}), f32[32,64,256]{2,0,1:T(8,128)}, u32[]{:S(2)}, u32[]{:S(2)}) async-start(f32[32,64,256]{2,0,1:T(8,128)} %copy.121), calls=%async_computation | async-start | bytes 4194304 | tf_op jit(solution)/shard_map/all_to_all | solution.py:81
  38.9 5.4 %copy.131 = f32[1024,1024]{0,1:T(8,128)} copy(f32[1024,1024]{1,0:T(8,128)} %param.9) | data formatting | bytes 8388608 | tf_op args[4]
  44.2 2.5 reshape_reshape.3
  46.8 3.0 %copy.134 = f32[16,64,8,32]{1,0,3,2:T(8,128)S(1)} copy(f32[16,64,8,32]{3,1,2,0:T(8,128)} %bitcast.91) | data formatting | bytes 2097152 | tf_op jit(solution)/shard_map/transpose | solution.py:121
  50.3 5.0 %fusion = f32[128,8,256]{2,1,0:T(8,128)} fusion(f32[1024,1024]{0,1:T(8,128)} %copy.131, f32[1024,256]{0,1:T(8,128)S(1)} %reshape.31), kind=kOutput, calls=%fused_computation | convolution fusion | flops 1610612736 | bytes 6291456 | tf_op jit(solution)/shard_map/dot_general | solution.py:76
  55.3 8.9 %all-to-all-done = f32[32,64,256]{2,0,1:T(8,128)} async-done(((f32[32,64,256]{2,0,1:T(8,128)}), f32[32,64,256]{2,0,1:T(8,128)}, u32[]{:S(2)}, u32[]{:S(2)}) %all-to-all-start) | async-done | bytes 2097184 | tf_op jit(solution)/shard_map/all_to_all | solution.py:81
  64.2 2.8 %copy.123 = f32[8,32,8,256]{3,2,1,0:T(8,128)S(1)} copy(f32[8,32,8,256]{3,1,2,0:T(8,128)} %bitcast.2) | data formatting | bytes 4194304 | tf_op jit(solution)/shard_map/all_to_all | solution.py:81
  71.5 38.7 %all_to_all.56 = f32[128,8,512]{2,1,0:T(8,128)S(1)} all-to-all(f32[128,8,512]{2,1,0:T(8,128)S(1)} %pad_maximum_fusion.1), channel_id=1, replica_groups=mesh['px'=8,'py'=16] {'py','px'}, dimensions={0} | all-to-all | bytes 4194304 | tf_op jit(solution)/shard_map/all_to_all | solution.py:95
  113.8 1.9 convolution_bitcast_fusion.2
  115.7 3.0 %collective-permute-start.2 = (f32[128,1,256]{2,1,0:T(1,128)S(1)}, f32[128,1,256]{2,1,0:T(1,128)S(1)}, u32[]{:S(2)}, u32[]{:S(2)}) collective-permute-start(f32[128,1,256]{2,1,0:T(1,128)S(1)} %get-tuple-element.13), channel_id=1, source_target_pairs={{16,0},{32,16},{48,32},{64,48},{80,64},{96,80},{112,96},{1,112},{1... | collective-permute-start | bytes 393224 | tf_op jit(solution)/shard_map/ppermute | solution.py:60
  118.7 2.3 collective-permute-start.3
  121.4 5.7 %collective-permute-done.3 = f32[128,1,256]{2,1,0:T(1,128)S(1)} collective-permute-done((f32[128,1,256]{2,1,0:T(1,128)S(1)}, f32[128,1,256]{2,1,0:T(1,128)S(1)}, u32[]{:S(2)}, u32[]{:S(2)}) %collective-permute-start.3) | collective-permute-done | bytes 131104 | tf_op jit(solution)/shard_map/ppermute | solution.py:59
  128.0 35.2 %all_to_all.57 = f32[128,8,512]{2,1,0:T(8,128)S(1)} all-to-all(f32[128,8,512]{2,1,0:T(8,128)S(1)} %pad_maximum_fusion.2), channel_id=1, replica_groups=mesh['px'=8,'py'=16] {'py','px'}, dimensions={0} | all-to-all | bytes 4194304 | tf_op jit(solution)/shard_map/all_to_all | solution.py:95
  164.5 4.5 %convolution_bitcast_fusion.1 = f32[128,8,256]{2,1,0:T(8,128)} fusion(f32[1024,1024]{1,0:T(8,128)S(1)} %copy-done.1, f32[1024,512]{1,0:T(8,128)S(1)} %bitcast.87), kind=kOutput, calls=%fused_computation.14 | convolution fusion | flops 1610612736 | bytes 6291456 | tf_op jit(solution)/shard_map/dot_general | solution.py:76
  169.0 6.0 %all-to-all-start.4 = ((f32[128,8,256]{2,1,0:T(8,128)}), f32[128,8,256]{2,1,0:T(8,128)}, u32[]{:S(2)}, u32[]{:S(2)}) async-start(f32[128,8,256]{2,1,0:T(8,128)} %convolution_bitcast_fusion.1), calls=%async_computation.4 | async-start | bytes 2097152 | tf_op jit(solution)/shard_map/all_to_all | solution.py:105
  176.7 5.9 %collective-permute-start.4 = (f32[128,1,256]{2,1,0:T(1,128)S(1)}, f32[128,1,256]{2,1,0:T(1,128)S(1)}, u32[]{:S(2)}, u32[]{:S(2)}) collective-permute-start(f32[128,1,256]{2,1,0:T(1,128)S(1)} %get-tuple-element.11), channel_id=1, source_target_pairs={{16,0},{32,16},{48,32},{64,48},{80,64},{96,80},{112,96},{1,112},{1... | collective-permute-start | bytes 393224 | tf_op jit(solution)/shard_map/ppermute | solution.py:60
  182.6 2.2 collective-permute-start.5
  185.2 5.0 %collective-permute-done.4 = f32[128,1,256]{2,1,0:T(1,128)S(1)} collective-permute-done((f32[128,1,256]{2,1,0:T(1,128)S(1)}, f32[128,1,256]{2,1,0:T(1,128)S(1)}, u32[]{:S(2)}, u32[]{:S(2)}) %collective-permute-start.4) | collective-permute-done | bytes 131104 | tf_op jit(solution)/shard_map/ppermute | solution.py:60
  190.2 5.0 %collective-permute-done.5 = f32[128,1,256]{2,1,0:T(1,128)S(1)} collective-permute-done((f32[128,1,256]{2,1,0:T(1,128)S(1)}, f32[128,1,256]{2,1,0:T(1,128)S(1)}, u32[]{:S(2)}, u32[]{:S(2)}) %collective-permute-start.5) | collective-permute-done | bytes 131104 | tf_op jit(solution)/shard_map/ppermute | solution.py:59
  200.2 4.1 %bitcast_multiply_fusion.1 = (f32[128,8,256]{2,1,0:T(8,128)S(1)}, f32[256,8,128]{0,1,2:T(8,128)S(1)}) fusion(f32[256,8,128]{0,1,2:T(8,128)S(1)} %copy.164, f32[128,8,256]{2,1,0:T(8,128)} %all-to-all-done.4, f32[127,8,256]{2,1,0:T(8,128)S(1)} %slice.212, f32[128,8,256]{2,1,0:T(8,128)S(1)} %fusion.67, f32[127,8,256]{2,1,0:T(8,128)S(1)} %copy-done.8, ...), kind=kLoop, calls=%fused_computation.71 | loop fusion | flops 3932160 | bytes 15679488 | tf_op jit(solution)/shard_map/mul | solution.py:38
  204.4 3.2 %convolution_bitcast_fusion = f32[256,8,128]{0,1,2:T(8,128)S(1)} fusion(f32[128,8,256]{2,1,0:T(8,128)} %all-to-all-done.4, f32[127,8,256]{2,1,0:T(8,128)S(1)} %slice.213, f32[256,8,128]{0,1,2:T(8,128)S(1)} %copy.164, f32[127,8,256]{2,1,0:T(8,128)S(1)} %slice.212, f32[256,256]{1,0:T(8,128)S(1)} %copy-done), kind=kOutput, calls=%fused_computation.13 | convolution fusion | flops 405012480 | bytes 5488640 | tf_op jit(solution)/shard_map/dot_general | solution.py:71
  207.7 2.0 copy.150
  209.8 30.7 %all_to_all.58 = f32[256,8,256]{2,1,0:T(8,128)S(1)} all-to-all(f32[256,8,256]{2,1,0:T(8,128)} %copy.150), channel_id=1, replica_groups=mesh['px'=8,'py'=16] {'px'}, dimensions={0} | all-to-all | bytes 4194304 | tf_op jit(solution)/shard_map/all_to_all | solution.py:88
  241.1 2.8 %collective-permute-start.6 = (f32[32,1,128]{2,1,0:T(1,128)S(1)}, f32[32,1,128]{2,1,0:T(1,128)S(1)}, u32[]{:S(2)}, u32[]{:S(2)}) collective-permute-start(f32[32,1,128]{2,1,0:T(1,128)S(1)} %get-tuple-element.5), channel_id=1, source_target_pairs={{1,0},{2,1},{3,2},{4,3},{5,4},{6,5},{7,6},{8,7},{9,8},{10,9},{11,1... | collective-permute-start | bytes 49160 | tf_op jit(solution)/shard_map/ppermute | solution.py:15
  243.9 4.4 %collective-permute-start.7 = (f32[32,1,128]{2,1,0:T(1,128)S(1)}, f32[32,1,128]{2,1,0:T(1,128)S(1)}, u32[]{:S(2)}, u32[]{:S(2)}) collective-permute-start(f32[32,1,128]{2,1,0:T(1,128)S(1)} %get-tuple-element.6), channel_id=1, source_target_pairs={{0,1},{1,2},{2,3},{3,4},{4,5},{5,6},{6,7},{7,8},{8,9},{9,10},{10,1... | collective-permute-start | bytes 49160 | tf_op jit(solution)/shard_map/ppermute | solution.py:14
  248.3 1.8 slice_subtract_fusion
  (85 shorter events, 24.4 us)
Async XLA Ops:
  0.6 67.7 %copy-start = (f32[256,256]{1,0:T(8,128)S(1)}, f32[256,256]{1,0:T(8,128)}, u32[]{:S(2)}) copy-start(f32[256,256]{1,0:T(8,128)} %param.8) | copy-start | bytes 786436
  2.5 12.9 %copy-start.5 = (f32[32,64,128]{2,1,0:T(8,128)S(1)}, f32[32,64,128]{2,1,0:T(8,128)}, u32[]{:S(2)}) copy-start(f32[32,64,128]{2,1,0:T(8,128)} %param.5) | copy-start | bytes 3145732
  3.9 19.0 %copy-start.13 = (f32[32,64,128]{2,1,0:T(8,128)S(1)}, f32[32,64,128]{2,1,0:T(8,128)}, u32[]{:S(2)}) copy-start(f32[32,64,128]{2,1,0:T(8,128)} %param.6) | copy-start | bytes 3145732
  3.9 30.4 %all-to-all-start.1 = ((f32[128,8,256]{2,1,0:T(8,128)}), f32[128,8,256]{2,1,0:T(8,128)S(1)}, u32[]{:S(2)}, u32[]{:S(2)}) async-start(f32[128,8,256]{2,1,0:T(8,128)} %copy.133), calls=%async_computation.1 | async-start | bytes 2097152 | tf_op jit(solution)/shard_map/all_to_all | solution.py:95
  15.5 15.0 %collective-permute-start = (f32[32,1,128]{2,1,0:T(1,128)S(1)}, f32[32,1,128]{2,1,0:T(1,128)S(1)}, u32[]{:S(2)}, u32[]{:S(2)}) collective-permute-start(f32[32,1,128]{2,1,0:T(1,128)S(1)} %get-tuple-element.15), channel_id=1, source_target_pairs={{1,0},{2,1},{3,2},{4,3},{5,4},{6,5},{7,6},{8,7},{9,8},{10,9},{11,1... | collective-permute-start | bytes 49160 | tf_op jit(solution)/shard_map/ppermute | solution.py:15
  18.4 12.0 %collective-permute-start.1 = (f32[32,1,128]{2,1,0:T(1,128)S(1)}, f32[32,1,128]{2,1,0:T(1,128)S(1)}, u32[]{:S(2)}, u32[]{:S(2)}) collective-permute-start(f32[32,1,128]{2,1,0:T(1,128)S(1)} %get-tuple-element.16), channel_id=1, source_target_pairs={{0,1},{1,2},{2,3},{3,4},{4,5},{5,6},{6,7},{7,8},{8,9},{9,10},{10,1... | collective-permute-start | bytes 49160 | tf_op jit(solution)/shard_map/ppermute | solution.py:14
  22.9 1.0 copy-start.11
  34.3 29.9 %all-to-all-start = ((f32[32,64,256]{2,0,1:T(8,128)}), f32[32,64,256]{2,0,1:T(8,128)}, u32[]{:S(2)}, u32[]{:S(2)}) async-start(f32[32,64,256]{2,0,1:T(8,128)} %copy.121), calls=%async_computation | async-start | bytes 4194304 | tf_op jit(solution)/shard_map/all_to_all | solution.py:81
  69.0 1.0 copy-start.7
  70.0 1.2 copy-start.18
  110.3 2.6 %copy-start.2 = (f32[128,8,512]{2,1,0:T(8,128)}, f32[128,8,512]{2,1,0:T(8,128)S(1)}, u32[]{:S(2)}) copy-start(f32[128,8,512]{2,1,0:T(8,128)S(1)} %all_to_all.56) | copy-start | bytes 6291460
  110.5 1.2 copy-start.9
  111.6 2.2 copy-start.1
  113.8 7.2 %copy-start.16 = (f32[127,8,256]{2,1,0:T(8,128)}, f32[127,8,256]{2,1,0:T(8,128)S(1)}, u32[]{:S(2)}) copy-start(f32[127,8,256]{2,1,0:T(8,128)S(1)} %slice.208) | copy-start | bytes 3121156
  115.7 5.7 %collective-permute-start.2 = (f32[128,1,256]{2,1,0:T(1,128)S(1)}, f32[128,1,256]{2,1,0:T(1,128)S(1)}, u32[]{:S(2)}, u32[]{:S(2)}) collective-permute-start(f32[128,1,256]{2,1,0:T(1,128)S(1)} %get-tuple-element.13), channel_id=1, source_target_pairs={{16,0},{32,16},{48,32},{64,48},{80,64},{96,80},{112,96},{1,112},{1... | collective-permute-start | bytes 393224 | tf_op jit(solution)/shard_map/ppermute | solution.py:60
  118.7 8.4 %collective-permute-start.3 = (f32[128,1,256]{2,1,0:T(1,128)S(1)}, f32[128,1,256]{2,1,0:T(1,128)S(1)}, u32[]{:S(2)}, u32[]{:S(2)}) collective-permute-start(f32[128,1,256]{2,1,0:T(1,128)S(1)} %get-tuple-element.14), channel_id=1, source_target_pairs={{0,16},{16,32},{32,48},{48,64},{64,80},{80,96},{96,112},{112,1},{1... | collective-permute-start | bytes 393224 | tf_op jit(solution)/shard_map/ppermute | solution.py:59
  163.2 1.3 copy-start.3
  169.0 29.4 %all-to-all-start.4 = ((f32[128,8,256]{2,1,0:T(8,128)}), f32[128,8,256]{2,1,0:T(8,128)}, u32[]{:S(2)}, u32[]{:S(2)}) async-start(f32[128,8,256]{2,1,0:T(8,128)} %convolution_bitcast_fusion.1), calls=%async_computation.4 | async-start | bytes 2097152 | tf_op jit(solution)/shard_map/all_to_all | solution.py:105
  175.0 9.8 %copy-start.4 = (f32[128,8,512]{2,1,0:T(8,128)S(1)}, f32[128,8,512]{2,1,0:T(8,128)}, u32[]{:S(2)}) copy-start(f32[128,8,512]{2,1,0:T(8,128)} %copy-done.3) | copy-start | bytes 6291460
  176.6 8.5 %copy-start.17 = (f32[127,8,256]{2,1,0:T(8,128)}, f32[127,8,256]{2,1,0:T(8,128)S(1)}, u32[]{:S(2)}) copy-start(f32[127,8,256]{2,1,0:T(8,128)S(1)} %slice.217) | copy-start | bytes 3121156
  176.7 13.5 %collective-permute-start.4 = (f32[128,1,256]{2,1,0:T(1,128)S(1)}, f32[128,1,256]{2,1,0:T(1,128)S(1)}, u32[]{:S(2)}, u32[]{:S(2)}) collective-permute-start(f32[128,1,256]{2,1,0:T(1,128)S(1)} %get-tuple-element.11), channel_id=1, source_target_pairs={{16,0},{32,16},{48,32},{64,48},{80,64},{96,80},{112,96},{1,112},{1... | collective-permute-start | bytes 393224 | tf_op jit(solution)/shard_map/ppermute | solution.py:60
  182.6 12.6 %collective-permute-start.5 = (f32[128,1,256]{2,1,0:T(1,128)S(1)}, f32[128,1,256]{2,1,0:T(1,128)S(1)}, u32[]{:S(2)}, u32[]{:S(2)}) collective-permute-start(f32[128,1,256]{2,1,0:T(1,128)S(1)} %get-tuple-element.12), channel_id=1, source_target_pairs={{0,16},{16,32},{32,48},{48,64},{64,80},{80,96},{96,112},{112,1},{1... | collective-permute-start | bytes 393224 | tf_op jit(solution)/shard_map/ppermute | solution.py:59
  196.4 1.0 copy-start.15
  198.4 1.5 copy-start.8
  198.4 1.8 copy-start.10
  240.5 7.8 %copy-start.14 = (f32[32,64,128]{2,1,0:T(8,128)S(1)}, f32[32,64,128]{2,1,0:T(8,128)}, u32[]{:S(2)}) copy-start(f32[32,64,128]{2,1,0:T(8,128)} %param.6) | copy-start | bytes 3145732
  240.7 7.6 %copy-start.6 = (f32[32,64,128]{2,1,0:T(8,128)S(1)}, f32[32,64,128]{2,1,0:T(8,128)}, u32[]{:S(2)}) copy-start(f32[32,64,128]{2,1,0:T(8,128)} %param.5) | copy-start | bytes 3145732
  240.7 7.6 %copy-start.12 = (f32[32,64,127]{2,1,0:T(8,128)S(1)}, f32[32,64,127]{2,1,0:T(8,128)}, u32[]{:S(2)}) copy-start(f32[32,64,127]{2,1,0:T(8,128)} %copy-done.11) | copy-start | bytes 3121156
  241.1 9.1 %collective-permute-start.6 = (f32[32,1,128]{2,1,0:T(1,128)S(1)}, f32[32,1,128]{2,1,0:T(1,128)S(1)}, u32[]{:S(2)}, u32[]{:S(2)}) collective-permute-start(f32[32,1,128]{2,1,0:T(1,128)S(1)} %get-tuple-element.5), channel_id=1, source_target_pairs={{1,0},{2,1},{3,2},{4,3},{5,4},{6,5},{7,6},{8,7},{9,8},{10,9},{11,1... | collective-permute-start | bytes 49160 | tf_op jit(solution)/shard_map/ppermute | solution.py:15
  243.9 6.3 %collective-permute-start.7 = (f32[32,1,128]{2,1,0:T(1,128)S(1)}, f32[32,1,128]{2,1,0:T(1,128)S(1)}, u32[]{:S(2)}, u32[]{:S(2)}) collective-permute-start(f32[32,1,128]{2,1,0:T(1,128)S(1)} %get-tuple-element.6), channel_id=1, source_target_pairs={{0,1},{1,2},{2,3},{3,4},{4,5},{5,6},{6,7},{7,8},{8,9},{9,10},{10,1... | collective-permute-start | bytes 49160 | tf_op jit(solution)/shard_map/ppermute | solution.py:14

commit v9 on v7

--- a/solution.py
+++ b/solution.py
@@ -130,7 +130,7 @@
     ty = planes_to_y(tp, (initial.shape[0], initial.shape[1]))
     lam_second1_y = along_y(inv_y, ty, True)
     first0 = initial + RATE * (ydiff_block(initial) + zoperate_block(initial, conduct))
-    f0x, cx = block_to_x(first0, conduct)
+    f0x, cx = [rows(v) for v in block_to_x(first0, conduct)]
     half0 = along_x(f0x, inv_x, False)
     second0 = half0 + RATE * (xdiff(half0) + zoperate(half0, cx))
     count = lax.axis_size(LINES)

time: 253 us -> 253 us (level)
    unnamed x41 -> x42, local copies, waits for them, and re-layouts: 13.9 us -> 14.5 us
where the time goes in v9:
time: 253 us; the launch traced here: 252 us
  blocking collectives  105 us (42%)
  starting transfers between devices  49.6 us (20%)
  local copies, waits for them, and re-layouts  35.4 us (14%)
  waiting for transfers between devices  31.8 us (13%)
  matrix products  17.3 us (7%)
  other arithmetic  11.7 us (5%)
    all_to_all x2, blocking collectives, x_to_y(): lax.all_to_all(joined, LINES, split_axis=0, concat_axis=0, tiled=True)  74 us
    all_to_all x1, blocking collectives, x_to_block(): lax.all_to_all(joined, 'px', split_axis=0, concat_axis=1, tiled=True)  30.7 us
    unnamed x42, local copies, waits for them, and re-layouts  14.5 us
    all_to_all x1, starting transfers between devices, x_to_y(): lax.all_to_all(joined, LINES, split_axis=0, concat_axis=0, tiled=True)  11.5 us
    dot_general x3, matrix products, along_y(): return lax.dot_general(matrix, field, dims, precision=HIGH)  11.4 us
    ppermute x2, waiting for transfers between devices, ydiff(): lax.ppermute(jnp.concatenate([f[:, -1:] for f in fields]), ('px', 'py'), up)  10.7 us
    all_to_all x1, waiting for transfers between devices, block_to_x(): lax.all_to_all(joined, 'px', split_axis=1, concat_axis=0, tiled=True)  8.89 us
    ppermute x2, starting transfers between devices, ydiff(): lax.ppermute(jnp.concatenate([f[:, :1] for f in fields]), ('px', 'py'), d...  8.86 us
  transfers between devices with their start and end apart: 11, of which 7 were waited for; matrix products, arithmetic and copies ran while one was open for 11% of the time, Pallas kernels for 0%

profile of v9, /device:TPU:1, one launch (start us, length us, event | category | flops | bytes accessed | tf_op | source)
XLA Modules:
  0.0 251.7 jit_solution(17955555762730385222)
XLA Ops:
  0.6 1.9 copy.136
  3.9 11.5 %all-to-all-start.1 = ((f32[128,8,256]{2,1,0:T(8,128)}), f32[128,8,256]{2,1,0:T(8,128)S(1)}, u32[]{:S(2)}, u32[]{:S(2)}) async-start(f32[128,8,256]{2,1,0:T(8,128)} %copy.137), calls=%async_computation.1 | async-start | bytes 2097152 | tf_op jit(solution)/shard_map/all_to_all | solution.py:95
  15.5 3.0 %collective-permute-start = (f32[32,1,128]{2,1,0:T(1,128)S(1)}, f32[32,1,128]{2,1,0:T(1,128)S(1)}, u32[]{:S(2)}, u32[]{:S(2)}) collective-permute-start(f32[32,1,128]{2,1,0:T(1,128)S(1)} %get-tuple-element.15), channel_id=1, source_target_pairs={{1,0},{2,1},{3,2},{4,3},{5,4},{6,5},{7,6},{8,7},{9,8},{10,9},{11,1... | collective-permute-start | bytes 49160 | tf_op jit(solution)/shard_map/ppermute | solution.py:15
  18.4 4.1 %collective-permute-start.1 = (f32[32,1,128]{2,1,0:T(1,128)S(1)}, f32[32,1,128]{2,1,0:T(1,128)S(1)}, u32[]{:S(2)}, u32[]{:S(2)}) collective-permute-start(f32[32,1,128]{2,1,0:T(1,128)S(1)} %get-tuple-element.16), channel_id=1, source_target_pairs={{0,1},{1,2},{2,3},{3,4},{4,5},{5,6},{6,7},{7,8},{8,9},{9,10},{10,1... | collective-permute-start | bytes 49160 | tf_op jit(solution)/shard_map/ppermute | solution.py:14
  23.9 6.6 %collective-permute-done = f32[32,1,128]{2,1,0:T(1,128)S(1)} collective-permute-done((f32[32,1,128]{2,1,0:T(1,128)S(1)}, f32[32,1,128]{2,1,0:T(1,128)S(1)}, u32[]{:S(2)}, u32[]{:S(2)}) %collective-permute-start) | collective-permute-done | bytes 16416 | tf_op jit(solution)/shard_map/ppermute | solution.py:15
  31.2 2.6 %copy.124 = f32[32,64,256]{2,0,1:T(8,128)} copy(f32[32,64,256]{2,1,0:T(8,128)S(1)} %pad_maximum_fusion) | data formatting | bytes 4194304 | tf_op jit(solution)/shard_map/concatenate | solution.py:80
  34.3 4.5 %all-to-all-start = ((f32[32,64,256]{2,0,1:T(8,128)}), f32[32,64,256]{2,0,1:T(8,128)}, u32[]{:S(2)}, u32[]{:S(2)}) async-start(f32[32,64,256]{2,0,1:T(8,128)} %copy.124), calls=%async_computation | async-start | bytes 4194304 | tf_op jit(solution)/shard_map/all_to_all | solution.py:81
  38.9 5.4 %copy.135 = f32[1024,1024]{0,1:T(8,128)} copy(f32[1024,1024]{1,0:T(8,128)} %param.9) | data formatting | bytes 8388608 | tf_op args[4]
  44.2 2.5 reshape_reshape.3
  46.8 3.0 %copy.138 = f32[16,64,8,32]{1,0,3,2:T(8,128)S(1)} copy(f32[16,64,8,32]{3,1,2,0:T(8,128)} %bitcast.90) | data formatting | bytes 2097152 | tf_op jit(solution)/shard_map/transpose | solution.py:121
  50.3 5.0 %fusion = f32[128,8,256]{2,1,0:T(8,128)} fusion(f32[1024,1024]{0,1:T(8,128)} %copy.135, f32[1024,256]{0,1:T(8,128)S(1)} %reshape.31), kind=kOutput, calls=%fused_computation | convolution fusion | flops 1610612736 | bytes 6291456 | tf_op jit(solution)/shard_map/dot_general | solution.py:76
  55.3 8.9 %all-to-all-done = f32[32,64,256]{2,0,1:T(8,128)} async-done(((f32[32,64,256]{2,0,1:T(8,128)}), f32[32,64,256]{2,0,1:T(8,128)}, u32[]{:S(2)}, u32[]{:S(2)}) %all-to-all-start) | async-done | bytes 2097184 | tf_op jit(solution)/shard_map/all_to_all | solution.py:81
  64.2 2.8 %copy.126 = f32[8,32,8,256]{3,2,1,0:T(8,128)S(1)} copy(f32[8,32,8,256]{3,1,2,0:T(8,128)} %bitcast.2) | data formatting | bytes 4194304 | tf_op jit(solution)/shard_map/all_to_all | solution.py:81
  71.5 38.7 %all_to_all.56 = f32[128,8,512]{2,1,0:T(8,128)S(1)} all-to-all(f32[128,8,512]{2,1,0:T(8,128)S(1)} %pad_maximum_fusion.1), channel_id=1, replica_groups=mesh['px'=8,'py'=16] {'py','px'}, dimensions={0} | all-to-all | bytes 4194304 | tf_op jit(solution)/shard_map/all_to_all | solution.py:95
  113.8 1.9 convolution_bitcast_fusion.2
  115.7 3.0 %collective-permute-start.2 = (f32[128,1,256]{2,1,0:T(1,128)S(1)}, f32[128,1,256]{2,1,0:T(1,128)S(1)}, u32[]{:S(2)}, u32[]{:S(2)}) collective-permute-start(f32[128,1,256]{2,1,0:T(1,128)S(1)} %get-tuple-element.13), channel_id=1, source_target_pairs={{16,0},{32,16},{48,32},{64,48},{80,64},{96,80},{112,96},{1,112},{1... | collective-permute-start | bytes 393224 | tf_op jit(solution)/shard_map/ppermute | solution.py:60
  118.7 2.3 collective-permute-start.3
  121.4 5.7 %collective-permute-done.3 = f32[128,1,256]{2,1,0:T(1,128)S(1)} collective-permute-done((f32[128,1,256]{2,1,0:T(1,128)S(1)}, f32[128,1,256]{2,1,0:T(1,128)S(1)}, u32[]{:S(2)}, u32[]{:S(2)}) %collective-permute-start.3) | collective-permute-done | bytes 131104 | tf_op jit(solution)/shard_map/ppermute | solution.py:59
  128.0 35.2 %all_to_all.57 = f32[128,8,512]{2,1,0:T(8,128)S(1)} all-to-all(f32[128,8,512]{2,1,0:T(8,128)S(1)} %pad_maximum_fusion.2), channel_id=1, replica_groups=mesh['px'=8,'py'=16] {'py','px'}, dimensions={0} | all-to-all | bytes 4194304 | tf_op jit(solution)/shard_map/all_to_all | solution.py:95
  164.5 4.5 %convolution_bitcast_fusion.1 = f32[128,8,256]{2,1,0:T(8,128)} fusion(f32[1024,1024]{1,0:T(8,128)S(1)} %copy-done.1, f32[1024,512]{1,0:T(8,128)S(1)} %bitcast.86), kind=kOutput, calls=%fused_computation.14 | convolution fusion | flops 1610612736 | bytes 6291456 | tf_op jit(solution)/shard_map/dot_general | solution.py:76
  169.0 6.0 %all-to-all-start.4 = ((f32[128,8,256]{2,1,0:T(8,128)}), f32[128,8,256]{2,1,0:T(8,128)}, u32[]{:S(2)}, u32[]{:S(2)}) async-start(f32[128,8,256]{2,1,0:T(8,128)} %convolution_bitcast_fusion.1), calls=%async_computation.4 | async-start | bytes 2097152 | tf_op jit(solution)/shard_map/all_to_all | solution.py:105
  176.7 5.9 %collective-permute-start.4 = (f32[128,1,256]{2,1,0:T(1,128)S(1)}, f32[128,1,256]{2,1,0:T(1,128)S(1)}, u32[]{:S(2)}, u32[]{:S(2)}) collective-permute-start(f32[128,1,256]{2,1,0:T(1,128)S(1)} %get-tuple-element.11), channel_id=1, source_target_pairs={{16,0},{32,16},{48,32},{64,48},{80,64},{96,80},{112,96},{1,112},{1... | collective-permute-start | bytes 393224 | tf_op jit(solution)/shard_map/ppermute | solution.py:60
  182.6 2.2 collective-permute-start.5
  185.2 5.0 %collective-permute-done.4 = f32[128,1,256]{2,1,0:T(1,128)S(1)} collective-permute-done((f32[128,1,256]{2,1,0:T(1,128)S(1)}, f32[128,1,256]{2,1,0:T(1,128)S(1)}, u32[]{:S(2)}, u32[]{:S(2)}) %collective-permute-start.4) | collective-permute-done | bytes 131104 | tf_op jit(solution)/shard_map/ppermute | solution.py:60
  190.2 5.0 %collective-permute-done.5 = f32[128,1,256]{2,1,0:T(1,128)S(1)} collective-permute-done((f32[128,1,256]{2,1,0:T(1,128)S(1)}, f32[128,1,256]{2,1,0:T(1,128)S(1)}, u32[]{:S(2)}, u32[]{:S(2)}) %collective-permute-start.5) | collective-permute-done | bytes 131104 | tf_op jit(solution)/shard_map/ppermute | solution.py:59
  200.2 4.1 %bitcast_multiply_fusion = (f32[128,8,256]{2,1,0:T(8,128)S(1)}, f32[256,8,128]{0,1,2:T(8,128)S(1)}) fusion(f32[256,8,128]{0,1,2:T(8,128)S(1)} %copy.168, f32[128,8,256]{2,1,0:T(8,128)} %all-to-all-done.4, f32[127,8,256]{2,1,0:T(8,128)S(1)} %slice.212, f32[128,8,256]{2,1,0:T(8,128)S(1)} %fusion.47, f32[127,8,256]{2,1,0:T(8,128)S(1)} %copy-done.8, ...), kind=kLoop, calls=%fused_computation.69 | loop fusion | flops 3932160 | bytes 15679488 | tf_op jit(solution)/shard_map/mul | solution.py:38
  204.4 3.2 %convolution_bitcast_fusion = f32[256,8,128]{0,1,2:T(8,128)S(1)} fusion(f32[128,8,256]{2,1,0:T(8,128)} %all-to-all-done.4, f32[127,8,256]{2,1,0:T(8,128)S(1)} %slice.213, f32[256,8,128]{0,1,2:T(8,128)S(1)} %copy.168, f32[127,8,256]{2,1,0:T(8,128)S(1)} %slice.212, f32[256,256]{1,0:T(8,128)S(1)} %copy-done), kind=kOutput, calls=%fused_computation.13 | convolution fusion | flops 405012480 | bytes 5488640 | tf_op jit(solution)/shard_map/dot_general | solution.py:71
  207.7 2.0 copy.154
  209.8 30.7 %all_to_all.58 = f32[256,8,256]{2,1,0:T(8,128)S(1)} all-to-all(f32[256,8,256]{2,1,0:T(8,128)} %copy.154), channel_id=1, replica_groups=mesh['px'=8,'py'=16] {'px'}, dimensions={0} | all-to-all | bytes 4194304 | tf_op jit(solution)/shard_map/all_to_all | solution.py:88
  241.1 2.8 %collective-permute-start.6 = (f32[32,1,128]{2,1,0:T(1,128)S(1)}, f32[32,1,128]{2,1,0:T(1,128)S(1)}, u32[]{:S(2)}, u32[]{:S(2)}) collective-permute-start(f32[32,1,128]{2,1,0:T(1,128)S(1)} %get-tuple-element.5), channel_id=1, source_target_pairs={{1,0},{2,1},{3,2},{4,3},{5,4},{6,5},{7,6},{8,7},{9,8},{10,9},{11,1... | collective-permute-start | bytes 49160 | tf_op jit(solution)/shard_map/ppermute | solution.py:15
  243.9 4.4 %collective-permute-start.7 = (f32[32,1,128]{2,1,0:T(1,128)S(1)}, f32[32,1,128]{2,1,0:T(1,128)S(1)}, u32[]{:S(2)}, u32[]{:S(2)}) collective-permute-start(f32[32,1,128]{2,1,0:T(1,128)S(1)} %get-tuple-element.6), channel_id=1, source_target_pairs={{0,1},{1,2},{2,3},{3,4},{4,5},{5,6},{6,7},{7,8},{8,9},{9,10},{10,1... | collective-permute-start | bytes 49160 | tf_op jit(solution)/shard_map/ppermute | solution.py:14
  248.3 1.8 slice_subtract_fusion
  (85 shorter events, 24.4 us)
Async XLA Ops:
  0.6 67.7 %copy-start = (f32[256,256]{1,0:T(8,128)S(1)}, f32[256,256]{1,0:T(8,128)}, u32[]{:S(2)}) copy-start(f32[256,256]{1,0:T(8,128)} %param.8) | copy-start | bytes 786436
  2.5 12.9 %copy-start.5 = (f32[32,64,128]{2,1,0:T(8,128)S(1)}, f32[32,64,128]{2,1,0:T(8,128)}, u32[]{:S(2)}) copy-start(f32[32,64,128]{2,1,0:T(8,128)} %param.5) | copy-start | bytes 3145732
  3.9 19.0 %copy-start.13 = (f32[32,64,128]{2,1,0:T(8,128)S(1)}, f32[32,64,128]{2,1,0:T(8,128)}, u32[]{:S(2)}) copy-start(f32[32,64,128]{2,1,0:T(8,128)} %param.6) | copy-start | bytes 3145732
  3.9 30.4 %all-to-all-start.1 = ((f32[128,8,256]{2,1,0:T(8,128)}), f32[128,8,256]{2,1,0:T(8,128)S(1)}, u32[]{:S(2)}, u32[]{:S(2)}) async-start(f32[128,8,256]{2,1,0:T(8,128)} %copy.137), calls=%async_computation.1 | async-start | bytes 2097152 | tf_op jit(solution)/shard_map/all_to_all | solution.py:95
  15.5 15.0 %collective-permute-start = (f32[32,1,128]{2,1,0:T(1,128)S(1)}, f32[32,1,128]{2,1,0:T(1,128)S(1)}, u32[]{:S(2)}, u32[]{:S(2)}) collective-permute-start(f32[32,1,128]{2,1,0:T(1,128)S(1)} %get-tuple-element.15), channel_id=1, source_target_pairs={{1,0},{2,1},{3,2},{4,3},{5,4},{6,5},{7,6},{8,7},{9,8},{10,9},{11,1... | collective-permute-start | bytes 49160 | tf_op jit(solution)/shard_map/ppermute | solution.py:15
  18.4 12.0 %collective-permute-start.1 = (f32[32,1,128]{2,1,0:T(1,128)S(1)}, f32[32,1,128]{2,1,0:T(1,128)S(1)}, u32[]{:S(2)}, u32[]{:S(2)}) collective-permute-start(f32[32,1,128]{2,1,0:T(1,128)S(1)} %get-tuple-element.16), channel_id=1, source_target_pairs={{0,1},{1,2},{2,3},{3,4},{4,5},{5,6},{6,7},{7,8},{8,9},{9,10},{10,1... | collective-permute-start | bytes 49160 | tf_op jit(solution)/shard_map/ppermute | solution.py:14
  22.9 1.0 copy-start.11
  34.3 29.9 %all-to-all-start = ((f32[32,64,256]{2,0,1:T(8,128)}), f32[32,64,256]{2,0,1:T(8,128)}, u32[]{:S(2)}, u32[]{:S(2)}) async-start(f32[32,64,256]{2,0,1:T(8,128)} %copy.124), calls=%async_computation | async-start | bytes 4194304 | tf_op jit(solution)/shard_map/all_to_all | solution.py:81
  69.0 1.0 copy-start.7
  70.0 1.2 copy-start.18
  110.3 2.6 %copy-start.2 = (f32[128,8,512]{2,1,0:T(8,128)}, f32[128,8,512]{2,1,0:T(8,128)S(1)}, u32[]{:S(2)}) copy-start(f32[128,8,512]{2,1,0:T(8,128)S(1)} %all_to_all.56) | copy-start | bytes 6291460
  110.5 1.2 copy-start.9
  111.6 2.2 copy-start.1
  113.8 7.2 %copy-start.16 = (f32[127,8,256]{2,1,0:T(8,128)}, f32[127,8,256]{2,1,0:T(8,128)S(1)}, u32[]{:S(2)}) copy-start(f32[127,8,256]{2,1,0:T(8,128)S(1)} %slice.208) | copy-start | bytes 3121156
  115.7 5.7 %collective-permute-start.2 = (f32[128,1,256]{2,1,0:T(1,128)S(1)}, f32[128,1,256]{2,1,0:T(1,128)S(1)}, u32[]{:S(2)}, u32[]{:S(2)}) collective-permute-start(f32[128,1,256]{2,1,0:T(1,128)S(1)} %get-tuple-element.13), channel_id=1, source_target_pairs={{16,0},{32,16},{48,32},{64,48},{80,64},{96,80},{112,96},{1,112},{1... | collective-permute-start | bytes 393224 | tf_op jit(solution)/shard_map/ppermute | solution.py:60
  118.7 8.4 %collective-permute-start.3 = (f32[128,1,256]{2,1,0:T(1,128)S(1)}, f32[128,1,256]{2,1,0:T(1,128)S(1)}, u32[]{:S(2)}, u32[]{:S(2)}) collective-permute-start(f32[128,1,256]{2,1,0:T(1,128)S(1)} %get-tuple-element.14), channel_id=1, source_target_pairs={{0,16},{16,32},{32,48},{48,64},{64,80},{80,96},{96,112},{112,1},{1... | collective-permute-start | bytes 393224 | tf_op jit(solution)/shard_map/ppermute | solution.py:59
  163.2 1.3 copy-start.3
  169.0 29.4 %all-to-all-start.4 = ((f32[128,8,256]{2,1,0:T(8,128)}), f32[128,8,256]{2,1,0:T(8,128)}, u32[]{:S(2)}, u32[]{:S(2)}) async-start(f32[128,8,256]{2,1,0:T(8,128)} %convolution_bitcast_fusion.1), calls=%async_computation.4 | async-start | bytes 2097152 | tf_op jit(solution)/shard_map/all_to_all | solution.py:105
  175.0 9.8 %copy-start.4 = (f32[128,8,512]{2,1,0:T(8,128)S(1)}, f32[128,8,512]{2,1,0:T(8,128)}, u32[]{:S(2)}) copy-start(f32[128,8,512]{2,1,0:T(8,128)} %copy-done.3) | copy-start | bytes 6291460
  176.6 8.5 %copy-start.17 = (f32[127,8,256]{2,1,0:T(8,128)}, f32[127,8,256]{2,1,0:T(8,128)S(1)}, u32[]{:S(2)}) copy-start(f32[127,8,256]{2,1,0:T(8,128)S(1)} %slice.217) | copy-start | bytes 3121156
  176.7 13.5 %collective-permute-start.4 = (f32[128,1,256]{2,1,0:T(1,128)S(1)}, f32[128,1,256]{2,1,0:T(1,128)S(1)}, u32[]{:S(2)}, u32[]{:S(2)}) collective-permute-start(f32[128,1,256]{2,1,0:T(1,128)S(1)} %get-tuple-element.11), channel_id=1, source_target_pairs={{16,0},{32,16},{48,32},{64,48},{80,64},{96,80},{112,96},{1,112},{1... | collective-permute-start | bytes 393224 | tf_op jit(solution)/shard_map/ppermute | solution.py:60
  182.6 12.6 %collective-permute-start.5 = (f32[128,1,256]{2,1,0:T(1,128)S(1)}, f32[128,1,256]{2,1,0:T(1,128)S(1)}, u32[]{:S(2)}, u32[]{:S(2)}) collective-permute-start(f32[128,1,256]{2,1,0:T(1,128)S(1)} %get-tuple-element.12), channel_id=1, source_target_pairs={{0,16},{16,32},{32,48},{48,64},{64,80},{80,96},{96,112},{112,1},{1... | collective-permute-start | bytes 393224 | tf_op jit(solution)/shard_map/ppermute | solution.py:59
  196.4 1.0 copy-start.15
  198.4 1.5 copy-start.8
  198.4 1.8 copy-start.10
  240.5 7.8 %copy-start.14 = (f32[32,64,128]{2,1,0:T(8,128)S(1)}, f32[32,64,128]{2,1,0:T(8,128)}, u32[]{:S(2)}) copy-start(f32[32,64,128]{2,1,0:T(8,128)} %param.6) | copy-start | bytes 3145732
  240.7 7.6 %copy-start.6 = (f32[32,64,128]{2,1,0:T(8,128)S(1)}, f32[32,64,128]{2,1,0:T(8,128)}, u32[]{:S(2)}) copy-start(f32[32,64,128]{2,1,0:T(8,128)} %param.5) | copy-start | bytes 3145732
  240.7 7.6 %copy-start.12 = (f32[32,64,127]{2,1,0:T(8,128)S(1)}, f32[32,64,127]{2,1,0:T(8,128)}, u32[]{:S(2)}) copy-start(f32[32,64,127]{2,1,0:T(8,128)} %copy-done.11) | copy-start | bytes 3121156
  241.1 9.1 %collective-permute-start.6 = (f32[32,1,128]{2,1,0:T(1,128)S(1)}, f32[32,1,128]{2,1,0:T(1,128)S(1)}, u32[]{:S(2)}, u32[]{:S(2)}) collective-permute-start(f32[32,1,128]{2,1,0:T(1,128)S(1)} %get-tuple-element.5), channel_id=1, source_target_pairs={{1,0},{2,1},{3,2},{4,3},{5,4},{6,5},{7,6},{8,7},{9,8},{10,9},{11,1... | collective-permute-start | bytes 49160 | tf_op jit(solution)/shard_map/ppermute | solution.py:15
  243.9 6.3 %collective-permute-start.7 = (f32[32,1,128]{2,1,0:T(1,128)S(1)}, f32[32,1,128]{2,1,0:T(1,128)S(1)}, u32[]{:S(2)}, u32[]{:S(2)}) collective-permute-start(f32[32,1,128]{2,1,0:T(1,128)S(1)} %get-tuple-element.6), channel_id=1, source_target_pairs={{0,1},{1,2},{2,3},{3,4},{4,5},{5,6},{6,7},{7,8},{8,9},{9,10},{10,1... | collective-permute-start | bytes 49160 | tf_op jit(solution)/shard_map/ppermute | solution.py:14

commit v10 on v7

--- a/solution.py
+++ b/solution.py
@@ -109,7 +109,7 @@
 
 def block_planes(field):
     count = lax.axis_size(LINES)
-    planes = jnp.transpose(field, (2, 1, 0))
+    planes = jnp.transpose(field, (2, 0, 1))
     return planes.reshape(count, -1, field.shape[0] * field.shape[1] * field.shape[2] // count // 8)
 
 
@@ -117,8 +117,8 @@
     rows = lax.axis_size("px")
     cols = lax.axis_size("py")
     depth, width = block[0], block[1]
-    tiles = pieces.reshape(cols, rows, width, depth)
-    return jnp.transpose(tiles, (0, 2, 1, 3)).reshape(cols * width, rows * depth)
+    tiles = pieces.reshape(cols, rows, depth, width)
+    return jnp.transpose(tiles, (0, 3, 1, 2)).reshape(cols * width, rows * depth)
 
 
 def rows(field):

time: 253 us -> 250 us (0.988)
    unnamed x41 -> x40, local copies, waits for them, and re-layouts: 13.9 us -> 12.4 us
where the time goes in v10:
time: 250 us; the launch traced here: 249 us
  blocking collectives  105 us (42%)
  starting transfers between devices  48.9 us (20%)
  local copies, waits for them, and re-layouts  35.5 us (14%)
  waiting for transfers between devices  29.5 us (12%)
  matrix products  17.3 us (7%)
  other arithmetic  11.7 us (5%)
    all_to_all x2, blocking collectives, x_to_y(): lax.all_to_all(joined, LINES, split_axis=0, concat_axis=0, tiled=True)  74.7 us
    all_to_all x1, blocking collectives, x_to_block(): lax.all_to_all(joined, 'px', split_axis=0, concat_axis=1, tiled=True)  30.7 us
    unnamed x40, local copies, waits for them, and re-layouts  12.4 us
    all_to_all x1, starting transfers between devices, x_to_y(): lax.all_to_all(joined, LINES, split_axis=0, concat_axis=0, tiled=True)  11.5 us
    dot_general x3, matrix products, along_y(): return lax.dot_general(matrix, field, dims, precision=HIGH)  11.4 us
    ppermute x2, waiting for transfers between devices, ydiff(): lax.ppermute(jnp.concatenate([f[:, -1:] for f in fields]), ('px', 'py'), up)  10.7 us
    ppermute x2, starting transfers between devices, ydiff(): lax.ppermute(jnp.concatenate([f[:, :1] for f in fields]), ('px', 'py'), d...  8.86 us
    ppermute x2, starting transfers between devices, ydiff_block(): lax.ppermute(field[:, -1:], 'py', [(i, i + 1) for i in range(count - 1)])  8.53 us
  transfers between devices with their start and end apart: 11, of which 7 were waited for; matrix products, arithmetic and copies ran while one was open for 11% of the time, Pallas kernels for 0%

profile of v10, /device:TPU:1, one launch (start us, length us, event | category | flops | bytes accessed | tf_op | source)
XLA Modules:
  0.0 249.5 jit_solution(4912618870930267132)
XLA Ops:
  0.7 2.7 %copy.129 = f32[128,8,256]{2,1,0:T(8,128)} copy(f32[128,8,256]{0,2,1:T(8,128)} %bitcast.100) | data formatting | bytes 2097152 | tf_op jit(solution)/shard_map/reshape | solution.py:113
  3.4 11.5 %all-to-all-start.1 = ((f32[128,8,256]{2,1,0:T(8,128)}), f32[128,8,256]{2,1,0:T(8,128)S(1)}, u32[]{:S(2)}, u32[]{:S(2)}) async-start(f32[128,8,256]{2,1,0:T(8,128)} %copy.129), calls=%async_computation.1 | async-start | bytes 2097152 | tf_op jit(solution)/shard_map/all_to_all | solution.py:95
  14.9 3.0 %collective-permute-start = (f32[32,1,128]{2,1,0:T(1,128)S(1)}, f32[32,1,128]{2,1,0:T(1,128)S(1)}, u32[]{:S(2)}, u32[]{:S(2)}) collective-permute-start(f32[32,1,128]{2,1,0:T(1,128)S(1)} %get-tuple-element.15), channel_id=1, source_target_pairs={{1,0},{2,1},{3,2},{4,3},{5,4},{6,5},{7,6},{8,7},{9,8},{10,9},{11,1... | collective-permute-start | bytes 49160 | tf_op jit(solution)/shard_map/ppermute | solution.py:15
  17.9 4.1 %collective-permute-start.1 = (f32[32,1,128]{2,1,0:T(1,128)S(1)}, f32[32,1,128]{2,1,0:T(1,128)S(1)}, u32[]{:S(2)}, u32[]{:S(2)}) collective-permute-start(f32[32,1,128]{2,1,0:T(1,128)S(1)} %get-tuple-element.16), channel_id=1, source_target_pairs={{0,1},{1,2},{2,3},{3,4},{4,5},{5,6},{6,7},{7,8},{8,9},{9,10},{10,1... | collective-permute-start | bytes 49160 | tf_op jit(solution)/shard_map/ppermute | solution.py:14
  23.6 6.3 %collective-permute-done = f32[32,1,128]{2,1,0:T(1,128)S(1)} collective-permute-done((f32[32,1,128]{2,1,0:T(1,128)S(1)}, f32[32,1,128]{2,1,0:T(1,128)S(1)}, u32[]{:S(2)}, u32[]{:S(2)}) %collective-permute-start) | collective-permute-done | bytes 16416 | tf_op jit(solution)/shard_map/ppermute | solution.py:15
  30.7 2.6 %copy.118 = f32[32,64,256]{2,0,1:T(8,128)} copy(f32[32,64,256]{2,1,0:T(8,128)S(1)} %pad_maximum_fusion) | data formatting | bytes 4194304 | tf_op jit(solution)/shard_map/concatenate | solution.py:80
  33.8 3.8 %all-to-all-start = ((f32[32,64,256]{2,0,1:T(8,128)}), f32[32,64,256]{2,0,1:T(8,128)S(1)}, u32[]{:S(2)}, u32[]{:S(2)}) async-start(f32[32,64,256]{2,0,1:T(8,128)} %copy.118), calls=%async_computation | async-start | bytes 4194304 | tf_op jit(solution)/shard_map/all_to_all | solution.py:81
  37.6 5.4 %copy.128 = f32[1024,1024]{0,1:T(8,128)} copy(f32[1024,1024]{1,0:T(8,128)} %param.9) | data formatting | bytes 8388608 | tf_op args[4]
  42.9 1.7 reshape_reshape.3
  44.7 4.2 %copy.130 = f32[16,64,8,32]{1,0,3,2:T(8,128)} copy(f32[16,64,8,32]{1,3,2,0:T(8,128)} %bitcast.98) | data formatting | bytes 2097152 | tf_op jit(solution)/shard_map/transpose | solution.py:121
  48.8 2.0 reshape.31
  50.8 5.0 %fusion = f32[128,8,256]{2,1,0:T(8,128)} fusion(f32[1024,1024]{0,1:T(8,128)} %copy.128, f32[1024,256]{0,1:T(8,128)S(1)} %reshape.31), kind=kOutput, calls=%fused_computation | convolution fusion | flops 1610612736 | bytes 6291456 | tf_op jit(solution)/shard_map/dot_general | solution.py:76
  55.8 7.0 %all-to-all-done = f32[32,64,256]{2,0,1:T(8,128)S(1)} async-done(((f32[32,64,256]{2,0,1:T(8,128)}), f32[32,64,256]{2,0,1:T(8,128)S(1)}, u32[]{:S(2)}, u32[]{:S(2)}) %all-to-all-start) | async-done | bytes 2097184 | tf_op jit(solution)/shard_map/all_to_all | solution.py:81
  68.5 39.5 %all_to_all.56 = f32[128,8,512]{2,1,0:T(8,128)S(1)} all-to-all(f32[128,8,512]{2,1,0:T(8,128)S(1)} %pad_maximum_fusion.1), channel_id=1, replica_groups=mesh['px'=8,'py'=16] {'py','px'}, dimensions={0} | all-to-all | bytes 4194304 | tf_op jit(solution)/shard_map/all_to_all | solution.py:95
  111.6 1.9 convolution_bitcast_fusion.2
  113.5 3.0 %collective-permute-start.2 = (f32[128,1,256]{2,1,0:T(1,128)S(1)}, f32[128,1,256]{2,1,0:T(1,128)S(1)}, u32[]{:S(2)}, u32[]{:S(2)}) collective-permute-start(f32[128,1,256]{2,1,0:T(1,128)S(1)} %get-tuple-element.13), channel_id=1, source_target_pairs={{16,0},{32,16},{48,32},{64,48},{80,64},{96,80},{112,96},{1,112},{1... | collective-permute-start | bytes 393224 | tf_op jit(solution)/shard_map/ppermute | solution.py:60
  116.5 2.3 collective-permute-start.3
  119.2 5.7 %collective-permute-done.3 = f32[128,1,256]{2,1,0:T(1,128)S(1)} collective-permute-done((f32[128,1,256]{2,1,0:T(1,128)S(1)}, f32[128,1,256]{2,1,0:T(1,128)S(1)}, u32[]{:S(2)}, u32[]{:S(2)}) %collective-permute-start.3) | collective-permute-done | bytes 131104 | tf_op jit(solution)/shard_map/ppermute | solution.py:59
  125.8 35.2 %all_to_all.57 = f32[128,8,512]{2,1,0:T(8,128)S(1)} all-to-all(f32[128,8,512]{2,1,0:T(8,128)S(1)} %pad_maximum_fusion.2), channel_id=1, replica_groups=mesh['px'=8,'py'=16] {'py','px'}, dimensions={0} | all-to-all | bytes 4194304 | tf_op jit(solution)/shard_map/all_to_all | solution.py:95
  162.3 4.5 %convolution_bitcast_fusion.1 = f32[128,8,256]{2,1,0:T(8,128)} fusion(f32[1024,1024]{1,0:T(8,128)S(1)} %copy-done.1, f32[1024,512]{1,0:T(8,128)S(1)} %bitcast.87), kind=kOutput, calls=%fused_computation.14 | convolution fusion | flops 1610612736 | bytes 6291456 | tf_op jit(solution)/shard_map/dot_general | solution.py:76
  166.8 6.0 %all-to-all-start.4 = ((f32[128,8,256]{2,1,0:T(8,128)}), f32[128,8,256]{2,1,0:T(8,128)}, u32[]{:S(2)}, u32[]{:S(2)}) async-start(f32[128,8,256]{2,1,0:T(8,128)} %convolution_bitcast_fusion.1), calls=%async_computation.4 | async-start | bytes 2097152 | tf_op jit(solution)/shard_map/all_to_all | solution.py:105
  174.5 5.9 %collective-permute-start.4 = (f32[128,1,256]{2,1,0:T(1,128)S(1)}, f32[128,1,256]{2,1,0:T(1,128)S(1)}, u32[]{:S(2)}, u32[]{:S(2)}) collective-permute-start(f32[128,1,256]{2,1,0:T(1,128)S(1)} %get-tuple-element.11), channel_id=1, source_target_pairs={{16,0},{32,16},{48,32},{64,48},{80,64},{96,80},{112,96},{1,112},{1... | collective-permute-start | bytes 393224 | tf_op jit(solution)/shard_map/ppermute | solution.py:60
  180.4 2.2 collective-permute-start.5
  182.9 5.0 %collective-permute-done.4 = f32[128,1,256]{2,1,0:T(1,128)S(1)} collective-permute-done((f32[128,1,256]{2,1,0:T(1,128)S(1)}, f32[128,1,256]{2,1,0:T(1,128)S(1)}, u32[]{:S(2)}, u32[]{:S(2)}) %collective-permute-start.4) | collective-permute-done | bytes 131104 | tf_op jit(solution)/shard_map/ppermute | solution.py:60
  188.0 5.0 %collective-permute-done.5 = f32[128,1,256]{2,1,0:T(1,128)S(1)} collective-permute-done((f32[128,1,256]{2,1,0:T(1,128)S(1)}, f32[128,1,256]{2,1,0:T(1,128)S(1)}, u32[]{:S(2)}, u32[]{:S(2)}) %collective-permute-start.5) | collective-permute-done | bytes 131104 | tf_op jit(solution)/shard_map/ppermute | solution.py:59
  198.0 4.1 %bitcast_multiply_fusion.1 = (f32[128,8,256]{2,1,0:T(8,128)S(1)}, f32[256,8,128]{0,1,2:T(8,128)S(1)}) fusion(f32[256,8,128]{0,1,2:T(8,128)S(1)} %copy.160, f32[128,8,256]{2,1,0:T(8,128)} %all-to-all-done.4, f32[127,8,256]{2,1,0:T(8,128)S(1)} %slice.212, f32[128,8,256]{2,1,0:T(8,128)S(1)} %fusion.67, f32[127,8,256]{2,1,0:T(8,128)S(1)} %copy-done.8, ...), kind=kLoop, calls=%fused_computation.71 | loop fusion | flops 3932160 | bytes 15679488 | tf_op jit(solution)/shard_map/mul | solution.py:38
  202.2 3.2 %convolution_bitcast_fusion = f32[256,8,128]{0,1,2:T(8,128)S(1)} fusion(f32[128,8,256]{2,1,0:T(8,128)} %all-to-all-done.4, f32[127,8,256]{2,1,0:T(8,128)S(1)} %slice.213, f32[256,8,128]{0,1,2:T(8,128)S(1)} %copy.160, f32[127,8,256]{2,1,0:T(8,128)S(1)} %slice.212, f32[256,256]{1,0:T(8,128)S(1)} %copy-done), kind=kOutput, calls=%fused_computation.13 | convolution fusion | flops 405012480 | bytes 5488640 | tf_op jit(solution)/shard_map/dot_general | solution.py:71
  205.5 2.0 copy.146
  207.6 30.7 %all_to_all.58 = f32[256,8,256]{2,1,0:T(8,128)S(1)} all-to-all(f32[256,8,256]{2,1,0:T(8,128)} %copy.146), channel_id=1, replica_groups=mesh['px'=8,'py'=16] {'px'}, dimensions={0} | all-to-all | bytes 4194304 | tf_op jit(solution)/shard_map/all_to_all | solution.py:88
  238.9 2.8 %collective-permute-start.6 = (f32[32,1,128]{2,1,0:T(1,128)S(1)}, f32[32,1,128]{2,1,0:T(1,128)S(1)}, u32[]{:S(2)}, u32[]{:S(2)}) collective-permute-start(f32[32,1,128]{2,1,0:T(1,128)S(1)} %get-tuple-element.5), channel_id=1, source_target_pairs={{1,0},{2,1},{3,2},{4,3},{5,4},{6,5},{7,6},{8,7},{9,8},{10,9},{11,1... | collective-permute-start | bytes 49160 | tf_op jit(solution)/shard_map/ppermute | solution.py:15
  241.6 4.4 %collective-permute-start.7 = (f32[32,1,128]{2,1,0:T(1,128)S(1)}, f32[32,1,128]{2,1,0:T(1,128)S(1)}, u32[]{:S(2)}, u32[]{:S(2)}) collective-permute-start(f32[32,1,128]{2,1,0:T(1,128)S(1)} %get-tuple-element.6), channel_id=1, source_target_pairs={{0,1},{1,2},{2,3},{3,4},{4,5},{5,6},{6,7},{7,8},{8,9},{9,10},{10,1... | collective-permute-start | bytes 49160 | tf_op jit(solution)/shard_map/ppermute | solution.py:14
  246.1 1.8 slice_subtract_fusion
  (84 shorter events, 23.9 us)
Async XLA Ops:
  0.6 64.7 %copy-start = (f32[256,256]{1,0:T(8,128)S(1)}, f32[256,256]{1,0:T(8,128)}, u32[]{:S(2)}) copy-start(f32[256,256]{1,0:T(8,128)} %param.8) | copy-start | bytes 786436
  0.6 14.2 %copy-start.5 = (f32[32,64,128]{2,1,0:T(8,128)S(1)}, f32[32,64,128]{2,1,0:T(8,128)}, u32[]{:S(2)}) copy-start(f32[32,64,128]{2,1,0:T(8,128)} %param.5) | copy-start | bytes 3145732
  3.4 19.9 %copy-start.13 = (f32[32,64,128]{2,1,0:T(8,128)S(1)}, f32[32,64,128]{2,1,0:T(8,128)}, u32[]{:S(2)}) copy-start(f32[32,64,128]{2,1,0:T(8,128)} %param.6) | copy-start | bytes 3145732
  3.4 30.4 %all-to-all-start.1 = ((f32[128,8,256]{2,1,0:T(8,128)}), f32[128,8,256]{2,1,0:T(8,128)S(1)}, u32[]{:S(2)}, u32[]{:S(2)}) async-start(f32[128,8,256]{2,1,0:T(8,128)} %copy.129), calls=%async_computation.1 | async-start | bytes 2097152 | tf_op jit(solution)/shard_map/all_to_all | solution.py:95
  14.9 15.0 %collective-permute-start = (f32[32,1,128]{2,1,0:T(1,128)S(1)}, f32[32,1,128]{2,1,0:T(1,128)S(1)}, u32[]{:S(2)}, u32[]{:S(2)}) collective-permute-start(f32[32,1,128]{2,1,0:T(1,128)S(1)} %get-tuple-element.15), channel_id=1, source_target_pairs={{1,0},{2,1},{3,2},{4,3},{5,4},{6,5},{7,6},{8,7},{9,8},{10,9},{11,1... | collective-permute-start | bytes 49160 | tf_op jit(solution)/shard_map/ppermute | solution.py:15
  17.9 12.0 %collective-permute-start.1 = (f32[32,1,128]{2,1,0:T(1,128)S(1)}, f32[32,1,128]{2,1,0:T(1,128)S(1)}, u32[]{:S(2)}, u32[]{:S(2)}) collective-permute-start(f32[32,1,128]{2,1,0:T(1,128)S(1)} %get-tuple-element.16), channel_id=1, source_target_pairs={{0,1},{1,2},{2,3},{3,4},{4,5},{5,6},{6,7},{7,8},{8,9},{9,10},{10,1... | collective-permute-start | bytes 49160 | tf_op jit(solution)/shard_map/ppermute | solution.py:14
  22.3 1.0 copy-start.11
  33.8 29.0 %all-to-all-start = ((f32[32,64,256]{2,0,1:T(8,128)}), f32[32,64,256]{2,0,1:T(8,128)S(1)}, u32[]{:S(2)}, u32[]{:S(2)}) async-start(f32[32,64,256]{2,0,1:T(8,128)} %copy.118), calls=%async_computation | async-start | bytes 4194304 | tf_op jit(solution)/shard_map/all_to_all | solution.py:81
  66.0 1.0 copy-start.7
  67.0 1.2 copy-start.18
  108.1 2.6 %copy-start.2 = (f32[128,8,512]{2,1,0:T(8,128)}, f32[128,8,512]{2,1,0:T(8,128)S(1)}, u32[]{:S(2)}) copy-start(f32[128,8,512]{2,1,0:T(8,128)S(1)} %all_to_all.56) | copy-start | bytes 6291460
  108.2 1.2 copy-start.9
  109.4 2.2 copy-start.1
  111.6 7.2 %copy-start.16 = (f32[127,8,256]{2,1,0:T(8,128)}, f32[127,8,256]{2,1,0:T(8,128)S(1)}, u32[]{:S(2)}) copy-start(f32[127,8,256]{2,1,0:T(8,128)S(1)} %slice.208) | copy-start | bytes 3121156
  113.5 5.7 %collective-permute-start.2 = (f32[128,1,256]{2,1,0:T(1,128)S(1)}, f32[128,1,256]{2,1,0:T(1,128)S(1)}, u32[]{:S(2)}, u32[]{:S(2)}) collective-permute-start(f32[128,1,256]{2,1,0:T(1,128)S(1)} %get-tuple-element.13), channel_id=1, source_target_pairs={{16,0},{32,16},{48,32},{64,48},{80,64},{96,80},{112,96},{1,112},{1... | collective-permute-start | bytes 393224 | tf_op jit(solution)/shard_map/ppermute | solution.py:60
  116.5 8.4 %collective-permute-start.3 = (f32[128,1,256]{2,1,0:T(1,128)S(1)}, f32[128,1,256]{2,1,0:T(1,128)S(1)}, u32[]{:S(2)}, u32[]{:S(2)}) collective-permute-start(f32[128,1,256]{2,1,0:T(1,128)S(1)} %get-tuple-element.14), channel_id=1, source_target_pairs={{0,16},{16,32},{32,48},{48,64},{64,80},{80,96},{96,112},{112,1},{1... | collective-permute-start | bytes 393224 | tf_op jit(solution)/shard_map/ppermute | solution.py:59
  161.0 1.3 copy-start.3
  166.8 29.4 %all-to-all-start.4 = ((f32[128,8,256]{2,1,0:T(8,128)}), f32[128,8,256]{2,1,0:T(8,128)}, u32[]{:S(2)}, u32[]{:S(2)}) async-start(f32[128,8,256]{2,1,0:T(8,128)} %convolution_bitcast_fusion.1), calls=%async_computation.4 | async-start | bytes 2097152 | tf_op jit(solution)/shard_map/all_to_all | solution.py:105
  172.8 9.8 %copy-start.4 = (f32[128,8,512]{2,1,0:T(8,128)S(1)}, f32[128,8,512]{2,1,0:T(8,128)}, u32[]{:S(2)}) copy-start(f32[128,8,512]{2,1,0:T(8,128)} %copy-done.3) | copy-start | bytes 6291460
  174.3 8.5 %copy-start.17 = (f32[127,8,256]{2,1,0:T(8,128)}, f32[127,8,256]{2,1,0:T(8,128)S(1)}, u32[]{:S(2)}) copy-start(f32[127,8,256]{2,1,0:T(8,128)S(1)} %slice.217) | copy-start | bytes 3121156
  174.5 13.5 %collective-permute-start.4 = (f32[128,1,256]{2,1,0:T(1,128)S(1)}, f32[128,1,256]{2,1,0:T(1,128)S(1)}, u32[]{:S(2)}, u32[]{:S(2)}) collective-permute-start(f32[128,1,256]{2,1,0:T(1,128)S(1)} %get-tuple-element.11), channel_id=1, source_target_pairs={{16,0},{32,16},{48,32},{64,48},{80,64},{96,80},{112,96},{1,112},{1... | collective-permute-start | bytes 393224 | tf_op jit(solution)/shard_map/ppermute | solution.py:60
  180.4 12.6 %collective-permute-start.5 = (f32[128,1,256]{2,1,0:T(1,128)S(1)}, f32[128,1,256]{2,1,0:T(1,128)S(1)}, u32[]{:S(2)}, u32[]{:S(2)}) collective-permute-start(f32[128,1,256]{2,1,0:T(1,128)S(1)} %get-tuple-element.12), channel_id=1, source_target_pairs={{0,16},{16,32},{32,48},{48,64},{64,80},{80,96},{96,112},{112,1},{1... | collective-permute-start | bytes 393224 | tf_op jit(solution)/shard_map/ppermute | solution.py:59
  194.1 1.0 copy-start.15
  196.2 1.5 copy-start.8
  196.2 1.8 copy-start.10
  238.2 7.8 %copy-start.14 = (f32[32,64,128]{2,1,0:T(8,128)S(1)}, f32[32,64,128]{2,1,0:T(8,128)}, u32[]{:S(2)}) copy-start(f32[32,64,128]{2,1,0:T(8,128)} %param.6) | copy-start | bytes 3145732
  238.5 7.6 %copy-start.6 = (f32[32,64,128]{2,1,0:T(8,128)S(1)}, f32[32,64,128]{2,1,0:T(8,128)}, u32[]{:S(2)}) copy-start(f32[32,64,128]{2,1,0:T(8,128)} %param.5) | copy-start | bytes 3145732
  238.5 7.6 %copy-start.12 = (f32[32,64,127]{2,1,0:T(8,128)S(1)}, f32[32,64,127]{2,1,0:T(8,128)}, u32[]{:S(2)}) copy-start(f32[32,64,127]{2,1,0:T(8,128)} %copy-done.11) | copy-start | bytes 3121156
  238.9 9.1 %collective-permute-start.6 = (f32[32,1,128]{2,1,0:T(1,128)S(1)}, f32[32,1,128]{2,1,0:T(1,128)S(1)}, u32[]{:S(2)}, u32[]{:S(2)}) collective-permute-start(f32[32,1,128]{2,1,0:T(1,128)S(1)} %get-tuple-element.5), channel_id=1, source_target_pairs={{1,0},{2,1},{3,2},{4,3},{5,4},{6,5},{7,6},{8,7},{9,8},{10,9},{11,1... | collective-permute-start | bytes 49160 | tf_op jit(solution)/shard_map/ppermute | solution.py:15
  241.6 6.3 %collective-permute-start.7 = (f32[32,1,128]{2,1,0:T(1,128)S(1)}, f32[32,1,128]{2,1,0:T(1,128)S(1)}, u32[]{:S(2)}, u32[]{:S(2)}) collective-permute-start(f32[32,1,128]{2,1,0:T(1,128)S(1)} %get-tuple-element.6), channel_id=1, source_target_pairs={{0,1},{1,2},{2,3},{3,4},{4,5},{5,6},{6,7},{7,8},{8,9},{9,10},{10,1... | collective-permute-start | bytes 49160 | tf_op jit(solution)/shard_map/ppermute | solution.py:14

commit v11 on v10

--- a/solution.py
+++ b/solution.py
@@ -64,6 +64,16 @@
         padded = jnp.concatenate([below[edge], field, above[edge]], axis=1)
         diffs.append(padded[:, 2:] + padded[:, :-2] - 2.0 * field)
     return diffs
+
+
+def ydiff_early(field, first_row, last_row):
+    count = lax.axis_size(LINES)
+    up = [(mesh_index(i), mesh_index(i + 1)) for i in range(count - 1)]
+    down = [(b, a) for a, b in up]
+    below = lax.ppermute(last_row, ("px", "py"), up)
+    above = lax.ppermute(first_row, ("px", "py"), down)
+    padded = jnp.concatenate([below, field, above], axis=1)
+    return padded[:, 2:] + padded[:, :-2] - 2.0 * field
 
 
 def along_x(field, matrix, transpose):
@@ -139,7 +149,11 @@
     state1_y = rows(along_y(inv_y, s0y, False))
     lam_half1 = ls1 + RATE * (xdiff(ls1) + zoperate(ls1, cx))
     lam_first1 = along_x(lam_half1, inv_x, True)
-    (dy_lam_first1,) = ydiff(lam_first1)
+    dy_lam_first1 = ydiff_early(
+        lam_first1,
+        along_x(lam_half1[:, :1], inv_x, True),
+        along_x(lam_half1[:, -1:], inv_x, True),
+    )
     lam_state1 = lam_first1 + RATE * (dy_lam_first1 + zoperate(lam_first1, cx))
     lsy, state1 = x_to_y(rows(lam_state1), state1_y.reshape(lam_state1.shape))
     state1 = rows(state1.reshape(lam_state1.shape))

time: 250 us -> 256 us (1.024)
  blocking collectives: 105 us -> 111 us
  waiting for transfers between devices: 29.5 us -> 24.6 us
    ppermute x0 -> x2, starting transfers between devices: none -> 7.67 us  [the longest x1 5.47 us: ydiff_early(): above = lax.ppermute(first_row, ('px', 'py'), down)]
    all_to_all x2, blocking collectives: 74.7 us -> 80.7 us  [x_to_y(): lax.all_to_all(joined, LINES, split_axis=0, concat_axis=0, tiled=True)]
    ppermute x2 -> x1, waiting for transfers between devices: 10.7 us -> 5.01 us  [ydiff(): lax.ppermute(jnp.concatenate([f[:, -1:] for f in fields]), ('px', 'py'), up)]
    ppermute x2 -> x1, starting transfers between devices: 8.86 us -> 5.86 us  [ydiff(): lax.ppermute(jnp.concatenate([f[:, :1] for f in fields]), ('px', 'py'), d...]
    unnamed x40 -> x44, local copies, waits for them, and re-layouts: 12.4 us -> 13.8 us
    dot_general x4 -> x6, matrix products: 5.92 us -> 5.94 us  [along_x(): return lax.dot_general(field, matrix, dims, precision=HIGH)]
  transfers between devices with their start and end apart: 11 -> 11, of which waited for: 7 -> 6; matrix products, arithmetic and copies ran while one was open for 11% -> 11% of each run, Pallas kernels for 0% -> 0%
where the time goes in v11:
time: 256 us; the launch traced here: 255 us
  blocking collectives  111 us (43%)
  starting transfers between devices  51.2 us (20%)
  local copies, waits for them, and re-layouts  37.1 us (14%)
  waiting for transfers between devices  24.6 us (10%)
  matrix products  17.2 us (7%)
  other arithmetic  12.5 us (5%)
    all_to_all x2, blocking collectives, x_to_y(): lax.all_to_all(joined, LINES, split_axis=0, concat_axis=0, tiled=True)  80.7 us
    all_to_all x1, blocking collectives, x_to_block(): lax.all_to_all(joined, 'px', split_axis=0, concat_axis=1, tiled=True)  30.7 us
    unnamed x44, local copies, waits for them, and re-layouts  13.8 us
    all_to_all x1, starting transfers between devices, x_to_y(): lax.all_to_all(joined, LINES, split_axis=0, concat_axis=0, tiled=True)  11.5 us
    dot_general x3, matrix products, along_y(): return lax.dot_general(matrix, field, dims, precision=HIGH)  11.2 us
    ppermute x2, starting transfers between devices, ydiff_block(): lax.ppermute(field[:, -1:], 'py', [(i, i + 1) for i in range(count - 1)])  8.53 us
    all_to_all x1, waiting for transfers between devices, block_to_x(): lax.all_to_all(joined, 'px', split_axis=1, concat_axis=0, tiled=True)  6.85 us
    ppermute x2, waiting for transfers between devices, ydiff_block(): lax.ppermute(field[:, :1], 'py', [(i + 1, i) for i in range(count - 1)])  6.3 us
  transfers between devices with their start and end apart: 11, of which 6 were waited for; matrix products, arithmetic and copies ran while one was open for 11% of the time, Pallas kernels for 0%

profile of v11, /device:TPU:1, one launch (start us, length us, event | category | flops | bytes accessed | tf_op | source)
XLA Modules:
  0.0 255.2 jit_solution(9673865226510502291)
XLA Ops:
  0.7 2.7 %copy.121 = f32[128,8,256]{2,1,0:T(8,128)} copy(f32[128,8,256]{0,2,1:T(8,128)} %bitcast.108) | data formatting | bytes 2097152 | tf_op jit(solution)/shard_map/reshape | solution.py:123
  3.4 11.5 %all-to-all-start.1 = ((f32[128,8,256]{2,1,0:T(8,128)}), f32[128,8,256]{2,1,0:T(8,128)S(1)}, u32[]{:S(2)}, u32[]{:S(2)}) async-start(f32[128,8,256]{2,1,0:T(8,128)} %copy.121), calls=%async_computation.1 | async-start | bytes 2097152 | tf_op jit(solution)/shard_map/all_to_all | solution.py:105
  14.9 3.0 %collective-permute-start = (f32[32,1,128]{2,1,0:T(1,128)S(1)}, f32[32,1,128]{2,1,0:T(1,128)S(1)}, u32[]{:S(2)}, u32[]{:S(2)}) collective-permute-start(f32[32,1,128]{2,1,0:T(1,128)S(1)} %get-tuple-element.15), channel_id=1, source_target_pairs={{1,0},{2,1},{3,2},{4,3},{5,4},{6,5},{7,6},{8,7},{9,8},{10,9},{11,1... | collective-permute-start | bytes 49160 | tf_op jit(solution)/shard_map/ppermute | solution.py:15
  17.9 4.1 %collective-permute-start.1 = (f32[32,1,128]{2,1,0:T(1,128)S(1)}, f32[32,1,128]{2,1,0:T(1,128)S(1)}, u32[]{:S(2)}, u32[]{:S(2)}) collective-permute-start(f32[32,1,128]{2,1,0:T(1,128)S(1)} %get-tuple-element.16), channel_id=1, source_target_pairs={{0,1},{1,2},{2,3},{3,4},{4,5},{5,6},{6,7},{7,8},{8,9},{9,10},{10,1... | collective-permute-start | bytes 49160 | tf_op jit(solution)/shard_map/ppermute | solution.py:14
  23.6 6.3 %collective-permute-done = f32[32,1,128]{2,1,0:T(1,128)S(1)} collective-permute-done((f32[32,1,128]{2,1,0:T(1,128)S(1)}, f32[32,1,128]{2,1,0:T(1,128)S(1)}, u32[]{:S(2)}, u32[]{:S(2)}) %collective-permute-start) | collective-permute-done | bytes 16416 | tf_op jit(solution)/shard_map/ppermute | solution.py:15
  30.7 2.6 %copy.110 = f32[32,64,256]{2,0,1:T(8,128)} copy(f32[32,64,256]{2,1,0:T(8,128)S(1)} %pad_maximum_fusion) | data formatting | bytes 4194304 | tf_op jit(solution)/shard_map/concatenate | solution.py:90
  34.7 3.8 %all-to-all-start = ((f32[32,64,256]{2,0,1:T(8,128)}), f32[32,64,256]{2,0,1:T(8,128)S(1)}, u32[]{:S(2)}, u32[]{:S(2)}) async-start(f32[32,64,256]{2,0,1:T(8,128)} %copy.110), calls=%async_computation | async-start | bytes 4194304 | tf_op jit(solution)/shard_map/all_to_all | solution.py:91
  38.5 5.5 %copy.120 = f32[1024,1024]{0,1:T(8,128)} copy(f32[1024,1024]{1,0:T(8,128)} %param.9) | data formatting | bytes 8388608 | tf_op args[4]
  44.0 1.8 reshape_reshape.3
  45.8 4.2 %copy.122 = f32[16,64,8,32]{1,0,3,2:T(8,128)} copy(f32[16,64,8,32]{1,3,2,0:T(8,128)} %bitcast.106) | data formatting | bytes 2097152 | tf_op jit(solution)/shard_map/transpose | solution.py:131
  49.9 2.0 reshape.39
  51.9 5.0 %fusion = f32[128,8,256]{2,1,0:T(8,128)} fusion(f32[1024,1024]{0,1:T(8,128)} %copy.120, f32[1024,256]{0,1:T(8,128)S(1)} %reshape.39), kind=kOutput, calls=%fused_computation | convolution fusion | flops 1610612736 | bytes 6291456 | tf_op jit(solution)/shard_map/dot_general | solution.py:86
  56.9 6.8 %all-to-all-done = f32[32,64,256]{2,0,1:T(8,128)S(1)} async-done(((f32[32,64,256]{2,0,1:T(8,128)}), f32[32,64,256]{2,0,1:T(8,128)S(1)}, u32[]{:S(2)}, u32[]{:S(2)}) %all-to-all-start) | async-done | bytes 2097184 | tf_op jit(solution)/shard_map/all_to_all | solution.py:91
  69.5 39.5 %all_to_all.56 = f32[128,8,512]{2,1,0:T(8,128)S(1)} all-to-all(f32[128,8,512]{2,1,0:T(8,128)S(1)} %pad_maximum_fusion.1), channel_id=1, replica_groups=mesh['px'=8,'py'=16] {'py','px'}, dimensions={0} | all-to-all | bytes 4194304 | tf_op jit(solution)/shard_map/all_to_all | solution.py:105
  112.5 1.8 convolution_bitcast_fusion.2
  115.0 2.2 collective-permute-start.3
  117.2 5.5 %collective-permute-start.2 = (f32[128,1,256]{2,1,0:T(1,128)S(1)}, f32[128,1,256]{2,1,0:T(1,128)S(1)}, u32[]{:S(2)}, u32[]{:S(2)}) collective-permute-start(f32[128,1,256]{2,1,0:T(1,128)S(1)} %dot_general.45), channel_id=1, source_target_pairs={{16,0},{32,16},{48,32},{64,48},{80,64},{96,80},{112,96},{1,112},{1... | collective-permute-start | bytes 393224 | tf_op jit(solution)/shard_map/ppermute | solution.py:74
  125.5 41.2 %all_to_all.57 = f32[128,8,512]{2,1,0:T(8,128)S(1)} all-to-all(f32[128,8,512]{2,1,0:T(8,128)S(1)} %pad_maximum_fusion.2), channel_id=1, replica_groups=mesh['px'=8,'py'=16] {'py','px'}, dimensions={0} | all-to-all | bytes 4194304 | tf_op jit(solution)/shard_map/all_to_all | solution.py:105
  168.1 4.4 %convolution_bitcast_fusion.1 = f32[128,8,256]{2,1,0:T(8,128)} fusion(f32[1024,1024]{1,0:T(8,128)S(1)} %copy-done.1, f32[1024,512]{1,0:T(8,128)S(1)} %bitcast.95), kind=kOutput, calls=%fused_computation.14 | convolution fusion | flops 1610612736 | bytes 6291456 | tf_op jit(solution)/shard_map/dot_general | solution.py:86
  172.6 6.0 %all-to-all-start.4 = ((f32[128,8,256]{2,1,0:T(8,128)}), f32[128,8,256]{2,1,0:T(8,128)}, u32[]{:S(2)}, u32[]{:S(2)}) async-start(f32[128,8,256]{2,1,0:T(8,128)} %convolution_bitcast_fusion.1), calls=%async_computation.4 | async-start | bytes 2097152 | tf_op jit(solution)/shard_map/all_to_all | solution.py:115
  180.3 5.9 %collective-permute-start.4 = (f32[128,1,256]{2,1,0:T(1,128)S(1)}, f32[128,1,256]{2,1,0:T(1,128)S(1)}, u32[]{:S(2)}, u32[]{:S(2)}) collective-permute-start(f32[128,1,256]{2,1,0:T(1,128)S(1)} %get-tuple-element.11), channel_id=1, source_target_pairs={{16,0},{32,16},{48,32},{64,48},{80,64},{96,80},{112,96},{1,112},{1... | collective-permute-start | bytes 393224 | tf_op jit(solution)/shard_map/ppermute | solution.py:60
  186.1 2.2 collective-permute-start.5
  188.7 5.0 %collective-permute-done.4 = f32[128,1,256]{2,1,0:T(1,128)S(1)} collective-permute-done((f32[128,1,256]{2,1,0:T(1,128)S(1)}, f32[128,1,256]{2,1,0:T(1,128)S(1)}, u32[]{:S(2)}, u32[]{:S(2)}) %collective-permute-start.4) | collective-permute-done | bytes 131104 | tf_op jit(solution)/shard_map/ppermute | solution.py:60
  193.7 5.0 %collective-permute-done.5 = f32[128,1,256]{2,1,0:T(1,128)S(1)} collective-permute-done((f32[128,1,256]{2,1,0:T(1,128)S(1)}, f32[128,1,256]{2,1,0:T(1,128)S(1)}, u32[]{:S(2)}, u32[]{:S(2)}) %collective-permute-start.5) | collective-permute-done | bytes 131104 | tf_op jit(solution)/shard_map/ppermute | solution.py:59
  203.7 4.1 %bitcast_multiply_fusion.1 = (f32[128,8,256]{2,1,0:T(8,128)S(1)}, f32[256,8,128]{0,1,2:T(8,128)S(1)}) fusion(f32[256,8,128]{0,1,2:T(8,128)S(1)} %copy.152, f32[128,8,256]{2,1,0:T(8,128)} %all-to-all-done.4, f32[127,8,256]{2,1,0:T(8,128)S(1)} %slice.212, f32[128,8,256]{2,1,0:T(8,128)S(1)} %fusion.61, f32[127,8,256]{2,1,0:T(8,128)S(1)} %copy-done.8, ...), kind=kLoop, calls=%fused_computation.70 | loop fusion | flops 3932160 | bytes 15679488 | tf_op jit(solution)/shard_map/mul | solution.py:38
  207.9 3.2 %convolution_bitcast_fusion = f32[256,8,128]{0,1,2:T(8,128)S(1)} fusion(f32[128,8,256]{2,1,0:T(8,128)} %all-to-all-done.4, f32[127,8,256]{2,1,0:T(8,128)S(1)} %slice.213, f32[256,8,128]{0,1,2:T(8,128)S(1)} %copy.152, f32[127,8,256]{2,1,0:T(8,128)S(1)} %slice.212, f32[256,256]{1,0:T(8,128)S(1)} %copy-done), kind=kOutput, calls=%fused_computation.13 | convolution fusion | flops 405012480 | bytes 5488640 | tf_op jit(solution)/shard_map/dot_general | solution.py:81
  211.2 2.0 copy.136
  213.3 30.7 %all_to_all.58 = f32[256,8,256]{2,1,0:T(8,128)S(1)} all-to-all(f32[256,8,256]{2,1,0:T(8,128)} %copy.136), channel_id=1, replica_groups=mesh['px'=8,'py'=16] {'px'}, dimensions={0} | all-to-all | bytes 4194304 | tf_op jit(solution)/shard_map/all_to_all | solution.py:98
  244.6 2.8 %collective-permute-start.6 = (f32[32,1,128]{2,1,0:T(1,128)S(1)}, f32[32,1,128]{2,1,0:T(1,128)S(1)}, u32[]{:S(2)}, u32[]{:S(2)}) collective-permute-start(f32[32,1,128]{2,1,0:T(1,128)S(1)} %get-tuple-element.5), channel_id=1, source_target_pairs={{1,0},{2,1},{3,2},{4,3},{5,4},{6,5},{7,6},{8,7},{9,8},{10,9},{11,1... | collective-permute-start | bytes 49160 | tf_op jit(solution)/shard_map/ppermute | solution.py:15
  247.4 4.4 %collective-permute-start.7 = (f32[32,1,128]{2,1,0:T(1,128)S(1)}, f32[32,1,128]{2,1,0:T(1,128)S(1)}, u32[]{:S(2)}, u32[]{:S(2)}) collective-permute-start(f32[32,1,128]{2,1,0:T(1,128)S(1)} %get-tuple-element.6), channel_id=1, source_target_pairs={{0,1},{1,2},{2,3},{3,4},{4,5},{5,6},{6,7},{7,8},{8,9},{9,10},{10,1... | collective-permute-start | bytes 49160 | tf_op jit(solution)/shard_map/ppermute | solution.py:14
  251.8 1.8 slice_subtract_fusion
  253.7 1.5 fusion.22
  (93 shorter events, 25.6 us)
Async XLA Ops:
  0.6 65.6 %copy-start = (f32[256,256]{1,0:T(8,128)S(1)}, f32[256,256]{1,0:T(8,128)}, u32[]{:S(2)}) copy-start(f32[256,256]{1,0:T(8,128)} %param.8) | copy-start | bytes 786436
  0.6 14.2 %copy-start.5 = (f32[32,64,128]{2,1,0:T(8,128)S(1)}, f32[32,64,128]{2,1,0:T(8,128)}, u32[]{:S(2)}) copy-start(f32[32,64,128]{2,1,0:T(8,128)} %param.5) | copy-start | bytes 3145732
  3.4 19.9 %copy-start.13 = (f32[32,64,128]{2,1,0:T(8,128)S(1)}, f32[32,64,128]{2,1,0:T(8,128)}, u32[]{:S(2)}) copy-start(f32[32,64,128]{2,1,0:T(8,128)} %param.6) | copy-start | bytes 3145732
  3.4 30.4 %all-to-all-start.1 = ((f32[128,8,256]{2,1,0:T(8,128)}), f32[128,8,256]{2,1,0:T(8,128)S(1)}, u32[]{:S(2)}, u32[]{:S(2)}) async-start(f32[128,8,256]{2,1,0:T(8,128)} %copy.121), calls=%async_computation.1 | async-start | bytes 2097152 | tf_op jit(solution)/shard_map/all_to_all | solution.py:105
  14.9 15.0 %collective-permute-start = (f32[32,1,128]{2,1,0:T(1,128)S(1)}, f32[32,1,128]{2,1,0:T(1,128)S(1)}, u32[]{:S(2)}, u32[]{:S(2)}) collective-permute-start(f32[32,1,128]{2,1,0:T(1,128)S(1)} %get-tuple-element.15), channel_id=1, source_target_pairs={{1,0},{2,1},{3,2},{4,3},{5,4},{6,5},{7,6},{8,7},{9,8},{10,9},{11,1... | collective-permute-start | bytes 49160 | tf_op jit(solution)/shard_map/ppermute | solution.py:15
  17.9 12.0 %collective-permute-start.1 = (f32[32,1,128]{2,1,0:T(1,128)S(1)}, f32[32,1,128]{2,1,0:T(1,128)S(1)}, u32[]{:S(2)}, u32[]{:S(2)}) collective-permute-start(f32[32,1,128]{2,1,0:T(1,128)S(1)} %get-tuple-element.16), channel_id=1, source_target_pairs={{0,1},{1,2},{2,3},{3,4},{4,5},{5,6},{6,7},{7,8},{8,9},{9,10},{10,1... | collective-permute-start | bytes 49160 | tf_op jit(solution)/shard_map/ppermute | solution.py:14
  22.3 1.0 copy-start.11
  33.8 1.0 copy-start.18
  34.7 29.0 %all-to-all-start = ((f32[32,64,256]{2,0,1:T(8,128)}), f32[32,64,256]{2,0,1:T(8,128)S(1)}, u32[]{:S(2)}, u32[]{:S(2)}) async-start(f32[32,64,256]{2,0,1:T(8,128)} %copy.110), calls=%async_computation | async-start | bytes 4194304 | tf_op jit(solution)/shard_map/all_to_all | solution.py:91
  38.5 5.5 %copy-start.19 = (f32[128,8,256]{2,1,0:T(8,128)S(1)}, f32[128,8,256]{2,1,0:T(8,128)}, u32[]{:S(2)}) copy-start(f32[128,8,256]{2,1,0:T(8,128)} %copy-done.18) | copy-start | bytes 3145732
  67.0 1.0 copy-start.7
  68.0 1.2 copy-start.20
  109.0 2.9 %copy-start.2 = (f32[128,8,512]{2,1,0:T(8,128)}, f32[128,8,512]{2,1,0:T(8,128)S(1)}, u32[]{:S(2)}) copy-start(f32[128,8,512]{2,1,0:T(8,128)S(1)} %all_to_all.56) | copy-start | bytes 6291460
  109.2 1.1 copy-start.9
  110.3 2.2 copy-start.1
  115.0 8.7 %collective-permute-start.3 = (f32[128,1,256]{2,1,0:T(1,128)S(1)}, f32[128,1,256]{2,1,0:T(1,128)S(1)}, u32[]{:S(2)}, u32[]{:S(2)}) collective-permute-start(f32[128,1,256]{2,1,0:T(1,128)S(1)} %dot_general.47), channel_id=1, source_target_pairs={{0,16},{16,32},{32,48},{48,64},{64,80},{80,96},{96,112},{112,1},{1... | collective-permute-start | bytes 393224 | tf_op jit(solution)/shard_map/ppermute | solution.py:73
  117.2 7.4 %collective-permute-start.2 = (f32[128,1,256]{2,1,0:T(1,128)S(1)}, f32[128,1,256]{2,1,0:T(1,128)S(1)}, u32[]{:S(2)}, u32[]{:S(2)}) collective-permute-start(f32[128,1,256]{2,1,0:T(1,128)S(1)} %dot_general.45), channel_id=1, source_target_pairs={{16,0},{32,16},{48,32},{64,48},{80,64},{96,80},{112,96},{1,112},{1... | collective-permute-start | bytes 393224 | tf_op jit(solution)/shard_map/ppermute | solution.py:74
  122.8 1.0 copy-start.16
  166.8 1.3 copy-start.3
  172.6 29.3 %all-to-all-start.4 = ((f32[128,8,256]{2,1,0:T(8,128)}), f32[128,8,256]{2,1,0:T(8,128)}, u32[]{:S(2)}, u32[]{:S(2)}) async-start(f32[128,8,256]{2,1,0:T(8,128)} %convolution_bitcast_fusion.1), calls=%async_computation.4 | async-start | bytes 2097152 | tf_op jit(solution)/shard_map/all_to_all | solution.py:115
  178.6 9.8 %copy-start.4 = (f32[128,8,512]{2,1,0:T(8,128)S(1)}, f32[128,8,512]{2,1,0:T(8,128)}, u32[]{:S(2)}) copy-start(f32[128,8,512]{2,1,0:T(8,128)} %copy-done.3) | copy-start | bytes 6291460
  180.1 8.5 %copy-start.17 = (f32[127,8,256]{2,1,0:T(8,128)}, f32[127,8,256]{2,1,0:T(8,128)S(1)}, u32[]{:S(2)}) copy-start(f32[127,8,256]{2,1,0:T(8,128)S(1)} %slice.217) | copy-start | bytes 3121156
  180.3 13.5 %collective-permute-start.4 = (f32[128,1,256]{2,1,0:T(1,128)S(1)}, f32[128,1,256]{2,1,0:T(1,128)S(1)}, u32[]{:S(2)}, u32[]{:S(2)}) collective-permute-start(f32[128,1,256]{2,1,0:T(1,128)S(1)} %get-tuple-element.11), channel_id=1, source_target_pairs={{16,0},{32,16},{48,32},{64,48},{80,64},{96,80},{112,96},{1,112},{1... | collective-permute-start | bytes 393224 | tf_op jit(solution)/shard_map/ppermute | solution.py:60
  186.1 12.6 %collective-permute-start.5 = (f32[128,1,256]{2,1,0:T(1,128)S(1)}, f32[128,1,256]{2,1,0:T(1,128)S(1)}, u32[]{:S(2)}, u32[]{:S(2)}) collective-permute-start(f32[128,1,256]{2,1,0:T(1,128)S(1)} %get-tuple-element.12), channel_id=1, source_target_pairs={{0,16},{16,32},{32,48},{48,64},{64,80},{80,96},{96,112},{112,1},{1... | collective-permute-start | bytes 393224 | tf_op jit(solution)/shard_map/ppermute | solution.py:59
  199.9 1.0 copy-start.15
  201.9 1.5 copy-start.8
  201.9 1.8 copy-start.10
  244.0 7.8 %copy-start.14 = (f32[32,64,128]{2,1,0:T(8,128)S(1)}, f32[32,64,128]{2,1,0:T(8,128)}, u32[]{:S(2)}) copy-start(f32[32,64,128]{2,1,0:T(8,128)} %param.6) | copy-start | bytes 3145732
  244.2 7.6 %copy-start.6 = (f32[32,64,128]{2,1,0:T(8,128)S(1)}, f32[32,64,128]{2,1,0:T(8,128)}, u32[]{:S(2)}) copy-start(f32[32,64,128]{2,1,0:T(8,128)} %param.5) | copy-start | bytes 3145732
  244.2 7.6 %copy-start.12 = (f32[32,64,127]{2,1,0:T(8,128)S(1)}, f32[32,64,127]{2,1,0:T(8,128)}, u32[]{:S(2)}) copy-start(f32[32,64,127]{2,1,0:T(8,128)} %copy-done.11) | copy-start | bytes 3121156
  244.6 9.1 %collective-permute-start.6 = (f32[32,1,128]{2,1,0:T(1,128)S(1)}, f32[32,1,128]{2,1,0:T(1,128)S(1)}, u32[]{:S(2)}, u32[]{:S(2)}) collective-permute-start(f32[32,1,128]{2,1,0:T(1,128)S(1)} %get-tuple-element.5), channel_id=1, source_target_pairs={{1,0},{2,1},{3,2},{4,3},{5,4},{6,5},{7,6},{8,7},{9,8},{10,9},{11,1... | collective-permute-start | bytes 49160 | tf_op jit(solution)/shard_map/ppermute | solution.py:15
  247.4 6.3 %collective-permute-start.7 = (f32[32,1,128]{2,1,0:T(1,128)S(1)}, f32[32,1,128]{2,1,0:T(1,128)S(1)}, u32[]{:S(2)}, u32[]{:S(2)}) collective-permute-start(f32[32,1,128]{2,1,0:T(1,128)S(1)} %get-tuple-element.6), channel_id=1, source_target_pairs={{0,1},{1,2},{2,3},{3,4},{4,5},{5,6},{6,7},{7,8},{8,9},{9,10},{10,1... | collective-permute-start | bytes 49160 | tf_op jit(solution)/shard_map/ppermute | solution.py:14

commit v12 on v10

--- a/solution.py
+++ b/solution.py
@@ -84,7 +84,7 @@
 
 
 def x_to_block(*fields):
-    joined = jnp.concatenate([jnp.transpose(f, (2, 1, 0)) for f in fields], axis=2)
+    joined = jnp.transpose(jnp.concatenate(fields, axis=0), (2, 1, 0))
     block = lax.all_to_all(joined, "px", split_axis=0, concat_axis=1, tiled=True)
     depth = fields[0].shape[0]
     return [block[:, :, k * depth:(k + 1) * depth] for k in range(len(fields))]

time: 250 us -> 250 us (level)
  no operation moved by 1% of the time
where the time goes in v12:
time: 250 us; the launch traced here: 249 us
  blocking collectives  105 us (42%)
  starting transfers between devices  48.9 us (20%)
  local copies, waits for them, and re-layouts  35.5 us (14%)
  waiting for transfers between devices  29.5 us (12%)
  matrix products  17.3 us (7%)
  other arithmetic  11.7 us (5%)
    all_to_all x2, blocking collectives, x_to_y(): lax.all_to_all(joined, LINES, split_axis=0, concat_axis=0, tiled=True)  74.7 us
    all_to_all x1, blocking collectives, x_to_block(): lax.all_to_all(joined, 'px', split_axis=0, concat_axis=1, tiled=True)  30.7 us
    unnamed x40, local copies, waits for them, and re-layouts  12.4 us
    all_to_all x1, starting transfers between devices, x_to_y(): lax.all_to_all(joined, LINES, split_axis=0, concat_axis=0, tiled=True)  11.5 us
    dot_general x3, matrix products, along_y(): return lax.dot_general(matrix, field, dims, precision=HIGH)  11.4 us
    ppermute x2, waiting for transfers between devices, ydiff(): lax.ppermute(jnp.concatenate([f[:, -1:] for f in fields]), ('px', 'py'), up)  10.7 us
    ppermute x2, starting transfers between devices, ydiff(): lax.ppermute(jnp.concatenate([f[:, :1] for f in fields]), ('px', 'py'), d...  8.86 us
    ppermute x2, starting transfers between devices, ydiff_block(): lax.ppermute(field[:, -1:], 'py', [(i, i + 1) for i in range(count - 1)])  8.53 us
  transfers between devices with their start and end apart: 11, of which 7 were waited for; matrix products, arithmetic and copies ran while one was open for 11% of the time, Pallas kernels for 0%

profile of v12, /device:TPU:1, one launch (start us, length us, event | category | flops | bytes accessed | tf_op | source)
XLA Modules:
  0.0 249.5 jit_solution(4912618870930267132)
XLA Ops:
  0.7 2.7 %copy.133 = f32[128,8,256]{2,1,0:T(8,128)} copy(f32[128,8,256]{0,2,1:T(8,128)} %bitcast.98) | data formatting | bytes 2097152 | tf_op jit(solution)/shard_map/reshape | solution.py:113
  3.4 11.5 %all-to-all-start.1 = ((f32[128,8,256]{2,1,0:T(8,128)}), f32[128,8,256]{2,1,0:T(8,128)S(1)}, u32[]{:S(2)}, u32[]{:S(2)}) async-start(f32[128,8,256]{2,1,0:T(8,128)} %copy.133), calls=%async_computation.1 | async-start | bytes 2097152 | tf_op jit(solution)/shard_map/all_to_all | solution.py:95
  14.9 3.0 %collective-permute-start = (f32[32,1,128]{2,1,0:T(1,128)S(1)}, f32[32,1,128]{2,1,0:T(1,128)S(1)}, u32[]{:S(2)}, u32[]{:S(2)}) collective-permute-start(f32[32,1,128]{2,1,0:T(1,128)S(1)} %get-tuple-element.15), channel_id=1, source_target_pairs={{1,0},{2,1},{3,2},{4,3},{5,4},{6,5},{7,6},{8,7},{9,8},{10,9},{11,1... | collective-permute-start | bytes 49160 | tf_op jit(solution)/shard_map/ppermute | solution.py:15
  17.9 4.1 %collective-permute-start.1 = (f32[32,1,128]{2,1,0:T(1,128)S(1)}, f32[32,1,128]{2,1,0:T(1,128)S(1)}, u32[]{:S(2)}, u32[]{:S(2)}) collective-permute-start(f32[32,1,128]{2,1,0:T(1,128)S(1)} %get-tuple-element.16), channel_id=1, source_target_pairs={{0,1},{1,2},{2,3},{3,4},{4,5},{5,6},{6,7},{7,8},{8,9},{9,10},{10,1... | collective-permute-start | bytes 49160 | tf_op jit(solution)/shard_map/ppermute | solution.py:14
  23.6 6.3 %collective-permute-done = f32[32,1,128]{2,1,0:T(1,128)S(1)} collective-permute-done((f32[32,1,128]{2,1,0:T(1,128)S(1)}, f32[32,1,128]{2,1,0:T(1,128)S(1)}, u32[]{:S(2)}, u32[]{:S(2)}) %collective-permute-start) | collective-permute-done | bytes 16416 | tf_op jit(solution)/shard_map/ppermute | solution.py:15
  30.7 2.6 %copy.122 = f32[32,64,256]{2,0,1:T(8,128)} copy(f32[32,64,256]{2,1,0:T(8,128)S(1)} %pad_maximum_fusion) | data formatting | bytes 4194304 | tf_op jit(solution)/shard_map/concatenate | solution.py:80
  33.8 3.8 %all-to-all-start = ((f32[32,64,256]{2,0,1:T(8,128)}), f32[32,64,256]{2,0,1:T(8,128)S(1)}, u32[]{:S(2)}, u32[]{:S(2)}) async-start(f32[32,64,256]{2,0,1:T(8,128)} %copy.122), calls=%async_computation | async-start | bytes 4194304 | tf_op jit(solution)/shard_map/all_to_all | solution.py:81
  37.6 5.4 %copy.132 = f32[1024,1024]{0,1:T(8,128)} copy(f32[1024,1024]{1,0:T(8,128)} %param.9) | data formatting | bytes 8388608 | tf_op args[4]
  42.9 1.7 reshape_reshape.3
  44.7 4.2 %copy.134 = f32[16,64,8,32]{1,0,3,2:T(8,128)} copy(f32[16,64,8,32]{1,3,2,0:T(8,128)} %bitcast.96) | data formatting | bytes 2097152 | tf_op jit(solution)/shard_map/transpose | solution.py:121
  48.8 2.0 reshape.31
  50.8 5.0 %fusion = f32[128,8,256]{2,1,0:T(8,128)} fusion(f32[1024,1024]{0,1:T(8,128)} %copy.132, f32[1024,256]{0,1:T(8,128)S(1)} %reshape.31), kind=kOutput, calls=%fused_computation | convolution fusion | flops 1610612736 | bytes 6291456 | tf_op jit(solution)/shard_map/dot_general | solution.py:76
  55.8 7.0 %all-to-all-done = f32[32,64,256]{2,0,1:T(8,128)S(1)} async-done(((f32[32,64,256]{2,0,1:T(8,128)}), f32[32,64,256]{2,0,1:T(8,128)S(1)}, u32[]{:S(2)}, u32[]{:S(2)}) %all-to-all-start) | async-done | bytes 2097184 | tf_op jit(solution)/shard_map/all_to_all | solution.py:81
  68.5 39.5 %all_to_all.56 = f32[128,8,512]{2,1,0:T(8,128)S(1)} all-to-all(f32[128,8,512]{2,1,0:T(8,128)S(1)} %pad_maximum_fusion.1), channel_id=1, replica_groups=mesh['px'=8,'py'=16] {'py','px'}, dimensions={0} | all-to-all | bytes 4194304 | tf_op jit(solution)/shard_map/all_to_all | solution.py:95
  111.6 1.9 convolution_bitcast_fusion.1
  113.5 3.0 %collective-permute-start.2 = (f32[128,1,256]{2,1,0:T(1,128)S(1)}, f32[128,1,256]{2,1,0:T(1,128)S(1)}, u32[]{:S(2)}, u32[]{:S(2)}) collective-permute-start(f32[128,1,256]{2,1,0:T(1,128)S(1)} %get-tuple-element.13), channel_id=1, source_target_pairs={{16,0},{32,16},{48,32},{64,48},{80,64},{96,80},{112,96},{1,112},{1... | collective-permute-start | bytes 393224 | tf_op jit(solution)/shard_map/ppermute | solution.py:60
  116.5 2.3 collective-permute-start.3
  119.2 5.7 %collective-permute-done.3 = f32[128,1,256]{2,1,0:T(1,128)S(1)} collective-permute-done((f32[128,1,256]{2,1,0:T(1,128)S(1)}, f32[128,1,256]{2,1,0:T(1,128)S(1)}, u32[]{:S(2)}, u32[]{:S(2)}) %collective-permute-start.3) | collective-permute-done | bytes 131104 | tf_op jit(solution)/shard_map/ppermute | solution.py:59
  125.8 35.2 %all_to_all.57 = f32[128,8,512]{2,1,0:T(8,128)S(1)} all-to-all(f32[128,8,512]{2,1,0:T(8,128)S(1)} %pad_maximum_fusion.2), channel_id=1, replica_groups=mesh['px'=8,'py'=16] {'py','px'}, dimensions={0} | all-to-all | bytes 4194304 | tf_op jit(solution)/shard_map/all_to_all | solution.py:95
  162.3 4.5 %convolution_bitcast_fusion = f32[128,8,256]{2,1,0:T(8,128)} fusion(f32[1024,1024]{1,0:T(8,128)S(1)} %copy-done.1, f32[1024,512]{1,0:T(8,128)S(1)} %bitcast.85), kind=kOutput, calls=%fused_computation.13 | convolution fusion | flops 1610612736 | bytes 6291456 | tf_op jit(solution)/shard_map/dot_general | solution.py:76
  166.8 6.0 %all-to-all-start.4 = ((f32[128,8,256]{2,1,0:T(8,128)}), f32[128,8,256]{2,1,0:T(8,128)}, u32[]{:S(2)}, u32[]{:S(2)}) async-start(f32[128,8,256]{2,1,0:T(8,128)} %convolution_bitcast_fusion), calls=%async_computation.4 | async-start | bytes 2097152 | tf_op jit(solution)/shard_map/all_to_all | solution.py:105
  174.5 5.9 %collective-permute-start.4 = (f32[128,1,256]{2,1,0:T(1,128)S(1)}, f32[128,1,256]{2,1,0:T(1,128)S(1)}, u32[]{:S(2)}, u32[]{:S(2)}) collective-permute-start(f32[128,1,256]{2,1,0:T(1,128)S(1)} %get-tuple-element.11), channel_id=1, source_target_pairs={{16,0},{32,16},{48,32},{64,48},{80,64},{96,80},{112,96},{1,112},{1... | collective-permute-start | bytes 393224 | tf_op jit(solution)/shard_map/ppermute | solution.py:60
  180.4 2.2 collective-permute-start.5
  182.9 5.0 %collective-permute-done.4 = f32[128,1,256]{2,1,0:T(1,128)S(1)} collective-permute-done((f32[128,1,256]{2,1,0:T(1,128)S(1)}, f32[128,1,256]{2,1,0:T(1,128)S(1)}, u32[]{:S(2)}, u32[]{:S(2)}) %collective-permute-start.4) | collective-permute-done | bytes 131104 | tf_op jit(solution)/shard_map/ppermute | solution.py:60
  188.0 5.0 %collective-permute-done.5 = f32[128,1,256]{2,1,0:T(1,128)S(1)} collective-permute-done((f32[128,1,256]{2,1,0:T(1,128)S(1)}, f32[128,1,256]{2,1,0:T(1,128)S(1)}, u32[]{:S(2)}, u32[]{:S(2)}) %collective-permute-start.5) | collective-permute-done | bytes 131104 | tf_op jit(solution)/shard_map/ppermute | solution.py:59
  198.0 4.1 %bitcast_multiply_fusion.1 = (f32[128,8,256]{2,1,0:T(8,128)S(1)}, f32[128,8,256]{2,1,0:T(8,128)S(1)}) fusion(f32[256,8,128]{0,1,2:T(8,128)S(1)} %copy.168, f32[128,8,256]{2,1,0:T(8,128)} %all-to-all-done.4, f32[127,8,256]{2,1,0:T(8,128)S(1)} %slice.212, f32[128,8,256]{2,1,0:T(8,128)S(1)} %fusion.68, f32[127,8,256]{2,1,0:T(8,128)S(1)} %copy-done.8, ...), kind=kLoop, calls=%fused_computation.71 | loop fusion | flops 3932160 | bytes 15679488 | tf_op jit(solution)/shard_map/mul | solution.py:38
  202.2 3.2 %fusion.19 = f32[128,8,256]{2,1,0:T(8,128)S(1)} fusion(f32[128,8,256]{2,1,0:T(8,128)} %all-to-all-done.4, f32[127,8,256]{2,1,0:T(8,128)S(1)} %slice.213, f32[256,8,128]{0,1,2:T(8,128)S(1)} %copy.168, f32[127,8,256]{2,1,0:T(8,128)S(1)} %slice.212, f32[256,256]{1,0:T(8,128)S(1)} %copy-done), kind=kOutput, calls=%fused_computation.31 | convolution fusion | flops 405012480 | bytes 5488640 | tf_op jit(solution)/shard_map/dot_general | solution.py:71
  205.5 2.0 copy.152
  207.6 30.7 %all_to_all.58 = f32[256,8,256]{2,1,0:T(8,128)S(1)} all-to-all(f32[256,8,256]{2,1,0:T(8,128)} %copy.152), channel_id=1, replica_groups=mesh['px'=8,'py'=16] {'px'}, dimensions={0} | all-to-all | bytes 4194304 | tf_op jit(solution)/shard_map/all_to_all | solution.py:88
  238.9 2.8 %collective-permute-start.6 = (f32[32,1,128]{2,1,0:T(1,128)S(1)}, f32[32,1,128]{2,1,0:T(1,128)S(1)}, u32[]{:S(2)}, u32[]{:S(2)}) collective-permute-start(f32[32,1,128]{2,1,0:T(1,128)S(1)} %get-tuple-element.5), channel_id=1, source_target_pairs={{1,0},{2,1},{3,2},{4,3},{5,4},{6,5},{7,6},{8,7},{9,8},{10,9},{11,1... | collective-permute-start | bytes 49160 | tf_op jit(solution)/shard_map/ppermute | solution.py:15
  241.6 4.4 %collective-permute-start.7 = (f32[32,1,128]{2,1,0:T(1,128)S(1)}, f32[32,1,128]{2,1,0:T(1,128)S(1)}, u32[]{:S(2)}, u32[]{:S(2)}) collective-permute-start(f32[32,1,128]{2,1,0:T(1,128)S(1)} %get-tuple-element.6), channel_id=1, source_target_pairs={{0,1},{1,2},{2,3},{3,4},{4,5},{5,6},{6,7},{7,8},{8,9},{9,10},{10,1... | collective-permute-start | bytes 49160 | tf_op jit(solution)/shard_map/ppermute | solution.py:14
  246.1 1.8 slice_subtract_fusion
  (84 shorter events, 23.9 us)
Async XLA Ops:
  0.6 64.7 %copy-start = (f32[256,256]{1,0:T(8,128)S(1)}, f32[256,256]{1,0:T(8,128)}, u32[]{:S(2)}) copy-start(f32[256,256]{1,0:T(8,128)} %param.8) | copy-start | bytes 786436
  0.6 14.2 %copy-start.5 = (f32[32,64,128]{2,1,0:T(8,128)S(1)}, f32[32,64,128]{2,1,0:T(8,128)}, u32[]{:S(2)}) copy-start(f32[32,64,128]{2,1,0:T(8,128)} %param.5) | copy-start | bytes 3145732
  3.4 19.9 %copy-start.13 = (f32[32,64,128]{2,1,0:T(8,128)S(1)}, f32[32,64,128]{2,1,0:T(8,128)}, u32[]{:S(2)}) copy-start(f32[32,64,128]{2,1,0:T(8,128)} %param.6) | copy-start | bytes 3145732
  3.4 30.4 %all-to-all-start.1 = ((f32[128,8,256]{2,1,0:T(8,128)}), f32[128,8,256]{2,1,0:T(8,128)S(1)}, u32[]{:S(2)}, u32[]{:S(2)}) async-start(f32[128,8,256]{2,1,0:T(8,128)} %copy.133), calls=%async_computation.1 | async-start | bytes 2097152 | tf_op jit(solution)/shard_map/all_to_all | solution.py:95
  14.9 15.0 %collective-permute-start = (f32[32,1,128]{2,1,0:T(1,128)S(1)}, f32[32,1,128]{2,1,0:T(1,128)S(1)}, u32[]{:S(2)}, u32[]{:S(2)}) collective-permute-start(f32[32,1,128]{2,1,0:T(1,128)S(1)} %get-tuple-element.15), channel_id=1, source_target_pairs={{1,0},{2,1},{3,2},{4,3},{5,4},{6,5},{7,6},{8,7},{9,8},{10,9},{11,1... | collective-permute-start | bytes 49160 | tf_op jit(solution)/shard_map/ppermute | solution.py:15
  17.9 12.0 %collective-permute-start.1 = (f32[32,1,128]{2,1,0:T(1,128)S(1)}, f32[32,1,128]{2,1,0:T(1,128)S(1)}, u32[]{:S(2)}, u32[]{:S(2)}) collective-permute-start(f32[32,1,128]{2,1,0:T(1,128)S(1)} %get-tuple-element.16), channel_id=1, source_target_pairs={{0,1},{1,2},{2,3},{3,4},{4,5},{5,6},{6,7},{7,8},{8,9},{9,10},{10,1... | collective-permute-start | bytes 49160 | tf_op jit(solution)/shard_map/ppermute | solution.py:14
  22.3 1.0 copy-start.11
  33.8 29.0 %all-to-all-start = ((f32[32,64,256]{2,0,1:T(8,128)}), f32[32,64,256]{2,0,1:T(8,128)S(1)}, u32[]{:S(2)}, u32[]{:S(2)}) async-start(f32[32,64,256]{2,0,1:T(8,128)} %copy.122), calls=%async_computation | async-start | bytes 4194304 | tf_op jit(solution)/shard_map/all_to_all | solution.py:81
  66.0 1.0 copy-start.7
  67.0 1.2 copy-start.18
  108.1 2.6 %copy-start.2 = (f32[128,8,512]{2,1,0:T(8,128)}, f32[128,8,512]{2,1,0:T(8,128)S(1)}, u32[]{:S(2)}) copy-start(f32[128,8,512]{2,1,0:T(8,128)S(1)} %all_to_all.56) | copy-start | bytes 6291460
  108.2 1.2 copy-start.9
  109.4 2.2 copy-start.1
  111.6 7.2 %copy-start.16 = (f32[127,8,256]{2,1,0:T(8,128)}, f32[127,8,256]{2,1,0:T(8,128)S(1)}, u32[]{:S(2)}) copy-start(f32[127,8,256]{2,1,0:T(8,128)S(1)} %slice.208) | copy-start | bytes 3121156
  113.5 5.7 %collective-permute-start.2 = (f32[128,1,256]{2,1,0:T(1,128)S(1)}, f32[128,1,256]{2,1,0:T(1,128)S(1)}, u32[]{:S(2)}, u32[]{:S(2)}) collective-permute-start(f32[128,1,256]{2,1,0:T(1,128)S(1)} %get-tuple-element.13), channel_id=1, source_target_pairs={{16,0},{32,16},{48,32},{64,48},{80,64},{96,80},{112,96},{1,112},{1... | collective-permute-start | bytes 393224 | tf_op jit(solution)/shard_map/ppermute | solution.py:60
  116.5 8.4 %collective-permute-start.3 = (f32[128,1,256]{2,1,0:T(1,128)S(1)}, f32[128,1,256]{2,1,0:T(1,128)S(1)}, u32[]{:S(2)}, u32[]{:S(2)}) collective-permute-start(f32[128,1,256]{2,1,0:T(1,128)S(1)} %get-tuple-element.14), channel_id=1, source_target_pairs={{0,16},{16,32},{32,48},{48,64},{64,80},{80,96},{96,112},{112,1},{1... | collective-permute-start | bytes 393224 | tf_op jit(solution)/shard_map/ppermute | solution.py:59
  161.0 1.3 copy-start.3
  166.8 29.4 %all-to-all-start.4 = ((f32[128,8,256]{2,1,0:T(8,128)}), f32[128,8,256]{2,1,0:T(8,128)}, u32[]{:S(2)}, u32[]{:S(2)}) async-start(f32[128,8,256]{2,1,0:T(8,128)} %convolution_bitcast_fusion), calls=%async_computation.4 | async-start | bytes 2097152 | tf_op jit(solution)/shard_map/all_to_all | solution.py:105
  172.8 9.8 %copy-start.4 = (f32[128,8,512]{2,1,0:T(8,128)S(1)}, f32[128,8,512]{2,1,0:T(8,128)}, u32[]{:S(2)}) copy-start(f32[128,8,512]{2,1,0:T(8,128)} %copy-done.3) | copy-start | bytes 6291460
  174.3 8.5 %copy-start.17 = (f32[127,8,256]{2,1,0:T(8,128)}, f32[127,8,256]{2,1,0:T(8,128)S(1)}, u32[]{:S(2)}) copy-start(f32[127,8,256]{2,1,0:T(8,128)S(1)} %slice.217) | copy-start | bytes 3121156
  174.5 13.5 %collective-permute-start.4 = (f32[128,1,256]{2,1,0:T(1,128)S(1)}, f32[128,1,256]{2,1,0:T(1,128)S(1)}, u32[]{:S(2)}, u32[]{:S(2)}) collective-permute-start(f32[128,1,256]{2,1,0:T(1,128)S(1)} %get-tuple-element.11), channel_id=1, source_target_pairs={{16,0},{32,16},{48,32},{64,48},{80,64},{96,80},{112,96},{1,112},{1... | collective-permute-start | bytes 393224 | tf_op jit(solution)/shard_map/ppermute | solution.py:60
  180.4 12.6 %collective-permute-start.5 = (f32[128,1,256]{2,1,0:T(1,128)S(1)}, f32[128,1,256]{2,1,0:T(1,128)S(1)}, u32[]{:S(2)}, u32[]{:S(2)}) collective-permute-start(f32[128,1,256]{2,1,0:T(1,128)S(1)} %get-tuple-element.12), channel_id=1, source_target_pairs={{0,16},{16,32},{32,48},{48,64},{64,80},{80,96},{96,112},{112,1},{1... | collective-permute-start | bytes 393224 | tf_op jit(solution)/shard_map/ppermute | solution.py:59
  194.1 1.0 copy-start.15
  196.2 1.5 copy-start.8
  196.2 1.8 copy-start.10
  238.2 7.8 %copy-start.14 = (f32[32,64,128]{2,1,0:T(8,128)S(1)}, f32[32,64,128]{2,1,0:T(8,128)}, u32[]{:S(2)}) copy-start(f32[32,64,128]{2,1,0:T(8,128)} %param.6) | copy-start | bytes 3145732
  238.5 7.6 %copy-start.6 = (f32[32,64,128]{2,1,0:T(8,128)S(1)}, f32[32,64,128]{2,1,0:T(8,128)}, u32[]{:S(2)}) copy-start(f32[32,64,128]{2,1,0:T(8,128)} %param.5) | copy-start | bytes 3145732
  238.5 7.6 %copy-start.12 = (f32[32,64,127]{2,1,0:T(8,128)S(1)}, f32[32,64,127]{2,1,0:T(8,128)}, u32[]{:S(2)}) copy-start(f32[32,64,127]{2,1,0:T(8,128)} %copy-done.11) | copy-start | bytes 3121156
  238.9 9.1 %collective-permute-start.6 = (f32[32,1,128]{2,1,0:T(1,128)S(1)}, f32[32,1,128]{2,1,0:T(1,128)S(1)}, u32[]{:S(2)}, u32[]{:S(2)}) collective-permute-start(f32[32,1,128]{2,1,0:T(1,128)S(1)} %get-tuple-element.5), channel_id=1, source_target_pairs={{1,0},{2,1},{3,2},{4,3},{5,4},{6,5},{7,6},{8,7},{9,8},{10,9},{11,1... | collective-permute-start | bytes 49160 | tf_op jit(solution)/shard_map/ppermute | solution.py:15
  241.6 6.3 %collective-permute-start.7 = (f32[32,1,128]{2,1,0:T(1,128)S(1)}, f32[32,1,128]{2,1,0:T(1,128)S(1)}, u32[]{:S(2)}, u32[]{:S(2)}) collective-permute-start(f32[32,1,128]{2,1,0:T(1,128)S(1)} %get-tuple-element.6), channel_id=1, source_target_pairs={{0,1},{1,2},{2,3},{3,4},{4,5},{5,6},{6,7},{7,8},{8,9},{9,10},{10,1... | collective-permute-start | bytes 49160 | tf_op jit(solution)/shard_map/ppermute | solution.py:14

commit v13 on v10

--- a/solution.py
+++ b/solution.py
@@ -135,7 +135,7 @@
     second0 = half0 + RATE * (xdiff(half0) + zoperate(half0, cx))
     count = lax.axis_size(LINES)
     s0y, ls1 = x_to_y(second0, lam_second1_y.reshape(count, -1, lam_second1_y.shape[1]))
-    ls1 = rows(ls1.reshape(second0.shape))
+    ls1 = ls1.reshape(second0.shape)
     state1_y = rows(along_y(inv_y, s0y, False))
     lam_half1 = ls1 + RATE * (xdiff(ls1) + zoperate(ls1, cx))
     lam_first1 = along_x(lam_half1, inv_x, True)

time: 250 us -> 249 us (level)
  transfers between devices with their start and end apart: 11 -> 11, of which waited for: 7 -> 7; matrix products, arithmetic and copies ran while one was open for 11% -> 12% of each run, Pallas kernels for 0% -> 0%
where the time goes in v13:
time: 249 us; the launch traced here: 248 us
  blocking collectives  105 us (42%)
  starting transfers between devices  48.9 us (20%)
  local copies, waits for them, and re-layouts  33.9 us (14%)
  waiting for transfers between devices  29.6 us (12%)
  matrix products  17.3 us (7%)
  other arithmetic  11.7 us (5%)
    all_to_all x2, blocking collectives, x_to_y(): lax.all_to_all(joined, LINES, split_axis=0, concat_axis=0, tiled=True)  74.7 us
    all_to_all x1, blocking collectives, x_to_block(): lax.all_to_all(joined, 'px', split_axis=0, concat_axis=1, tiled=True)  30.7 us
    all_to_all x1, starting transfers between devices, x_to_y(): lax.all_to_all(joined, LINES, split_axis=0, concat_axis=0, tiled=True)  11.5 us
    dot_general x3, matrix products, along_y(): return lax.dot_general(matrix, field, dims, precision=HIGH)  11.4 us
    unnamed x40, local copies, waits for them, and re-layouts  10.8 us
    ppermute x2, waiting for transfers between devices, ydiff(): lax.ppermute(jnp.concatenate([f[:, -1:] for f in fields]), ('px', 'py'), up)  10.7 us
    ppermute x2, starting transfers between devices, ydiff(): lax.ppermute(jnp.concatenate([f[:, :1] for f in fields]), ('px', 'py'), d...  8.87 us
    ppermute x2, starting transfers between devices, ydiff_block(): lax.ppermute(field[:, -1:], 'py', [(i, i + 1) for i in range(count - 1)])  8.53 us
  transfers between devices with their start and end apart: 11, of which 7 were waited for; matrix products, arithmetic and copies ran while one was open for 12% of the time, Pallas kernels for 0%

profile of v13, /device:TPU:1, one launch (start us, length us, event | category | flops | bytes accessed | tf_op | source)
XLA Modules:
  0.0 247.9 jit_solution(633726064491413368)
XLA Ops:
  0.7 2.7 %copy.129 = f32[128,8,256]{2,1,0:T(8,128)} copy(f32[128,8,256]{0,2,1:T(8,128)} %bitcast.103) | data formatting | bytes 2097152 | tf_op jit(solution)/shard_map/reshape | solution.py:113
  3.4 11.5 %all-to-all-start.1 = ((f32[128,8,256]{2,1,0:T(8,128)}), f32[128,8,256]{2,1,0:T(8,128)S(1)}, u32[]{:S(2)}, u32[]{:S(2)}) async-start(f32[128,8,256]{2,1,0:T(8,128)} %copy.129), calls=%async_computation.1 | async-start | bytes 2097152 | tf_op jit(solution)/shard_map/all_to_all | solution.py:95
  14.9 3.0 %collective-permute-start = (f32[32,1,128]{2,1,0:T(1,128)S(1)}, f32[32,1,128]{2,1,0:T(1,128)S(1)}, u32[]{:S(2)}, u32[]{:S(2)}) collective-permute-start(f32[32,1,128]{2,1,0:T(1,128)S(1)} %get-tuple-element.15), channel_id=1, source_target_pairs={{1,0},{2,1},{3,2},{4,3},{5,4},{6,5},{7,6},{8,7},{9,8},{10,9},{11,1... | collective-permute-start | bytes 49160 | tf_op jit(solution)/shard_map/ppermute | solution.py:15
  17.9 4.1 %collective-permute-start.1 = (f32[32,1,128]{2,1,0:T(1,128)S(1)}, f32[32,1,128]{2,1,0:T(1,128)S(1)}, u32[]{:S(2)}, u32[]{:S(2)}) collective-permute-start(f32[32,1,128]{2,1,0:T(1,128)S(1)} %get-tuple-element.16), channel_id=1, source_target_pairs={{0,1},{1,2},{2,3},{3,4},{4,5},{5,6},{6,7},{7,8},{8,9},{9,10},{10,1... | collective-permute-start | bytes 49160 | tf_op jit(solution)/shard_map/ppermute | solution.py:14
  23.6 6.3 %collective-permute-done = f32[32,1,128]{2,1,0:T(1,128)S(1)} collective-permute-done((f32[32,1,128]{2,1,0:T(1,128)S(1)}, f32[32,1,128]{2,1,0:T(1,128)S(1)}, u32[]{:S(2)}, u32[]{:S(2)}) %collective-permute-start) | collective-permute-done | bytes 16416 | tf_op jit(solution)/shard_map/ppermute | solution.py:15
  30.7 2.6 %copy.118 = f32[32,64,256]{2,0,1:T(8,128)} copy(f32[32,64,256]{2,1,0:T(8,128)S(1)} %pad_maximum_fusion) | data formatting | bytes 4194304 | tf_op jit(solution)/shard_map/concatenate | solution.py:80
  33.8 3.8 %all-to-all-start = ((f32[32,64,256]{2,0,1:T(8,128)}), f32[32,64,256]{2,0,1:T(8,128)S(1)}, u32[]{:S(2)}, u32[]{:S(2)}) async-start(f32[32,64,256]{2,0,1:T(8,128)} %copy.118), calls=%async_computation | async-start | bytes 4194304 | tf_op jit(solution)/shard_map/all_to_all | solution.py:81
  37.6 5.4 %copy.128 = f32[1024,1024]{0,1:T(8,128)} copy(f32[1024,1024]{1,0:T(8,128)} %param.9) | data formatting | bytes 8388608 | tf_op args[4]
  42.9 1.7 reshape_reshape.3
  44.7 4.2 %copy.130 = f32[16,64,8,32]{1,0,3,2:T(8,128)} copy(f32[16,64,8,32]{1,3,2,0:T(8,128)} %bitcast.101) | data formatting | bytes 2097152 | tf_op jit(solution)/shard_map/transpose | solution.py:121
  48.8 2.0 reshape.32
  50.8 5.0 %fusion = f32[128,8,256]{2,1,0:T(8,128)} fusion(f32[1024,1024]{0,1:T(8,128)} %copy.128, f32[1024,256]{0,1:T(8,128)S(1)} %reshape.32), kind=kOutput, calls=%fused_computation | convolution fusion | flops 1610612736 | bytes 6291456 | tf_op jit(solution)/shard_map/dot_general | solution.py:76
  55.8 7.0 %all-to-all-done = f32[32,64,256]{2,0,1:T(8,128)S(1)} async-done(((f32[32,64,256]{2,0,1:T(8,128)}), f32[32,64,256]{2,0,1:T(8,128)S(1)}, u32[]{:S(2)}, u32[]{:S(2)}) %all-to-all-start) | async-done | bytes 2097184 | tf_op jit(solution)/shard_map/all_to_all | solution.py:81
  68.6 39.5 %all_to_all.56 = f32[128,8,512]{2,1,0:T(8,128)S(1)} all-to-all(f32[128,8,512]{2,1,0:T(8,128)S(1)} %pad_maximum_fusion.1), channel_id=1, replica_groups=mesh['px'=8,'py'=16] {'py','px'}, dimensions={0} | all-to-all | bytes 4194304 | tf_op jit(solution)/shard_map/all_to_all | solution.py:95
  108.2 1.9 convolution_bitcast_fusion.2
  112.0 3.0 %collective-permute-start.2 = (f32[128,1,256]{2,1,0:T(1,128)S(1)}, f32[128,1,256]{2,1,0:T(1,128)S(1)}, u32[]{:S(2)}, u32[]{:S(2)}) collective-permute-start(f32[128,1,256]{2,1,0:T(1,128)S(1)} %get-tuple-element.13), channel_id=1, source_target_pairs={{16,0},{32,16},{48,32},{64,48},{80,64},{96,80},{112,96},{1,112},{1... | collective-permute-start | bytes 393224 | tf_op jit(solution)/shard_map/ppermute | solution.py:60
  115.0 2.3 collective-permute-start.3
  117.7 5.7 %collective-permute-done.3 = f32[128,1,256]{2,1,0:T(1,128)S(1)} collective-permute-done((f32[128,1,256]{2,1,0:T(1,128)S(1)}, f32[128,1,256]{2,1,0:T(1,128)S(1)}, u32[]{:S(2)}, u32[]{:S(2)}) %collective-permute-start.3) | collective-permute-done | bytes 131104 | tf_op jit(solution)/shard_map/ppermute | solution.py:59
  124.2 35.2 %all_to_all.57 = f32[128,8,512]{2,1,0:T(8,128)S(1)} all-to-all(f32[128,8,512]{2,1,0:T(8,128)S(1)} %pad_maximum_fusion.2), channel_id=1, replica_groups=mesh['px'=8,'py'=16] {'py','px'}, dimensions={0} | all-to-all | bytes 4194304 | tf_op jit(solution)/shard_map/all_to_all | solution.py:95
  160.8 4.5 %convolution_bitcast_fusion.1 = f32[128,8,256]{2,1,0:T(8,128)} fusion(f32[1024,1024]{1,0:T(8,128)S(1)} %copy-done.1, f32[1024,512]{1,0:T(8,128)S(1)} %bitcast.90), kind=kOutput, calls=%fused_computation.14 | convolution fusion | flops 1610612736 | bytes 6291456 | tf_op jit(solution)/shard_map/dot_general | solution.py:76
  165.3 6.0 %all-to-all-start.4 = ((f32[128,8,256]{2,1,0:T(8,128)}), f32[128,8,256]{2,1,0:T(8,128)}, u32[]{:S(2)}, u32[]{:S(2)}) async-start(f32[128,8,256]{2,1,0:T(8,128)} %convolution_bitcast_fusion.1), calls=%async_computation.4 | async-start | bytes 2097152 | tf_op jit(solution)/shard_map/all_to_all | solution.py:105
  173.0 5.9 %collective-permute-start.4 = (f32[128,1,256]{2,1,0:T(1,128)S(1)}, f32[128,1,256]{2,1,0:T(1,128)S(1)}, u32[]{:S(2)}, u32[]{:S(2)}) collective-permute-start(f32[128,1,256]{2,1,0:T(1,128)S(1)} %get-tuple-element.11), channel_id=1, source_target_pairs={{16,0},{32,16},{48,32},{64,48},{80,64},{96,80},{112,96},{1,112},{1... | collective-permute-start | bytes 393224 | tf_op jit(solution)/shard_map/ppermute | solution.py:60
  178.8 2.2 collective-permute-start.5
  181.4 5.0 %collective-permute-done.4 = f32[128,1,256]{2,1,0:T(1,128)S(1)} collective-permute-done((f32[128,1,256]{2,1,0:T(1,128)S(1)}, f32[128,1,256]{2,1,0:T(1,128)S(1)}, u32[]{:S(2)}, u32[]{:S(2)}) %collective-permute-start.4) | collective-permute-done | bytes 131104 | tf_op jit(solution)/shard_map/ppermute | solution.py:60
  186.5 5.0 %collective-permute-done.5 = f32[128,1,256]{2,1,0:T(1,128)S(1)} collective-permute-done((f32[128,1,256]{2,1,0:T(1,128)S(1)}, f32[128,1,256]{2,1,0:T(1,128)S(1)}, u32[]{:S(2)}, u32[]{:S(2)}) %collective-permute-start.5) | collective-permute-done | bytes 131104 | tf_op jit(solution)/shard_map/ppermute | solution.py:59
  196.5 4.1 %bitcast_multiply_fusion.1 = (f32[128,8,256]{2,1,0:T(8,128)S(1)}, f32[256,8,128]{0,1,2:T(8,128)S(1)}) fusion(f32[256,8,128]{0,1,2:T(8,128)S(1)} %copy.160, f32[128,8,256]{2,1,0:T(8,128)} %all-to-all-done.4, f32[127,8,256]{2,1,0:T(8,128)S(1)} %slice.217, f32[128,8,256]{2,1,0:T(8,128)S(1)} %fusion.67, f32[127,8,256]{2,1,0:T(8,128)S(1)} %copy-done.8, ...), kind=kLoop, calls=%fused_computation.71 | loop fusion | flops 3932160 | bytes 15679488 | tf_op jit(solution)/shard_map/mul | solution.py:38
  200.7 3.2 %convolution_bitcast_fusion = f32[256,8,128]{0,1,2:T(8,128)S(1)} fusion(f32[128,8,256]{2,1,0:T(8,128)} %all-to-all-done.4, f32[127,8,256]{2,1,0:T(8,128)S(1)} %slice.218, f32[256,8,128]{0,1,2:T(8,128)S(1)} %copy.160, f32[127,8,256]{2,1,0:T(8,128)S(1)} %slice.217, f32[256,256]{1,0:T(8,128)S(1)} %copy-done), kind=kOutput, calls=%fused_computation.13 | convolution fusion | flops 405012480 | bytes 5488640 | tf_op jit(solution)/shard_map/dot_general | solution.py:71
  204.0 2.0 copy.146
  206.0 30.7 %all_to_all.58 = f32[256,8,256]{2,1,0:T(8,128)S(1)} all-to-all(f32[256,8,256]{2,1,0:T(8,128)} %copy.146), channel_id=1, replica_groups=mesh['px'=8,'py'=16] {'px'}, dimensions={0} | all-to-all | bytes 4194304 | tf_op jit(solution)/shard_map/all_to_all | solution.py:88
  237.3 2.8 %collective-permute-start.6 = (f32[32,1,128]{2,1,0:T(1,128)S(1)}, f32[32,1,128]{2,1,0:T(1,128)S(1)}, u32[]{:S(2)}, u32[]{:S(2)}) collective-permute-start(f32[32,1,128]{2,1,0:T(1,128)S(1)} %get-tuple-element.5), channel_id=1, source_target_pairs={{1,0},{2,1},{3,2},{4,3},{5,4},{6,5},{7,6},{8,7},{9,8},{10,9},{11,1... | collective-permute-start | bytes 49160 | tf_op jit(solution)/shard_map/ppermute | solution.py:15
  240.1 4.4 %collective-permute-start.7 = (f32[32,1,128]{2,1,0:T(1,128)S(1)}, f32[32,1,128]{2,1,0:T(1,128)S(1)}, u32[]{:S(2)}, u32[]{:S(2)}) collective-permute-start(f32[32,1,128]{2,1,0:T(1,128)S(1)} %get-tuple-element.6), channel_id=1, source_target_pairs={{0,1},{1,2},{2,3},{3,4},{4,5},{5,6},{6,7},{7,8},{8,9},{9,10},{10,1... | collective-permute-start | bytes 49160 | tf_op jit(solution)/shard_map/ppermute | solution.py:14
  244.6 1.8 slice_subtract_fusion
  (84 shorter events, 22.4 us)
Async XLA Ops:
  0.6 64.7 %copy-start = (f32[256,256]{1,0:T(8,128)S(1)}, f32[256,256]{1,0:T(8,128)}, u32[]{:S(2)}) copy-start(f32[256,256]{1,0:T(8,128)} %param.8) | copy-start | bytes 786436
  0.6 14.2 %copy-start.5 = (f32[32,64,128]{2,1,0:T(8,128)S(1)}, f32[32,64,128]{2,1,0:T(8,128)}, u32[]{:S(2)}) copy-start(f32[32,64,128]{2,1,0:T(8,128)} %param.5) | copy-start | bytes 3145732
  3.4 19.9 %copy-start.13 = (f32[32,64,128]{2,1,0:T(8,128)S(1)}, f32[32,64,128]{2,1,0:T(8,128)}, u32[]{:S(2)}) copy-start(f32[32,64,128]{2,1,0:T(8,128)} %param.6) | copy-start | bytes 3145732
  3.4 30.4 %all-to-all-start.1 = ((f32[128,8,256]{2,1,0:T(8,128)}), f32[128,8,256]{2,1,0:T(8,128)S(1)}, u32[]{:S(2)}, u32[]{:S(2)}) async-start(f32[128,8,256]{2,1,0:T(8,128)} %copy.129), calls=%async_computation.1 | async-start | bytes 2097152 | tf_op jit(solution)/shard_map/all_to_all | solution.py:95
  14.9 15.0 %collective-permute-start = (f32[32,1,128]{2,1,0:T(1,128)S(1)}, f32[32,1,128]{2,1,0:T(1,128)S(1)}, u32[]{:S(2)}, u32[]{:S(2)}) collective-permute-start(f32[32,1,128]{2,1,0:T(1,128)S(1)} %get-tuple-element.15), channel_id=1, source_target_pairs={{1,0},{2,1},{3,2},{4,3},{5,4},{6,5},{7,6},{8,7},{9,8},{10,9},{11,1... | collective-permute-start | bytes 49160 | tf_op jit(solution)/shard_map/ppermute | solution.py:15
  17.9 12.0 %collective-permute-start.1 = (f32[32,1,128]{2,1,0:T(1,128)S(1)}, f32[32,1,128]{2,1,0:T(1,128)S(1)}, u32[]{:S(2)}, u32[]{:S(2)}) collective-permute-start(f32[32,1,128]{2,1,0:T(1,128)S(1)} %get-tuple-element.16), channel_id=1, source_target_pairs={{0,1},{1,2},{2,3},{3,4},{4,5},{5,6},{6,7},{7,8},{8,9},{9,10},{10,1... | collective-permute-start | bytes 49160 | tf_op jit(solution)/shard_map/ppermute | solution.py:14
  22.3 1.0 copy-start.11
  33.8 29.0 %all-to-all-start = ((f32[32,64,256]{2,0,1:T(8,128)}), f32[32,64,256]{2,0,1:T(8,128)S(1)}, u32[]{:S(2)}, u32[]{:S(2)}) async-start(f32[32,64,256]{2,0,1:T(8,128)} %copy.118), calls=%async_computation | async-start | bytes 4194304 | tf_op jit(solution)/shard_map/all_to_all | solution.py:81
  66.0 1.0 copy-start.7
  67.0 1.2 copy-start.18
  68.5 39.6 %copy-start.1 = (f32[1024,1024]{1,0:T(8,128)S(1)}, f32[1024,1024]{1,0:T(8,128)}, u32[]{:S(2)}) copy-start(f32[1024,1024]{1,0:T(8,128)} %param.9) | copy-start | bytes 12582916
  108.1 2.1 copy-start.2
  108.2 2.4 copy-start.9
  111.9 5.6 %copy-start.16 = (f32[127,8,256]{2,1,0:T(8,128)}, f32[127,8,256]{2,1,0:T(8,128)S(1)}, u32[]{:S(2)}) copy-start(f32[127,8,256]{2,1,0:T(8,128)S(1)} %slice.213) | copy-start | bytes 3121156
  112.0 5.7 %collective-permute-start.2 = (f32[128,1,256]{2,1,0:T(1,128)S(1)}, f32[128,1,256]{2,1,0:T(1,128)S(1)}, u32[]{:S(2)}, u32[]{:S(2)}) collective-permute-start(f32[128,1,256]{2,1,0:T(1,128)S(1)} %get-tuple-element.13), channel_id=1, source_target_pairs={{16,0},{32,16},{48,32},{64,48},{80,64},{96,80},{112,96},{1,112},{1... | collective-permute-start | bytes 393224 | tf_op jit(solution)/shard_map/ppermute | solution.py:60
  115.0 8.4 %collective-permute-start.3 = (f32[128,1,256]{2,1,0:T(1,128)S(1)}, f32[128,1,256]{2,1,0:T(1,128)S(1)}, u32[]{:S(2)}, u32[]{:S(2)}) collective-permute-start(f32[128,1,256]{2,1,0:T(1,128)S(1)} %get-tuple-element.14), channel_id=1, source_target_pairs={{0,16},{16,32},{32,48},{48,64},{64,80},{80,96},{96,112},{112,1},{1... | collective-permute-start | bytes 393224 | tf_op jit(solution)/shard_map/ppermute | solution.py:59
  159.4 1.3 copy-start.3
  165.3 29.4 %all-to-all-start.4 = ((f32[128,8,256]{2,1,0:T(8,128)}), f32[128,8,256]{2,1,0:T(8,128)}, u32[]{:S(2)}, u32[]{:S(2)}) async-start(f32[128,8,256]{2,1,0:T(8,128)} %convolution_bitcast_fusion.1), calls=%async_computation.4 | async-start | bytes 2097152 | tf_op jit(solution)/shard_map/all_to_all | solution.py:105
  171.3 9.8 %copy-start.4 = (f32[128,8,512]{2,1,0:T(8,128)S(1)}, f32[128,8,512]{2,1,0:T(8,128)}, u32[]{:S(2)}) copy-start(f32[128,8,512]{2,1,0:T(8,128)} %copy-done.3) | copy-start | bytes 6291460
  172.8 8.5 %copy-start.17 = (f32[127,8,256]{2,1,0:T(8,128)}, f32[127,8,256]{2,1,0:T(8,128)S(1)}, u32[]{:S(2)}) copy-start(f32[127,8,256]{2,1,0:T(8,128)S(1)} %slice.222) | copy-start | bytes 3121156
  173.0 13.5 %collective-permute-start.4 = (f32[128,1,256]{2,1,0:T(1,128)S(1)}, f32[128,1,256]{2,1,0:T(1,128)S(1)}, u32[]{:S(2)}, u32[]{:S(2)}) collective-permute-start(f32[128,1,256]{2,1,0:T(1,128)S(1)} %get-tuple-element.11), channel_id=1, source_target_pairs={{16,0},{32,16},{48,32},{64,48},{80,64},{96,80},{112,96},{1,112},{1... | collective-permute-start | bytes 393224 | tf_op jit(solution)/shard_map/ppermute | solution.py:60
  178.8 12.6 %collective-permute-start.5 = (f32[128,1,256]{2,1,0:T(1,128)S(1)}, f32[128,1,256]{2,1,0:T(1,128)S(1)}, u32[]{:S(2)}, u32[]{:S(2)}) collective-permute-start(f32[128,1,256]{2,1,0:T(1,128)S(1)} %get-tuple-element.12), channel_id=1, source_target_pairs={{0,16},{16,32},{32,48},{48,64},{64,80},{80,96},{96,112},{112,1},{1... | collective-permute-start | bytes 393224 | tf_op jit(solution)/shard_map/ppermute | solution.py:59
  192.6 1.0 copy-start.15
  194.6 1.5 copy-start.8
  194.6 1.8 copy-start.10
  236.7 7.8 %copy-start.14 = (f32[32,64,128]{2,1,0:T(8,128)S(1)}, f32[32,64,128]{2,1,0:T(8,128)}, u32[]{:S(2)}) copy-start(f32[32,64,128]{2,1,0:T(8,128)} %param.6) | copy-start | bytes 3145732
  236.9 7.6 %copy-start.6 = (f32[32,64,128]{2,1,0:T(8,128)S(1)}, f32[32,64,128]{2,1,0:T(8,128)}, u32[]{:S(2)}) copy-start(f32[32,64,128]{2,1,0:T(8,128)} %param.5) | copy-start | bytes 3145732
  237.0 7.6 %copy-start.12 = (f32[32,64,127]{2,1,0:T(8,128)S(1)}, f32[32,64,127]{2,1,0:T(8,128)}, u32[]{:S(2)}) copy-start(f32[32,64,127]{2,1,0:T(8,128)} %copy-done.11) | copy-start | bytes 3121156
  237.3 9.1 %collective-permute-start.6 = (f32[32,1,128]{2,1,0:T(1,128)S(1)}, f32[32,1,128]{2,1,0:T(1,128)S(1)}, u32[]{:S(2)}, u32[]{:S(2)}) collective-permute-start(f32[32,1,128]{2,1,0:T(1,128)S(1)} %get-tuple-element.5), channel_id=1, source_target_pairs={{1,0},{2,1},{3,2},{4,3},{5,4},{6,5},{7,6},{8,7},{9,8},{10,9},{11,1... | collective-permute-start | bytes 49160 | tf_op jit(solution)/shard_map/ppermute | solution.py:15
  240.1 6.3 %collective-permute-start.7 = (f32[32,1,128]{2,1,0:T(1,128)S(1)}, f32[32,1,128]{2,1,0:T(1,128)S(1)}, u32[]{:S(2)}, u32[]{:S(2)}) collective-permute-start(f32[32,1,128]{2,1,0:T(1,128)S(1)} %get-tuple-element.6), channel_id=1, source_target_pairs={{0,1},{1,2},{2,3},{3,4},{4,5},{5,6},{6,7},{7,8},{8,9},{9,10},{10,1... | collective-permute-start | bytes 49160 | tf_op jit(solution)/shard_map/ppermute | solution.py:14

commit v14 on v13

--- a/solution.py
+++ b/solution.py
@@ -142,7 +142,7 @@
     (dy_lam_first1,) = ydiff(lam_first1)
     lam_state1 = lam_first1 + RATE * (dy_lam_first1 + zoperate(lam_first1, cx))
     lsy, state1 = x_to_y(rows(lam_state1), state1_y.reshape(lam_state1.shape))
-    state1 = rows(state1.reshape(lam_state1.shape))
+    state1 = state1.reshape(lam_state1.shape)
     (dy_state1,) = ydiff(state1)
     first1 = state1 + RATE * (dy_state1 + zoperate(state1, cx))
     half1 = along_x(first1, inv_x, False)

time: 249 us -> 250 us (level)
  local copies, waits for them, and re-layouts: 33.9 us -> 36.4 us
    unnamed x40 -> x42, local copies, waits for them, and re-layouts: 10.8 us -> 10.7 us
where the time goes in v14:
time: 250 us; the launch traced here: 249 us
  blocking collectives  106 us (42%)
  starting transfers between devices  48.9 us (20%)
  local copies, waits for them, and re-layouts  36.4 us (15%)
  waiting for transfers between devices  27.6 us (11%)
  matrix products  17.3 us (7%)
  other arithmetic  11.7 us (5%)
    all_to_all x2, blocking collectives, x_to_y(): lax.all_to_all(joined, LINES, split_axis=0, concat_axis=0, tiled=True)  74.7 us
    all_to_all x1, blocking collectives, x_to_block(): lax.all_to_all(joined, 'px', split_axis=0, concat_axis=1, tiled=True)  31.2 us
    all_to_all x1, starting transfers between devices, x_to_y(): lax.all_to_all(joined, LINES, split_axis=0, concat_axis=0, tiled=True)  11.5 us
    dot_general x3, matrix products, along_y(): return lax.dot_general(matrix, field, dims, precision=HIGH)  11.4 us
    ppermute x2, waiting for transfers between devices, ydiff(): lax.ppermute(jnp.concatenate([f[:, -1:] for f in fields]), ('px', 'py'), up)  10.9 us
    unnamed x42, local copies, waits for them, and re-layouts  10.7 us
    ppermute x2, starting transfers between devices, ydiff(): lax.ppermute(jnp.concatenate([f[:, :1] for f in fields]), ('px', 'py'), d...  8.86 us
    ppermute x2, starting transfers between devices, ydiff_block(): lax.ppermute(field[:, -1:], 'py', [(i, i + 1) for i in range(count - 1)])  8.71 us
  transfers between devices with their start and end apart: 11, of which 7 were waited for; matrix products, arithmetic and copies ran while one was open for 12% of the time, Pallas kernels for 0%

profile of v14, /device:TPU:1, one launch (start us, length us, event | category | flops | bytes accessed | tf_op | source)
XLA Modules:
  0.0 248.9 jit_solution(4729065358446858863)
XLA Ops:
  0.7 2.7 %copy.129 = f32[128,8,256]{2,1,0:T(8,128)} copy(f32[128,8,256]{0,2,1:T(8,128)} %bitcast.106) | data formatting | bytes 2097152 | tf_op jit(solution)/shard_map/reshape | solution.py:113
  3.4 11.5 %all-to-all-start.1 = ((f32[128,8,256]{2,1,0:T(8,128)}), f32[128,8,256]{2,1,0:T(8,128)S(1)}, u32[]{:S(2)}, u32[]{:S(2)}) async-start(f32[128,8,256]{2,1,0:T(8,128)} %copy.129), calls=%async_computation.1 | async-start | bytes 2097152 | tf_op jit(solution)/shard_map/all_to_all | solution.py:95
  14.9 3.0 %collective-permute-start = (f32[32,1,128]{2,1,0:T(1,128)S(1)}, f32[32,1,128]{2,1,0:T(1,128)S(1)}, u32[]{:S(2)}, u32[]{:S(2)}) collective-permute-start(f32[32,1,128]{2,1,0:T(1,128)S(1)} %get-tuple-element.15), channel_id=1, source_target_pairs={{1,0},{2,1},{3,2},{4,3},{5,4},{6,5},{7,6},{8,7},{9,8},{10,9},{11,1... | collective-permute-start | bytes 49160 | tf_op jit(solution)/shard_map/ppermute | solution.py:15
  17.9 4.1 %collective-permute-start.1 = (f32[32,1,128]{2,1,0:T(1,128)S(1)}, f32[32,1,128]{2,1,0:T(1,128)S(1)}, u32[]{:S(2)}, u32[]{:S(2)}) collective-permute-start(f32[32,1,128]{2,1,0:T(1,128)S(1)} %get-tuple-element.16), channel_id=1, source_target_pairs={{0,1},{1,2},{2,3},{3,4},{4,5},{5,6},{6,7},{7,8},{8,9},{9,10},{10,1... | collective-permute-start | bytes 49160 | tf_op jit(solution)/shard_map/ppermute | solution.py:14
  23.6 6.3 %collective-permute-done = f32[32,1,128]{2,1,0:T(1,128)S(1)} collective-permute-done((f32[32,1,128]{2,1,0:T(1,128)S(1)}, f32[32,1,128]{2,1,0:T(1,128)S(1)}, u32[]{:S(2)}, u32[]{:S(2)}) %collective-permute-start) | collective-permute-done | bytes 16416 | tf_op jit(solution)/shard_map/ppermute | solution.py:15
  30.7 2.6 %copy.118 = f32[32,64,256]{2,0,1:T(8,128)} copy(f32[32,64,256]{2,1,0:T(8,128)S(1)} %pad_maximum_fusion) | data formatting | bytes 4194304 | tf_op jit(solution)/shard_map/concatenate | solution.py:80
  33.8 3.8 %all-to-all-start = ((f32[32,64,256]{2,0,1:T(8,128)}), f32[32,64,256]{2,0,1:T(8,128)S(1)}, u32[]{:S(2)}, u32[]{:S(2)}) async-start(f32[32,64,256]{2,0,1:T(8,128)} %copy.118), calls=%async_computation | async-start | bytes 4194304 | tf_op jit(solution)/shard_map/all_to_all | solution.py:81
  37.6 5.4 %copy.128 = f32[1024,1024]{0,1:T(8,128)} copy(f32[1024,1024]{1,0:T(8,128)} %param.9) | data formatting | bytes 8388608 | tf_op args[4]
  44.7 4.2 %copy.130 = f32[16,64,8,32]{1,0,3,2:T(8,128)} copy(f32[16,64,8,32]{1,3,2,0:T(8,128)} %bitcast.104) | data formatting | bytes 2097152 | tf_op jit(solution)/shard_map/transpose | solution.py:121
  48.8 2.0 reshape.33
  50.9 5.0 %fusion = f32[128,8,256]{2,1,0:T(8,128)} fusion(f32[1024,1024]{0,1:T(8,128)} %copy.128, f32[1024,256]{0,1:T(8,128)S(1)} %reshape.33), kind=kOutput, calls=%fused_computation | convolution fusion | flops 1610612736 | bytes 6291456 | tf_op jit(solution)/shard_map/dot_general | solution.py:76
  55.8 7.0 %all-to-all-done = f32[32,64,256]{2,0,1:T(8,128)S(1)} async-done(((f32[32,64,256]{2,0,1:T(8,128)}), f32[32,64,256]{2,0,1:T(8,128)S(1)}, u32[]{:S(2)}, u32[]{:S(2)}) %all-to-all-start) | async-done | bytes 2097184 | tf_op jit(solution)/shard_map/all_to_all | solution.py:81
  68.6 39.5 %all_to_all.56 = f32[128,8,512]{2,1,0:T(8,128)S(1)} all-to-all(f32[128,8,512]{2,1,0:T(8,128)S(1)} %pad_maximum_fusion.1), channel_id=1, replica_groups=mesh['px'=8,'py'=16] {'py','px'}, dimensions={0} | all-to-all | bytes 4194304 | tf_op jit(solution)/shard_map/all_to_all | solution.py:95
  108.2 1.9 convolution_bitcast_fusion.2
  112.0 3.0 %collective-permute-start.2 = (f32[128,1,256]{2,1,0:T(1,128)S(1)}, f32[128,1,256]{2,1,0:T(1,128)S(1)}, u32[]{:S(2)}, u32[]{:S(2)}) collective-permute-start(f32[128,1,256]{2,1,0:T(1,128)S(1)} %get-tuple-element.13), channel_id=1, source_target_pairs={{16,0},{32,16},{48,32},{64,48},{80,64},{96,80},{112,96},{1,112},{1... | collective-permute-start | bytes 393224 | tf_op jit(solution)/shard_map/ppermute | solution.py:60
  115.0 2.3 collective-permute-start.3
  117.7 5.7 %collective-permute-done.3 = f32[128,1,256]{2,1,0:T(1,128)S(1)} collective-permute-done((f32[128,1,256]{2,1,0:T(1,128)S(1)}, f32[128,1,256]{2,1,0:T(1,128)S(1)}, u32[]{:S(2)}, u32[]{:S(2)}) %collective-permute-start.3) | collective-permute-done | bytes 131104 | tf_op jit(solution)/shard_map/ppermute | solution.py:59
  124.2 35.2 %all_to_all.57 = f32[128,8,512]{2,1,0:T(8,128)S(1)} all-to-all(f32[128,8,512]{2,1,0:T(8,128)S(1)} %pad_maximum_fusion.2), channel_id=1, replica_groups=mesh['px'=8,'py'=16] {'py','px'}, dimensions={0} | all-to-all | bytes 4194304 | tf_op jit(solution)/shard_map/all_to_all | solution.py:95
  161.1 4.5 %convolution_bitcast_fusion.1 = f32[128,8,256]{2,1,0:T(8,128)} fusion(f32[1024,1024]{1,0:T(8,128)S(1)} %copy-done.1, f32[1024,512]{1,0:T(8,128)S(1)} %bitcast.93), kind=kOutput, calls=%fused_computation.14 | convolution fusion | flops 1610612736 | bytes 6291456 | tf_op jit(solution)/shard_map/dot_general | solution.py:76
  165.6 6.0 %all-to-all-start.4 = ((f32[128,8,256]{2,1,0:T(8,128)}), f32[128,8,256]{2,1,0:T(8,128)}, u32[]{:S(2)}, u32[]{:S(2)}) async-start(f32[128,8,256]{2,1,0:T(8,128)} %convolution_bitcast_fusion.1), calls=%async_computation.4 | async-start | bytes 2097152 | tf_op jit(solution)/shard_map/all_to_all | solution.py:105
  171.6 1.9 fusion.81
  173.5 5.9 %collective-permute-start.4 = (f32[128,1,256]{2,1,0:T(1,128)S(1)}, f32[128,1,256]{2,1,0:T(1,128)S(1)}, u32[]{:S(2)}, u32[]{:S(2)}) collective-permute-start(f32[128,1,256]{2,1,0:T(1,128)S(1)} %get-tuple-element.11), channel_id=1, source_target_pairs={{16,0},{32,16},{48,32},{64,48},{80,64},{96,80},{112,96},{1,112},{1... | collective-permute-start | bytes 393224 | tf_op jit(solution)/shard_map/ppermute | solution.py:60
  179.4 2.2 collective-permute-start.5
  183.9 2.9 %collective-permute-done.4 = f32[128,1,256]{2,1,0:T(1,128)S(1)} collective-permute-done((f32[128,1,256]{2,1,0:T(1,128)S(1)}, f32[128,1,256]{2,1,0:T(1,128)S(1)}, u32[]{:S(2)}, u32[]{:S(2)}) %collective-permute-start.4) | collective-permute-done | bytes 131104 | tf_op jit(solution)/shard_map/ppermute | solution.py:60
  186.8 5.2 %collective-permute-done.5 = f32[128,1,256]{2,1,0:T(1,128)S(1)} collective-permute-done((f32[128,1,256]{2,1,0:T(1,128)S(1)}, f32[128,1,256]{2,1,0:T(1,128)S(1)}, u32[]{:S(2)}, u32[]{:S(2)}) %collective-permute-start.5) | collective-permute-done | bytes 131104 | tf_op jit(solution)/shard_map/ppermute | solution.py:59
  197.0 4.1 %bitcast_multiply_fusion.1 = (f32[128,8,256]{2,1,0:T(8,128)S(1)}, f32[256,8,128]{0,1,2:T(8,128)S(1)}) fusion(f32[256,8,128]{0,1,2:T(8,128)S(1)} %copy.160, f32[128,8,256]{2,1,0:T(8,128)} %all-to-all-done.4, f32[127,8,256]{2,1,0:T(8,128)S(1)} %slice.222, f32[128,8,256]{2,1,0:T(8,128)S(1)} %fusion.67, f32[127,8,256]{2,1,0:T(8,128)S(1)} %copy-done.8, ...), kind=kLoop, calls=%fused_computation.71 | loop fusion | flops 3932160 | bytes 15679488 | tf_op jit(solution)/shard_map/mul | solution.py:38
  201.2 3.2 %convolution_bitcast_fusion = f32[256,8,128]{0,1,2:T(8,128)S(1)} fusion(f32[128,8,256]{2,1,0:T(8,128)} %all-to-all-done.4, f32[127,8,256]{2,1,0:T(8,128)S(1)} %slice.223, f32[256,8,128]{0,1,2:T(8,128)S(1)} %copy.160, f32[127,8,256]{2,1,0:T(8,128)S(1)} %slice.222, f32[256,256]{1,0:T(8,128)S(1)} %copy-done), kind=kOutput, calls=%fused_computation.13 | convolution fusion | flops 405012480 | bytes 5488640 | tf_op jit(solution)/shard_map/dot_general | solution.py:71
  204.5 2.0 copy.146
  206.5 31.2 %all_to_all.58 = f32[256,8,256]{2,1,0:T(8,128)S(1)} all-to-all(f32[256,8,256]{2,1,0:T(8,128)} %copy.146), channel_id=1, replica_groups=mesh['px'=8,'py'=16] {'px'}, dimensions={0} | all-to-all | bytes 4194304 | tf_op jit(solution)/shard_map/all_to_all | solution.py:88
  238.3 2.6 %collective-permute-start.6 = (f32[32,1,128]{2,1,0:T(1,128)S(1)}, f32[32,1,128]{2,1,0:T(1,128)S(1)}, u32[]{:S(2)}, u32[]{:S(2)}) collective-permute-start(f32[32,1,128]{2,1,0:T(1,128)S(1)} %get-tuple-element.5), channel_id=1, source_target_pairs={{1,0},{2,1},{3,2},{4,3},{5,4},{6,5},{7,6},{8,7},{9,8},{10,9},{11,1... | collective-permute-start | bytes 49160 | tf_op jit(solution)/shard_map/ppermute | solution.py:15
  240.9 4.6 %collective-permute-start.7 = (f32[32,1,128]{2,1,0:T(1,128)S(1)}, f32[32,1,128]{2,1,0:T(1,128)S(1)}, u32[]{:S(2)}, u32[]{:S(2)}) collective-permute-start(f32[32,1,128]{2,1,0:T(1,128)S(1)} %get-tuple-element.6), channel_id=1, source_target_pairs={{0,1},{1,2},{2,3},{3,4},{4,5},{5,6},{6,7},{7,8},{8,9},{9,10},{10,1... | collective-permute-start | bytes 49160 | tf_op jit(solution)/shard_map/ppermute | solution.py:14
  245.6 1.8 slice_subtract_fusion
  (86 shorter events, 24.8 us)
Async XLA Ops:
  0.6 64.7 %copy-start = (f32[256,256]{1,0:T(8,128)S(1)}, f32[256,256]{1,0:T(8,128)}, u32[]{:S(2)}) copy-start(f32[256,256]{1,0:T(8,128)} %param.8) | copy-start | bytes 786436
  0.6 14.2 %copy-start.5 = (f32[32,64,128]{2,1,0:T(8,128)S(1)}, f32[32,64,128]{2,1,0:T(8,128)}, u32[]{:S(2)}) copy-start(f32[32,64,128]{2,1,0:T(8,128)} %param.5) | copy-start | bytes 3145732
  3.4 20.0 %copy-start.13 = (f32[32,64,128]{2,1,0:T(8,128)S(1)}, f32[32,64,128]{2,1,0:T(8,128)}, u32[]{:S(2)}) copy-start(f32[32,64,128]{2,1,0:T(8,128)} %param.6) | copy-start | bytes 3145732
  3.4 30.4 %all-to-all-start.1 = ((f32[128,8,256]{2,1,0:T(8,128)}), f32[128,8,256]{2,1,0:T(8,128)S(1)}, u32[]{:S(2)}, u32[]{:S(2)}) async-start(f32[128,8,256]{2,1,0:T(8,128)} %copy.129), calls=%async_computation.1 | async-start | bytes 2097152 | tf_op jit(solution)/shard_map/all_to_all | solution.py:95
  14.9 15.0 %collective-permute-start = (f32[32,1,128]{2,1,0:T(1,128)S(1)}, f32[32,1,128]{2,1,0:T(1,128)S(1)}, u32[]{:S(2)}, u32[]{:S(2)}) collective-permute-start(f32[32,1,128]{2,1,0:T(1,128)S(1)} %get-tuple-element.15), channel_id=1, source_target_pairs={{1,0},{2,1},{3,2},{4,3},{5,4},{6,5},{7,6},{8,7},{9,8},{10,9},{11,1... | collective-permute-start | bytes 49160 | tf_op jit(solution)/shard_map/ppermute | solution.py:15
  17.9 12.0 %collective-permute-start.1 = (f32[32,1,128]{2,1,0:T(1,128)S(1)}, f32[32,1,128]{2,1,0:T(1,128)S(1)}, u32[]{:S(2)}, u32[]{:S(2)}) collective-permute-start(f32[32,1,128]{2,1,0:T(1,128)S(1)} %get-tuple-element.16), channel_id=1, source_target_pairs={{0,1},{1,2},{2,3},{3,4},{4,5},{5,6},{6,7},{7,8},{8,9},{9,10},{10,1... | collective-permute-start | bytes 49160 | tf_op jit(solution)/shard_map/ppermute | solution.py:14
  22.3 1.0 copy-start.11
  33.8 29.0 %all-to-all-start = ((f32[32,64,256]{2,0,1:T(8,128)}), f32[32,64,256]{2,0,1:T(8,128)S(1)}, u32[]{:S(2)}, u32[]{:S(2)}) async-start(f32[32,64,256]{2,0,1:T(8,128)} %copy.118), calls=%async_computation | async-start | bytes 4194304 | tf_op jit(solution)/shard_map/all_to_all | solution.py:81
  66.0 1.0 copy-start.7
  67.0 1.2 copy-start.19
  68.5 39.6 %copy-start.1 = (f32[1024,1024]{1,0:T(8,128)S(1)}, f32[1024,1024]{1,0:T(8,128)}, u32[]{:S(2)}) copy-start(f32[1024,1024]{1,0:T(8,128)} %param.9) | copy-start | bytes 12582916
  108.1 2.1 copy-start.2
  108.2 2.4 copy-start.9
  111.9 5.6 %copy-start.16 = (f32[127,8,256]{2,1,0:T(8,128)}, f32[127,8,256]{2,1,0:T(8,128)S(1)}, u32[]{:S(2)}) copy-start(f32[127,8,256]{2,1,0:T(8,128)S(1)} %slice.218) | copy-start | bytes 3121156
  112.0 5.7 %collective-permute-start.2 = (f32[128,1,256]{2,1,0:T(1,128)S(1)}, f32[128,1,256]{2,1,0:T(1,128)S(1)}, u32[]{:S(2)}, u32[]{:S(2)}) collective-permute-start(f32[128,1,256]{2,1,0:T(1,128)S(1)} %get-tuple-element.13), channel_id=1, source_target_pairs={{16,0},{32,16},{48,32},{64,48},{80,64},{96,80},{112,96},{1,112},{1... | collective-permute-start | bytes 393224 | tf_op jit(solution)/shard_map/ppermute | solution.py:60
  115.0 8.4 %collective-permute-start.3 = (f32[128,1,256]{2,1,0:T(1,128)S(1)}, f32[128,1,256]{2,1,0:T(1,128)S(1)}, u32[]{:S(2)}, u32[]{:S(2)}) collective-permute-start(f32[128,1,256]{2,1,0:T(1,128)S(1)} %get-tuple-element.14), channel_id=1, source_target_pairs={{0,16},{16,32},{32,48},{48,64},{64,80},{80,96},{96,112},{112,1},{1... | collective-permute-start | bytes 393224 | tf_op jit(solution)/shard_map/ppermute | solution.py:59
  159.4 1.7 copy-start.3
  165.6 29.5 %all-to-all-start.4 = ((f32[128,8,256]{2,1,0:T(8,128)}), f32[128,8,256]{2,1,0:T(8,128)}, u32[]{:S(2)}, u32[]{:S(2)}) async-start(f32[128,8,256]{2,1,0:T(8,128)} %convolution_bitcast_fusion.1), calls=%async_computation.4 | async-start | bytes 2097152 | tf_op jit(solution)/shard_map/all_to_all | solution.py:105
  171.6 11.2 %copy-start.4 = (f32[128,8,512]{2,1,0:T(8,128)S(1)}, f32[128,8,512]{2,1,0:T(8,128)}, u32[]{:S(2)}) copy-start(f32[128,8,512]{2,1,0:T(8,128)} %copy-done.3) | copy-start | bytes 6291460
  173.5 13.3 %collective-permute-start.4 = (f32[128,1,256]{2,1,0:T(1,128)S(1)}, f32[128,1,256]{2,1,0:T(1,128)S(1)}, u32[]{:S(2)}, u32[]{:S(2)}) collective-permute-start(f32[128,1,256]{2,1,0:T(1,128)S(1)} %get-tuple-element.11), channel_id=1, source_target_pairs={{16,0},{32,16},{48,32},{64,48},{80,64},{96,80},{112,96},{1,112},{1... | collective-permute-start | bytes 393224 | tf_op jit(solution)/shard_map/ppermute | solution.py:60
  179.4 12.6 %collective-permute-start.5 = (f32[128,1,256]{2,1,0:T(1,128)S(1)}, f32[128,1,256]{2,1,0:T(1,128)S(1)}, u32[]{:S(2)}, u32[]{:S(2)}) collective-permute-start(f32[128,1,256]{2,1,0:T(1,128)S(1)} %get-tuple-element.12), channel_id=1, source_target_pairs={{0,16},{16,32},{32,48},{48,64},{64,80},{80,96},{96,112},{112,1},{1... | collective-permute-start | bytes 393224 | tf_op jit(solution)/shard_map/ppermute | solution.py:59
  182.9 1.1 copy-start.17
  182.9 9.1 %copy-start.18 = (f32[128,8,256]{2,1,0:T(8,128)S(1)}, f32[128,8,256]{2,1,0:T(8,128)}, u32[]{:S(2)}) copy-start(f32[128,8,256]{2,1,0:T(8,128)} %slice_bitcast_fusion) | copy-start | bytes 3145732
  193.1 1.0 copy-start.15
  195.1 1.5 copy-start.8
  195.1 1.8 copy-start.10
  237.7 7.8 %copy-start.14 = (f32[32,64,128]{2,1,0:T(8,128)S(1)}, f32[32,64,128]{2,1,0:T(8,128)}, u32[]{:S(2)}) copy-start(f32[32,64,128]{2,1,0:T(8,128)} %param.6) | copy-start | bytes 3145732
  237.9 7.6 %copy-start.6 = (f32[32,64,128]{2,1,0:T(8,128)S(1)}, f32[32,64,128]{2,1,0:T(8,128)}, u32[]{:S(2)}) copy-start(f32[32,64,128]{2,1,0:T(8,128)} %param.5) | copy-start | bytes 3145732
  237.9 7.6 %copy-start.12 = (f32[32,64,127]{2,1,0:T(8,128)S(1)}, f32[32,64,127]{2,1,0:T(8,128)}, u32[]{:S(2)}) copy-start(f32[32,64,127]{2,1,0:T(8,128)} %copy-done.11) | copy-start | bytes 3121156
  238.3 9.1 %collective-permute-start.6 = (f32[32,1,128]{2,1,0:T(1,128)S(1)}, f32[32,1,128]{2,1,0:T(1,128)S(1)}, u32[]{:S(2)}, u32[]{:S(2)}) collective-permute-start(f32[32,1,128]{2,1,0:T(1,128)S(1)} %get-tuple-element.5), channel_id=1, source_target_pairs={{1,0},{2,1},{3,2},{4,3},{5,4},{6,5},{7,6},{8,7},{9,8},{10,9},{11,1... | collective-permute-start | bytes 49160 | tf_op jit(solution)/shard_map/ppermute | solution.py:15
  240.9 6.5 %collective-permute-start.7 = (f32[32,1,128]{2,1,0:T(1,128)S(1)}, f32[32,1,128]{2,1,0:T(1,128)S(1)}, u32[]{:S(2)}, u32[]{:S(2)}) collective-permute-start(f32[32,1,128]{2,1,0:T(1,128)S(1)} %get-tuple-element.6), channel_id=1, source_target_pairs={{0,1},{1,2},{2,3},{3,4},{4,5},{5,6},{6,7},{7,8},{8,9},{9,10},{10,1... | collective-permute-start | bytes 49160 | tf_op jit(solution)/shard_map/ppermute | solution.py:14

commit v15 on v13

--- a/solution.py
+++ b/solution.py
@@ -141,7 +141,7 @@
     lam_first1 = along_x(lam_half1, inv_x, True)
     (dy_lam_first1,) = ydiff(lam_first1)
     lam_state1 = lam_first1 + RATE * (dy_lam_first1 + zoperate(lam_first1, cx))
-    lsy, state1 = x_to_y(rows(lam_state1), state1_y.reshape(lam_state1.shape))
+    lsy, state1 = x_to_y(lam_state1, state1_y.reshape(lam_state1.shape))
     state1 = rows(state1.reshape(lam_state1.shape))
     (dy_state1,) = ydiff(state1)
     first1 = state1 + RATE * (dy_state1 + zoperate(state1, cx))

time: 249 us -> 249 us (level)
  no operation moved by 1% of the time
where the time goes in v15:
time: 249 us; the launch traced here: 248 us
  blocking collectives  105 us (42%)
  starting transfers between devices  48.9 us (20%)
  local copies, waits for them, and re-layouts  33.9 us (14%)
  waiting for transfers between devices  29.6 us (12%)
  matrix products  17.3 us (7%)
  other arithmetic  11.7 us (5%)
    all_to_all x2, blocking collectives, x_to_y(): lax.all_to_all(joined, LINES, split_axis=0, concat_axis=0, tiled=True)  74.7 us
    all_to_all x1, blocking collectives, x_to_block(): lax.all_to_all(joined, 'px', split_axis=0, concat_axis=1, tiled=True)  30.7 us
    all_to_all x1, starting transfers between devices, x_to_y(): lax.all_to_all(joined, LINES, split_axis=0, concat_axis=0, tiled=True)  11.5 us
    dot_general x3, matrix products, along_y(): return lax.dot_general(matrix, field, dims, precision=HIGH)  11.4 us
    unnamed x40, local copies, waits for them, and re-layouts  10.8 us
    ppermute x2, waiting for transfers between devices, ydiff(): lax.ppermute(jnp.concatenate([f[:, -1:] for f in fields]), ('px', 'py'), up)  10.7 us
    ppermute x2, starting transfers between devices, ydiff(): lax.ppermute(jnp.concatenate([f[:, :1] for f in fields]), ('px', 'py'), d...  8.87 us
    ppermute x2, starting transfers between devices, ydiff_block(): lax.ppermute(field[:, -1:], 'py', [(i, i + 1) for i in range(count - 1)])  8.53 us
  transfers between devices with their start and end apart: 11, of which 7 were waited for; matrix products, arithmetic and copies ran while one was open for 12% of the time, Pallas kernels for 0%

profile of v15, /device:TPU:1, one launch (start us, length us, event | category | flops | bytes accessed | tf_op | source)
XLA Modules:
  0.0 247.9 jit_solution(633726064491413368)
XLA Ops:
  0.7 2.7 %copy.129 = f32[128,8,256]{2,1,0:T(8,128)} copy(f32[128,8,256]{0,2,1:T(8,128)} %bitcast.103) | data formatting | bytes 2097152 | tf_op jit(solution)/shard_map/reshape | solution.py:113
  3.4 11.5 %all-to-all-start.1 = ((f32[128,8,256]{2,1,0:T(8,128)}), f32[128,8,256]{2,1,0:T(8,128)S(1)}, u32[]{:S(2)}, u32[]{:S(2)}) async-start(f32[128,8,256]{2,1,0:T(8,128)} %copy.129), calls=%async_computation.1 | async-start | bytes 2097152 | tf_op jit(solution)/shard_map/all_to_all | solution.py:95
  14.9 3.0 %collective-permute-start = (f32[32,1,128]{2,1,0:T(1,128)S(1)}, f32[32,1,128]{2,1,0:T(1,128)S(1)}, u32[]{:S(2)}, u32[]{:S(2)}) collective-permute-start(f32[32,1,128]{2,1,0:T(1,128)S(1)} %get-tuple-element.15), channel_id=1, source_target_pairs={{1,0},{2,1},{3,2},{4,3},{5,4},{6,5},{7,6},{8,7},{9,8},{10,9},{11,1... | collective-permute-start | bytes 49160 | tf_op jit(solution)/shard_map/ppermute | solution.py:15
  17.9 4.1 %collective-permute-start.1 = (f32[32,1,128]{2,1,0:T(1,128)S(1)}, f32[32,1,128]{2,1,0:T(1,128)S(1)}, u32[]{:S(2)}, u32[]{:S(2)}) collective-permute-start(f32[32,1,128]{2,1,0:T(1,128)S(1)} %get-tuple-element.16), channel_id=1, source_target_pairs={{0,1},{1,2},{2,3},{3,4},{4,5},{5,6},{6,7},{7,8},{8,9},{9,10},{10,1... | collective-permute-start | bytes 49160 | tf_op jit(solution)/shard_map/ppermute | solution.py:14
  23.6 6.3 %collective-permute-done = f32[32,1,128]{2,1,0:T(1,128)S(1)} collective-permute-done((f32[32,1,128]{2,1,0:T(1,128)S(1)}, f32[32,1,128]{2,1,0:T(1,128)S(1)}, u32[]{:S(2)}, u32[]{:S(2)}) %collective-permute-start) | collective-permute-done | bytes 16416 | tf_op jit(solution)/shard_map/ppermute | solution.py:15
  30.7 2.6 %copy.118 = f32[32,64,256]{2,0,1:T(8,128)} copy(f32[32,64,256]{2,1,0:T(8,128)S(1)} %pad_maximum_fusion) | data formatting | bytes 4194304 | tf_op jit(solution)/shard_map/concatenate | solution.py:80
  33.8 3.8 %all-to-all-start = ((f32[32,64,256]{2,0,1:T(8,128)}), f32[32,64,256]{2,0,1:T(8,128)S(1)}, u32[]{:S(2)}, u32[]{:S(2)}) async-start(f32[32,64,256]{2,0,1:T(8,128)} %copy.118), calls=%async_computation | async-start | bytes 4194304 | tf_op jit(solution)/shard_map/all_to_all | solution.py:81
  37.6 5.4 %copy.128 = f32[1024,1024]{0,1:T(8,128)} copy(f32[1024,1024]{1,0:T(8,128)} %param.9) | data formatting | bytes 8388608 | tf_op args[4]
  42.9 1.7 reshape_reshape.3
  44.7 4.2 %copy.130 = f32[16,64,8,32]{1,0,3,2:T(8,128)} copy(f32[16,64,8,32]{1,3,2,0:T(8,128)} %bitcast.101) | data formatting | bytes 2097152 | tf_op jit(solution)/shard_map/transpose | solution.py:121
  48.8 2.0 reshape.32
  50.8 5.0 %fusion = f32[128,8,256]{2,1,0:T(8,128)} fusion(f32[1024,1024]{0,1:T(8,128)} %copy.128, f32[1024,256]{0,1:T(8,128)S(1)} %reshape.32), kind=kOutput, calls=%fused_computation | convolution fusion | flops 1610612736 | bytes 6291456 | tf_op jit(solution)/shard_map/dot_general | solution.py:76
  55.8 7.0 %all-to-all-done = f32[32,64,256]{2,0,1:T(8,128)S(1)} async-done(((f32[32,64,256]{2,0,1:T(8,128)}), f32[32,64,256]{2,0,1:T(8,128)S(1)}, u32[]{:S(2)}, u32[]{:S(2)}) %all-to-all-start) | async-done | bytes 2097184 | tf_op jit(solution)/shard_map/all_to_all | solution.py:81
  68.6 39.5 %all_to_all.56 = f32[128,8,512]{2,1,0:T(8,128)S(1)} all-to-all(f32[128,8,512]{2,1,0:T(8,128)S(1)} %pad_maximum_fusion.1), channel_id=1, replica_groups=mesh['px'=8,'py'=16] {'py','px'}, dimensions={0} | all-to-all | bytes 4194304 | tf_op jit(solution)/shard_map/all_to_all | solution.py:95
  108.2 1.9 convolution_bitcast_fusion.2
  112.0 3.0 %collective-permute-start.2 = (f32[128,1,256]{2,1,0:T(1,128)S(1)}, f32[128,1,256]{2,1,0:T(1,128)S(1)}, u32[]{:S(2)}, u32[]{:S(2)}) collective-permute-start(f32[128,1,256]{2,1,0:T(1,128)S(1)} %get-tuple-element.13), channel_id=1, source_target_pairs={{16,0},{32,16},{48,32},{64,48},{80,64},{96,80},{112,96},{1,112},{1... | collective-permute-start | bytes 393224 | tf_op jit(solution)/shard_map/ppermute | solution.py:60
  115.0 2.3 collective-permute-start.3
  117.7 5.7 %collective-permute-done.3 = f32[128,1,256]{2,1,0:T(1,128)S(1)} collective-permute-done((f32[128,1,256]{2,1,0:T(1,128)S(1)}, f32[128,1,256]{2,1,0:T(1,128)S(1)}, u32[]{:S(2)}, u32[]{:S(2)}) %collective-permute-start.3) | collective-permute-done | bytes 131104 | tf_op jit(solution)/shard_map/ppermute | solution.py:59
  124.2 35.2 %all_to_all.57 = f32[128,8,512]{2,1,0:T(8,128)S(1)} all-to-all(f32[128,8,512]{2,1,0:T(8,128)S(1)} %pad_maximum_fusion.2), channel_id=1, replica_groups=mesh['px'=8,'py'=16] {'py','px'}, dimensions={0} | all-to-all | bytes 4194304 | tf_op jit(solution)/shard_map/all_to_all | solution.py:95
  160.8 4.5 %convolution_bitcast_fusion.1 = f32[128,8,256]{2,1,0:T(8,128)} fusion(f32[1024,1024]{1,0:T(8,128)S(1)} %copy-done.1, f32[1024,512]{1,0:T(8,128)S(1)} %bitcast.90), kind=kOutput, calls=%fused_computation.14 | convolution fusion | flops 1610612736 | bytes 6291456 | tf_op jit(solution)/shard_map/dot_general | solution.py:76
  165.3 6.0 %all-to-all-start.4 = ((f32[128,8,256]{2,1,0:T(8,128)}), f32[128,8,256]{2,1,0:T(8,128)}, u32[]{:S(2)}, u32[]{:S(2)}) async-start(f32[128,8,256]{2,1,0:T(8,128)} %convolution_bitcast_fusion.1), calls=%async_computation.4 | async-start | bytes 2097152 | tf_op jit(solution)/shard_map/all_to_all | solution.py:105
  173.0 5.9 %collective-permute-start.4 = (f32[128,1,256]{2,1,0:T(1,128)S(1)}, f32[128,1,256]{2,1,0:T(1,128)S(1)}, u32[]{:S(2)}, u32[]{:S(2)}) collective-permute-start(f32[128,1,256]{2,1,0:T(1,128)S(1)} %get-tuple-element.11), channel_id=1, source_target_pairs={{16,0},{32,16},{48,32},{64,48},{80,64},{96,80},{112,96},{1,112},{1... | collective-permute-start | bytes 393224 | tf_op jit(solution)/shard_map/ppermute | solution.py:60
  178.8 2.2 collective-permute-start.5
  181.4 5.0 %collective-permute-done.4 = f32[128,1,256]{2,1,0:T(1,128)S(1)} collective-permute-done((f32[128,1,256]{2,1,0:T(1,128)S(1)}, f32[128,1,256]{2,1,0:T(1,128)S(1)}, u32[]{:S(2)}, u32[]{:S(2)}) %collective-permute-start.4) | collective-permute-done | bytes 131104 | tf_op jit(solution)/shard_map/ppermute | solution.py:60
  186.5 5.0 %collective-permute-done.5 = f32[128,1,256]{2,1,0:T(1,128)S(1)} collective-permute-done((f32[128,1,256]{2,1,0:T(1,128)S(1)}, f32[128,1,256]{2,1,0:T(1,128)S(1)}, u32[]{:S(2)}, u32[]{:S(2)}) %collective-permute-start.5) | collective-permute-done | bytes 131104 | tf_op jit(solution)/shard_map/ppermute | solution.py:59
  196.5 4.1 %bitcast_multiply_fusion.1 = (f32[128,8,256]{2,1,0:T(8,128)S(1)}, f32[256,8,128]{0,1,2:T(8,128)S(1)}) fusion(f32[256,8,128]{0,1,2:T(8,128)S(1)} %copy.160, f32[128,8,256]{2,1,0:T(8,128)} %all-to-all-done.4, f32[127,8,256]{2,1,0:T(8,128)S(1)} %slice.217, f32[128,8,256]{2,1,0:T(8,128)S(1)} %fusion.67, f32[127,8,256]{2,1,0:T(8,128)S(1)} %copy-done.8, ...), kind=kLoop, calls=%fused_computation.71 | loop fusion | flops 3932160 | bytes 15679488 | tf_op jit(solution)/shard_map/mul | solution.py:38
  200.7 3.2 %convolution_bitcast_fusion = f32[256,8,128]{0,1,2:T(8,128)S(1)} fusion(f32[128,8,256]{2,1,0:T(8,128)} %all-to-all-done.4, f32[127,8,256]{2,1,0:T(8,128)S(1)} %slice.218, f32[256,8,128]{0,1,2:T(8,128)S(1)} %copy.160, f32[127,8,256]{2,1,0:T(8,128)S(1)} %slice.217, f32[256,256]{1,0:T(8,128)S(1)} %copy-done), kind=kOutput, calls=%fused_computation.13 | convolution fusion | flops 405012480 | bytes 5488640 | tf_op jit(solution)/shard_map/dot_general | solution.py:71
  204.0 2.0 copy.146
  206.0 30.7 %all_to_all.58 = f32[256,8,256]{2,1,0:T(8,128)S(1)} all-to-all(f32[256,8,256]{2,1,0:T(8,128)} %copy.146), channel_id=1, replica_groups=mesh['px'=8,'py'=16] {'px'}, dimensions={0} | all-to-all | bytes 4194304 | tf_op jit(solution)/shard_map/all_to_all | solution.py:88
  237.3 2.8 %collective-permute-start.6 = (f32[32,1,128]{2,1,0:T(1,128)S(1)}, f32[32,1,128]{2,1,0:T(1,128)S(1)}, u32[]{:S(2)}, u32[]{:S(2)}) collective-permute-start(f32[32,1,128]{2,1,0:T(1,128)S(1)} %get-tuple-element.5), channel_id=1, source_target_pairs={{1,0},{2,1},{3,2},{4,3},{5,4},{6,5},{7,6},{8,7},{9,8},{10,9},{11,1... | collective-permute-start | bytes 49160 | tf_op jit(solution)/shard_map/ppermute | solution.py:15
  240.1 4.4 %collective-permute-start.7 = (f32[32,1,128]{2,1,0:T(1,128)S(1)}, f32[32,1,128]{2,1,0:T(1,128)S(1)}, u32[]{:S(2)}, u32[]{:S(2)}) collective-permute-start(f32[32,1,128]{2,1,0:T(1,128)S(1)} %get-tuple-element.6), channel_id=1, source_target_pairs={{0,1},{1,2},{2,3},{3,4},{4,5},{5,6},{6,7},{7,8},{8,9},{9,10},{10,1... | collective-permute-start | bytes 49160 | tf_op jit(solution)/shard_map/ppermute | solution.py:14
  244.6 1.8 slice_subtract_fusion
  (84 shorter events, 22.4 us)
Async XLA Ops:
  0.6 64.7 %copy-start = (f32[256,256]{1,0:T(8,128)S(1)}, f32[256,256]{1,0:T(8,128)}, u32[]{:S(2)}) copy-start(f32[256,256]{1,0:T(8,128)} %param.8) | copy-start | bytes 786436
  0.6 14.2 %copy-start.5 = (f32[32,64,128]{2,1,0:T(8,128)S(1)}, f32[32,64,128]{2,1,0:T(8,128)}, u32[]{:S(2)}) copy-start(f32[32,64,128]{2,1,0:T(8,128)} %param.5) | copy-start | bytes 3145732
  3.4 19.9 %copy-start.13 = (f32[32,64,128]{2,1,0:T(8,128)S(1)}, f32[32,64,128]{2,1,0:T(8,128)}, u32[]{:S(2)}) copy-start(f32[32,64,128]{2,1,0:T(8,128)} %param.6) | copy-start | bytes 3145732
  3.4 30.4 %all-to-all-start.1 = ((f32[128,8,256]{2,1,0:T(8,128)}), f32[128,8,256]{2,1,0:T(8,128)S(1)}, u32[]{:S(2)}, u32[]{:S(2)}) async-start(f32[128,8,256]{2,1,0:T(8,128)} %copy.129), calls=%async_computation.1 | async-start | bytes 2097152 | tf_op jit(solution)/shard_map/all_to_all | solution.py:95
  14.9 15.0 %collective-permute-start = (f32[32,1,128]{2,1,0:T(1,128)S(1)}, f32[32,1,128]{2,1,0:T(1,128)S(1)}, u32[]{:S(2)}, u32[]{:S(2)}) collective-permute-start(f32[32,1,128]{2,1,0:T(1,128)S(1)} %get-tuple-element.15), channel_id=1, source_target_pairs={{1,0},{2,1},{3,2},{4,3},{5,4},{6,5},{7,6},{8,7},{9,8},{10,9},{11,1... | collective-permute-start | bytes 49160 | tf_op jit(solution)/shard_map/ppermute | solution.py:15
  17.9 12.0 %collective-permute-start.1 = (f32[32,1,128]{2,1,0:T(1,128)S(1)}, f32[32,1,128]{2,1,0:T(1,128)S(1)}, u32[]{:S(2)}, u32[]{:S(2)}) collective-permute-start(f32[32,1,128]{2,1,0:T(1,128)S(1)} %get-tuple-element.16), channel_id=1, source_target_pairs={{0,1},{1,2},{2,3},{3,4},{4,5},{5,6},{6,7},{7,8},{8,9},{9,10},{10,1... | collective-permute-start | bytes 49160 | tf_op jit(solution)/shard_map/ppermute | solution.py:14
  22.3 1.0 copy-start.11
  33.8 29.0 %all-to-all-start = ((f32[32,64,256]{2,0,1:T(8,128)}), f32[32,64,256]{2,0,1:T(8,128)S(1)}, u32[]{:S(2)}, u32[]{:S(2)}) async-start(f32[32,64,256]{2,0,1:T(8,128)} %copy.118), calls=%async_computation | async-start | bytes 4194304 | tf_op jit(solution)/shard_map/all_to_all | solution.py:81
  66.0 1.0 copy-start.7
  67.0 1.2 copy-start.18
  68.5 39.6 %copy-start.1 = (f32[1024,1024]{1,0:T(8,128)S(1)}, f32[1024,1024]{1,0:T(8,128)}, u32[]{:S(2)}) copy-start(f32[1024,1024]{1,0:T(8,128)} %param.9) | copy-start | bytes 12582916
  108.1 2.1 copy-start.2
  108.2 2.4 copy-start.9
  111.9 5.6 %copy-start.16 = (f32[127,8,256]{2,1,0:T(8,128)}, f32[127,8,256]{2,1,0:T(8,128)S(1)}, u32[]{:S(2)}) copy-start(f32[127,8,256]{2,1,0:T(8,128)S(1)} %slice.213) | copy-start | bytes 3121156
  112.0 5.7 %collective-permute-start.2 = (f32[128,1,256]{2,1,0:T(1,128)S(1)}, f32[128,1,256]{2,1,0:T(1,128)S(1)}, u32[]{:S(2)}, u32[]{:S(2)}) collective-permute-start(f32[128,1,256]{2,1,0:T(1,128)S(1)} %get-tuple-element.13), channel_id=1, source_target_pairs={{16,0},{32,16},{48,32},{64,48},{80,64},{96,80},{112,96},{1,112},{1... | collective-permute-start | bytes 393224 | tf_op jit(solution)/shard_map/ppermute | solution.py:60
  115.0 8.4 %collective-permute-start.3 = (f32[128,1,256]{2,1,0:T(1,128)S(1)}, f32[128,1,256]{2,1,0:T(1,128)S(1)}, u32[]{:S(2)}, u32[]{:S(2)}) collective-permute-start(f32[128,1,256]{2,1,0:T(1,128)S(1)} %get-tuple-element.14), channel_id=1, source_target_pairs={{0,16},{16,32},{32,48},{48,64},{64,80},{80,96},{96,112},{112,1},{1... | collective-permute-start | bytes 393224 | tf_op jit(solution)/shard_map/ppermute | solution.py:59
  159.4 1.3 copy-start.3
  165.3 29.4 %all-to-all-start.4 = ((f32[128,8,256]{2,1,0:T(8,128)}), f32[128,8,256]{2,1,0:T(8,128)}, u32[]{:S(2)}, u32[]{:S(2)}) async-start(f32[128,8,256]{2,1,0:T(8,128)} %convolution_bitcast_fusion.1), calls=%async_computation.4 | async-start | bytes 2097152 | tf_op jit(solution)/shard_map/all_to_all | solution.py:105
  171.3 9.8 %copy-start.4 = (f32[128,8,512]{2,1,0:T(8,128)S(1)}, f32[128,8,512]{2,1,0:T(8,128)}, u32[]{:S(2)}) copy-start(f32[128,8,512]{2,1,0:T(8,128)} %copy-done.3) | copy-start | bytes 6291460
  172.8 8.5 %copy-start.17 = (f32[127,8,256]{2,1,0:T(8,128)}, f32[127,8,256]{2,1,0:T(8,128)S(1)}, u32[]{:S(2)}) copy-start(f32[127,8,256]{2,1,0:T(8,128)S(1)} %slice.222) | copy-start | bytes 3121156
  173.0 13.5 %collective-permute-start.4 = (f32[128,1,256]{2,1,0:T(1,128)S(1)}, f32[128,1,256]{2,1,0:T(1,128)S(1)}, u32[]{:S(2)}, u32[]{:S(2)}) collective-permute-start(f32[128,1,256]{2,1,0:T(1,128)S(1)} %get-tuple-element.11), channel_id=1, source_target_pairs={{16,0},{32,16},{48,32},{64,48},{80,64},{96,80},{112,96},{1,112},{1... | collective-permute-start | bytes 393224 | tf_op jit(solution)/shard_map/ppermute | solution.py:60
  178.8 12.6 %collective-permute-start.5 = (f32[128,1,256]{2,1,0:T(1,128)S(1)}, f32[128,1,256]{2,1,0:T(1,128)S(1)}, u32[]{:S(2)}, u32[]{:S(2)}) collective-permute-start(f32[128,1,256]{2,1,0:T(1,128)S(1)} %get-tuple-element.12), channel_id=1, source_target_pairs={{0,16},{16,32},{32,48},{48,64},{64,80},{80,96},{96,112},{112,1},{1... | collective-permute-start | bytes 393224 | tf_op jit(solution)/shard_map/ppermute | solution.py:59
  192.6 1.0 copy-start.15
  194.6 1.5 copy-start.8
  194.6 1.8 copy-start.10
  236.7 7.8 %copy-start.14 = (f32[32,64,128]{2,1,0:T(8,128)S(1)}, f32[32,64,128]{2,1,0:T(8,128)}, u32[]{:S(2)}) copy-start(f32[32,64,128]{2,1,0:T(8,128)} %param.6) | copy-start | bytes 3145732
  236.9 7.6 %copy-start.6 = (f32[32,64,128]{2,1,0:T(8,128)S(1)}, f32[32,64,128]{2,1,0:T(8,128)}, u32[]{:S(2)}) copy-start(f32[32,64,128]{2,1,0:T(8,128)} %param.5) | copy-start | bytes 3145732
  237.0 7.6 %copy-start.12 = (f32[32,64,127]{2,1,0:T(8,128)S(1)}, f32[32,64,127]{2,1,0:T(8,128)}, u32[]{:S(2)}) copy-start(f32[32,64,127]{2,1,0:T(8,128)} %copy-done.11) | copy-start | bytes 3121156
  237.3 9.1 %collective-permute-start.6 = (f32[32,1,128]{2,1,0:T(1,128)S(1)}, f32[32,1,128]{2,1,0:T(1,128)S(1)}, u32[]{:S(2)}, u32[]{:S(2)}) collective-permute-start(f32[32,1,128]{2,1,0:T(1,128)S(1)} %get-tuple-element.5), channel_id=1, source_target_pairs={{1,0},{2,1},{3,2},{4,3},{5,4},{6,5},{7,6},{8,7},{9,8},{10,9},{11,1... | collective-permute-start | bytes 49160 | tf_op jit(solution)/shard_map/ppermute | solution.py:15
  240.1 6.3 %collective-permute-start.7 = (f32[32,1,128]{2,1,0:T(1,128)S(1)}, f32[32,1,128]{2,1,0:T(1,128)S(1)}, u32[]{:S(2)}, u32[]{:S(2)}) collective-permute-start(f32[32,1,128]{2,1,0:T(1,128)S(1)} %get-tuple-element.6), channel_id=1, source_target_pairs={{0,1},{1,2},{2,3},{3,4},{4,5},{5,6},{6,7},{7,8},{8,9},{9,10},{10,1... | collective-permute-start | bytes 49160 | tf_op jit(solution)/shard_map/ppermute | solution.py:14
